TPU v7x, 32 devices: a whole 2x2x4 slice. The times are simulated.
32 devices in a mesh: group: 2 (over x), src: 4 (over z), tile: 4 (over y, core).
Axes of the slice: x: 2, y: 2, z: 4, core: 2. Of those that a mesh axis runs over, the one named last changes fastest.
Arguments:
- mask_param: float32 [2048, 256], P(('group', 'tile')), parts along dimension 0, may hold values from -6 to 6
- target_image: float32 [2048, 256], P(('group', 'tile')), parts along dimension 0, may hold values from 0 to 1
- source_weights: float32 [128], P(('group', 'src')), parts along dimension 0, may hold values from 0.36 to 8.2
- source_shifts: int32 [64, 2], P('src'), may hold values from -16 to 16, as said below
- pupil_map: float32 [2, 32, 32], replicated, may hold values from -1.4 to 1.4, as said below
Outputs:
- mask_final: float32 [2048, 256], P(('group', 'tile')), parts along dimension 0
- weights_final: float32 [128], P(('group', 'src')), parts along dimension 0
There are 2 independent parts, one for each index of `group`. A program takes and returns all parts, laid end to end along the dimension named above; an argument that names none is the same for every part. Nothing has to cross between parts.
Inputs may be any that keep to these rules, and one draw needn't show every extreme that they name: `source_shifts`: each of the two columns takes the value 16 on some source and the value -16 on another. `pupil_map`: zero outside the disc of radius 32 // 2 - 1 around box index (16, 16).
All inputs are finite; a program needn't handle non-finite values.
Results may differ from a plain program's by a relative error of at most 0.0003.
Values sent between devices are 32-bit elements; how exact they have to be, the bound alone decides.
No kernel may reach another device: no remote copies, remote signals or barrier semaphores. Data moves between devices by JAX's collectives and lax.ppermute only.
A program may use at most 64 MiB of HBM per device.

v0:
```python
import functools
import math

import jax
import jax.numpy as jnp
import ml_dtypes
import numpy as np
from jax import lax
from jax.experimental import pallas as pl
from jax.experimental.pallas import tpu as pltpu
from jax.sharding import PartitionSpec as P

MARGIN = 64
MAX_SHIFT = 16
MASK_RATE = 0.5
WEIGHT_RATE = 0.3
TINY_EPS = 1e-06
CHUNK = 8

bf16 = jnp.bfloat16
f32 = jnp.float32


def np_split(table):
    table = np.asarray(table, np.float64)
    high = table.astype(np.float32).astype(ml_dtypes.bfloat16)
    low = (table - high.astype(np.float64)).astype(np.float32).astype(ml_dtypes.bfloat16)
    return high, low


def phases(freqs, pixels, period):
    return 2.0 * math.pi * np.mod(np.outer(freqs, pixels), period) / period


def make_tables(tile_len, box_len, max_shift):
    period = tile_len + 2 * MARGIN
    grid = box_len + 2 * max_shift
    wide = np.arange(grid) - grid // 2
    pix = np.arange(tile_len)
    full = np.arange(period)
    points = np.arange(grid)
    box = np.arange(box_len)
    out = {}
    ang = phases(wide, pix, period)
    high, low = np_split(np.concatenate([np.cos(ang), -np.sin(ang)], 0).T / (period * tile_len))
    out["spec_cols"] = np.concatenate([high, low], 1)
    ang_rows = phases(wide, full, period)
    high, low = np_split(np.concatenate([np.cos(ang_rows), np.sin(ang_rows)], 0))
    out["spec_rows"] = np.concatenate([high, low], 0)
    ang = phases(points, points, grid)
    cos, sin = np.cos(ang), np.sin(ang)
    for name, table in (
        ("lane_fwd", np.block([[cos, sin], [-sin, cos]])),
        ("lane_back", np.block([[cos, -sin], [sin, cos]])),
    ):
        high, low = np_split(table)
        out[name] = np.block([[high, low], [high, np.zeros_like(low)]])
    ang = phases(points, box, grid)
    high, low = np_split(np.concatenate([np.cos(ang), np.sin(ang)], 0))
    out["row_fwd"] = np.concatenate([high, high, low], 1)
    high, low = np_split(np.concatenate([np.cos(ang).T, np.sin(ang).T], 0))
    out["row_back"] = np.concatenate([high, high, low], 1)
    def dirichlet(offset):
        theta = 2.0 * math.pi * ((pix + offset)[None, :] / period - points[:, None] / grid)
        orders = np.arange(1, box_len)
        return 1.0 + 2.0 * np.cos(orders[:, None, None] * theta[None]).sum(0)

    rows, cols = dirichlet(MARGIN), dirichlet(0)
    high, low = np_split(rows @ rows.T / grid)
    out["mix_rows"] = np.concatenate([high, high, low], 1)
    mix = cols @ cols.T / grid
    high, low = np_split(np.block([[mix, mix], [mix, mix]]))
    out["mix_cols"] = np.block([[high, low], [high, np.zeros_like(low)]])
    high, low = np_split(rows)
    out["target_rows"] = np.concatenate([high, low], 0)
    high, low = np_split(np.concatenate([cols, cols], 0).T)
    out["target_cols"] = np.concatenate([high, low], 1)
    ang = phases(wide, pix, period)
    cos, sin = np.cos(ang), np.sin(ang)
    high, low = np_split(np.block([[cos, sin], [-sin, cos]]))
    out["grad_cols"] = np.concatenate([high, high, low], 0)
    high, low = np_split(np.concatenate([np.cos(ang_rows).T, -np.sin(ang_rows).T], 1))
    out["grad_rows"] = np.concatenate([high, high, low], 1)
    return out


def split(value):
    high = value.astype(bf16)
    return high, (value - high.astype(f32)).astype(bf16)


def dot(left, right):
    return jnp.dot(left, right, preferred_element_type=f32)


def halves(value):
    width = value.shape[1] // 2
    return value[:, :width] + value[:, width:]


def lane_sign(rows, lanes, first):
    lane = lax.broadcasted_iota(jnp.int32, (rows, lanes), 1)
    return jnp.where(lane < lanes // 2, first, -first).astype(f32)


def swap(value):
    return pltpu.roll(value, value.shape[1] // 2, 1)


def sigmoid(value):
    return 1.0 / (1.0 + jnp.exp(-value))


def window_spectrum(window, t):
    grid = t["spec_cols"].shape[1] // 4
    high, low = split(window)
    cols = t["spec_cols"]
    mid = halves(dot(high, cols[...])) + dot(low, cols[:, : 2 * grid])
    mid_high, mid_low = split(mid)
    rows = t["spec_rows"]
    both = halves(dot(rows[: 2 * grid, :], jnp.concatenate([mid_high, mid_low], 1)))
    both = both + dot(rows[2 * grid :, :], mid_high)
    return both[:grid] + lane_sign(grid, 2 * grid, 1.0) * swap(both[grid:])


def lane_stage(blocks, table):
    rows = []
    for block in blocks:
        high, low = split(block)
        rows.append(jnp.concatenate([high, low], 1))
    return halves(dot(jnp.concatenate(rows, 0), table[...]))


def row_stage(blocks, table, sign):
    stacks = []
    for block in blocks:
        high, low = split(block)
        stacks.append(jnp.concatenate([high, low, high], 0))
    both = dot(table[...], jnp.concatenate(stacks, 1))
    width = blocks[0].shape[1]
    half = both.shape[0] // 2
    outs = []
    for i in range(len(blocks)):
        part = both[:, i * width : (i + 1) * width]
        outs.append(part[:half] + sign * swap(part[half:]))
    return outs


def place_pupils(shifts, roots, pupil_re, pupil_im, pr, pi):
    count = pr.shape[0]

    def one(s, carry):
        by = shifts[s, 1] + MAX_SHIFT
        pr[s] = pltpu.roll(pupil_re[...], by, 1) * roots[s]
        pi[s] = pltpu.roll(pupil_im[...], by, 1) * roots[s]
        return carry

    lax.fori_loop(0, count, one, 0, unroll=8)


def grid_fields(spec, shifts, t, pr, pi, plain, crossed, fields):
    count, box_len, lanes = pr.shape
    grid = lanes // 2
    plain[...] = spec
    crossed[...] = swap(spec)
    sign = lane_sign(grid, lanes, -1.0)

    def chunk(c, power):
        blocks = []
        for i in range(CHUNK):
            s = c * CHUNK + i
            at = shifts[s, 0] + MAX_SHIFT
            rows = pl.ds(at, box_len)
            blocks.append(pr[s] * plain[rows, :] + pi[s] * crossed[rows, :])
        mid = lane_stage(blocks, t["lane_fwd"])
        mids = [mid[i * box_len : (i + 1) * box_len] for i in range(CHUNK)]
        for i, field in enumerate(row_stage(mids, t["row_fwd"], sign)):
            fields[c * CHUNK + i] = field
            power = power + field * field
        return power

    return lax.fori_loop(0, count // CHUNK, chunk, jnp.zeros((grid, lanes), f32))


def grid_misfit(power, inv_dose, target, t):
    high, low = split(power)
    mid = halves(dot(jnp.concatenate([high, low], 1), t["mix_cols"][...]))
    high, low = split(mid)
    lit = dot(t["mix_rows"][...], jnp.concatenate([high, low, high], 0))
    return lit * inv_dose - target


def gather_back(misfit, shifts, scale, t, pr, pi, fields, acc_re, acc_im):
    count, box_len, lanes = pr.shape
    grid = lanes // 2
    acc_re[...] = jnp.zeros_like(acc_re)
    acc_im[...] = jnp.zeros_like(acc_im)
    sign = lane_sign(box_len, lanes, 1.0)

    def chunk(c, carry):
        blocks = [fields[c * CHUNK + i] * misfit for i in range(CHUNK)]
        mids = row_stage(blocks, t["row_back"], sign)
        hits = lane_stage(mids, t["lane_back"])
        for i in range(CHUNK):
            s = c * CHUNK + i
            rows = pl.ds(shifts[s, 0] + MAX_SHIFT, box_len)
            hit = hits[i * box_len : (i + 1) * box_len]
            acc_re[rows, :] += pr[s] * hit
            acc_im[rows, :] += pi[s] * hit
        return carry

    lax.fori_loop(0, count // CHUNK, chunk, 0)
    return (acc_re[...] + swap(acc_im[...])) * scale


def window_grads(backs, t):
    count = len(backs)
    grid = backs[0].shape[0]
    rows = []
    for back in backs:
        high, low = split(back)
        rows.append(jnp.concatenate([high, low, high], 1))
    mid = dot(jnp.concatenate(rows, 0), t["grad_cols"][...])
    width = mid.shape[1] // 2
    outs = []
    for k in range(count):
        part = mid[k * grid : (k + 1) * grid]
        high, low = split(jnp.concatenate([part[:, :width], part[:, width:]], 0))
        outs.append(dot(t["grad_rows"][...], jnp.concatenate([high, low, high], 0)))
    return outs


def updated_params(params, backs, t, tile, tiles):
    wins = window_grads(backs, t)
    tile_len = params[0].shape[0]
    grads, square = [], None
    for k in range(tiles):
        own = lax.rem(tile + tiles - k, tiles)
        has_prev = (own > 0).astype(f32)
        has_next = (own < tiles - 1).astype(f32)
        core = wins[k][MARGIN : MARGIN + tile_len]
        above = wins[(k + 1) % tiles][MARGIN + tile_len :] * has_prev
        below = wins[(k - 1) % tiles][:MARGIN] * has_next
        total = jnp.concatenate(
            [core[:MARGIN] + above, core[MARGIN:-MARGIN], core[-MARGIN:] + below], 0
        )
        mask = sigmoid(params[k])
        grad = total * (mask * (1.0 - mask))
        grads.append(grad)
        part = jnp.sum(grad * grad, axis=0, keepdims=True)
        square = part if square is None else square + part
    pixels = tiles * tile_len * tile_len
    rms = jnp.sqrt(jnp.sum(square, axis=1, keepdims=True) / pixels + TINY_EPS)
    rate = MASK_RATE / rms
    return [params[k] - grads[k] * rate for k in range(tiles)]


def tile_window(own, before, after, tile, tiles):
    has_prev = (tile > 0).astype(f32)
    has_next = (tile < tiles - 1).astype(f32)
    return jnp.concatenate(
        [sigmoid(before) * has_prev, sigmoid(own), sigmoid(after) * has_next], 0
    )


def target_kernel(names, target, *refs):
    t = dict(zip(names, refs))
    out = refs[len(names)]
    grid = out.shape[0]
    high, low = split(target[...])
    rows = t["target_rows"]
    both = dot(rows[...], high)
    mid = both[:grid] + both[grid:] + dot(rows[:grid, :], low)
    high, low = split(mid)
    cols = t["target_cols"]
    out[...] = halves(dot(high, cols[...])) + dot(low, cols[:, : 2 * grid])


def first_kernel(names, tiles, tile, shifts, roots, scal, pupil_re, pupil_im, target,
                 own, before, after, *refs):
    t = dict(zip(names, refs))
    back, pr, pi, plain, crossed, fields, acc_re, acc_im = refs[len(names):]
    here = tile[0]
    spec = window_spectrum(tile_window(own[...], before[...], after[...], here, tiles), t)
    place_pupils(shifts, roots, pupil_re, pupil_im, pr, pi)
    power = grid_fields(spec, shifts, t, pr, pi, plain, crossed, fields)
    misfit = grid_misfit(power, scal[0], target[...], t)
    back[...] = gather_back(misfit, shifts, scal[1], t, pr, pi, fields, acc_re, acc_im)


def next_kernel(names, tiles, tile, shifts, roots, scal, pupil_re, pupil_im, target, *refs):
    params = [ref[...] for ref in refs[:tiles]]
    backs = [ref[...] for ref in refs[tiles : 2 * tiles]]
    refs = refs[2 * tiles :]
    t = dict(zip(names, refs))
    outs = refs[len(names) : len(names) + tiles]
    back, pr, pi, plain, crossed, fields, acc_re, acc_im = refs[len(names) + tiles :]
    here = tile[0]
    params = updated_params(params, backs, t, here, tiles)
    for out, value in zip(outs, params):
        out[...] = value
    window = tile_window(params[0], params[1][-MARGIN:], params[-1][:MARGIN], here, tiles)
    spec = window_spectrum(window, t)
    place_pupils(shifts, roots, pupil_re, pupil_im, pr, pi)
    power = grid_fields(spec, shifts, t, pr, pi, plain, crossed, fields)
    misfit = grid_misfit(power, scal[0], target[...], t)
    back[...] = gather_back(misfit, shifts, scal[1], t, pr, pi, fields, acc_re, acc_im)


def last_kernel(names, tiles, tile, shifts, roots, scal, pupil_re, pupil_im, target, *refs):
    params = [ref[...] for ref in refs[:tiles]]
    backs = [ref[...] for ref in refs[tiles : 2 * tiles]]
    refs = refs[2 * tiles :]
    t = dict(zip(names, refs))
    final, terms, pr, pi, plain, crossed, fields = refs[len(names):]
    here = tile[0]
    params = updated_params(params, backs, t, here, tiles)
    final[...] = params[0]
    window = tile_window(params[0], params[1][-MARGIN:], params[-1][:MARGIN], here, tiles)
    spec = window_spectrum(window, t)
    place_pupils(shifts, roots, pupil_re, pupil_im, pr, pi)
    power = grid_fields(spec, shifts, t, pr, pi, plain, crossed, fields)
    misfit = grid_misfit(power, scal[0], target[...], t)

    def chunk(c, carry):
        rows = []
        for i in range(CHUNK):
            field = fields[c * CHUNK + i]
            rows.append(jnp.sum(field * field * misfit, axis=0, keepdims=True))
        terms[pl.ds(pl.multiple_of(c * CHUNK, CHUNK), CHUNK), :] = jnp.concatenate(rows, 0)
        return carry

    lax.fori_loop(0, fields.shape[0] // CHUNK, chunk, 0)


def weight_kernel(tiles, scale, tile, place, weights, *refs):
    terms = refs[:tiles]
    out, stack, new = refs[tiles:]
    for k in range(tiles):
        stack[k] = terms[k][...]
    here = tile[0]
    total = stack[lax.rem(here, tiles)]
    for k in range(1, tiles):
        total = total + stack[lax.rem(here + tiles - k, tiles)]
    weight = weights[...]
    dose = jnp.sum(weight, axis=0, keepdims=True)
    summed = jnp.sum(total, axis=1, keepdims=True) * scale
    mean = jnp.sum(summed, axis=0, keepdims=True) / dose
    grad = (summed / weight - mean) / dose
    count = weight.shape[0]
    spread = jnp.sqrt(jnp.sum(grad * grad, axis=0, keepdims=True) / count + TINY_EPS)
    new[...] = jnp.broadcast_to(weight * jnp.exp(-WEIGHT_RATE * grad / spread), new.shape)
    size = out.shape[0]
    out[...] = new[pl.ds(pl.multiple_of(place[0] * size, 8), size), :]


def ring(value, axis):
    peers = lax.axis_size(axis)
    got = [value]
    for k in range(1, peers):
        got.append(lax.ppermute(value, axis, [(i, (i + k) % peers) for i in range(peers)]))
    return got


def per_device(mask_param, target_image, source_weights, source_shifts, pupil_map):
    tile_len = mask_param.shape[1]
    box_len = pupil_map.shape[1]
    grid = box_len + 2 * MAX_SHIFT
    lanes = 2 * grid
    tiles = lax.axis_size("tile")
    peers = lax.axis_size("src")
    local = source_weights.shape[0]
    count = local * peers
    tables = make_tables(tile_len, box_len, MAX_SHIFT)

    tile = lax.axis_index("tile").astype(jnp.int32).reshape(1)
    place = lax.axis_index("src").astype(jnp.int32).reshape(1)

    packed = jnp.stack(
        [source_weights, source_shifts[:, 0].astype(f32), source_shifts[:, 1].astype(f32)]
    )
    slot = lax.broadcasted_iota(jnp.int32, (3, peers, local), 1)
    packed = jnp.where(slot == place[0], packed[:, None, :], 0.0).reshape(3, count)
    packed = sum(ring(packed, "src"))
    weights = packed[0]
    shifts = packed[1:].astype(jnp.int32).T
    dose = jnp.sum(weights)
    roots = jnp.sqrt(weights)
    scal = jnp.stack([1.0 / dose, 2.0 / (dose * (grid * grid) * ((tile_len + 2 * MARGIN) * tile_len))])

    down = [(i, (i + 1) % tiles) for i in range(tiles)]
    up = [(j, i) for i, j in down]
    before = lax.ppermute(mask_param[-MARGIN:], "tile", down)
    after = lax.ppermute(mask_param[:MARGIN], "tile", up)
    params = ring(mask_param, "tile")

    pad = ((0, 0), (0, grid - box_len))
    real, imag = jnp.pad(pupil_map[0], pad), jnp.pad(pupil_map[1], pad)
    pupil_re = jnp.concatenate([real, real], 1)
    pupil_im = jnp.concatenate([-imag, imag], 1)

    vmem = pl.BlockSpec(memory_space=pltpu.VMEM)
    smem = pl.BlockSpec(memory_space=pltpu.SMEM)
    params_of = pltpu.CompilerParams(vmem_limit_bytes=48 << 20)

    def struct(*shape):
        return jax.ShapeDtypeStruct(shape, f32)

    def pick(*names):
        return names, [jnp.asarray(tables[n]) for n in names]

    names, values = pick("target_rows", "target_cols")
    target = pl.pallas_call(
        functools.partial(target_kernel, names),
        out_shape=struct(grid, lanes),
        in_specs=[vmem] * (1 + len(names)),
        out_specs=vmem,
        compiler_params=params_of,
        cost_estimate=pl.CostEstimate(flops=4 << 24, bytes_accessed=1 << 20, transcendentals=0),
        name="target_terms",
    )(target_image, *values)

    core_scratch = [
        pltpu.VMEM((count, box_len, lanes), f32),
        pltpu.VMEM((count, box_len, lanes), f32),
        pltpu.VMEM((grid, lanes), f32),
        pltpu.VMEM((grid, lanes), f32),
        pltpu.VMEM((count, grid, lanes), f32),
    ]
    sums = [pltpu.VMEM((grid, lanes), f32)] * 2
    shared = (tile, shifts, roots, scal, pupil_re, pupil_im, target)
    shared_specs = [smem] * 4 + [vmem] * 3
    cost = pl.CostEstimate(flops=1 << 32, bytes_accessed=4 << 20, transcendentals=0)

    fwd = ("spec_cols", "spec_rows", "lane_fwd", "row_fwd", "mix_cols", "mix_rows")
    names, values = pick(*fwd, "lane_back", "row_back")
    back = pl.pallas_call(
        functools.partial(first_kernel, names, tiles),
        out_shape=struct(grid, lanes),
        in_specs=shared_specs + [vmem] * (3 + len(names)),
        out_specs=vmem,
        scratch_shapes=core_scratch + sums,
        compiler_params=params_of,
        cost_estimate=cost,
        name="first_step",
    )(*shared, mask_param, before, after, *values)

    backs = ring(back, "tile")
    names, values = pick(*fwd, "lane_back", "row_back", "grad_cols", "grad_rows")
    outs = pl.pallas_call(
        functools.partial(next_kernel, names, tiles),
        out_shape=[struct(tile_len, tile_len)] * tiles + [struct(grid, lanes)],
        in_specs=shared_specs + [vmem] * (2 * tiles + len(names)),
        out_specs=[vmem] * (tiles + 1),
        scratch_shapes=core_scratch + sums,
        compiler_params=params_of,
        cost_estimate=cost,
        name="next_step",
    )(*shared, *params, *backs, *values)
    params, back = outs[:tiles], outs[tiles]

    backs = ring(back, "tile")
    names, values = pick(*fwd, "grad_cols", "grad_rows")
    final, terms = pl.pallas_call(
        functools.partial(last_kernel, names, tiles),
        out_shape=[struct(tile_len, tile_len), struct(count, lanes)],
        in_specs=shared_specs + [vmem] * (2 * tiles + len(names)),
        out_specs=[vmem] * 2,
        scratch_shapes=core_scratch,
        compiler_params=params_of,
        cost_estimate=cost,
        name="last_step",
    )(*shared, *params, *backs, *values)

    terms = ring(terms, "tile")
    out = pl.pallas_call(
        functools.partial(weight_kernel, tiles, 1.0 / (grid * grid)),
        out_shape=struct(local, lanes),
        in_specs=[smem] * 2 + [vmem] * (1 + tiles),
        out_specs=vmem,
        scratch_shapes=[pltpu.VMEM((tiles, count, lanes), f32), pltpu.VMEM((count, lanes), f32)],
        compiler_params=params_of,
        name="weight_step",
    )(tile, place, weights[:, None], *terms)
    return final, out[:, 0]


def solution(mesh):
    in_specs = (
        P(("group", "tile"), None),
        P(("group", "tile"), None),
        P(("group", "src")),
        P("src", None),
        P(),
    )
    out_specs = (P(("group", "tile"), None), P(("group", "src")))
    return jax.shard_map(
        per_device, mesh=mesh, in_specs=in_specs, out_specs=out_specs, check_vma=False
    )
```

profile of v0, /device:TPU:0, one launch (start us, length us, event | category | flops | bytes accessed | tf_op | source)
XLA Modules:
  0.0 73.1 jit_solution(16546146125816833566)
XLA Ops:
  1.4 0.7 copy-done.18
  2.2 4.1 %collective-permute-start.1 = (f32[3,64]{0,1:T(8,128)S(1)}, f32[3,64]{0,1:T(8,128)S(1)}, u32[]{:S(2)}, u32[]{:S(2)}) collective-permute-start(f32[3,64]{0,1:T(8,128)S(1)} %bitcast_select_fusion), channel_id=1, source_target_pairs={{0,8},{4,12},{8,0},{12,4},{1,9},{5,13},{9,1},{13,5},{2,10},{6,14},... | collective-permute-start | bytes 2312 | tf_op jit(solution)/shard_map/ppermute | solution.py:361
  6.4 1.3 %collective-permute-start.2 = (f32[3,64]{0,1:T(8,128)S(1)}, f32[3,64]{0,1:T(8,128)S(1)}, u32[]{:S(2)}, u32[]{:S(2)}) collective-permute-start(f32[3,64]{0,1:T(8,128)S(1)} %bitcast_select_fusion), channel_id=1, source_target_pairs={{0,12},{4,0},{8,4},{12,8},{1,13},{5,1},{9,5},{13,9},{2,14},{6,2},{... | collective-permute-start | bytes 2312 | tf_op jit(solution)/shard_map/ppermute | solution.py:361
  7.7 0.7 collective-permute-start
  8.5 1.4 %collective-permute-start.4 = (f32[256,256]{1,0:T(8,128)}, f32[256,256]{1,0:T(8,128)S(1)}, u32[]{:S(2)}, u32[]{:S(2)}) collective-permute-start(f32[256,256]{1,0:T(8,128)} %refs_0_.3), channel_id=1, source_target_pairs={{0,2},{1,3},{2,0},{3,1},{4,6},{5,7},{6,4},{7,5},{8,10},{9,11},{10,... | collective-permute-start | bytes 786440 | tf_op jit(solution)/shard_map/ppermute | solution.py:361
  9.9 0.9 %fusion.1 = (f32[64,256]{1,0:T(8,128)S(1)}, f32[64,256]{1,0:T(8,128)S(1)}) fusion(f32[256,256]{1,0:T(8,128)} %refs_0_.3), kind=kLoop, calls=%fused_computation.18 | loop fusion | bytes 262144 | tf_op jit(solution)/shard_map/slice | solution.py:394
  11.0 0.7 %copy-done.1 = bf16[256,256]{1,0:T(8,128)(2,1)S(1)} copy-done((bf16[256,256]{1,0:T(8,128)(2,1)S(1)}, bf16[256,256]{1,0:T(8,128)(2,1)}, u32[]{:S(2)}) %copy-start.1) | copy-done | bytes 131096
  12.9 1.5 %collective-permute-start.7 = (f32[64,256]{1,0:T(8,128)S(1)}, f32[64,256]{1,0:T(8,128)S(1)}, u32[]{:S(2)}, u32[]{:S(2)}) collective-permute-start(f32[64,256]{1,0:T(8,128)S(1)} %get-tuple-element.18), channel_id=1, source_target_pairs={{1,0},{2,1},{3,2},{0,3},{5,4},{6,5},{7,6},{4,7},{9,8},{10,9},{11,1... | collective-permute-start | bytes 196616 | tf_op jit(solution)/shard_map/ppermute | solution.py:394
  16.7 4.8 %collective-permute-done.7.after = f32[64,256]{1,0:T(8,128)S(1)} collective-permute-done((f32[64,256]{1,0:T(8,128)S(1)}, f32[64,256]{1,0:T(8,128)S(1)}, u32[]{:S(2)}, u32[]{:S(2)}) %collective-permute-start.7) | collective-permute-done | bytes 65568 | tf_op jit(solution)/shard_map/ppermute | solution.py:394
  21.5 2.8 %collective-permute-done.6.before = f32[64,256]{1,0:T(8,128)S(1)} collective-permute-done((f32[64,256]{1,0:T(8,128)S(1)}, f32[64,256]{1,0:T(8,128)S(1)}, u32[]{:S(2)}, u32[]{:S(2)}) %collective-permute-start.6) | collective-permute-done | bytes 65568 | tf_op jit(solution)/shard_map/ppermute | solution.py:393
  24.4 0.9 %copy-done.9 = bf16[256,256]{1,0:T(8,128)(2,1)S(1)} copy-done((bf16[256,256]{1,0:T(8,128)(2,1)S(1)}, bf16[256,256]{1,0:T(8,128)(2,1)}, u32[]{:S(2)}) %copy-start.9) | copy-done | bytes 131096
  25.3 0.9 %copy-done.11 = bf16[256,256]{1,0:T(8,128)(2,1)S(1)} copy-done((bf16[256,256]{1,0:T(8,128)(2,1)S(1)}, bf16[256,256]{1,0:T(8,128)(2,1)}, u32[]{:S(2)}) %copy-start.11) | copy-done | bytes 131096
  26.2 10.5 %first_step.1.refs_4_ = f32[64,128]{1,0:T(8,128)S(1)} custom-call(s32[1]{0:T(128)} %bitcast.tile, s32[64,2]{1,0:T(8,128)S(1)} %fusion.shifts, f32[64]{0:T(128)S(1)} %get-tuple-element.17.roots, f32[2]{0:T(128)S(1)} %pad_maximum_fusion.3.scal, f32[32,128]{1,0:T(8,128)S(1)} %get-tuple-element.27.pupil_re, f32[32,128]{1,0:T(8,128)S(1)} %get-tuple-element.28.pupil_im, ...), custom_call_target="tpu_custom_call" | custom-call | flops 4294967296 | bytes 4194304 | tf_op jit(solution)/shard_map/first_step/pallas_call | solution.py:437
  36.7 1.7 %collective-permute-start.9 = (f32[64,128]{1,0:T(8,128)S(1)}, f32[64,128]{1,0:T(8,128)S(1)}, u32[]{:S(2)}, u32[]{:S(2)}) collective-permute-start(f32[64,128]{1,0:T(8,128)S(1)} %first_step.1.refs_4_), channel_id=1, source_target_pairs={{0,2},{1,3},{2,0},{3,1},{4,6},{5,7},{6,4},{7,5},{8,10},{9,11},{10,... | collective-permute-start | bytes 98312 | tf_op jit(solution)/shard_map/ppermute | solution.py:361
  38.4 1.9 %collective-permute-start.8 = (f32[64,128]{1,0:T(8,128)S(1)}, f32[64,128]{1,0:T(8,128)S(1)}, u32[]{:S(2)}, u32[]{:S(2)}) collective-permute-start(f32[64,128]{1,0:T(8,128)S(1)} %first_step.1.refs_4_), channel_id=1, source_target_pairs={{0,1},{1,2},{2,3},{3,0},{4,5},{5,6},{6,7},{7,4},{8,9},{9,10},{10,1... | collective-permute-start | bytes 98312 | tf_op jit(solution)/shard_map/ppermute | solution.py:361
  40.9 1.0 %collective-permute-done.8.refs_5_ = f32[64,128]{1,0:T(8,128)S(1)} collective-permute-done((f32[64,128]{1,0:T(8,128)S(1)}, f32[64,128]{1,0:T(8,128)S(1)}, u32[]{:S(2)}, u32[]{:S(2)}) %collective-permute-start.8) | collective-permute-done | bytes 32800 | tf_op jit(solution)/shard_map/ppermute | solution.py:361
  41.9 11.8 %next_step.1 = (f32[256,256]{1,0:T(8,128)S(1)}, f32[256,256]{1,0:T(8,128)S(1)}, f32[256,256]{1,0:T(8,128)S(1)}, f32[256,256]{1,0:T(8,128)S(1)}, f32[64,128]{1,0:T(8,128)S(1)}) custom-call(s32[1]{0:T(128)} %bitcast.tile, s32[64,2]{1,0:T(8,128)S(1)} %fusion.shifts, f32[64]{0:T(128)S(1)} %get-tuple-element.17.roots, f32[2]{0:T(128)S(1)} %pad_maximum_fusion.3.scal, ...), custom_call_target="tpu_custom_call" | custom-call | flops 4294967296 | bytes 4194304 | tf_op jit(solution)/shard_map/next_step/pallas_call | solution.py:450
  53.7 1.8 %collective-permute-start.12 = (f32[64,128]{1,0:T(8,128)S(1)}, f32[64,128]{1,0:T(8,128)S(1)}, u32[]{:S(2)}, u32[]{:S(2)}) collective-permute-start(f32[64,128]{1,0:T(8,128)S(1)} %get-tuple-element.13.refs_4_), channel_id=1, source_target_pairs={{0,2},{1,3},{2,0},{3,1},{4,6},{5,7},{6,4},{7,5},{8,10},{9,11},{10,... | collective-permute-start | bytes 98312 | tf_op jit(solution)/shard_map/ppermute | solution.py:361
  55.7 2.2 %collective-permute-done.12.refs_6_ = f32[64,128]{1,0:T(8,128)S(1)} collective-permute-done((f32[64,128]{1,0:T(8,128)S(1)}, f32[64,128]{1,0:T(8,128)S(1)}, u32[]{:S(2)}, u32[]{:S(2)}) %collective-permute-start.12) | collective-permute-done | bytes 32800 | tf_op jit(solution)/shard_map/ppermute | solution.py:361
  57.9 1.0 %collective-permute-done.11.refs_5_ = f32[64,128]{1,0:T(8,128)S(1)} collective-permute-done((f32[64,128]{1,0:T(8,128)S(1)}, f32[64,128]{1,0:T(8,128)S(1)}, u32[]{:S(2)}, u32[]{:S(2)}) %collective-permute-start.11) | collective-permute-done | bytes 32800 | tf_op jit(solution)/shard_map/ppermute | solution.py:361
  58.8 9.1 %last_step.1 = (f32[256,256]{1,0:T(8,128)}, f32[64,128]{1,0:T(8,128)S(1)}) custom-call(s32[1]{0:T(128)} %bitcast.tile, s32[64,2]{1,0:T(8,128)S(1)} %fusion.shifts, f32[64]{0:T(128)S(1)} %get-tuple-element.17.roots, f32[2]{0:T(128)S(1)} %pad_maximum_fusion.3.scal, f32[32,128]{1,0:T(8,128)S(1)} %get-tuple-element.27.pupil_re, ...), custom_call_target="tpu_custom_call" | custom-call | flops 4294967296 | bytes 4194304 | tf_op jit(solution)/shard_map/last_step/pallas_call | solution.py:464
  67.9 0.8 %collective-permute-start.15 = (f32[64,128]{1,0:T(8,128)S(1)}, f32[64,128]{1,0:T(8,128)S(1)}, u32[]{:S(2)}, u32[]{:S(2)}) collective-permute-start(f32[64,128]{1,0:T(8,128)S(1)} %get-tuple-element.15.refs_0_), channel_id=1, source_target_pairs={{0,2},{1,3},{2,0},{3,1},{4,6},{5,7},{6,4},{7,5},{8,10},{9,11},{10,... | collective-permute-start | bytes 98312 | tf_op jit(solution)/shard_map/ppermute | solution.py:361
  69.5 2.5 %collective-permute-done.15.refs_2_ = f32[64,128]{1,0:T(8,128)S(1)} collective-permute-done((f32[64,128]{1,0:T(8,128)S(1)}, f32[64,128]{1,0:T(8,128)S(1)}, u32[]{:S(2)}, u32[]{:S(2)}) %collective-permute-start.15) | collective-permute-done | bytes 32800 | tf_op jit(solution)/shard_map/ppermute | solution.py:361
  72.5 0.6 slice_reduce_fusion.1
  (70 shorter events, 5.2 us)
Async XLA Ops:
  2.2 9.9 %collective-permute-start.1 = (f32[3,64]{0,1:T(8,128)S(1)}, f32[3,64]{0,1:T(8,128)S(1)}, u32[]{:S(2)}, u32[]{:S(2)}) collective-permute-start(f32[3,64]{0,1:T(8,128)S(1)} %bitcast_select_fusion), channel_id=1, source_target_pairs={{0,8},{4,12},{8,0},{12,4},{1,9},{5,13},{9,1},{13,5},{2,10},{6,14},... | collective-permute-start | bytes 2312 | tf_op jit(solution)/shard_map/ppermute | solution.py:361
  6.4 6.5 %collective-permute-start.2 = (f32[3,64]{0,1:T(8,128)S(1)}, f32[3,64]{0,1:T(8,128)S(1)}, u32[]{:S(2)}, u32[]{:S(2)}) collective-permute-start(f32[3,64]{0,1:T(8,128)S(1)} %bitcast_select_fusion), channel_id=1, source_target_pairs={{0,12},{4,0},{8,4},{12,8},{1,13},{5,1},{9,5},{13,9},{2,14},{6,2},{... | collective-permute-start | bytes 2312 | tf_op jit(solution)/shard_map/ppermute | solution.py:361
  7.7 6.7 %collective-permute-start = (f32[3,64]{0,1:T(8,128)S(1)}, f32[3,64]{0,1:T(8,128)S(1)}, u32[]{:S(2)}, u32[]{:S(2)}) collective-permute-start(f32[3,64]{0,1:T(8,128)S(1)} %bitcast_select_fusion), channel_id=1, source_target_pairs={{0,4},{4,8},{8,12},{12,0},{1,5},{5,9},{9,13},{13,1},{2,6},{6,10},{... | collective-permute-start | bytes 2312 | tf_op jit(solution)/shard_map/ppermute | solution.py:361
  8.4 33.4 %collective-permute-start.5 = (f32[256,256]{1,0:T(8,128)}, f32[256,256]{1,0:T(8,128)S(1)}, u32[]{:S(2)}, u32[]{:S(2)}) collective-permute-start(f32[256,256]{1,0:T(8,128)} %refs_0_.3), channel_id=1, source_target_pairs={{0,3},{1,0},{2,1},{3,2},{4,7},{5,4},{6,5},{7,6},{8,11},{9,8},{10,9... | collective-permute-start | bytes 786440 | tf_op jit(solution)/shard_map/ppermute | solution.py:361
  8.5 33.3 %collective-permute-start.4 = (f32[256,256]{1,0:T(8,128)}, f32[256,256]{1,0:T(8,128)S(1)}, u32[]{:S(2)}, u32[]{:S(2)}) collective-permute-start(f32[256,256]{1,0:T(8,128)} %refs_0_.3), channel_id=1, source_target_pairs={{0,2},{1,3},{2,0},{3,1},{4,6},{5,7},{6,4},{7,5},{8,10},{9,11},{10,... | collective-permute-start | bytes 786440 | tf_op jit(solution)/shard_map/ppermute | solution.py:361
  10.9 13.4 %copy-start.15 = (bf16[64,192]{1,0:T(8,128)(2,1)S(1)}, bf16[64,192]{1,0:T(8,128)(2,1)}, u32[]{:S(2)}) copy-start(bf16[64,192]{1,0:T(8,128)(2,1)} %constant.52.clone.refs_7_.refs_15_) | copy-start | bytes 73732
  11.7 12.6 %copy-start.7 = (bf16[256,256]{1,0:T(8,128)(2,1)S(1)}, bf16[256,256]{1,0:T(8,128)(2,1)}, u32[]{:S(2)}) copy-start(bf16[256,256]{1,0:T(8,128)(2,1)} %constant.49.clone.refs_4_.refs_12_) | copy-start | bytes 393220
  11.7 12.6 %copy-start.8 = (bf16[256,256]{1,0:T(8,128)(2,1)S(1)}, bf16[256,256]{1,0:T(8,128)(2,1)}, u32[]{:S(2)}) copy-start(bf16[256,256]{1,0:T(8,128)(2,1)} %constant.47.clone.refs_2_.refs_10_) | copy-start | bytes 393220
  12.7 29.2 %collective-permute-start.3 = (f32[256,256]{1,0:T(8,128)S(1)}, f32[256,256]{1,0:T(8,128)S(1)}, u32[]{:S(2)}, u32[]{:S(2)}) collective-permute-start(f32[256,256]{1,0:T(8,128)S(1)} %copy-done.3), channel_id=1, source_target_pairs={{0,1},{1,2},{2,3},{3,0},{4,5},{5,6},{6,7},{7,4},{8,9},{9,10},{10,1... | collective-permute-start | bytes 786440 | tf_op jit(solution)/shard_map/ppermute | solution.py:361
  12.9 8.6 %collective-permute-start.7 = (f32[64,256]{1,0:T(8,128)S(1)}, f32[64,256]{1,0:T(8,128)S(1)}, u32[]{:S(2)}, u32[]{:S(2)}) collective-permute-start(f32[64,256]{1,0:T(8,128)S(1)} %get-tuple-element.18), channel_id=1, source_target_pairs={{1,0},{2,1},{3,2},{0,3},{5,4},{6,5},{7,6},{4,7},{9,8},{10,9},{11,1... | collective-permute-start | bytes 196616 | tf_op jit(solution)/shard_map/ppermute | solution.py:394
  14.4 9.9 %collective-permute-start.6 = (f32[64,256]{1,0:T(8,128)S(1)}, f32[64,256]{1,0:T(8,128)S(1)}, u32[]{:S(2)}, u32[]{:S(2)}) collective-permute-start(f32[64,256]{1,0:T(8,128)S(1)} %get-tuple-element.19), channel_id=1, source_target_pairs={{0,1},{1,2},{2,3},{3,0},{4,5},{5,6},{6,7},{7,4},{8,9},{9,10},{10,1... | collective-permute-start | bytes 196616 | tf_op jit(solution)/shard_map/ppermute | solution.py:393
  26.2 15.7 %copy-start.4 = (bf16[384,512]{1,0:T(8,128)(2,1)S(1)}, bf16[384,512]{1,0:T(8,128)(2,1)}, u32[]{:S(2)}) copy-start(bf16[384,512]{1,0:T(8,128)(2,1)} %constant.53.clone.refs_16_.refs_14_) | copy-start | bytes 1179652
  26.2 15.7 %copy-start.5 = (bf16[384,384]{1,0:T(8,128)(2,1)S(1)}, bf16[384,384]{1,0:T(8,128)(2,1)}, u32[]{:S(2)}) copy-start(bf16[384,384]{1,0:T(8,128)(2,1)} %constant.54.clone.refs_17_.refs_15_) | copy-start | bytes 884740
  26.2 15.7 %copy-start.10 = (bf16[256,256]{1,0:T(8,128)(2,1)S(1)}, bf16[256,256]{1,0:T(8,128)(2,1)}, u32[]{:S(2)}) copy-start(bf16[256,256]{1,0:T(8,128)(2,1)} %constant.45.clone.refs_0_.refs_8_) | copy-start | bytes 393220
  26.2 15.7 %copy-start.12 = (bf16[256,256]{1,0:T(8,128)(2,1)S(1)}, bf16[256,256]{1,0:T(8,128)(2,1)}, u32[]{:S(2)}) copy-start(bf16[256,256]{1,0:T(8,128)(2,1)} %constant.51.clone.refs_6_.refs_14_) | copy-start | bytes 393220
  36.7 1.7 %collective-permute-start.10 = (f32[64,128]{1,0:T(8,128)S(1)}, f32[64,128]{1,0:T(8,128)S(1)}, u32[]{:S(2)}, u32[]{:S(2)}) collective-permute-start(f32[64,128]{1,0:T(8,128)S(1)} %first_step.1.refs_4_), channel_id=1, source_target_pairs={{0,3},{1,0},{2,1},{3,2},{4,7},{5,4},{6,5},{7,6},{8,11},{9,8},{10,9... | collective-permute-start | bytes 98312 | tf_op jit(solution)/shard_map/ppermute | solution.py:361
  36.7 4.1 %collective-permute-start.9 = (f32[64,128]{1,0:T(8,128)S(1)}, f32[64,128]{1,0:T(8,128)S(1)}, u32[]{:S(2)}, u32[]{:S(2)}) collective-permute-start(f32[64,128]{1,0:T(8,128)S(1)} %first_step.1.refs_4_), channel_id=1, source_target_pairs={{0,2},{1,3},{2,0},{3,1},{4,6},{5,7},{6,4},{7,5},{8,10},{9,11},{10,... | collective-permute-start | bytes 98312 | tf_op jit(solution)/shard_map/ppermute | solution.py:361
  38.4 3.4 %collective-permute-start.8 = (f32[64,128]{1,0:T(8,128)S(1)}, f32[64,128]{1,0:T(8,128)S(1)}, u32[]{:S(2)}, u32[]{:S(2)}) collective-permute-start(f32[64,128]{1,0:T(8,128)S(1)} %first_step.1.refs_4_), channel_id=1, source_target_pairs={{0,1},{1,2},{2,3},{3,0},{4,5},{5,6},{6,7},{7,4},{8,9},{9,10},{10,1... | collective-permute-start | bytes 98312 | tf_op jit(solution)/shard_map/ppermute | solution.py:361
  53.7 2.0 %collective-permute-start.13 = (f32[64,128]{1,0:T(8,128)S(1)}, f32[64,128]{1,0:T(8,128)S(1)}, u32[]{:S(2)}, u32[]{:S(2)}) collective-permute-start(f32[64,128]{1,0:T(8,128)S(1)} %get-tuple-element.13.refs_4_), channel_id=1, source_target_pairs={{0,3},{1,0},{2,1},{3,2},{4,7},{5,4},{6,5},{7,6},{8,11},{9,8},{10,9... | collective-permute-start | bytes 98312 | tf_op jit(solution)/shard_map/ppermute | solution.py:361
  53.7 4.1 %collective-permute-start.12 = (f32[64,128]{1,0:T(8,128)S(1)}, f32[64,128]{1,0:T(8,128)S(1)}, u32[]{:S(2)}, u32[]{:S(2)}) collective-permute-start(f32[64,128]{1,0:T(8,128)S(1)} %get-tuple-element.13.refs_4_), channel_id=1, source_target_pairs={{0,2},{1,3},{2,0},{3,1},{4,6},{5,7},{6,4},{7,5},{8,10},{9,11},{10,... | collective-permute-start | bytes 98312 | tf_op jit(solution)/shard_map/ppermute | solution.py:361
  55.5 3.3 %collective-permute-start.11 = (f32[64,128]{1,0:T(8,128)S(1)}, f32[64,128]{1,0:T(8,128)S(1)}, u32[]{:S(2)}, u32[]{:S(2)}) collective-permute-start(f32[64,128]{1,0:T(8,128)S(1)} %get-tuple-element.13.refs_4_), channel_id=1, source_target_pairs={{0,1},{1,2},{2,3},{3,0},{4,5},{5,6},{6,7},{7,4},{8,9},{9,10},{10,1... | collective-permute-start | bytes 98312 | tf_op jit(solution)/shard_map/ppermute | solution.py:361
  67.9 1.6 %collective-permute-start.16 = (f32[64,128]{1,0:T(8,128)S(1)}, f32[64,128]{1,0:T(8,128)S(1)}, u32[]{:S(2)}, u32[]{:S(2)}) collective-permute-start(f32[64,128]{1,0:T(8,128)S(1)} %get-tuple-element.15.refs_0_), channel_id=1, source_target_pairs={{0,3},{1,0},{2,1},{3,2},{4,7},{5,4},{6,5},{7,6},{8,11},{9,8},{10,9... | collective-permute-start | bytes 98312 | tf_op jit(solution)/shard_map/ppermute | solution.py:361
  67.9 4.1 %collective-permute-start.15 = (f32[64,128]{1,0:T(8,128)S(1)}, f32[64,128]{1,0:T(8,128)S(1)}, u32[]{:S(2)}, u32[]{:S(2)}) collective-permute-start(f32[64,128]{1,0:T(8,128)S(1)} %get-tuple-element.15.refs_0_), channel_id=1, source_target_pairs={{0,2},{1,3},{2,0},{3,1},{4,6},{5,7},{6,4},{7,5},{8,10},{9,11},{10,... | collective-permute-start | bytes 98312 | tf_op jit(solution)/shard_map/ppermute | solution.py:361
  68.7 3.5 %collective-permute-start.14 = (f32[64,128]{1,0:T(8,128)S(1)}, f32[64,128]{1,0:T(8,128)S(1)}, u32[]{:S(2)}, u32[]{:S(2)}) collective-permute-start(f32[64,128]{1,0:T(8,128)S(1)} %get-tuple-element.15.refs_0_), channel_id=1, source_target_pairs={{0,1},{1,2},{2,3},{3,0},{4,5},{5,6},{6,7},{7,4},{8,9},{9,10},{10,1... | collective-permute-start | bytes 98312 | tf_op jit(solution)/shard_map/ppermute | solution.py:361
  (12 other events, 55.0 us)
where the time goes:
time: 73.4 us; the launch traced here: 73.1 us
  Pallas kernels  32 us (44%)
  starting transfers between devices  16 us (22%)
  waiting for transfers between devices  15.6 us (21%)
  local copies, waits for them, and re-layouts  6.22 us (8%)
  between operations  2.25 us (3%)
  other arithmetic  1.02 us (1%)
    ppermute x15, starting transfers between devices, ring(): lax.ppermute(value, axis, [(i, (i + k) % peers) for i in range(peers)])  14.5 us
    pallas_call x1, Pallas kernels, per_device(): pl.pallas_call(functools.partial(next_kernel, names, tiles), out_shape=[s...  11.8 us
    pallas_call x1, Pallas kernels, per_device(): pl.pallas_call(functools.partial(first_kernel, names, tiles), out_shape=s...  10.5 us
    pallas_call x1, Pallas kernels, per_device(): pl.pallas_call(functools.partial(last_kernel, names, tiles), out_shape=[s...  9.1 us
    ppermute x15, waiting for transfers between devices, ring(): lax.ppermute(value, axis, [(i, (i + k) % peers) for i in range(peers)])  7.99 us
    ppermute x1, waiting for transfers between devices, per_device(): after = lax.ppermute(mask_param[:MARGIN], 'tile', up)  4.83 us
    unnamed x38, local copies, waits for them, and re-layouts  4.44 us
    ppermute x1, waiting for transfers between devices, per_device(): before = lax.ppermute(mask_param[-MARGIN:], 'tile', down)  2.8 us
  transfers between devices with their start and end apart: 17, of which 9 were waited for; matrix products, arithmetic and copies ran while one was open for 2% of the time, Pallas kernels for 15%

commit v1 on v0

v1 whole, which is shorter than its diff:
```python
import functools
import math

import jax
import jax.numpy as jnp
import ml_dtypes
import numpy as np
from jax import lax
from jax.experimental import pallas as pl
from jax.experimental.pallas import tpu as pltpu
from jax.sharding import PartitionSpec as P

MARGIN = 64
MAX_SHIFT = 16
MASK_RATE = 0.5
WEIGHT_RATE = 0.3
TINY_EPS = 1e-06
CHUNK = 16

bf16 = jnp.bfloat16
f32 = jnp.float32


def np_split(table):
    table = np.asarray(table, np.float64)
    high = table.astype(np.float32).astype(ml_dtypes.bfloat16)
    low = (table - high.astype(np.float64)).astype(np.float32).astype(ml_dtypes.bfloat16)
    return high, low


def phases(freqs, pixels, period):
    return 2.0 * math.pi * np.mod(np.outer(freqs, pixels), period) / period


def make_tables(tile_len, box_len, max_shift):
    period = tile_len + 2 * MARGIN
    grid = box_len + 2 * max_shift
    wide = np.arange(grid) - grid // 2
    pix = np.arange(tile_len)
    full = np.arange(period)
    points = np.arange(grid)
    box = np.arange(box_len)
    out = {}
    ang = phases(wide, pix, period)
    high, low = np_split(np.concatenate([np.cos(ang), -np.sin(ang)], 0).T / (period * tile_len))
    out["spec_cols"] = np.concatenate([high, low], 1)
    ang_rows = phases(wide, full, period)
    high, low = np_split(np.concatenate([np.cos(ang_rows), np.sin(ang_rows)], 0))
    out["spec_rows"] = np.concatenate([high, low], 0)
    ang = phases(points, points, grid)
    cos, sin = np.cos(ang), np.sin(ang)
    for name, table in (
        ("lane_fwd", np.block([[cos, sin], [-sin, cos]])),
        ("lane_back", np.block([[cos, -sin], [sin, cos]])),
    ):
        high, low = np_split(table)
        out[name] = np.block([[high, low], [high, np.zeros_like(low)]])
    ang = phases(points, box, grid)
    high, low = np_split(np.concatenate([np.cos(ang), np.sin(ang)], 1))
    out["row_fwd"] = np.concatenate([high, high, low], 1)
    high, low = np_split(np.concatenate([np.cos(ang).T, np.sin(ang).T], 0))
    out["row_back"] = np.concatenate([high, high, low], 1)
    def dirichlet(offset):
        theta = 2.0 * math.pi * ((pix + offset)[None, :] / period - points[:, None] / grid)
        orders = np.arange(1, box_len)
        return 1.0 + 2.0 * np.cos(orders[:, None, None] * theta[None]).sum(0)

    rows, cols = dirichlet(MARGIN), dirichlet(0)
    high, low = np_split(rows @ rows.T / grid)
    out["mix_rows"] = np.concatenate([high, high, low], 1)
    mix = cols @ cols.T / grid
    high, low = np_split(np.block([[mix, mix], [mix, mix]]))
    out["mix_cols"] = np.block([[high, low], [high, np.zeros_like(low)]])
    high, low = np_split(rows)
    out["target_rows"] = np.concatenate([high, low], 0)
    high, low = np_split(np.concatenate([cols, cols], 0).T)
    out["target_cols"] = np.concatenate([high, low], 1)
    ang = phases(wide, pix, period)
    cos, sin = np.cos(ang), np.sin(ang)
    high, low = np_split(np.block([[cos, sin], [-sin, cos]]))
    out["grad_cols"] = np.concatenate([high, high, low], 0)
    high, low = np_split(np.concatenate([np.cos(ang_rows).T, -np.sin(ang_rows).T], 1))
    out["grad_rows"] = np.concatenate([high, high, low], 1)
    return out


def split(value):
    high = value.astype(bf16)
    return high, (value - high.astype(f32)).astype(bf16)


def dot(left, right):
    return jnp.dot(left, right, preferred_element_type=f32)


def halves(value):
    width = value.shape[1] // 2
    return value[:, :width] + value[:, width:]


def lane_sign(rows, lanes, first):
    lane = lax.broadcasted_iota(jnp.int32, (rows, lanes), 1)
    return jnp.where(lane < lanes // 2, first, -first).astype(f32)


def swap(value):
    return pltpu.roll(value, value.shape[1] // 2, 1)


def half_tanh(value):
    return jnp.tanh(0.5 * value)


def sigmoid(value):
    return 0.5 * half_tanh(value) + 0.5


def window_spectrum(window, t):
    grid = t["spec_cols"].shape[1] // 4
    high, low = split(window)
    cols = t["spec_cols"]
    mid = halves(dot(high, cols[...])) + dot(low, cols[:, : 2 * grid])
    mid_high, mid_low = split(mid)
    rows = t["spec_rows"]
    both = halves(dot(rows[: 2 * grid, :], jnp.concatenate([mid_high, mid_low], 1)))
    both = both + dot(rows[2 * grid :, :], mid_high)
    return both[:grid] + lane_sign(grid, 2 * grid, 1.0) * swap(both[grid:])


def skewed(count, first, second, carry):
    chunks = count // CHUNK
    first(0)

    def body(c, carry):
        carry = second(c - 1, carry)
        first(c)
        return carry

    carry = lax.fori_loop(1, chunks, body, carry)
    return second(chunks - 1, carry)


def place_pupils(shifts, roots, pupil_re, pupil_im, pr, pi):
    count = pr.shape[0]

    def one(s, carry):
        by = shifts[2, s] + MAX_SHIFT
        pr[s] = pltpu.roll(pupil_re[...], by, 1) * roots[3, s]
        pi[s] = pltpu.roll(pupil_im[...], by, 1) * roots[3, s]
        return carry

    lax.fori_loop(0, count, one, 0, unroll=8)


def grid_fields(spec, shifts, t, pr, pi, work):
    plain, crossed, fields, stage = work
    count, box_len, lanes = pr.shape
    grid = lanes // 2
    plain[...] = spec
    crossed[...] = swap(spec)
    sign = lane_sign(box_len, lanes, -1.0)

    def first(c):
        rows = []
        for i in range(CHUNK):
            s = c * CHUNK + i
            at = pl.ds(shifts[1, s] + MAX_SHIFT, box_len)
            high, low = split(pr[s] * plain[at, :] + pi[s] * crossed[at, :])
            rows.append(jnp.concatenate([high, low], 1))
        mid = halves(dot(jnp.concatenate(rows, 0), t["lane_fwd"][...]))
        for i in range(CHUNK):
            part = mid[i * box_len : (i + 1) * box_len]
            at = slice(i * lanes, (i + 1) * lanes)
            high, low = split(part)
            stage[:box_len, at] = high
            stage[2 * box_len : 3 * box_len, at] = low
            high, low = split(sign * swap(part))
            stage[box_len : 2 * box_len, at] = high
            stage[3 * box_len :, at] = low

    def second(c, power):
        value = stage[...]
        out = dot(t["row_fwd"][...], jnp.concatenate([value, value[: 2 * box_len]], 0))
        for i in range(CHUNK):
            field = out[:, i * lanes : (i + 1) * lanes]
            fields[c * CHUNK + i] = field
            power = power + field * field
        return power

    return skewed(count, first, second, jnp.zeros((grid, lanes), f32))


def grid_misfit(power, inv_dose, target, t):
    high, low = split(power)
    mid = halves(dot(jnp.concatenate([high, low], 1), t["mix_cols"][...]))
    high, low = split(mid)
    lit = dot(t["mix_rows"][...], jnp.concatenate([high, low, high], 0))
    return lit * inv_dose - target


def gather_back(misfit, shifts, scale, t, pr, pi, fields, stage, sums):
    count, box_len, lanes = pr.shape
    for ref in sums:
        ref[...] = jnp.zeros_like(ref)
    sign = lane_sign(box_len, lanes, 1.0)

    def first(c):
        stacks = []
        for i in range(CHUNK):
            high, low = split(fields[c * CHUNK + i] * misfit)
            stacks.append(jnp.concatenate([high, low, high], 0))
        both = dot(t["row_back"][...], jnp.concatenate(stacks, 1))
        for i in range(CHUNK):
            part = both[:, i * lanes : (i + 1) * lanes]
            part = part[:box_len] + sign * swap(part[box_len:])
            at = slice(i * box_len, (i + 1) * box_len)
            high, low = split(part)
            stage[at, :lanes] = high
            stage[at, lanes:] = low

    def second(c, carry):
        hits = halves(dot(stage[...], t["lane_back"][...]))
        for i in range(CHUNK):
            s = c * CHUNK + i
            rows = pl.ds(shifts[1, s] + MAX_SHIFT, box_len)
            hit = hits[i * box_len : (i + 1) * box_len]
            one, two = sums[2 * (i % 2)], sums[2 * (i % 2) + 1]
            one[rows, :] += pr[s] * hit
            two[rows, :] += pi[s] * hit
        return carry

    skewed(count, first, second, 0)
    return (sums[0][...] + sums[2][...] + swap(sums[1][...] + sums[3][...])) * scale


def tile_of(k, tile, tiles):
    return lax.rem(tile + tiles - k, tiles)


def mask_grads(params, ids, backs, t, tile, tiles, zed, wins, grads):
    grid = backs[0].shape[0]
    tile_len = wins.shape[2]
    rows = []
    for back in backs:
        high, low = split(back[...])
        rows.append(jnp.concatenate([high, low, high], 1))
    mid = dot(jnp.concatenate(rows, 0), t["grad_cols"][...])
    wins[0, MARGIN + tile_len :, :] = jnp.zeros((MARGIN, tile_len), f32)
    wins[tiles + 1, :MARGIN, :] = jnp.zeros((MARGIN, tile_len), f32)
    for k in range(tiles):
        part = mid[k * grid : (k + 1) * grid]
        high, low = split(jnp.concatenate([part[:, :tile_len], part[:, tile_len:]], 0))
        out = dot(t["grad_rows"][...], jnp.concatenate([high, low, high], 0))
        wins[tile_of(k, tile, tiles) + 1] = out
    square = jnp.zeros((8, tile_len), f32)
    for k in range(tiles):
        own = ids[k]
        for low_row, high_row, near, shift in (
            (0, MARGIN, 0, tile_len),
            (MARGIN, tile_len - MARGIN, 1, 0),
            (tile_len - MARGIN, tile_len, 2, -tile_len),
        ):
            total = wins[own + 1, MARGIN + low_row : MARGIN + high_row, :]
            if near != 1:
                at = MARGIN + low_row + shift
                total = total + wins[own + near, at : at + MARGIN, :]
            lean = half_tanh(params(k, low_row, high_row))
            grad = total * (1.0 - lean * lean)
            grads[own, low_row:high_row, :] = grad
            square = square + jnp.sum((grad * grad).reshape(-1, 8, tile_len), axis=0)
    total = jnp.sum(jnp.sum(square, axis=0, keepdims=True), axis=1, keepdims=True)
    pixels = tiles * tile_len * tile_len
    return MASK_RATE / jnp.sqrt(total / pixels + TINY_EPS)


def edge_rows(tile, tiles, tile_len):
    above = pl.multiple_of(jnp.maximum(tile * tile_len - MARGIN, 0), MARGIN)
    below = jnp.minimum((tile + 1) * tile_len, tiles * tile_len - MARGIN)
    below = pl.multiple_of(below, MARGIN)
    return above, below, (tile > 0).astype(f32), (tile < tiles - 1).astype(f32)


def target_kernel(names, target, *refs):
    t = dict(zip(names, refs))
    out = refs[len(names)]
    grid = out.shape[0]
    high, low = split(target[...])
    rows = t["target_rows"]
    both = dot(rows[...], high)
    mid = both[:grid] + both[grid:] + dot(rows[:grid, :], low)
    high, low = split(mid)
    cols = t["target_cols"]
    out[...] = halves(dot(high, cols[...])) + dot(low, cols[:, : 2 * grid])


def pack_kernel(place, weights, shifts, out):
    local = weights.shape[1]
    out[...] = jnp.zeros_like(out)
    out[0:1, :local] = weights[...]
    out[1:3, :local] = shifts[...].astype(f32)
    out[3:4, :local] = jnp.sqrt(weights[...])
    out[...] = pltpu.roll(out[...], place[0] * local, 1)


def doses(info, scale):
    dose = jnp.sum(info[0:1, :], axis=1, keepdims=True)
    return 1.0 / dose, scale / dose


def first_kernel(names, peers, tiles, scale, tile, pupil_re, pupil_im, target,
                 own, before, after, *refs):
    parts = refs[:peers]
    t = dict(zip(names, refs[peers:]))
    back, pr, pi, info, whole = refs[peers + len(names) : peers + len(names) + 5]
    (plain, crossed, fields, stage, hold, *sums, shifts, roots, sems) = refs[
        peers + len(names) + 5 :
    ]
    here = tile[0]
    total = parts[0][...]
    for part in parts[1:]:
        total = total + part[...]
    info[...] = total
    whole[...] = total.astype(jnp.int32)
    copies = (
        pltpu.make_async_copy(whole, shifts, sems.at[0]),
        pltpu.make_async_copy(info, roots, sems.at[1]),
    )
    for copy in copies:
        copy.start()
    has_prev = (here > 0).astype(f32)
    has_next = (here < tiles - 1).astype(f32)
    window = jnp.concatenate(
        [sigmoid(before[...]) * has_prev, sigmoid(own[...]), sigmoid(after[...]) * has_next], 0
    )
    spec = window_spectrum(window, t)
    for copy in copies:
        copy.wait()
    place_pupils(shifts, roots, pupil_re, pupil_im, pr, pi)
    power = grid_fields(spec, shifts, t, pr, pi, (plain, crossed, fields, stage))
    inv_dose, factor = doses(total, scale)
    misfit = grid_misfit(power, inv_dose, target[...], t)
    back[...] = gather_back(misfit, shifts, factor, t, pr, pi, fields, hold, sums)


def next_kernel(names, tiles, scale, tile, shifts, info, pr, pi, target, *refs):
    params, backs = refs[:tiles], refs[tiles : 2 * tiles]
    refs = refs[2 * tiles :]
    t = dict(zip(names, refs))
    new, back, plain, crossed, fields, stage, hold, *rest = refs[len(names) :]
    sums, (wins, grads) = rest[:4], rest[4:]
    here = tile[0]
    tile_len = params[0].shape[0]
    ids = entry_ids(here, tiles)
    rate = mask_grads(
        lambda k, low, high: params[k][low:high, :], ids, backs, t, here, tiles, None, wins, grads
    )
    for k in range(tiles):
        own = ids[k]
        at = pl.ds(pl.multiple_of(own * tile_len, tile_len), tile_len)
        new[at, :] = params[k][...] - grads[own] * rate
    above, below, has_prev, has_next = edge_rows(here, tiles, tile_len)
    own = pl.ds(pl.multiple_of(here * tile_len, tile_len), tile_len)
    window = jnp.concatenate(
        [
            sigmoid(new[pl.ds(above, MARGIN), :]) * has_prev,
            sigmoid(new[own, :]),
            sigmoid(new[pl.ds(below, MARGIN), :]) * has_next,
        ],
        0,
    )
    spec = window_spectrum(window, t)
    power = grid_fields(spec, shifts, t, pr, pi, (plain, crossed, fields, stage))
    inv_dose, factor = doses(info[...], scale)
    misfit = grid_misfit(power, inv_dose, target[...], t)
    back[...] = gather_back(misfit, shifts, factor, t, pr, pi, fields, hold, sums)


def last_kernel(names, tiles, tile, shifts, info, pr, pi, target, params, *refs):
    backs = refs[:tiles]
    refs = refs[tiles:]
    t = dict(zip(names, refs))
    final, row, plain, crossed, fields, stage, terms, wins, grads = refs[len(names) :]
    here = tile[0]
    tile_len = final.shape[0]
    rate = mask_grads(
        lambda k, low, high: params[k * tile_len + low : k * tile_len + high, :],
        list(range(tiles)), backs, t, here, tiles, None, wins, grads,
    )
    above, below, has_prev, has_next = edge_rows(here, tiles, tile_len)
    own = pl.ds(pl.multiple_of(here * tile_len, tile_len), tile_len)
    final[...] = params[own, :] - grads[here] * rate
    prev, follow = jnp.maximum(here - 1, 0), jnp.minimum(here + 1, tiles - 1)
    window = jnp.concatenate(
        [
            sigmoid(params[pl.ds(above, MARGIN), :] - grads[prev, tile_len - MARGIN :, :] * rate)
            * has_prev,
            sigmoid(final[...]),
            sigmoid(params[pl.ds(below, MARGIN), :] - grads[follow, :MARGIN, :] * rate)
            * has_next,
        ],
        0,
    )
    spec = window_spectrum(window, t)
    power = grid_fields(spec, shifts, t, pr, pi, (plain, crossed, fields, stage))
    inv_dose, _ = doses(info[...], 1.0)
    misfit = grid_misfit(power, inv_dose, target[...], t)

    def chunk(c, carry):
        rows = []
        for i in range(CHUNK):
            field = fields[c * CHUNK + i]
            rows.append(jnp.sum(field * field * misfit, axis=0, keepdims=True))
        terms[pl.ds(pl.multiple_of(c * CHUNK, CHUNK), CHUNK), :] = jnp.concatenate(rows, 0)
        return carry

    count = fields.shape[0]
    lax.fori_loop(0, count // CHUNK, chunk, 0)
    high, low = split(terms[...])
    left = terms[...] - high.astype(f32) - low.astype(f32)
    ones = jnp.ones((8, terms.shape[1]), bf16)
    total = jnp.zeros((8, terms.shape[0]), f32)
    for part in (left.astype(bf16), low, high):
        total = total + lax.dot_general(
            ones, part, (((1,), (1,)), ((), ())), preferred_element_type=f32
        )
    row[...] = total


def weight_kernel(tiles, scale, tile, place, info, *refs):
    rows = refs[:tiles]
    out, stack = refs[tiles:]
    count = rows[0].shape[1]
    for k in range(tiles):
        stack[k] = rows[k][...]
    here = tile[0]
    total = stack[lax.rem(here, tiles)]
    for k in range(1, tiles):
        total = total + stack[tile_of(k, here, tiles)]
    summed = total[0:1] * scale
    weight = info[0:1, :count]
    dose = jnp.sum(weight, axis=1, keepdims=True)
    mean = jnp.sum(summed, axis=1, keepdims=True) / dose
    grad = (summed / weight - mean) / dose
    spread = jnp.sqrt(jnp.sum(grad * grad, axis=1, keepdims=True) / count + TINY_EPS)
    new = weight * jnp.exp(-WEIGHT_RATE * grad / spread)
    size = out.shape[1]
    lanes = info.shape[1]
    if count < lanes:
        new = jnp.concatenate([new, jnp.zeros((1, lanes - count), f32)], 1)
    new = pltpu.roll(jnp.broadcast_to(new, (8, lanes)), lanes - place[0] * size, 1)
    out[...] = new[0:1, :size]


def ring(value, axis):
    peers = lax.axis_size(axis)
    return [value] + [
        lax.ppermute(value, axis, [(i, (i + k) % peers) for i in range(peers)])
        for k in range(1, peers)
    ]


def mates(value):
    return lax.ppermute(value, "tile", [(i, i ^ 1) for i in range(lax.axis_size("tile"))])


def far_steps(tiles):
    return range(2, tiles, 2)


def entry_ids(tile, tiles):
    even = [tile] + [tile_of(k, tile, tiles) for k in far_steps(tiles)]
    return even + [one + 1 - 2 * lax.rem(one, 2) for one in even]


def per_device(mask_param, target_image, source_weights, source_shifts, pupil_map):
    tile_len = mask_param.shape[1]
    box_len = pupil_map.shape[1]
    grid = box_len + 2 * MAX_SHIFT
    lanes = 2 * grid
    tiles = lax.axis_size("tile")
    peers = lax.axis_size("src")
    local = source_weights.shape[0]
    count = local * peers
    assert tiles % 2 == 0 and count <= 128 and count % CHUNK == 0
    tables = make_tables(tile_len, box_len, MAX_SHIFT)

    tile = lax.axis_index("tile").astype(jnp.int32).reshape(1)
    place = lax.axis_index("src").astype(jnp.int32).reshape(1)

    vmem = pl.BlockSpec(memory_space=pltpu.VMEM)
    smem = pl.BlockSpec(memory_space=pltpu.SMEM)
    params_of = pltpu.CompilerParams(vmem_limit_bytes=48 << 20)

    def struct(*shape, kind=f32):
        return jax.ShapeDtypeStruct(shape, kind)

    def pick(*names):
        return names, [jnp.asarray(tables[n]) for n in names]

    def cost(flops):
        return pl.CostEstimate(flops=flops, bytes_accessed=1 << 20, transcendentals=0)

    down = [(i, (i + 1) % tiles) for i in range(tiles)]
    up = [(j, i) for i, j in down]
    before = lax.ppermute(mask_param[-MARGIN:], "tile", down)
    after = lax.ppermute(mask_param[:MARGIN], "tile", up)

    packed = pl.pallas_call(
        pack_kernel,
        out_shape=struct(8, 128),
        in_specs=[smem, vmem, vmem],
        out_specs=vmem,
        compiler_params=params_of,
        name="pack_sources",
    )(place, source_weights[None], source_shifts.T)
    packed = ring(packed, "src")

    pad = ((0, 0), (0, grid - box_len))
    real, imag = jnp.pad(pupil_map[0], pad), jnp.pad(pupil_map[1], pad)
    pupil_re = jnp.concatenate([real, real], 1)
    pupil_im = jnp.concatenate([-imag, imag], 1)

    names, values = pick("target_rows", "target_cols")
    target = pl.pallas_call(
        functools.partial(target_kernel, names),
        out_shape=struct(grid, lanes),
        in_specs=[vmem] * (1 + len(names)),
        out_specs=vmem,
        compiler_params=params_of,
        cost_estimate=cost(1 << 26),
        name="target_terms",
    )(target_image, *values)

    before, after, packed, source = lax.optimization_barrier((before, after, packed, mask_param))
    far = [
        lax.ppermute(source, "tile", [(i, (i + k) % tiles) for i in range(tiles)])
        for k in far_steps(tiles)
    ]
    mate = mates(source)

    work = [
        pltpu.VMEM((grid, lanes), f32),
        pltpu.VMEM((grid, lanes), f32),
        pltpu.VMEM((count, grid, lanes), f32),
        pltpu.VMEM((4 * box_len, CHUNK * lanes), bf16),
    ]
    hold = [pltpu.VMEM((CHUNK * box_len, 2 * lanes), bf16)]
    hold = hold + [pltpu.VMEM((grid, lanes), f32)] * 4
    steps = [
        pltpu.VMEM((tiles + 2, tile_len + 2 * MARGIN, tile_len), f32),
        pltpu.VMEM((tiles, tile_len, tile_len), f32),
    ]
    period = tile_len + 2 * MARGIN
    scale = 0.5 / (grid * grid * period * tile_len)
    source_len = struct(count, box_len, lanes)

    fwd = ("spec_cols", "spec_rows", "lane_fwd", "row_fwd", "mix_cols", "mix_rows")
    names, values = pick(*fwd, "lane_back", "row_back")
    back, pr, pi, info, whole = pl.pallas_call(
        functools.partial(first_kernel, names, peers, tiles, scale),
        out_shape=[struct(grid, lanes), source_len, source_len, struct(8, 128),
                   struct(8, 128, kind=jnp.int32)],
        in_specs=[smem] + [vmem] * (6 + peers + len(names)),
        out_specs=[vmem] * 5,
        scratch_shapes=work + hold + [
            pltpu.SMEM((8, 128), jnp.int32),
            pltpu.SMEM((8, 128), f32),
            pltpu.SemaphoreType.DMA((2,)),
        ],
        compiler_params=params_of,
        cost_estimate=cost(1 << 32),
        name="first_step",
    )(tile, pupil_re, pupil_im, target, mask_param, before, after, *packed, *values)

    shared = (tile, whole, info, pr, pi, target)
    shared_specs = [smem, smem] + [vmem] * 4

    backs = ring(back, "tile")
    entries = [mask_param, *far, mate, *[mates(one) for one in far]]
    names, values = pick(*fwd, "lane_back", "row_back", "grad_cols", "grad_rows")
    params, back = pl.pallas_call(
        functools.partial(next_kernel, names, tiles, scale),
        out_shape=[struct(tiles * tile_len, tile_len), struct(grid, lanes)],
        in_specs=shared_specs + [vmem] * (2 * tiles + len(names)),
        out_specs=[vmem] * 2,
        scratch_shapes=work + hold + steps,
        compiler_params=params_of,
        cost_estimate=cost(1 << 32),
        name="next_step",
    )(*shared, *entries, *backs, *values)

    backs = ring(back, "tile")
    names, values = pick(*fwd, "grad_cols", "grad_rows")
    final, row = pl.pallas_call(
        functools.partial(last_kernel, names, tiles),
        out_shape=[struct(tile_len, tile_len), struct(8, count)],
        in_specs=shared_specs + [vmem] * (1 + tiles + len(names)),
        out_specs=[vmem] * 2,
        scratch_shapes=work + [pltpu.VMEM((count, lanes), f32)] + steps,
        compiler_params=params_of,
        cost_estimate=cost(1 << 32),
        name="last_step",
    )(*shared, params, *backs, *values)

    rows = ring(row, "tile")
    out = pl.pallas_call(
        functools.partial(weight_kernel, tiles, 1.0 / (grid * grid)),
        out_shape=struct(1, local),
        in_specs=[smem] * 2 + [vmem] * (1 + tiles),
        out_specs=vmem,
        scratch_shapes=[pltpu.VMEM((tiles, 8, count), f32)],
        compiler_params=params_of,
        name="weight_step",
    )(tile, place, info, *rows)
    return final, out.reshape(local)


def solution(mesh):
    in_specs = (
        P(("group", "tile"), None),
        P(("group", "tile"), None),
        P(("group", "src")),
        P("src", None),
        P(),
    )
    out_specs = (P(("group", "tile"), None), P(("group", "src")))
    return jax.shard_map(
        per_device, mesh=mesh, in_specs=in_specs, out_specs=out_specs, check_vma=False
    )
```

time: 73.4 us -> 61.5 us (0.84)
  Pallas kernels: 32 us -> 20.5 us
  starting transfers between devices: 16 us -> 12.9 us
  waiting for transfers between devices: 15.6 us -> 18.1 us
  local copies, waits for them, and re-layouts: 6.22 us -> 8.62 us
  between operations: 2.25 us -> 0.8 us
  other arithmetic: 1.02 us -> 0.09 us
    pallas_call x2 -> x3, Pallas kernels: 22.3 us -> 13.7 us  [the longest x1 6.97 us: per_device(): pl.pallas_call(functools.partial(next_kernel, names, tiles, scale), out_s...]
    ppermute x15 -> x12, waiting for transfers between devices: 7.99 us -> 14 us  [ring(): lax.ppermute(value, axis, [(i, (i + k) % peers) for i in range(peers)])]
    ppermute x15 -> x12, starting transfers between devices: 14.5 us -> 9.29 us  [ring(): lax.ppermute(value, axis, [(i, (i + k) % peers) for i in range(peers)])]
    ppermute x1, waiting for transfers between devices: 4.83 us -> 0.01 us  [per_device(): after = lax.ppermute(mask_param[:MARGIN], 'tile', up)]
    ppermute x0 -> x3, waiting for transfers between devices: none -> 4.11 us  [the longest x1 4.11 us: per_device(): lax.ppermute(source, 'tile', [(i, (i + k) % tiles) for i in range(tiles)])]
    pallas_call x1, Pallas kernels: 9.1 us -> 5.7 us  [per_device(): pl.pallas_call(functools.partial(last_kernel, names, tiles), out_shape=[s...]
    ppermute x1, waiting for transfers between devices: 2.8 us -> 0.01 us  [per_device(): before = lax.ppermute(mask_param[-MARGIN:], 'tile', down)]
    unnamed x38, local copies, waits for them, and re-layouts: 4.44 us -> 6.94 us
  transfers between devices with their start and end apart: 17 -> 17, of which waited for: 9 -> 13; matrix products, arithmetic and copies ran while one was open for 2% -> 1% of each run, Pallas kernels for 15% -> 12%
where the time goes in v1:
time: 61.5 us; the launch traced here: 61 us
  Pallas kernels  20.5 us (33%)
  waiting for transfers between devices  18.1 us (29%)
  starting transfers between devices  12.9 us (21%)
  local copies, waits for them, and re-layouts  8.62 us (14%)
  between operations  0.8 us (1%)
    ppermute x12, waiting for transfers between devices, ring(): lax.ppermute(value, axis, [(i, (i + k) % peers) for i in range(peers)])  14 us
    ppermute x12, starting transfers between devices, ring(): lax.ppermute(value, axis, [(i, (i + k) % peers) for i in range(peers)])  9.29 us
    pallas_call x1, Pallas kernels, per_device(): pl.pallas_call(functools.partial(next_kernel, names, tiles, scale), out_s...  6.97 us
    unnamed x38, local copies, waits for them, and re-layouts  6.94 us
    pallas_call x1, Pallas kernels, per_device(): pl.pallas_call(functools.partial(first_kernel, names, peers, tiles, scale...  6.64 us
    pallas_call x1, Pallas kernels, per_device(): pl.pallas_call(functools.partial(last_kernel, names, tiles), out_shape=[s...  5.7 us
    ppermute x1, waiting for transfers between devices, per_device(): lax.ppermute(source, 'tile', [(i, (i + k) % tiles) for i in range(tiles)])  4.11 us
    ppermute x1, starting transfers between devices, per_device(): after = lax.ppermute(mask_param[:MARGIN], 'tile', up)  2.49 us
  transfers between devices with their start and end apart: 17, of which 13 were waited for; matrix products, arithmetic and copies ran while one was open for 1% of the time, Pallas kernels for 12%

profile of v1, /device:TPU:0, one launch (start us, length us, event | category | flops | bytes accessed | tf_op | source)
XLA Modules:
  0.0 61.0 jit_solution(1860565028327173090)
XLA Ops:
  0.7 0.9 %fusion = (f32[64,256]{1,0:T(8,128)S(1)}, f32[64,256]{1,0:T(8,128)S(1)}) fusion(f32[256,256]{1,0:T(8,128)} %refs_0_.2), kind=kLoop, calls=%fused_computation.5 | loop fusion | bytes 262144 | tf_op jit(solution)/shard_map/slice | solution.py:506
  1.6 2.5 %collective-permute-start.1 = (f32[64,256]{1,0:T(8,128)S(1)}, f32[64,256]{1,0:T(8,128)S(1)}, u32[]{:S(2)}, u32[]{:S(2)}) collective-permute-start(f32[64,256]{1,0:T(8,128)S(1)} %get-tuple-element.34), channel_id=1, source_target_pairs={{1,0},{2,1},{3,2},{0,3},{5,4},{6,5},{7,6},{4,7},{9,8},{10,9},{11,1... | collective-permute-start | bytes 196616 | tf_op jit(solution)/shard_map/ppermute | solution.py:506
  5.5 3.6 %collective-permute-start.4 = (f32[8,128]{1,0:T(8,128)S(1)}, f32[8,128]{1,0:T(8,128)S(1)}, u32[]{:S(2)}, u32[]{:S(2)}) collective-permute-start(f32[8,128]{1,0:T(8,128)S(1)} %pack_sources.1.refs_0_), channel_id=1, source_target_pairs={{0,12},{4,0},{8,4},{12,8},{1,13},{5,1},{9,5},{13,9},{2,14},{6,2},{... | collective-permute-start | bytes 12296 | tf_op jit(solution)/shard_map/ppermute | solution.py:457
  9.1 1.0 %collective-permute-start.2 = (f32[8,128]{1,0:T(8,128)S(1)}, f32[8,128]{1,0:T(8,128)S(1)}, u32[]{:S(2)}, u32[]{:S(2)}) collective-permute-start(f32[8,128]{1,0:T(8,128)S(1)} %pack_sources.1.refs_0_), channel_id=1, source_target_pairs={{0,4},{4,8},{8,12},{12,0},{1,5},{5,9},{9,13},{13,1},{2,6},{6,10},{... | collective-permute-start | bytes 12296 | tf_op jit(solution)/shard_map/ppermute | solution.py:457
  10.4 3.2 %collective-permute-done.3.refs_2_ = f32[8,128]{1,0:T(8,128)S(1)} collective-permute-done((f32[8,128]{1,0:T(8,128)S(1)}, f32[8,128]{1,0:T(8,128)S(1)}, u32[]{:S(2)}, u32[]{:S(2)}) %collective-permute-start.3) | collective-permute-done | bytes 4128 | tf_op jit(solution)/shard_map/ppermute | solution.py:457
  13.6 0.9 %collective-permute-done.2.refs_1_ = f32[8,128]{1,0:T(8,128)S(1)} collective-permute-done((f32[8,128]{1,0:T(8,128)S(1)}, f32[8,128]{1,0:T(8,128)S(1)}, u32[]{:S(2)}, u32[]{:S(2)}) %collective-permute-start.2) | collective-permute-done | bytes 4128 | tf_op jit(solution)/shard_map/ppermute | solution.py:457
  14.5 1.1 %collective-permute-start.5 = (f32[256,256]{1,0:T(8,128)}, f32[256,256]{1,0:T(8,128)S(1)}, u32[]{:S(2)}, u32[]{:S(2)}) collective-permute-start(f32[256,256]{1,0:T(8,128)} %refs_0_.2), channel_id=1, source_target_pairs={{0,2},{1,3},{2,0},{3,1},{4,6},{5,7},{6,4},{7,5},{8,10},{9,11},{10,... | collective-permute-start | bytes 786440 | tf_op jit(solution)/shard_map/ppermute | solution.py:536
  16.4 0.8 %copy-done.2 = bf16[128,256]{1,0:T(8,128)(2,1)S(1)} copy-done((bf16[128,256]{1,0:T(8,128)(2,1)S(1)}, bf16[128,256]{1,0:T(8,128)(2,1)}, u32[]{:S(2)}) %copy-start.2) | copy-done | bytes 65560
  18.1 4.1 %collective-permute-done.5.refs_1_ = f32[256,256]{1,0:T(8,128)S(1)} collective-permute-done((f32[256,256]{1,0:T(8,128)}, f32[256,256]{1,0:T(8,128)S(1)}, u32[]{:S(2)}, u32[]{:S(2)}) %collective-permute-start.5) | collective-permute-done | bytes 262176 | tf_op jit(solution)/shard_map/ppermute | solution.py:536
  22.3 0.9 %copy-done.10 = bf16[256,256]{1,0:T(8,128)(2,1)S(1)} copy-done((bf16[256,256]{1,0:T(8,128)(2,1)S(1)}, bf16[256,256]{1,0:T(8,128)(2,1)}, u32[]{:S(2)}) %copy-start.10) | copy-done | bytes 131096
  23.2 0.9 %copy-done.12 = bf16[256,256]{1,0:T(8,128)(2,1)S(1)} copy-done((bf16[256,256]{1,0:T(8,128)(2,1)S(1)}, bf16[256,256]{1,0:T(8,128)(2,1)}, u32[]{:S(2)}) %copy-start.12) | copy-done | bytes 131096
  24.1 0.9 %copy-done.13 = bf16[256,256]{1,0:T(8,128)(2,1)S(1)} copy-done((bf16[256,256]{1,0:T(8,128)(2,1)S(1)}, bf16[256,256]{1,0:T(8,128)(2,1)}, u32[]{:S(2)}) %copy-start.13) | copy-done | bytes 131096
  25.0 0.8 %copy-done.16 = bf16[64,192]{1,0:T(8,128)(2,1)S(1)} copy-done((bf16[64,192]{1,0:T(8,128)(2,1)S(1)}, bf16[64,192]{1,0:T(8,128)(2,1)}, u32[]{:S(2)}) %copy-start.16) | copy-done | bytes 24600
  26.5 6.6 %first_step.1 = (f32[64,128]{1,0:T(8,128)S(1)}, f32[64,32,128]{2,1,0:T(8,128)S(1)}, f32[64,32,128]{2,1,0:T(8,128)S(1)}, f32[8,128]{1,0:T(8,128)S(1)}, s32[8,128]{1,0:T(8,128)S(1)}) custom-call(s32[1]{0:T(128)} %bitcast.tile, f32[32,128]{1,0:T(8,128)S(1)} %get-tuple-element.40.pupil_re, f32[32,128]{1,0:T(8,128)S(1)} %get-tuple-element.41.pupil_im, ...), custom_call_target="tpu_custom_call" | custom-call | flops 4294967296 | bytes 1048576 | tf_op jit(solution)/shard_map/first_step/pallas_call | solution.py:559
  33.2 1.6 %collective-permute-start.10 = (f32[64,128]{1,0:T(8,128)S(1)}, f32[64,128]{1,0:T(8,128)S(1)}, u32[]{:S(2)}, u32[]{:S(2)}) collective-permute-start(f32[64,128]{1,0:T(8,128)S(1)} %get-tuple-element.29.refs_4_), channel_id=1, source_target_pairs={{0,3},{1,0},{2,1},{3,2},{4,7},{5,4},{6,5},{7,6},{8,11},{9,8},{10,9... | collective-permute-start | bytes 98312 | tf_op jit(solution)/shard_map/ppermute | solution.py:457
  35.4 1.0 %collective-permute-done.10.refs_7_ = f32[64,128]{1,0:T(8,128)S(1)} collective-permute-done((f32[64,128]{1,0:T(8,128)S(1)}, f32[64,128]{1,0:T(8,128)S(1)}, u32[]{:S(2)}, u32[]{:S(2)}) %collective-permute-start.10) | collective-permute-done | bytes 32800 | tf_op jit(solution)/shard_map/ppermute | solution.py:457
  36.3 2.6 %collective-permute-done.9.refs_6_ = f32[64,128]{1,0:T(8,128)S(1)} collective-permute-done((f32[64,128]{1,0:T(8,128)S(1)}, f32[64,128]{1,0:T(8,128)S(1)}, u32[]{:S(2)}, u32[]{:S(2)}) %collective-permute-start.9) | collective-permute-done | bytes 32800 | tf_op jit(solution)/shard_map/ppermute | solution.py:457
  39.0 7.0 %next_step.1 = (f32[1024,256]{1,0:T(8,128)S(1)}, f32[64,128]{1,0:T(8,128)S(1)}) custom-call(s32[1]{0:T(128)} %bitcast.tile, s32[8,128]{1,0:T(8,128)S(1)} %get-tuple-element.24.shifts, f32[8,128]{1,0:T(8,128)S(1)} %get-tuple-element.25.info, f32[64,32,128]{2,1,0:T(8,128)S(1)} %get-tuple-element.26.pr, f32[64,32,128]{2,1,0:T(8,128)S(1)} %get-tuple-element.27.pi, ...), custom_call_target="tpu_custom_call" | custom-call | flops 4294967296 | bytes 1048576 | tf_op jit(solution)/shard_map/next_step/pallas_call | solution.py:581
  46.0 1.2 %collective-permute-start.12 = (f32[64,128]{1,0:T(8,128)S(1)}, f32[64,128]{1,0:T(8,128)S(1)}, u32[]{:S(2)}, u32[]{:S(2)}) collective-permute-start(f32[64,128]{1,0:T(8,128)S(1)} %get-tuple-element.31.refs_0_), channel_id=1, source_target_pairs={{0,2},{1,3},{2,0},{3,1},{4,6},{5,7},{6,4},{7,5},{8,10},{9,11},{10,... | collective-permute-start | bytes 98312 | tf_op jit(solution)/shard_map/ppermute | solution.py:457
  47.6 2.4 %collective-permute-done.12.refs_2_ = f32[64,128]{1,0:T(8,128)S(1)} collective-permute-done((f32[64,128]{1,0:T(8,128)S(1)}, f32[64,128]{1,0:T(8,128)S(1)}, u32[]{:S(2)}, u32[]{:S(2)}) %collective-permute-start.12) | collective-permute-done | bytes 32800 | tf_op jit(solution)/shard_map/ppermute | solution.py:457
  50.5 5.7 %last_step.1 = (f32[256,256]{1,0:T(8,128)}, f32[8,64]{1,0:T(8,128)S(1)}) custom-call(s32[1]{0:T(128)} %bitcast.tile, s32[8,128]{1,0:T(8,128)S(1)} %get-tuple-element.24.shifts, f32[8,128]{1,0:T(8,128)S(1)} %get-tuple-element.25.info, f32[64,32,128]{2,1,0:T(8,128)S(1)} %get-tuple-element.26.pr, f32[64,32,128]{2,1,0:T(8,128)S(1)} %get-tuple-element.27.pi, ...), custom_call_target="tpu_custom_call" | custom-call | flops 4294967296 | bytes 1048576 | tf_op jit(solution)/shard_map/last_step/pallas_call | solution.py:594
  56.2 0.9 %collective-permute-start.15 = (f32[8,64]{1,0:T(8,128)S(1)}, f32[8,64]{1,0:T(8,128)S(1)}, u32[]{:S(2)}, u32[]{:S(2)}) collective-permute-start(f32[8,64]{1,0:T(8,128)S(1)} %get-tuple-element.33.refs_0_), channel_id=1, source_target_pairs={{0,2},{1,3},{2,0},{3,1},{4,6},{5,7},{6,4},{7,5},{8,10},{9,11},{10,... | collective-permute-start | bytes 6152 | tf_op jit(solution)/shard_map/ppermute | solution.py:457
  57.6 2.3 %collective-permute-done.15.refs_2_ = f32[8,64]{1,0:T(8,128)S(1)} collective-permute-done((f32[8,64]{1,0:T(8,128)S(1)}, f32[8,64]{1,0:T(8,128)S(1)}, u32[]{:S(2)}, u32[]{:S(2)}) %collective-permute-start.15) | collective-permute-done | bytes 2080 | tf_op jit(solution)/shard_map/ppermute | solution.py:457
  60.2 0.8 %weight_step.1 = f32[1,16]{1,0:T(1,128)} custom-call(s32[1]{0:T(128)} %bitcast.tile, s32[1]{0:T(128)} %bitcast.3.place, f32[8,128]{1,0:T(8,128)S(1)} %get-tuple-element.25.info, f32[8,64]{1,0:T(8,128)S(1)} %get-tuple-element.33.refs_0_, f32[8,64]{1,0:T(8,128)S(1)} %collective-permute-done.14.refs_1_, f32[8,64]{1,0:T(8,128)S(1)} %collective-permute-done.15.refs_2_, ...), custom_call_target="tpu_custom_call" | custom-call | tf_op jit(solution)/shard_map/weight_step/pallas_call | solution.py:606
  (59 shorter events, 6.6 us)
Async XLA Ops:
  0.6 15.7 %copy-start.1 = (bf16[256,256]{1,0:T(8,128)(2,1)S(1)}, bf16[256,256]{1,0:T(8,128)(2,1)}, u32[]{:S(2)}) copy-start(bf16[256,256]{1,0:T(8,128)(2,1)} %constant.35.clone.refs_1_) | copy-start | bytes 393220
  0.6 15.7 %copy-start = (f32[256,256]{1,0:T(8,128)S(1)}, f32[256,256]{1,0:T(8,128)}, u32[]{:S(2)}) copy-start(f32[256,256]{1,0:T(8,128)} %target.1) | copy-start | bytes 786436
  1.6 12.9 %collective-permute-start.1 = (f32[64,256]{1,0:T(8,128)S(1)}, f32[64,256]{1,0:T(8,128)S(1)}, u32[]{:S(2)}, u32[]{:S(2)}) collective-permute-start(f32[64,256]{1,0:T(8,128)S(1)} %get-tuple-element.34), channel_id=1, source_target_pairs={{1,0},{2,1},{3,2},{0,3},{5,4},{6,5},{7,6},{4,7},{9,8},{10,9},{11,1... | collective-permute-start | bytes 196616 | tf_op jit(solution)/shard_map/ppermute | solution.py:506
  4.1 10.4 %collective-permute-start = (f32[64,256]{1,0:T(8,128)S(1)}, f32[64,256]{1,0:T(8,128)S(1)}, u32[]{:S(2)}, u32[]{:S(2)}) collective-permute-start(f32[64,256]{1,0:T(8,128)S(1)} %get-tuple-element.35), channel_id=1, source_target_pairs={{0,1},{1,2},{2,3},{3,0},{4,5},{5,6},{6,7},{7,4},{8,9},{9,10},{10,1... | collective-permute-start | bytes 196616 | tf_op jit(solution)/shard_map/ppermute | solution.py:505
  5.5 4.9 %collective-permute-start.4 = (f32[8,128]{1,0:T(8,128)S(1)}, f32[8,128]{1,0:T(8,128)S(1)}, u32[]{:S(2)}, u32[]{:S(2)}) collective-permute-start(f32[8,128]{1,0:T(8,128)S(1)} %pack_sources.1.refs_0_), channel_id=1, source_target_pairs={{0,12},{4,0},{8,4},{12,8},{1,13},{5,1},{9,5},{13,9},{2,14},{6,2},{... | collective-permute-start | bytes 12296 | tf_op jit(solution)/shard_map/ppermute | solution.py:457
  9.1 4.5 %collective-permute-start.3 = (f32[8,128]{1,0:T(8,128)S(1)}, f32[8,128]{1,0:T(8,128)S(1)}, u32[]{:S(2)}, u32[]{:S(2)}) collective-permute-start(f32[8,128]{1,0:T(8,128)S(1)} %pack_sources.1.refs_0_), channel_id=1, source_target_pairs={{0,8},{4,12},{8,0},{12,4},{1,9},{5,13},{9,1},{13,5},{2,10},{6,14},... | collective-permute-start | bytes 12296 | tf_op jit(solution)/shard_map/ppermute | solution.py:457
  9.1 5.4 %collective-permute-start.2 = (f32[8,128]{1,0:T(8,128)S(1)}, f32[8,128]{1,0:T(8,128)S(1)}, u32[]{:S(2)}, u32[]{:S(2)}) collective-permute-start(f32[8,128]{1,0:T(8,128)S(1)} %pack_sources.1.refs_0_), channel_id=1, source_target_pairs={{0,4},{4,8},{8,12},{12,0},{1,5},{5,9},{9,13},{13,1},{2,6},{6,10},{... | collective-permute-start | bytes 12296 | tf_op jit(solution)/shard_map/ppermute | solution.py:457
  14.5 7.7 %collective-permute-start.5 = (f32[256,256]{1,0:T(8,128)}, f32[256,256]{1,0:T(8,128)S(1)}, u32[]{:S(2)}, u32[]{:S(2)}) collective-permute-start(f32[256,256]{1,0:T(8,128)} %refs_0_.2), channel_id=1, source_target_pairs={{0,2},{1,3},{2,0},{3,1},{4,6},{5,7},{6,4},{7,5},{8,10},{9,11},{10,... | collective-permute-start | bytes 786440 | tf_op jit(solution)/shard_map/ppermute | solution.py:536
  18.1 20.9 %collective-permute-start.6 = (f32[256,256]{1,0:T(8,128)S(1)}, f32[256,256]{1,0:T(8,128)S(1)}, u32[]{:S(2)}, u32[]{:S(2)}) collective-permute-start(f32[256,256]{1,0:T(8,128)S(1)} %copy-done.3), channel_id=1, source_target_pairs={{0,1},{1,0},{2,3},{3,2},{4,5},{5,4},{6,7},{7,6},{8,9},{9,8},{10,11... | collective-permute-start | bytes 786440 | tf_op jit(solution)/shard_map/ppermute | solution.py:463
  22.2 16.7 %collective-permute-start.7 = (f32[256,256]{1,0:T(8,128)S(1)}, f32[256,256]{1,0:T(8,128)S(1)}, u32[]{:S(2)}, u32[]{:S(2)}) collective-permute-start(f32[256,256]{1,0:T(8,128)S(1)} %collective-permute-done.5.refs_1_), channel_id=1, source_target_pairs={{0,1},{1,0},{2,3},{3,2},{4,5},{5,4},{6,7},{7,6},{8,9},{9,8},{10,11... | collective-permute-start | bytes 786440 | tf_op jit(solution)/shard_map/ppermute | solution.py:463
  26.5 12.5 %copy-start.6 = (bf16[384,512]{1,0:T(8,128)(2,1)S(1)}, bf16[384,512]{1,0:T(8,128)(2,1)}, u32[]{:S(2)}) copy-start(bf16[384,512]{1,0:T(8,128)(2,1)} %constant.44.clone.refs_16_.refs_10_) | copy-start | bytes 1179652
  26.5 12.5 %copy-start.7 = (bf16[384,384]{1,0:T(8,128)(2,1)S(1)}, bf16[384,384]{1,0:T(8,128)(2,1)}, u32[]{:S(2)}) copy-start(bf16[384,384]{1,0:T(8,128)(2,1)} %constant.45.clone.refs_17_.refs_11_) | copy-start | bytes 884740
  26.5 12.5 %copy-start.11 = (bf16[256,256]{1,0:T(8,128)(2,1)S(1)}, bf16[256,256]{1,0:T(8,128)(2,1)}, u32[]{:S(2)}) copy-start(bf16[256,256]{1,0:T(8,128)(2,1)} %constant.38.clone.refs_6_.refs_10_) | copy-start | bytes 393220
  26.5 12.5 %copy-start.14 = (bf16[256,256]{1,0:T(8,128)(2,1)S(1)}, bf16[256,256]{1,0:T(8,128)(2,1)}, u32[]{:S(2)}) copy-start(bf16[256,256]{1,0:T(8,128)(2,1)} %constant.42.clone.refs_10_.refs_14_) | copy-start | bytes 393220
  26.5 12.5 %copy-start.17 = (bf16[64,192]{1,0:T(8,128)(2,1)S(1)}, bf16[64,192]{1,0:T(8,128)(2,1)}, u32[]{:S(2)}) copy-start(bf16[64,192]{1,0:T(8,128)(2,1)} %constant.39.clone.refs_7_.refs_11_) | copy-start | bytes 73732
  33.2 3.1 %collective-permute-start.10 = (f32[64,128]{1,0:T(8,128)S(1)}, f32[64,128]{1,0:T(8,128)S(1)}, u32[]{:S(2)}, u32[]{:S(2)}) collective-permute-start(f32[64,128]{1,0:T(8,128)S(1)} %get-tuple-element.29.refs_4_), channel_id=1, source_target_pairs={{0,3},{1,0},{2,1},{3,2},{4,7},{5,4},{6,5},{7,6},{8,11},{9,8},{10,9... | collective-permute-start | bytes 98312 | tf_op jit(solution)/shard_map/ppermute | solution.py:457
  34.7 4.2 %collective-permute-start.9 = (f32[64,128]{1,0:T(8,128)S(1)}, f32[64,128]{1,0:T(8,128)S(1)}, u32[]{:S(2)}, u32[]{:S(2)}) collective-permute-start(f32[64,128]{1,0:T(8,128)S(1)} %get-tuple-element.29.refs_4_), channel_id=1, source_target_pairs={{0,2},{1,3},{2,0},{3,1},{4,6},{5,7},{6,4},{7,5},{8,10},{9,11},{10,... | collective-permute-start | bytes 98312 | tf_op jit(solution)/shard_map/ppermute | solution.py:457
  35.3 3.6 %collective-permute-start.8 = (f32[64,128]{1,0:T(8,128)S(1)}, f32[64,128]{1,0:T(8,128)S(1)}, u32[]{:S(2)}, u32[]{:S(2)}) collective-permute-start(f32[64,128]{1,0:T(8,128)S(1)} %get-tuple-element.29.refs_4_), channel_id=1, source_target_pairs={{0,1},{1,2},{2,3},{3,0},{4,5},{5,6},{6,7},{7,4},{8,9},{9,10},{10,1... | collective-permute-start | bytes 98312 | tf_op jit(solution)/shard_map/ppermute | solution.py:457
  46.0 1.6 %collective-permute-start.13 = (f32[64,128]{1,0:T(8,128)S(1)}, f32[64,128]{1,0:T(8,128)S(1)}, u32[]{:S(2)}, u32[]{:S(2)}) collective-permute-start(f32[64,128]{1,0:T(8,128)S(1)} %get-tuple-element.31.refs_0_), channel_id=1, source_target_pairs={{0,3},{1,0},{2,1},{3,2},{4,7},{5,4},{6,5},{7,6},{8,11},{9,8},{10,9... | collective-permute-start | bytes 98312 | tf_op jit(solution)/shard_map/ppermute | solution.py:457
  46.0 4.0 %collective-permute-start.12 = (f32[64,128]{1,0:T(8,128)S(1)}, f32[64,128]{1,0:T(8,128)S(1)}, u32[]{:S(2)}, u32[]{:S(2)}) collective-permute-start(f32[64,128]{1,0:T(8,128)S(1)} %get-tuple-element.31.refs_0_), channel_id=1, source_target_pairs={{0,2},{1,3},{2,0},{3,1},{4,6},{5,7},{6,4},{7,5},{8,10},{9,11},{10,... | collective-permute-start | bytes 98312 | tf_op jit(solution)/shard_map/ppermute | solution.py:457
  47.2 3.3 %collective-permute-start.11 = (f32[64,128]{1,0:T(8,128)S(1)}, f32[64,128]{1,0:T(8,128)S(1)}, u32[]{:S(2)}, u32[]{:S(2)}) collective-permute-start(f32[64,128]{1,0:T(8,128)S(1)} %get-tuple-element.31.refs_0_), channel_id=1, source_target_pairs={{0,1},{1,2},{2,3},{3,0},{4,5},{5,6},{6,7},{7,4},{8,9},{9,10},{10,1... | collective-permute-start | bytes 98312 | tf_op jit(solution)/shard_map/ppermute | solution.py:457
  56.2 1.3 %collective-permute-start.16 = (f32[8,64]{1,0:T(8,128)S(1)}, f32[8,64]{1,0:T(8,128)S(1)}, u32[]{:S(2)}, u32[]{:S(2)}) collective-permute-start(f32[8,64]{1,0:T(8,128)S(1)} %get-tuple-element.33.refs_0_), channel_id=1, source_target_pairs={{0,3},{1,0},{2,1},{3,2},{4,7},{5,4},{6,5},{7,6},{8,11},{9,8},{10,9... | collective-permute-start | bytes 6152 | tf_op jit(solution)/shard_map/ppermute | solution.py:457
  56.2 3.6 %collective-permute-start.15 = (f32[8,64]{1,0:T(8,128)S(1)}, f32[8,64]{1,0:T(8,128)S(1)}, u32[]{:S(2)}, u32[]{:S(2)}) collective-permute-start(f32[8,64]{1,0:T(8,128)S(1)} %get-tuple-element.33.refs_0_), channel_id=1, source_target_pairs={{0,2},{1,3},{2,0},{3,1},{4,6},{5,7},{6,4},{7,5},{8,10},{9,11},{10,... | collective-permute-start | bytes 6152 | tf_op jit(solution)/shard_map/ppermute | solution.py:457
  57.2 3.0 %collective-permute-start.14 = (f32[8,64]{1,0:T(8,128)S(1)}, f32[8,64]{1,0:T(8,128)S(1)}, u32[]{:S(2)}, u32[]{:S(2)}) collective-permute-start(f32[8,64]{1,0:T(8,128)S(1)} %get-tuple-element.33.refs_0_), channel_id=1, source_target_pairs={{0,1},{1,2},{2,3},{3,0},{4,5},{5,6},{6,7},{7,4},{8,9},{9,10},{10,1... | collective-permute-start | bytes 6152 | tf_op jit(solution)/shard_map/ppermute | solution.py:457
  (12 other events, 22.2 us)

commit v2 on v1

--- a/solution.py
+++ b/solution.py
@@ -84,6 +84,26 @@
     return out
 
 
+def pack_tables(tables):
+    wide = [n for n in tables if tables[n].shape[1] > 256]
+    narrow = sorted((n for n in tables if n not in wide), key=lambda n: -tables[n].shape[0])
+    place, heights = {}, [0, 0]
+    for n in wide:
+        place[n] = (heights[0], 0)
+        heights = [heights[0] + tables[n].shape[0]] * 2
+    for n in narrow:
+        side = int(heights[1] < heights[0])
+        place[n] = (heights[side], 256 * side)
+        heights[side] += tables[n].shape[0]
+    whole = np.zeros((max(heights), 512), ml_dtypes.bfloat16)
+    spots = {}
+    for n, (row, col) in place.items():
+        rows, cols = tables[n].shape
+        whole[row : row + rows, col : col + cols] = tables[n]
+        spots[n] = (slice(row, row + rows), slice(col, col + cols))
+    return whole, spots
+
+
 def split(value):
     high = value.astype(bf16)
     return high, (value - high.astype(f32)).astype(bf16)
@@ -127,67 +147,58 @@
     return both[:grid] + lane_sign(grid, 2 * grid, 1.0) * swap(both[grid:])
 
 
-def skewed(count, first, second, carry):
+def skewed(count, stages, first, second, carry):
     chunks = count // CHUNK
-    first(0)
-
-    def body(c, carry):
-        carry = second(c - 1, carry)
-        first(c)
-        return carry
-
-    carry = lax.fori_loop(1, chunks, body, carry)
-    return second(chunks - 1, carry)
-
-
-def place_pupils(shifts, roots, pupil_re, pupil_im, pr, pi):
-    count = pr.shape[0]
-
-    def one(s, carry):
+    first(0, stages[0])
+    for c in range(1, chunks):
+        first(c, stages[c % 2])
+        carry = second(c - 1, stages[(c - 1) % 2], carry)
+    return second(chunks - 1, stages[(chunks - 1) % 2], carry)
+
+
+def placed_pupils(shifts, roots, pupil_re, pupil_im, pr, pi):
+    def make(s):
         by = shifts[2, s] + MAX_SHIFT
-        pr[s] = pltpu.roll(pupil_re[...], by, 1) * roots[3, s]
-        pi[s] = pltpu.roll(pupil_im[...], by, 1) * roots[3, s]
-        return carry
-
-    lax.fori_loop(0, count, one, 0, unroll=8)
-
-
-def grid_fields(spec, shifts, t, pr, pi, work):
-    plain, crossed, fields, stage = work
-    count, box_len, lanes = pr.shape
-    grid = lanes // 2
+        real = pltpu.roll(pupil_re[...] * roots[3, s], by, 1)
+        imag = pltpu.roll(pupil_im[...] * roots[3, s], by, 1)
+        pr[s], pi[s] = real, imag
+        return real, imag
+
+    return make
+
+
+def grid_fields(spec, shifts, t, pupils, work):
+    plain, crossed, fields, *stages = work
+    count, grid, lanes = fields.shape
+    box_len = t["row_fwd"].shape[1] // 6
     plain[...] = spec
     crossed[...] = swap(spec)
     sign = lane_sign(box_len, lanes, -1.0)
 
-    def first(c):
+    def first(c, stage):
         rows = []
         for i in range(CHUNK):
             s = c * CHUNK + i
             at = pl.ds(shifts[1, s] + MAX_SHIFT, box_len)
-            high, low = split(pr[s] * plain[at, :] + pi[s] * crossed[at, :])
+            real, imag = pupils(s)
+            high, low = split(real * plain[at, :] + imag * crossed[at, :])
             rows.append(jnp.concatenate([high, low], 1))
-        mid = halves(dot(jnp.concatenate(rows, 0), t["lane_fwd"][...]))
+        stage[...] = halves(dot(jnp.concatenate(rows, 0), t["lane_fwd"][...]))
+
+    def second(c, stage, power):
+        stacks = []
         for i in range(CHUNK):
-            part = mid[i * box_len : (i + 1) * box_len]
-            at = slice(i * lanes, (i + 1) * lanes)
-            high, low = split(part)
-            stage[:box_len, at] = high
-            stage[2 * box_len : 3 * box_len, at] = low
-            high, low = split(sign * swap(part))
-            stage[box_len : 2 * box_len, at] = high
-            stage[3 * box_len :, at] = low
-
-    def second(c, power):
-        value = stage[...]
-        out = dot(t["row_fwd"][...], jnp.concatenate([value, value[: 2 * box_len]], 0))
+            part = stage[i * box_len : (i + 1) * box_len, :]
+            high, low = split(jnp.concatenate([part, sign * swap(part)], 0))
+            stacks.append(jnp.concatenate([high, low, high], 0))
+        out = dot(t["row_fwd"][...], jnp.concatenate(stacks, 1))
         for i in range(CHUNK):
             field = out[:, i * lanes : (i + 1) * lanes]
             fields[c * CHUNK + i] = field
             power = power + field * field
         return power
 
-    return skewed(count, first, second, jnp.zeros((grid, lanes), f32))
+    return skewed(count, stages, first, second, jnp.zeros((grid, lanes), f32))
 
 
 def grid_misfit(power, inv_dose, target, t):
@@ -198,13 +209,13 @@
     return lit * inv_dose - target
 
 
-def gather_back(misfit, shifts, scale, t, pr, pi, fields, stage, sums):
+def gather_back(misfit, shifts, scale, t, pr, pi, fields, stages, sums):
     count, box_len, lanes = pr.shape
     for ref in sums:
         ref[...] = jnp.zeros_like(ref)
     sign = lane_sign(box_len, lanes, 1.0)
 
-    def first(c):
+    def first(c, stage):
         stacks = []
         for i in range(CHUNK):
             high, low = split(fields[c * CHUNK + i] * misfit)
@@ -212,14 +223,13 @@
         both = dot(t["row_back"][...], jnp.concatenate(stacks, 1))
         for i in range(CHUNK):
             part = both[:, i * lanes : (i + 1) * lanes]
-            part = part[:box_len] + sign * swap(part[box_len:])
-            at = slice(i * box_len, (i + 1) * box_len)
-            high, low = split(part)
-            stage[at, :lanes] = high
-            stage[at, lanes:] = low
-
-    def second(c, carry):
-        hits = halves(dot(stage[...], t["lane_back"][...]))
+            stage[i * box_len : (i + 1) * box_len, :] = part[:box_len] + sign * swap(
+                part[box_len:]
+            )
+
+    def second(c, stage, carry):
+        high, low = split(stage[...])
+        hits = halves(dot(jnp.concatenate([high, low], 1), t["lane_back"][...]))
         for i in range(CHUNK):
             s = c * CHUNK + i
             rows = pl.ds(shifts[1, s] + MAX_SHIFT, box_len)
@@ -229,7 +239,7 @@
             two[rows, :] += pi[s] * hit
         return carry
 
-    skewed(count, first, second, 0)
+    skewed(count, stages, first, second, 0)
     return (sums[0][...] + sums[2][...] + swap(sums[1][...] + sums[3][...])) * scale
 
 
@@ -237,7 +247,7 @@
     return lax.rem(tile + tiles - k, tiles)
 
 
-def mask_grads(params, ids, backs, t, tile, tiles, zed, wins, grads):
+def mask_grads(params, ids, backs, t, tile, tiles, wins, grads):
     grid = backs[0].shape[0]
     tile_len = wins.shape[2]
     rows = []
@@ -280,26 +290,50 @@
     return above, below, (tile > 0).astype(f32), (tile < tiles - 1).astype(f32)
 
 
-def target_kernel(names, target, *refs):
-    t = dict(zip(names, refs))
-    out = refs[len(names)]
-    grid = out.shape[0]
+def start_all(pairs, sems):
+    copies = [pltpu.make_async_copy(a, b, sems.at[i]) for i, (a, b) in enumerate(pairs)]
+    for copy in copies:
+        copy.start()
+    return copies
+
+
+def open_kernel(place, mask, weights, shifts, own, top, low, packed, hold_w, hold_s, sems):
+    rows, local = mask.shape[0], weights.shape[1]
+    copies = start_all(
+        (
+            (weights, hold_w),
+            (shifts, hold_s),
+            (mask.at[pl.ds(0, MARGIN), :], top),
+            (mask.at[pl.ds(rows - MARGIN, MARGIN), :], low),
+            (mask, own),
+        ),
+        sems,
+    )
+    copies[0].wait()
+    copies[1].wait()
+    packed[...] = jnp.zeros_like(packed)
+    packed[0:1, :local] = hold_w[...]
+    packed[1:3, :local] = hold_s[...].astype(f32)
+    packed[3:4, :local] = jnp.sqrt(hold_w[...])
+    packed[...] = pltpu.roll(packed[...], place[0] * local, 1)
+    for copy in copies[2:]:
+        copy.wait()
+
+
+def target_kernel(spots, target, pupil, whole, out, pupil_re, pupil_im):
+    grid, size = out.shape[0], pupil.shape[1]
+    pupil_re[...] = jnp.zeros_like(pupil_re)
+    pupil_im[...] = jnp.zeros_like(pupil_im)
+    pupil_re[:, :size] = pupil[0]
+    pupil_re[:, grid : grid + size] = pupil[0]
+    pupil_im[:, :size] = -pupil[1]
+    pupil_im[:, grid : grid + size] = pupil[1]
+    rows, cols = whole.at[spots["target_rows"]], whole.at[spots["target_cols"]]
     high, low = split(target[...])
-    rows = t["target_rows"]
     both = dot(rows[...], high)
     mid = both[:grid] + both[grid:] + dot(rows[:grid, :], low)
     high, low = split(mid)
-    cols = t["target_cols"]
     out[...] = halves(dot(high, cols[...])) + dot(low, cols[:, : 2 * grid])
-
-
-def pack_kernel(place, weights, shifts, out):
-    local = weights.shape[1]
-    out[...] = jnp.zeros_like(out)
-    out[0:1, :local] = weights[...]
-    out[1:3, :local] = shifts[...].astype(f32)
-    out[3:4, :local] = jnp.sqrt(weights[...])
-    out[...] = pltpu.roll(out[...], place[0] * local, 1)
 
 
 def doses(info, scale):
@@ -307,14 +341,12 @@
     return 1.0 / dose, scale / dose
 
 
-def first_kernel(names, peers, tiles, scale, tile, pupil_re, pupil_im, target,
+def first_kernel(spots, peers, tiles, scale, tile, table, pupil_re, pupil_im, target,
                  own, before, after, *refs):
     parts = refs[:peers]
-    t = dict(zip(names, refs[peers:]))
-    back, pr, pi, info, whole = refs[peers + len(names) : peers + len(names) + 5]
-    (plain, crossed, fields, stage, hold, *sums, shifts, roots, sems) = refs[
-        peers + len(names) + 5 :
-    ]
+    t = {n: table.at[spot] for n, spot in spots.items()}
+    back, pr, pi, info, whole = refs[peers : peers + 5]
+    *work, s0, s1, s2, s3, shifts, roots, sems = refs[peers + 5 :]
     here = tile[0]
     total = parts[0][...]
     for part in parts[1:]:
@@ -335,24 +367,23 @@
     spec = window_spectrum(window, t)
     for copy in copies:
         copy.wait()
-    place_pupils(shifts, roots, pupil_re, pupil_im, pr, pi)
-    power = grid_fields(spec, shifts, t, pr, pi, (plain, crossed, fields, stage))
+    pupils = placed_pupils(shifts, roots, pupil_re, pupil_im, pr, pi)
+    power = grid_fields(spec, shifts, t, pupils, work)
     inv_dose, factor = doses(total, scale)
     misfit = grid_misfit(power, inv_dose, target[...], t)
-    back[...] = gather_back(misfit, shifts, factor, t, pr, pi, fields, hold, sums)
-
-
-def next_kernel(names, tiles, scale, tile, shifts, info, pr, pi, target, *refs):
+    sums = (s0, s1, s2, s3)
+    back[...] = gather_back(misfit, shifts, factor, t, pr, pi, work[2], work[3:], sums)
+
+
+def next_kernel(spots, tiles, scale, tile, table, shifts, info, pr, pi, target, *refs):
     params, backs = refs[:tiles], refs[tiles : 2 * tiles]
-    refs = refs[2 * tiles :]
-    t = dict(zip(names, refs))
-    new, back, plain, crossed, fields, stage, hold, *rest = refs[len(names) :]
-    sums, (wins, grads) = rest[:4], rest[4:]
+    t = {n: table.at[spot] for n, spot in spots.items()}
+    new, back, *work, s0, s1, s2, s3, wins, grads = refs[2 * tiles :]
     here = tile[0]
     tile_len = params[0].shape[0]
     ids = entry_ids(here, tiles)
     rate = mask_grads(
-        lambda k, low, high: params[k][low:high, :], ids, backs, t, here, tiles, None, wins, grads
+        lambda k, low, high: params[k][low:high, :], ids, backs, t, here, tiles, wins, grads
     )
     for k in range(tiles):
         own = ids[k]
@@ -369,22 +400,23 @@
         0,
     )
     spec = window_spectrum(window, t)
-    power = grid_fields(spec, shifts, t, pr, pi, (plain, crossed, fields, stage))
+    power = grid_fields(spec, shifts, t, lambda s: (pr[s], pi[s]), work)
     inv_dose, factor = doses(info[...], scale)
     misfit = grid_misfit(power, inv_dose, target[...], t)
-    back[...] = gather_back(misfit, shifts, factor, t, pr, pi, fields, hold, sums)
-
-
-def last_kernel(names, tiles, tile, shifts, info, pr, pi, target, params, *refs):
+    sums = (s0, s1, s2, s3)
+    back[...] = gather_back(misfit, shifts, factor, t, pr, pi, work[2], work[3:], sums)
+
+
+def last_kernel(spots, tiles, tile, table, shifts, info, pr, pi, target, params, *refs):
     backs = refs[:tiles]
-    refs = refs[tiles:]
-    t = dict(zip(names, refs))
-    final, row, plain, crossed, fields, stage, terms, wins, grads = refs[len(names) :]
+    t = {n: table.at[spot] for n, spot in spots.items()}
+    final, row, *work, terms, wins, grads = refs[tiles:]
+    fields = work[2]
     here = tile[0]
     tile_len = final.shape[0]
     rate = mask_grads(
         lambda k, low, high: params[k * tile_len + low : k * tile_len + high, :],
-        list(range(tiles)), backs, t, here, tiles, None, wins, grads,
+        list(range(tiles)), backs, t, here, tiles, wins, grads,
     )
     above, below, has_prev, has_next = edge_rows(here, tiles, tile_len)
     own = pl.ds(pl.multiple_of(here * tile_len, tile_len), tile_len)
@@ -401,7 +433,7 @@
         0,
     )
     spec = window_spectrum(window, t)
-    power = grid_fields(spec, shifts, t, pr, pi, (plain, crossed, fields, stage))
+    power = grid_fields(spec, shifts, t, lambda s: (pr[s], pi[s]), work)
     inv_dose, _ = doses(info[...], 1.0)
     misfit = grid_misfit(power, inv_dose, target[...], t)
 
@@ -489,49 +521,47 @@
 
     vmem = pl.BlockSpec(memory_space=pltpu.VMEM)
     smem = pl.BlockSpec(memory_space=pltpu.SMEM)
-    params_of = pltpu.CompilerParams(vmem_limit_bytes=48 << 20)
+    left = pl.BlockSpec(memory_space=pltpu.HBM)
+    params_of = pltpu.CompilerParams(vmem_limit_bytes=32 << 20)
 
     def struct(*shape, kind=f32):
         return jax.ShapeDtypeStruct(shape, kind)
 
-    def pick(*names):
-        return names, [jnp.asarray(tables[n]) for n in names]
-
     def cost(flops):
         return pl.CostEstimate(flops=flops, bytes_accessed=1 << 20, transcendentals=0)
 
+    own, top, low, packed = pl.pallas_call(
+        open_kernel,
+        out_shape=[struct(tile_len, tile_len), struct(MARGIN, tile_len),
+                   struct(MARGIN, tile_len), struct(8, 128)],
+        in_specs=[smem, left, left, left],
+        out_specs=[vmem] * 4,
+        scratch_shapes=[
+            pltpu.VMEM((1, local), f32),
+            pltpu.VMEM((2, local), jnp.int32),
+            pltpu.SemaphoreType.DMA((5,)),
+        ],
+        name="open_step",
+    )(place, mask_param, source_weights[None], source_shifts.T)
+    packed = ring(packed, "src")
     down = [(i, (i + 1) % tiles) for i in range(tiles)]
     up = [(j, i) for i, j in down]
-    before = lax.ppermute(mask_param[-MARGIN:], "tile", down)
-    after = lax.ppermute(mask_param[:MARGIN], "tile", up)
-
-    packed = pl.pallas_call(
-        pack_kernel,
-        out_shape=struct(8, 128),
-        in_specs=[smem, vmem, vmem],
-        out_specs=vmem,
-        compiler_params=params_of,
-        name="pack_sources",
-    )(place, source_weights[None], source_shifts.T)
-    packed = ring(packed, "src")
-
-    pad = ((0, 0), (0, grid - box_len))
-    real, imag = jnp.pad(pupil_map[0], pad), jnp.pad(pupil_map[1], pad)
-    pupil_re = jnp.concatenate([real, real], 1)
-    pupil_im = jnp.concatenate([-imag, imag], 1)
-
-    names, values = pick("target_rows", "target_cols")
-    target = pl.pallas_call(
-        functools.partial(target_kernel, names),
-        out_shape=struct(grid, lanes),
-        in_specs=[vmem] * (1 + len(names)),
-        out_specs=vmem,
+    before = lax.ppermute(low, "tile", down)
+    after = lax.ppermute(top, "tile", up)
+
+    whole, spots = pack_tables(tables)
+    table = jnp.asarray(whole)
+    target, pupil_re, pupil_im = pl.pallas_call(
+        functools.partial(target_kernel, spots),
+        out_shape=[struct(grid, lanes), struct(box_len, lanes), struct(box_len, lanes)],
+        in_specs=[vmem] * 3,
+        out_specs=[vmem] * 3,
         compiler_params=params_of,
         cost_estimate=cost(1 << 26),
         name="target_terms",
-    )(target_image, *values)
-
-    before, after, packed, source = lax.optimization_barrier((before, after, packed, mask_param))
+    )(target_image, pupil_map, table)
+
+    before, after, packed, source = lax.optimization_barrier((before, after, packed, own))
     far = [
         lax.ppermute(source, "tile", [(i, (i + k) % tiles) for i in range(tiles)])
         for k in far_steps(tiles)
@@ -542,10 +572,10 @@
         pltpu.VMEM((grid, lanes), f32),
         pltpu.VMEM((grid, lanes), f32),
         pltpu.VMEM((count, grid, lanes), f32),
-        pltpu.VMEM((4 * box_len, CHUNK * lanes), bf16),
+        pltpu.VMEM((CHUNK * box_len, lanes), f32),
+        pltpu.VMEM((CHUNK * box_len, lanes), f32),
     ]
-    hold = [pltpu.VMEM((CHUNK * box_len, 2 * lanes), bf16)]
-    hold = hold + [pltpu.VMEM((grid, lanes), f32)] * 4
+    hold = [pltpu.VMEM((grid, lanes), f32)] * 4
     steps = [
         pltpu.VMEM((tiles + 2, tile_len + 2 * MARGIN, tile_len), f32),
         pltpu.VMEM((tiles, tile_len, tile_len), f32),
@@ -554,13 +584,11 @@
     scale = 0.5 / (grid * grid * period * tile_len)
     source_len = struct(count, box_len, lanes)
 
-    fwd = ("spec_cols", "spec_rows", "lane_fwd", "row_fwd", "mix_cols", "mix_rows")
-    names, values = pick(*fwd, "lane_back", "row_back")
     back, pr, pi, info, whole = pl.pallas_call(
-        functools.partial(first_kernel, names, peers, tiles, scale),
+        functools.partial(first_kernel, spots, peers, tiles, scale),
         out_shape=[struct(grid, lanes), source_len, source_len, struct(8, 128),
                    struct(8, 128, kind=jnp.int32)],
-        in_specs=[smem] + [vmem] * (6 + peers + len(names)),
+        in_specs=[smem] + [vmem] * (7 + peers),
         out_specs=[vmem] * 5,
         scratch_shapes=work + hold + [
             pltpu.SMEM((8, 128), jnp.int32),
@@ -570,37 +598,36 @@
         compiler_params=params_of,
         cost_estimate=cost(1 << 32),
         name="first_step",
-    )(tile, pupil_re, pupil_im, target, mask_param, before, after, *packed, *values)
-
-    shared = (tile, whole, info, pr, pi, target)
-    shared_specs = [smem, smem] + [vmem] * 4
-
+    )(tile, table, pupil_re, pupil_im, target, own, before, after, *packed)
+
+    shared = (tile, table, whole, info, pr, pi, target)
+    shared_specs = [smem, vmem, smem] + [vmem] * 4
+
+    back, far = lax.optimization_barrier((back, far))
     backs = ring(back, "tile")
-    entries = [mask_param, *far, mate, *[mates(one) for one in far]]
-    names, values = pick(*fwd, "lane_back", "row_back", "grad_cols", "grad_rows")
+    entries = [own, *far, mate, *[mates(one) for one in far]]
     params, back = pl.pallas_call(
-        functools.partial(next_kernel, names, tiles, scale),
+        functools.partial(next_kernel, spots, tiles, scale),
         out_shape=[struct(tiles * tile_len, tile_len), struct(grid, lanes)],
-        in_specs=shared_specs + [vmem] * (2 * tiles + len(names)),
+        in_specs=shared_specs + [vmem] * (2 * tiles),
         out_specs=[vmem] * 2,
         scratch_shapes=work + hold + steps,
         compiler_params=params_of,
         cost_estimate=cost(1 << 32),
         name="next_step",
-    )(*shared, *entries, *backs, *values)
+    )(*shared, *entries, *backs)
 
     backs = ring(back, "tile")
-    names, values = pick(*fwd, "grad_cols", "grad_rows")
     final, row = pl.pallas_call(
-        functools.partial(last_kernel, names, tiles),
+        functools.partial(last_kernel, spots, tiles),
         out_shape=[struct(tile_len, tile_len), struct(8, count)],
-        in_specs=shared_specs + [vmem] * (1 + tiles + len(names)),
+        in_specs=shared_specs + [vmem] * (1 + tiles),
         out_specs=[vmem] * 2,
         scratch_shapes=work + [pltpu.VMEM((count, lanes), f32)] + steps,
         compiler_params=params_of,
         cost_estimate=cost(1 << 32),
         name="last_step",
-    )(*shared, params, *backs, *values)
+    )(*shared, params, *backs)
 
     rows = ring(row, "tile")
     out = pl.pallas_call(

time: 61.5 us -> 49.5 us (0.80)
  local copies, waits for them, and re-layouts: 8.62 us -> 3.24 us
  waiting for transfers between devices: 18.1 us -> 13.7 us
  Pallas kernels: 20.5 us -> 17.4 us
  starting transfers between devices: 12.9 us -> 14.2 us
    unnamed x38 -> x12, local copies, waits for them, and re-layouts: 6.94 us -> 3.24 us
    ppermute x12, waiting for transfers between devices: 14 us -> 10.7 us  [ring(): lax.ppermute(value, axis, [(i, (i + k) % peers) for i in range(peers)])]
    pallas_call x5, Pallas kernels: 19.7 us -> 16.6 us  [the longest x1 5.45 us: per_device(): pl.pallas_call(functools.partial(next_kernel, spots, tiles, scale), out_s...]
    ppermute x1, waiting for transfers between devices: 4.11 us -> 2.96 us  [per_device(): lax.ppermute(source, 'tile', [(i, (i + k) % tiles) for i in range(tiles)])]
    slice x1 -> x0, local copies, waits for them, and re-layouts: 0.93 us -> none  [per_device(): after = lax.ppermute(mask_param[:MARGIN], 'tile', up)]
    ppermute x12, starting transfers between devices: 9.29 us -> 10 us  [ring(): lax.ppermute(value, axis, [(i, (i + k) % peers) for i in range(peers)])]
    squeeze x1 -> x0, local copies, waits for them, and re-layouts: 0.74 us -> none  [per_device(): real, imag = (jnp.pad(pupil_map[0], pad), jnp.pad(pupil_map[1], pad))]
  transfers between devices with their start and end apart: 17 -> 17, of which waited for: 13 -> 11; matrix products, arithmetic and copies ran while one was open for 1% -> 0% of each run, Pallas kernels for 12% -> 9%
where the time goes in v2:
time: 49.5 us; the launch traced here: 49.2 us
  Pallas kernels  17.4 us (35%)
  starting transfers between devices  14.2 us (29%)
  waiting for transfers between devices  13.7 us (28%)
  local copies, waits for them, and re-layouts  3.24 us (7%)
  between operations  0.72 us (1%)
    ppermute x12, waiting for transfers between devices, ring(): lax.ppermute(value, axis, [(i, (i + k) % peers) for i in range(peers)])  10.7 us
    ppermute x12, starting transfers between devices, ring(): lax.ppermute(value, axis, [(i, (i + k) % peers) for i in range(peers)])  10 us
    pallas_call x1, Pallas kernels, per_device(): pl.pallas_call(functools.partial(next_kernel, spots, tiles, scale), out_s...  5.45 us
    pallas_call x1, Pallas kernels, per_device(): pl.pallas_call(functools.partial(last_kernel, spots, tiles), out_shape=[s...  4.83 us
    pallas_call x1, Pallas kernels, per_device(): pl.pallas_call(functools.partial(first_kernel, spots, peers, tiles, scale...  4.15 us
    unnamed x12, local copies, waits for them, and re-layouts  3.24 us
    ppermute x1, waiting for transfers between devices, per_device(): lax.ppermute(source, 'tile', [(i, (i + k) % tiles) for i in range(tiles)])  2.96 us
    ppermute x1, starting transfers between devices, per_device(): after = lax.ppermute(top, 'tile', up)  2.01 us
  transfers between devices with their start and end apart: 17, of which 11 were waited for; matrix products, arithmetic and copies ran while one was open for 0% of the time, Pallas kernels for 9%

profile of v2, /device:TPU:0, one launch (start us, length us, event | category | flops | bytes accessed | tf_op | source)
XLA Modules:
  0.0 49.2 jit_solution(15202919101024575543)
XLA Ops:
  0.6 1.8 %open_step.1 = (f32[256,256]{1,0:T(8,128)}, f32[64,256]{1,0:T(8,128)}, f32[64,256]{1,0:T(8,128)}, f32[8,128]{1,0:T(8,128)}) custom-call(s32[1]{0:T(128)} %bitcast.1.place, f32[256,256]{1,0:T(8,128)} %mask.1, f32[1,16]{1,0:T(1,128)} %bitcast.6, s32[2,16]{1,0:T(2,128)} %bitcast.5), custom_call_target="tpu_custom_call" | custom-call | tf_op jit(solution)/shard_map/open_step/pallas_call | solution.py:533
  2.5 0.5 %collective-permute-start = (f32[64,256]{1,0:T(8,128)}, f32[64,256]{1,0:T(8,128)S(1)}, u32[]{:S(2)}, u32[]{:S(2)}) collective-permute-start(f32[64,256]{1,0:T(8,128)} %get-tuple-element.31), channel_id=1, source_target_pairs={{0,1},{1,2},{2,3},{3,0},{4,5},{5,6},{6,7},{7,4},{8,9},{9,10},{10,1... | collective-permute-start | bytes 196616 | tf_op jit(solution)/shard_map/ppermute | solution.py:549
  3.0 2.0 %collective-permute-start.1 = (f32[64,256]{1,0:T(8,128)}, f32[64,256]{1,0:T(8,128)S(1)}, u32[]{:S(2)}, u32[]{:S(2)}) collective-permute-start(f32[64,256]{1,0:T(8,128)} %get-tuple-element.32), channel_id=1, source_target_pairs={{1,0},{2,1},{3,2},{0,3},{5,4},{6,5},{7,6},{4,7},{9,8},{10,9},{11,1... | collective-permute-start | bytes 196616 | tf_op jit(solution)/shard_map/ppermute | solution.py:550
  5.0 4.3 %collective-permute-start.4 = (f32[8,128]{1,0:T(8,128)}, f32[8,128]{1,0:T(8,128)S(1)}, u32[]{:S(2)}, u32[]{:S(2)}) collective-permute-start(f32[8,128]{1,0:T(8,128)} %get-tuple-element.36.refs_0_), channel_id=1, source_target_pairs={{0,12},{4,0},{8,4},{12,8},{1,13},{5,1},{9,5},{13,9},{2,14},{6,2},{... | collective-permute-start | bytes 12296 | tf_op jit(solution)/shard_map/ppermute | solution.py:489
  9.4 1.0 %collective-permute-start.2 = (f32[8,128]{1,0:T(8,128)}, f32[8,128]{1,0:T(8,128)S(1)}, u32[]{:S(2)}, u32[]{:S(2)}) collective-permute-start(f32[8,128]{1,0:T(8,128)} %get-tuple-element.36.refs_0_), channel_id=1, source_target_pairs={{0,4},{4,8},{8,12},{12,0},{1,5},{5,9},{9,13},{13,1},{2,6},{6,10},{... | collective-permute-start | bytes 12296 | tf_op jit(solution)/shard_map/ppermute | solution.py:489
  10.4 1.5 %copy-done = bf16[1856,512]{1,0:T(8,128)(2,1)S(1)} copy-done((bf16[1856,512]{1,0:T(8,128)(2,1)S(1)}, bf16[1856,512]{1,0:T(8,128)(2,1)}, u32[]{:S(2)}) %copy-start) | copy-done | bytes 1900568
  11.9 0.9 %copy-done.2 = f32[256,256]{1,0:T(8,128)S(1)} copy-done((f32[256,256]{1,0:T(8,128)S(1)}, f32[256,256]{1,0:T(8,128)}, u32[]{:S(2)}) %copy-start.2) | copy-done | bytes 262168
  12.8 0.8 %copy-done.3 = f32[2,32,32]{2,1,0:T(8,128)S(1)} copy-done((f32[2,32,32]{2,1,0:T(8,128)S(1)}, f32[2,32,32]{2,1,0:T(8,128)}, u32[]{:S(2)}) %copy-start.3) | copy-done | bytes 8216
  14.1 0.9 %collective-permute-done.2.refs_1_ = f32[8,128]{1,0:T(8,128)S(1)} collective-permute-done((f32[8,128]{1,0:T(8,128)}, f32[8,128]{1,0:T(8,128)S(1)}, u32[]{:S(2)}, u32[]{:S(2)}) %collective-permute-start.2) | collective-permute-done | bytes 4128 | tf_op jit(solution)/shard_map/ppermute | solution.py:489
  15.1 1.6 %collective-permute-start.5 = (f32[256,256]{1,0:T(8,128)S(1)}, f32[256,256]{1,0:T(8,128)S(1)}, u32[]{:S(2)}, u32[]{:S(2)}) collective-permute-start(f32[256,256]{1,0:T(8,128)S(1)} %copy-done.4), channel_id=1, source_target_pairs={{0,2},{1,3},{2,0},{3,1},{4,6},{5,7},{6,4},{7,5},{8,10},{9,11},{10,... | collective-permute-start | bytes 786440 | tf_op jit(solution)/shard_map/ppermute | solution.py:566
  16.7 4.1 %first_step.1 = (f32[64,128]{1,0:T(8,128)S(1)}, f32[64,32,128]{2,1,0:T(8,128)S(1)}, f32[64,32,128]{2,1,0:T(8,128)S(1)}, f32[8,128]{1,0:T(8,128)S(1)}, s32[8,128]{1,0:T(8,128)S(1)}) custom-call(s32[1]{0:T(128)} %bitcast.tile, bf16[1856,512]{1,0:T(8,128)(2,1)S(1)} %copy-done.1, f32[32,128]{1,0:T(8,128)S(1)} %get-tuple-element.27.pupil_re, ...), custom_call_target="tpu_custom_call" | custom-call | flops 4294967296 | bytes 1048576 | tf_op jit(solution)/shard_map/first_step/pallas_call | solution.py:587
  20.8 3.0 %collective-permute-done.5.refs_1_ = f32[256,256]{1,0:T(8,128)S(1)} collective-permute-done((f32[256,256]{1,0:T(8,128)S(1)}, f32[256,256]{1,0:T(8,128)S(1)}, u32[]{:S(2)}, u32[]{:S(2)}) %collective-permute-start.5) | collective-permute-done | bytes 262176 | tf_op jit(solution)/shard_map/ppermute | solution.py:566
  23.8 1.6 %collective-permute-start.10 = (f32[64,128]{1,0:T(8,128)S(1)}, f32[64,128]{1,0:T(8,128)S(1)}, u32[]{:S(2)}, u32[]{:S(2)}) collective-permute-start(f32[64,128]{1,0:T(8,128)S(1)} %get-tuple-element.47.refs_4_), channel_id=1, source_target_pairs={{0,3},{1,0},{2,1},{3,2},{4,7},{5,4},{6,5},{7,6},{8,11},{9,8},{10,9... | collective-permute-start | bytes 98312 | tf_op jit(solution)/shard_map/ppermute | solution.py:489
  25.4 0.5 %collective-permute-start.9 = (f32[64,128]{1,0:T(8,128)S(1)}, f32[64,128]{1,0:T(8,128)S(1)}, u32[]{:S(2)}, u32[]{:S(2)}) collective-permute-start(f32[64,128]{1,0:T(8,128)S(1)} %get-tuple-element.47.refs_4_), channel_id=1, source_target_pairs={{0,2},{1,3},{2,0},{3,1},{4,6},{5,7},{6,4},{7,5},{8,10},{9,11},{10,... | collective-permute-start | bytes 98312 | tf_op jit(solution)/shard_map/ppermute | solution.py:489
  25.9 1.1 %collective-permute-done.10.refs_7_ = f32[64,128]{1,0:T(8,128)S(1)} collective-permute-done((f32[64,128]{1,0:T(8,128)S(1)}, f32[64,128]{1,0:T(8,128)S(1)}, u32[]{:S(2)}, u32[]{:S(2)}) %collective-permute-start.10) | collective-permute-done | bytes 32800 | tf_op jit(solution)/shard_map/ppermute | solution.py:489
  27.0 2.6 %collective-permute-done.9.refs_6_ = f32[64,128]{1,0:T(8,128)S(1)} collective-permute-done((f32[64,128]{1,0:T(8,128)S(1)}, f32[64,128]{1,0:T(8,128)S(1)}, u32[]{:S(2)}, u32[]{:S(2)}) %collective-permute-start.9) | collective-permute-done | bytes 32800 | tf_op jit(solution)/shard_map/ppermute | solution.py:489
  29.6 5.4 %next_step.1 = (f32[1024,256]{1,0:T(8,128)S(1)}, f32[64,128]{1,0:T(8,128)S(1)}) custom-call(s32[1]{0:T(128)} %bitcast.tile, bf16[1856,512]{1,0:T(8,128)(2,1)S(1)} %copy-done.1, s32[8,128]{1,0:T(8,128)S(1)} %get-tuple-element.40.shifts, f32[8,128]{1,0:T(8,128)S(1)} %get-tuple-element.41.info, f32[64,32,128]{2,1,0:T(8,128)S(1)} %get-tuple-element.42.pr, ...), custom_call_target="tpu_custom_call" | custom-call | flops 4294967296 | bytes 1048576 | tf_op jit(solution)/shard_map/next_step/pallas_call | solution.py:609
  35.1 1.2 %collective-permute-start.12 = (f32[64,128]{1,0:T(8,128)S(1)}, f32[64,128]{1,0:T(8,128)S(1)}, u32[]{:S(2)}, u32[]{:S(2)}) collective-permute-start(f32[64,128]{1,0:T(8,128)S(1)} %get-tuple-element.49.refs_0_), channel_id=1, source_target_pairs={{0,2},{1,3},{2,0},{3,1},{4,6},{5,7},{6,4},{7,5},{8,10},{9,11},{10,... | collective-permute-start | bytes 98312 | tf_op jit(solution)/shard_map/ppermute | solution.py:489
  36.7 2.4 %collective-permute-done.12.refs_2_ = f32[64,128]{1,0:T(8,128)S(1)} collective-permute-done((f32[64,128]{1,0:T(8,128)S(1)}, f32[64,128]{1,0:T(8,128)S(1)}, u32[]{:S(2)}, u32[]{:S(2)}) %collective-permute-start.12) | collective-permute-done | bytes 32800 | tf_op jit(solution)/shard_map/ppermute | solution.py:489
  39.1 0.6 %collective-permute-done.11.refs_1_ = f32[64,128]{1,0:T(8,128)S(1)} collective-permute-done((f32[64,128]{1,0:T(8,128)S(1)}, f32[64,128]{1,0:T(8,128)S(1)}, u32[]{:S(2)}, u32[]{:S(2)}) %collective-permute-start.11) | collective-permute-done | bytes 32800 | tf_op jit(solution)/shard_map/ppermute | solution.py:489
  39.7 4.8 %last_step.1 = (f32[256,256]{1,0:T(8,128)}, f32[8,64]{1,0:T(8,128)S(1)}) custom-call(s32[1]{0:T(128)} %bitcast.tile, bf16[1856,512]{1,0:T(8,128)(2,1)S(1)} %copy-done.1, s32[8,128]{1,0:T(8,128)S(1)} %get-tuple-element.40.shifts, f32[8,128]{1,0:T(8,128)S(1)} %get-tuple-element.41.info, f32[64,32,128]{2,1,0:T(8,128)S(1)} %get-tuple-element.42.pr, ...), custom_call_target="tpu_custom_call" | custom-call | flops 4294967296 | bytes 1048576 | tf_op jit(solution)/shard_map/last_step/pallas_call | solution.py:621
  44.5 0.9 %collective-permute-start.15 = (f32[8,64]{1,0:T(8,128)S(1)}, f32[8,64]{1,0:T(8,128)S(1)}, u32[]{:S(2)}, u32[]{:S(2)}) collective-permute-start(f32[8,64]{1,0:T(8,128)S(1)} %get-tuple-element.51.refs_0_), channel_id=1, source_target_pairs={{0,2},{1,3},{2,0},{3,1},{4,6},{5,7},{6,4},{7,5},{8,10},{9,11},{10,... | collective-permute-start | bytes 6152 | tf_op jit(solution)/shard_map/ppermute | solution.py:489
  45.8 2.3 %collective-permute-done.15.refs_2_ = f32[8,64]{1,0:T(8,128)S(1)} collective-permute-done((f32[8,64]{1,0:T(8,128)S(1)}, f32[8,64]{1,0:T(8,128)S(1)}, u32[]{:S(2)}, u32[]{:S(2)}) %collective-permute-start.15) | collective-permute-done | bytes 2080 | tf_op jit(solution)/shard_map/ppermute | solution.py:489
  48.4 0.8 %weight_step.1 = f32[1,16]{1,0:T(1,128)} custom-call(s32[1]{0:T(128)} %bitcast.tile, s32[1]{0:T(128)} %bitcast.1.place, f32[8,128]{1,0:T(8,128)S(1)} %get-tuple-element.41.info, f32[8,64]{1,0:T(8,128)S(1)} %get-tuple-element.51.refs_0_, f32[8,64]{1,0:T(8,128)S(1)} %collective-permute-done.14.refs_1_, f32[8,64]{1,0:T(8,128)S(1)} %collective-permute-done.15.refs_2_, ...), custom_call_target="tpu_custom_call" | custom-call | tf_op jit(solution)/shard_map/weight_step/pallas_call | solution.py:633
  (28 shorter events, 1.7 us)
Async XLA Ops:
  2.5 14.2 %copy-start.5 = (f32[8,128]{1,0:T(8,128)S(1)}, f32[8,128]{1,0:T(8,128)}, u32[]{:S(2)}) copy-start(f32[8,128]{1,0:T(8,128)} %get-tuple-element.36.refs_0_) | copy-start | bytes 12292
  2.5 12.5 %collective-permute-start = (f32[64,256]{1,0:T(8,128)}, f32[64,256]{1,0:T(8,128)S(1)}, u32[]{:S(2)}, u32[]{:S(2)}) collective-permute-start(f32[64,256]{1,0:T(8,128)} %get-tuple-element.31), channel_id=1, source_target_pairs={{0,1},{1,2},{2,3},{3,0},{4,5},{5,6},{6,7},{7,4},{8,9},{9,10},{10,1... | collective-permute-start | bytes 196616 | tf_op jit(solution)/shard_map/ppermute | solution.py:549
  3.0 12.0 %collective-permute-start.1 = (f32[64,256]{1,0:T(8,128)}, f32[64,256]{1,0:T(8,128)S(1)}, u32[]{:S(2)}, u32[]{:S(2)}) collective-permute-start(f32[64,256]{1,0:T(8,128)} %get-tuple-element.32), channel_id=1, source_target_pairs={{1,0},{2,1},{3,2},{0,3},{5,4},{6,5},{7,6},{4,7},{9,8},{10,9},{11,1... | collective-permute-start | bytes 196616 | tf_op jit(solution)/shard_map/ppermute | solution.py:550
  5.0 8.9 %collective-permute-start.4 = (f32[8,128]{1,0:T(8,128)}, f32[8,128]{1,0:T(8,128)S(1)}, u32[]{:S(2)}, u32[]{:S(2)}) collective-permute-start(f32[8,128]{1,0:T(8,128)} %get-tuple-element.36.refs_0_), channel_id=1, source_target_pairs={{0,12},{4,0},{8,4},{12,8},{1,13},{5,1},{9,5},{13,9},{2,14},{6,2},{... | collective-permute-start | bytes 12296 | tf_op jit(solution)/shard_map/ppermute | solution.py:489
  9.4 4.7 %collective-permute-start.3 = (f32[8,128]{1,0:T(8,128)}, f32[8,128]{1,0:T(8,128)S(1)}, u32[]{:S(2)}, u32[]{:S(2)}) collective-permute-start(f32[8,128]{1,0:T(8,128)} %get-tuple-element.36.refs_0_), channel_id=1, source_target_pairs={{0,8},{4,12},{8,0},{12,4},{1,9},{5,13},{9,1},{13,5},{2,10},{6,14},... | collective-permute-start | bytes 12296 | tf_op jit(solution)/shard_map/ppermute | solution.py:489
  9.4 5.6 %collective-permute-start.2 = (f32[8,128]{1,0:T(8,128)}, f32[8,128]{1,0:T(8,128)S(1)}, u32[]{:S(2)}, u32[]{:S(2)}) collective-permute-start(f32[8,128]{1,0:T(8,128)} %get-tuple-element.36.refs_0_), channel_id=1, source_target_pairs={{0,4},{4,8},{8,12},{12,0},{1,5},{5,9},{9,13},{13,1},{2,6},{6,10},{... | collective-permute-start | bytes 12296 | tf_op jit(solution)/shard_map/ppermute | solution.py:489
  10.4 1.5 %copy-start = (bf16[1856,512]{1,0:T(8,128)(2,1)S(1)}, bf16[1856,512]{1,0:T(8,128)(2,1)}, u32[]{:S(2)}) copy-start(bf16[1856,512]{1,0:T(8,128)(2,1)} %constant.9.clone.whole.table) | copy-start | bytes 5701636
  11.9 0.9 %copy-start.2 = (f32[256,256]{1,0:T(8,128)S(1)}, f32[256,256]{1,0:T(8,128)}, u32[]{:S(2)}) copy-start(f32[256,256]{1,0:T(8,128)} %target.1) | copy-start | bytes 786436
  12.8 0.8 %copy-start.3 = (f32[2,32,32]{2,1,0:T(8,128)S(1)}, f32[2,32,32]{2,1,0:T(8,128)}, u32[]{:S(2)}) copy-start(f32[2,32,32]{2,1,0:T(8,128)} %pupil.1) | copy-start | bytes 24580
  13.6 1.4 %copy-start.4 = (f32[256,256]{1,0:T(8,128)S(1)}, f32[256,256]{1,0:T(8,128)}, u32[]{:S(2)}) copy-start(f32[256,256]{1,0:T(8,128)} %get-tuple-element.45.own.refs_0_) | copy-start | bytes 786436
  13.6 3.1 %copy-start.1 = (bf16[1856,512]{1,0:T(8,128)(2,1)S(1)}, bf16[1856,512]{1,0:T(8,128)(2,1)}, u32[]{:S(2)}) copy-start(bf16[1856,512]{1,0:T(8,128)(2,1)} %constant.9.clone.whole.table) | copy-start | bytes 5701636
  15.0 10.9 %collective-permute-start.6 = (f32[256,256]{1,0:T(8,128)S(1)}, f32[256,256]{1,0:T(8,128)S(1)}, u32[]{:S(2)}, u32[]{:S(2)}) collective-permute-start(f32[256,256]{1,0:T(8,128)S(1)} %copy-done.4), channel_id=1, source_target_pairs={{0,1},{1,0},{2,3},{3,2},{4,5},{5,4},{6,7},{7,6},{8,9},{9,8},{10,11... | collective-permute-start | bytes 786440 | tf_op jit(solution)/shard_map/ppermute | solution.py:495
  15.1 8.7 %collective-permute-start.5 = (f32[256,256]{1,0:T(8,128)S(1)}, f32[256,256]{1,0:T(8,128)S(1)}, u32[]{:S(2)}, u32[]{:S(2)}) collective-permute-start(f32[256,256]{1,0:T(8,128)S(1)} %copy-done.4), channel_id=1, source_target_pairs={{0,2},{1,3},{2,0},{3,1},{4,6},{5,7},{6,4},{7,5},{8,10},{9,11},{10,... | collective-permute-start | bytes 786440 | tf_op jit(solution)/shard_map/ppermute | solution.py:566
  23.8 5.8 %collective-permute-start.7 = (f32[256,256]{1,0:T(8,128)S(1)}, f32[256,256]{1,0:T(8,128)S(1)}, u32[]{:S(2)}, u32[]{:S(2)}) collective-permute-start(f32[256,256]{1,0:T(8,128)S(1)} %collective-permute-done.5.refs_1_), channel_id=1, source_target_pairs={{0,1},{1,0},{2,3},{3,2},{4,5},{5,4},{6,7},{7,6},{8,9},{9,8},{10,11... | collective-permute-start | bytes 786440 | tf_op jit(solution)/shard_map/ppermute | solution.py:495
  23.8 3.2 %collective-permute-start.10 = (f32[64,128]{1,0:T(8,128)S(1)}, f32[64,128]{1,0:T(8,128)S(1)}, u32[]{:S(2)}, u32[]{:S(2)}) collective-permute-start(f32[64,128]{1,0:T(8,128)S(1)} %get-tuple-element.47.refs_4_), channel_id=1, source_target_pairs={{0,3},{1,0},{2,1},{3,2},{4,7},{5,4},{6,5},{7,6},{8,11},{9,8},{10,9... | collective-permute-start | bytes 98312 | tf_op jit(solution)/shard_map/ppermute | solution.py:489
  25.4 4.2 %collective-permute-start.9 = (f32[64,128]{1,0:T(8,128)S(1)}, f32[64,128]{1,0:T(8,128)S(1)}, u32[]{:S(2)}, u32[]{:S(2)}) collective-permute-start(f32[64,128]{1,0:T(8,128)S(1)} %get-tuple-element.47.refs_4_), channel_id=1, source_target_pairs={{0,2},{1,3},{2,0},{3,1},{4,6},{5,7},{6,4},{7,5},{8,10},{9,11},{10,... | collective-permute-start | bytes 98312 | tf_op jit(solution)/shard_map/ppermute | solution.py:489
  25.9 3.7 %collective-permute-start.8 = (f32[64,128]{1,0:T(8,128)S(1)}, f32[64,128]{1,0:T(8,128)S(1)}, u32[]{:S(2)}, u32[]{:S(2)}) collective-permute-start(f32[64,128]{1,0:T(8,128)S(1)} %get-tuple-element.47.refs_4_), channel_id=1, source_target_pairs={{0,1},{1,2},{2,3},{3,0},{4,5},{5,6},{6,7},{7,4},{8,9},{9,10},{10,1... | collective-permute-start | bytes 98312 | tf_op jit(solution)/shard_map/ppermute | solution.py:489
  35.1 1.6 %collective-permute-start.13 = (f32[64,128]{1,0:T(8,128)S(1)}, f32[64,128]{1,0:T(8,128)S(1)}, u32[]{:S(2)}, u32[]{:S(2)}) collective-permute-start(f32[64,128]{1,0:T(8,128)S(1)} %get-tuple-element.49.refs_0_), channel_id=1, source_target_pairs={{0,3},{1,0},{2,1},{3,2},{4,7},{5,4},{6,5},{7,6},{8,11},{9,8},{10,9... | collective-permute-start | bytes 98312 | tf_op jit(solution)/shard_map/ppermute | solution.py:489
  35.1 4.0 %collective-permute-start.12 = (f32[64,128]{1,0:T(8,128)S(1)}, f32[64,128]{1,0:T(8,128)S(1)}, u32[]{:S(2)}, u32[]{:S(2)}) collective-permute-start(f32[64,128]{1,0:T(8,128)S(1)} %get-tuple-element.49.refs_0_), channel_id=1, source_target_pairs={{0,2},{1,3},{2,0},{3,1},{4,6},{5,7},{6,4},{7,5},{8,10},{9,11},{10,... | collective-permute-start | bytes 98312 | tf_op jit(solution)/shard_map/ppermute | solution.py:489
  36.3 3.3 %collective-permute-start.11 = (f32[64,128]{1,0:T(8,128)S(1)}, f32[64,128]{1,0:T(8,128)S(1)}, u32[]{:S(2)}, u32[]{:S(2)}) collective-permute-start(f32[64,128]{1,0:T(8,128)S(1)} %get-tuple-element.49.refs_0_), channel_id=1, source_target_pairs={{0,1},{1,2},{2,3},{3,0},{4,5},{5,6},{6,7},{7,4},{8,9},{9,10},{10,1... | collective-permute-start | bytes 98312 | tf_op jit(solution)/shard_map/ppermute | solution.py:489
  44.5 1.3 %collective-permute-start.16 = (f32[8,64]{1,0:T(8,128)S(1)}, f32[8,64]{1,0:T(8,128)S(1)}, u32[]{:S(2)}, u32[]{:S(2)}) collective-permute-start(f32[8,64]{1,0:T(8,128)S(1)} %get-tuple-element.51.refs_0_), channel_id=1, source_target_pairs={{0,3},{1,0},{2,1},{3,2},{4,7},{5,4},{6,5},{7,6},{8,11},{9,8},{10,9... | collective-permute-start | bytes 6152 | tf_op jit(solution)/shard_map/ppermute | solution.py:489
  44.5 3.6 %collective-permute-start.15 = (f32[8,64]{1,0:T(8,128)S(1)}, f32[8,64]{1,0:T(8,128)S(1)}, u32[]{:S(2)}, u32[]{:S(2)}) collective-permute-start(f32[8,64]{1,0:T(8,128)S(1)} %get-tuple-element.51.refs_0_), channel_id=1, source_target_pairs={{0,2},{1,3},{2,0},{3,1},{4,6},{5,7},{6,4},{7,5},{8,10},{9,11},{10,... | collective-permute-start | bytes 6152 | tf_op jit(solution)/shard_map/ppermute | solution.py:489
  45.4 3.0 %collective-permute-start.14 = (f32[8,64]{1,0:T(8,128)S(1)}, f32[8,64]{1,0:T(8,128)S(1)}, u32[]{:S(2)}, u32[]{:S(2)}) collective-permute-start(f32[8,64]{1,0:T(8,128)S(1)} %get-tuple-element.51.refs_0_), channel_id=1, source_target_pairs={{0,1},{1,2},{2,3},{3,0},{4,5},{5,6},{6,7},{7,4},{8,9},{9,10},{10,1... | collective-permute-start | bytes 6152 | tf_op jit(solution)/shard_map/ppermute | solution.py:489

commit v3 on v2

--- a/solution.py
+++ b/solution.py
@@ -10,12 +10,14 @@
 from jax.experimental.pallas import tpu as pltpu
 from jax.sharding import PartitionSpec as P
 
+
 MARGIN = 64
 MAX_SHIFT = 16
 MASK_RATE = 0.5
 WEIGHT_RATE = 0.3
 TINY_EPS = 1e-06
 CHUNK = 16
+
 
 bf16 = jnp.bfloat16
 f32 = jnp.float32
@@ -60,6 +62,7 @@
     out["row_fwd"] = np.concatenate([high, high, low], 1)
     high, low = np_split(np.concatenate([np.cos(ang).T, np.sin(ang).T], 0))
     out["row_back"] = np.concatenate([high, high, low], 1)
+
     def dirichlet(offset):
         theta = 2.0 * math.pi * ((pix + offset)[None, :] / period - points[:, None] / grid)
         orders = np.arange(1, box_len)
@@ -243,8 +246,8 @@
     return (sums[0][...] + sums[2][...] + swap(sums[1][...] + sums[3][...])) * scale
 
 
-def tile_of(k, tile, tiles):
-    return lax.rem(tile + tiles - k, tiles)
+def tile_of(k, tile):
+    return lax.bitwise_xor(tile, jnp.int32(k))
 
 
 def mask_grads(params, ids, backs, t, tile, tiles, wins, grads):
@@ -261,7 +264,7 @@
         part = mid[k * grid : (k + 1) * grid]
         high, low = split(jnp.concatenate([part[:, :tile_len], part[:, tile_len:]], 0))
         out = dot(t["grad_rows"][...], jnp.concatenate([high, low, high], 0))
-        wins[tile_of(k, tile, tiles) + 1] = out
+        wins[tile_of(k, tile) + 1] = out
     square = jnp.zeros((8, tile_len), f32)
     for k in range(tiles):
         own = ids[k]
@@ -297,26 +300,20 @@
     return copies
 
 
-def open_kernel(place, mask, weights, shifts, own, top, low, packed, hold_w, hold_s, sems):
-    rows, local = mask.shape[0], weights.shape[1]
-    copies = start_all(
-        (
-            (weights, hold_w),
-            (shifts, hold_s),
-            (mask.at[pl.ds(0, MARGIN), :], top),
-            (mask.at[pl.ds(rows - MARGIN, MARGIN), :], low),
-            (mask, own),
-        ),
-        sems,
-    )
-    copies[0].wait()
-    copies[1].wait()
+def pack_kernel(place, weights, shifts, packed, hold_w, hold_s, sems):
+    local = weights.shape[1]
+    for copy in start_all(((weights, hold_w), (shifts, hold_s)), sems):
+        copy.wait()
     packed[...] = jnp.zeros_like(packed)
     packed[0:1, :local] = hold_w[...]
     packed[1:3, :local] = hold_s[...].astype(f32)
     packed[3:4, :local] = jnp.sqrt(hold_w[...])
     packed[...] = pltpu.roll(packed[...], place[0] * local, 1)
-    for copy in copies[2:]:
+
+
+def edge_kernel(tile, mask, edge, sems):
+    at = pl.multiple_of(lax.rem(tile[0], 2) * (mask.shape[0] - MARGIN), MARGIN)
+    for copy in start_all(((mask.at[pl.ds(at, MARGIN), :], edge),), sems):
         copy.wait()
 
 
@@ -342,7 +339,7 @@
 
 
 def first_kernel(spots, peers, tiles, scale, tile, table, pupil_re, pupil_im, target,
-                 own, before, after, *refs):
+                 own, mate, cross, *refs):
     parts = refs[:peers]
     t = {n: table.at[spot] for n, spot in spots.items()}
     back, pr, pi, info, whole = refs[peers : peers + 5]
@@ -361,8 +358,11 @@
         copy.start()
     has_prev = (here > 0).astype(f32)
     has_next = (here < tiles - 1).astype(f32)
+    odd = lax.rem(here, 2) > 0
+    before = jnp.where(odd, mate[-MARGIN:, :], cross[...])
+    after = jnp.where(odd, cross[...], mate[:MARGIN, :])
     window = jnp.concatenate(
-        [sigmoid(before[...]) * has_prev, sigmoid(own[...]), sigmoid(after[...]) * has_next], 0
+        [sigmoid(before) * has_prev, sigmoid(own[...]), sigmoid(after) * has_next], 0
     )
     spec = window_spectrum(window, t)
     for copy in copies:
@@ -381,7 +381,7 @@
     new, back, *work, s0, s1, s2, s3, wins, grads = refs[2 * tiles :]
     here = tile[0]
     tile_len = params[0].shape[0]
-    ids = entry_ids(here, tiles)
+    ids = [tile_of(k, here) for k in range(tiles)]
     rate = mask_grads(
         lambda k, low, high: params[k][low:high, :], ids, backs, t, here, tiles, wins, grads
     )
@@ -465,9 +465,9 @@
     for k in range(tiles):
         stack[k] = rows[k][...]
     here = tile[0]
-    total = stack[lax.rem(here, tiles)]
+    total = stack[here]
     for k in range(1, tiles):
-        total = total + stack[tile_of(k, here, tiles)]
+        total = total + stack[tile_of(k, here)]
     summed = total[0:1] * scale
     weight = info[0:1, :count]
     dose = jnp.sum(weight, axis=1, keepdims=True)
@@ -483,25 +483,12 @@
     out[...] = new[0:1, :size]
 
 
-def ring(value, axis):
-    peers = lax.axis_size(axis)
-    return [value] + [
-        lax.ppermute(value, axis, [(i, (i + k) % peers) for i in range(peers)])
-        for k in range(1, peers)
-    ]
-
-
-def mates(value):
-    return lax.ppermute(value, "tile", [(i, i ^ 1) for i in range(lax.axis_size("tile"))])
-
-
-def far_steps(tiles):
-    return range(2, tiles, 2)
-
-
-def entry_ids(tile, tiles):
-    even = [tile] + [tile_of(k, tile, tiles) for k in far_steps(tiles)]
-    return even + [one + 1 - 2 * lax.rem(one, 2) for one in even]
+def crossed(value, axis, k):
+    return lax.ppermute(value, axis, [(i, i ^ k) for i in range(lax.axis_size(axis))])
+
+
+def all_of(value, axis):
+    return [value] + [crossed(value, axis, k) for k in range(1, lax.axis_size(axis))]
 
 
 def per_device(mask_param, target_image, source_weights, source_shifts, pupil_map):
@@ -513,7 +500,7 @@
     peers = lax.axis_size("src")
     local = source_weights.shape[0]
     count = local * peers
-    assert tiles % 2 == 0 and count <= 128 and count % CHUNK == 0
+    assert tiles & (tiles - 1) == 0 and peers & (peers - 1) == 0 and count <= 128 and count % CHUNK == 0
     tables = make_tables(tile_len, box_len, MAX_SHIFT)
 
     tile = lax.axis_index("tile").astype(jnp.int32).reshape(1)
@@ -530,24 +517,32 @@
     def cost(flops):
         return pl.CostEstimate(flops=flops, bytes_accessed=1 << 20, transcendentals=0)
 
-    own, top, low, packed = pl.pallas_call(
-        open_kernel,
-        out_shape=[struct(tile_len, tile_len), struct(MARGIN, tile_len),
-                   struct(MARGIN, tile_len), struct(8, 128)],
-        in_specs=[smem, left, left, left],
-        out_specs=[vmem] * 4,
+    packed = pl.pallas_call(
+        pack_kernel,
+        out_shape=struct(8, 128),
+        in_specs=[smem, left, left],
+        out_specs=vmem,
         scratch_shapes=[
             pltpu.VMEM((1, local), f32),
             pltpu.VMEM((2, local), jnp.int32),
-            pltpu.SemaphoreType.DMA((5,)),
+            pltpu.SemaphoreType.DMA((2,)),
         ],
-        name="open_step",
-    )(place, mask_param, source_weights[None], source_shifts.T)
-    packed = ring(packed, "src")
-    down = [(i, (i + 1) % tiles) for i in range(tiles)]
-    up = [(j, i) for i, j in down]
-    before = lax.ppermute(low, "tile", down)
-    after = lax.ppermute(top, "tile", up)
+        name="pack_sources",
+    )(place, source_weights[None], source_shifts.T)
+    packed = all_of(packed, "src")
+
+    edge = pl.pallas_call(
+        edge_kernel,
+        out_shape=struct(MARGIN, tile_len),
+        in_specs=[smem, left],
+        out_specs=vmem,
+        scratch_shapes=[pltpu.SemaphoreType.DMA((1,))],
+        name="edge_rows",
+    )(tile, mask_param)
+    pairs = [(i, (i + 1) % tiles) for i in range(1, tiles, 2)]
+    cross = lax.ppermute(edge, "tile", pairs + [(j, i) for i, j in pairs])
+    mate = crossed(mask_param, "tile", 1)
+    far = [crossed(mask_param, "tile", k) for k in range(2, tiles, 2)]
 
     whole, spots = pack_tables(tables)
     table = jnp.asarray(whole)
@@ -560,13 +555,6 @@
         cost_estimate=cost(1 << 26),
         name="target_terms",
     )(target_image, pupil_map, table)
-
-    before, after, packed, source = lax.optimization_barrier((before, after, packed, own))
-    far = [
-        lax.ppermute(source, "tile", [(i, (i + k) % tiles) for i in range(tiles)])
-        for k in far_steps(tiles)
-    ]
-    mate = mates(source)
 
     work = [
         pltpu.VMEM((grid, lanes), f32),
@@ -598,14 +586,16 @@
         compiler_params=params_of,
         cost_estimate=cost(1 << 32),
         name="first_step",
-    )(tile, table, pupil_re, pupil_im, target, own, before, after, *packed)
+    )(tile, table, pupil_re, pupil_im, target, mask_param, mate, cross, *packed)
 
     shared = (tile, table, whole, info, pr, pi, target)
     shared_specs = [smem, vmem, smem] + [vmem] * 4
 
     back, far = lax.optimization_barrier((back, far))
-    backs = ring(back, "tile")
-    entries = [own, *far, mate, *[mates(one) for one in far]]
+    backs = all_of(back, "tile")
+    entries = [mask_param, mate]
+    for one in far:
+        entries += [one, crossed(one, "tile", 1)]
     params, back = pl.pallas_call(
         functools.partial(next_kernel, spots, tiles, scale),
         out_shape=[struct(tiles * tile_len, tile_len), struct(grid, lanes)],
@@ -617,7 +607,7 @@
         name="next_step",
     )(*shared, *entries, *backs)
 
-    backs = ring(back, "tile")
+    backs = all_of(back, "tile")
     final, row = pl.pallas_call(
         functools.partial(last_kernel, spots, tiles),
         out_shape=[struct(tile_len, tile_len), struct(8, count)],
@@ -629,7 +619,7 @@
         name="last_step",
     )(*shared, params, *backs)
 
-    rows = ring(row, "tile")
+    rows = all_of(row, "tile")
     out = pl.pallas_call(
         functools.partial(weight_kernel, tiles, 1.0 / (grid * grid)),
         out_shape=struct(1, local),

time: 49.5 us -> 46.9 us (0.947)
  waiting for transfers between devices: 13.7 us -> 9.41 us
  Pallas kernels: 17.4 us -> 18.3 us
  local copies, waits for them, and re-layouts: 3.24 us -> 3.95 us
    ppermute x17 -> x16, waiting for transfers between devices: 13.7 us -> 9.41 us  [the longest x15 9.41 us: crossed(): lax.ppermute(value, axis, [(i, i ^ k) for i in range(lax.axis_size(axis))])]
    pallas_call x1 -> x2, Pallas kernels: 1.83 us -> 2.86 us  [the longest x1 1.48 us: per_device(): pl.pallas_call(edge_kernel, out_shape=struct(MARGIN, tile_len), in_specs=...]
    unnamed x12, local copies, waits for them, and re-layouts: 3.24 us -> 3.95 us
    ppermute x17 -> x16, starting transfers between devices: 14.2 us -> 14.1 us  [the longest x15 11.5 us: crossed(): lax.ppermute(value, axis, [(i, i ^ k) for i in range(lax.axis_size(axis))])]
  transfers between devices with their start and end apart: 17 -> 16, of which waited for: 11 -> 7; matrix products, arithmetic and copies ran while one was open for 0% -> 0% of each run, Pallas kernels for 9% -> 16%
where the time goes in v3:
time: 46.9 us; the launch traced here: 46.6 us
  Pallas kernels  18.3 us (39%)
  starting transfers between devices  14.1 us (30%)
  waiting for transfers between devices  9.41 us (20%)
  local copies, waits for them, and re-layouts  3.95 us (8%)
  between operations  0.72 us (2%)
    ppermute x15, starting transfers between devices, crossed(): lax.ppermute(value, axis, [(i, i ^ k) for i in range(lax.axis_size(axis))])  11.5 us
    ppermute x15, waiting for transfers between devices, crossed(): lax.ppermute(value, axis, [(i, i ^ k) for i in range(lax.axis_size(axis))])  9.41 us
    pallas_call x1, Pallas kernels, per_device(): pl.pallas_call(functools.partial(next_kernel, spots, tiles, scale), out_s...  5.44 us
    pallas_call x1, Pallas kernels, per_device(): pl.pallas_call(functools.partial(last_kernel, spots, tiles), out_shape=[s...  4.81 us
    pallas_call x1, Pallas kernels, per_device(): pl.pallas_call(functools.partial(first_kernel, spots, peers, tiles, scale...  4.14 us
    unnamed x12, local copies, waits for them, and re-layouts  3.95 us
    ppermute x1, starting transfers between devices, per_device(): cross = lax.ppermute(edge, 'tile', pairs + [(j, i) for i, j in pairs])  2.68 us
    pallas_call x1, Pallas kernels, per_device(): pl.pallas_call(edge_kernel, out_shape=struct(MARGIN, tile_len), in_specs=...  1.48 us
  transfers between devices with their start and end apart: 16, of which 7 were waited for; matrix products, arithmetic and copies ran while one was open for 0% of the time, Pallas kernels for 16%

profile of v3, /device:TPU:0, one launch (start us, length us, event | category | flops | bytes accessed | tf_op | source)
XLA Modules:
  0.0 46.6 jit_solution(18303475845210232848)
XLA Ops:
  1.2 1.5 %edge_rows.1 = f32[64,256]{1,0:T(8,128)} custom-call(s32[1]{0:T(128)} %bitcast.tile, f32[256,256]{1,0:T(8,128)} %refs_0_.1), custom_call_target="tpu_custom_call" | custom-call | tf_op jit(solution)/shard_map/edge_rows/pallas_call | solution.py:534
  2.7 2.7 %collective-permute-start.1 = (f32[64,256]{1,0:T(8,128)}, f32[64,256]{1,0:T(8,128)S(1)}, u32[]{:S(2)}, u32[]{:S(2)}) collective-permute-start(f32[64,256]{1,0:T(8,128)} %edge_rows.1), channel_id=1, source_target_pairs={{1,2},{3,0},{2,1},{0,3},{5,6},{7,4},{6,5},{4,7},{9,10},{11,8},{10,... | collective-permute-start | bytes 196616 | tf_op jit(solution)/shard_map/ppermute | solution.py:543
  5.4 1.4 %pack_sources.1.refs_0_ = f32[8,128]{1,0:T(8,128)} custom-call(s32[1]{0:T(128)} %bitcast.1.place, f32[1,16]{1,0:T(1,128)} %bitcast.6, s32[2,16]{1,0:T(2,128)} %bitcast.5), custom_call_target="tpu_custom_call" | custom-call | tf_op jit(solution)/shard_map/pack_sources/pallas_call | solution.py:520
  6.8 3.7 %collective-permute-start.4 = (f32[8,128]{1,0:T(8,128)}, f32[8,128]{1,0:T(8,128)S(1)}, u32[]{:S(2)}, u32[]{:S(2)}) collective-permute-start(f32[8,128]{1,0:T(8,128)} %pack_sources.1.refs_0_), channel_id=1, source_target_pairs={{0,12},{4,8},{8,4},{12,0},{1,13},{5,9},{9,5},{13,1},{2,14},{6,10},... | collective-permute-start | bytes 12296 | tf_op jit(solution)/shard_map/ppermute | solution.py:487
  10.4 0.8 %collective-permute-start.2 = (f32[8,128]{1,0:T(8,128)}, f32[8,128]{1,0:T(8,128)S(1)}, u32[]{:S(2)}, u32[]{:S(2)}) collective-permute-start(f32[8,128]{1,0:T(8,128)} %pack_sources.1.refs_0_), channel_id=1, source_target_pairs={{0,4},{4,0},{8,12},{12,8},{1,5},{5,1},{9,13},{13,9},{2,6},{6,2},{1... | collective-permute-start | bytes 12296 | tf_op jit(solution)/shard_map/ppermute | solution.py:487
  11.2 1.5 %copy-done = bf16[1856,512]{1,0:T(8,128)(2,1)S(1)} copy-done((bf16[1856,512]{1,0:T(8,128)(2,1)S(1)}, bf16[1856,512]{1,0:T(8,128)(2,1)}, u32[]{:S(2)}) %copy-start) | copy-done | bytes 1900568
  12.7 0.9 %copy-done.2 = f32[256,256]{1,0:T(8,128)S(1)} copy-done((f32[256,256]{1,0:T(8,128)S(1)}, f32[256,256]{1,0:T(8,128)}, u32[]{:S(2)}) %copy-start.2) | copy-done | bytes 262168
  13.7 0.8 %copy-done.4 = f32[2,32,32]{2,1,0:T(8,128)S(1)} copy-done((f32[2,32,32]{2,1,0:T(8,128)S(1)}, f32[2,32,32]{2,1,0:T(8,128)}, u32[]{:S(2)}) %copy-start.4) | copy-done | bytes 8216
  15.3 0.7 %copy-done.1 = bf16[1856,512]{1,0:T(8,128)(2,1)S(1)} copy-done((bf16[1856,512]{1,0:T(8,128)(2,1)S(1)}, bf16[1856,512]{1,0:T(8,128)(2,1)}, u32[]{:S(2)}) %copy-start.1) | copy-done | bytes 1900568
  16.0 4.1 %first_step.1 = (f32[64,128]{1,0:T(8,128)S(1)}, f32[64,32,128]{2,1,0:T(8,128)S(1)}, f32[64,32,128]{2,1,0:T(8,128)S(1)}, f32[8,128]{1,0:T(8,128)S(1)}, s32[8,128]{1,0:T(8,128)S(1)}) custom-call(s32[1]{0:T(128)} %bitcast.tile, bf16[1856,512]{1,0:T(8,128)(2,1)S(1)} %copy-done.1, f32[32,128]{1,0:T(8,128)S(1)} %get-tuple-element.16.pupil_re, ...), custom_call_target="tpu_custom_call" | custom-call | flops 4294967296 | bytes 1048576 | tf_op jit(solution)/shard_map/first_step/pallas_call | solution.py:575
  20.1 2.3 %collective-permute-done.5.refs_2_ = f32[256,256]{1,0:T(8,128)S(1)} collective-permute-done((f32[256,256]{1,0:T(8,128)S(1)}, f32[256,256]{1,0:T(8,128)S(1)}, u32[]{:S(2)}, u32[]{:S(2)}) %collective-permute-start.5) | collective-permute-done | bytes 262176 | tf_op jit(solution)/shard_map/ppermute | solution.py:487
  22.4 0.6 %collective-permute-start.9 = (f32[64,128]{1,0:T(8,128)S(1)}, f32[64,128]{1,0:T(8,128)S(1)}, u32[]{:S(2)}, u32[]{:S(2)}) collective-permute-start(f32[64,128]{1,0:T(8,128)S(1)} %get-tuple-element.25.refs_4_), channel_id=1, source_target_pairs={{0,3},{1,2},{2,1},{3,0},{4,7},{5,6},{6,5},{7,4},{8,11},{9,10},{10,... | collective-permute-start | bytes 98312 | tf_op jit(solution)/shard_map/ppermute | solution.py:487
  23.0 1.5 %collective-permute-start.8 = (f32[64,128]{1,0:T(8,128)S(1)}, f32[64,128]{1,0:T(8,128)S(1)}, u32[]{:S(2)}, u32[]{:S(2)}) collective-permute-start(f32[64,128]{1,0:T(8,128)S(1)} %get-tuple-element.25.refs_4_), channel_id=1, source_target_pairs={{0,2},{1,3},{2,0},{3,1},{4,6},{5,7},{6,4},{7,5},{8,10},{9,11},{10,... | collective-permute-start | bytes 98312 | tf_op jit(solution)/shard_map/ppermute | solution.py:487
  24.5 1.2 %collective-permute-done.9.refs_7_ = f32[64,128]{1,0:T(8,128)S(1)} collective-permute-done((f32[64,128]{1,0:T(8,128)S(1)}, f32[64,128]{1,0:T(8,128)S(1)}, u32[]{:S(2)}, u32[]{:S(2)}) %collective-permute-start.9) | collective-permute-done | bytes 32800 | tf_op jit(solution)/shard_map/ppermute | solution.py:487
  25.7 1.2 %collective-permute-done.8.refs_6_ = f32[64,128]{1,0:T(8,128)S(1)} collective-permute-done((f32[64,128]{1,0:T(8,128)S(1)}, f32[64,128]{1,0:T(8,128)S(1)}, u32[]{:S(2)}, u32[]{:S(2)}) %collective-permute-start.8) | collective-permute-done | bytes 32800 | tf_op jit(solution)/shard_map/ppermute | solution.py:487
  26.9 5.4 %next_step.1 = (f32[1024,256]{1,0:T(8,128)S(1)}, f32[64,128]{1,0:T(8,128)S(1)}) custom-call(s32[1]{0:T(128)} %bitcast.tile, bf16[1856,512]{1,0:T(8,128)(2,1)S(1)} %copy-done.1, s32[8,128]{1,0:T(8,128)S(1)} %get-tuple-element.19.shifts, f32[8,128]{1,0:T(8,128)S(1)} %get-tuple-element.20.info, f32[64,32,128]{2,1,0:T(8,128)S(1)} %get-tuple-element.21.pr, ...), custom_call_target="tpu_custom_call" | custom-call | flops 4294967296 | bytes 1048576 | tf_op jit(solution)/shard_map/next_step/pallas_call | solution.py:599
  32.4 1.6 %collective-permute-start.11 = (f32[64,128]{1,0:T(8,128)S(1)}, f32[64,128]{1,0:T(8,128)S(1)}, u32[]{:S(2)}, u32[]{:S(2)}) collective-permute-start(f32[64,128]{1,0:T(8,128)S(1)} %get-tuple-element.27.refs_0_), channel_id=1, source_target_pairs={{0,2},{1,3},{2,0},{3,1},{4,6},{5,7},{6,4},{7,5},{8,10},{9,11},{10,... | collective-permute-start | bytes 98312 | tf_op jit(solution)/shard_map/ppermute | solution.py:487
  34.3 1.7 %collective-permute-done.12.refs_3_ = f32[64,128]{1,0:T(8,128)S(1)} collective-permute-done((f32[64,128]{1,0:T(8,128)S(1)}, f32[64,128]{1,0:T(8,128)S(1)}, u32[]{:S(2)}, u32[]{:S(2)}) %collective-permute-start.12) | collective-permute-done | bytes 32800 | tf_op jit(solution)/shard_map/ppermute | solution.py:487
  36.4 4.8 %last_step.1 = (f32[256,256]{1,0:T(8,128)}, f32[8,64]{1,0:T(8,128)S(1)}) custom-call(s32[1]{0:T(128)} %bitcast.tile, bf16[1856,512]{1,0:T(8,128)(2,1)S(1)} %copy-done.1, s32[8,128]{1,0:T(8,128)S(1)} %get-tuple-element.19.shifts, f32[8,128]{1,0:T(8,128)S(1)} %get-tuple-element.20.info, f32[64,32,128]{2,1,0:T(8,128)S(1)} %get-tuple-element.21.pr, ...), custom_call_target="tpu_custom_call" | custom-call | flops 4294967296 | bytes 1048576 | tf_op jit(solution)/shard_map/last_step/pallas_call | solution.py:611
  41.2 0.9 %collective-permute-start.15 = (f32[8,64]{1,0:T(8,128)S(1)}, f32[8,64]{1,0:T(8,128)S(1)}, u32[]{:S(2)}, u32[]{:S(2)}) collective-permute-start(f32[8,64]{1,0:T(8,128)S(1)} %get-tuple-element.29.refs_0_), channel_id=1, source_target_pairs={{0,3},{1,2},{2,1},{3,0},{4,7},{5,6},{6,5},{7,4},{8,11},{9,10},{10,... | collective-permute-start | bytes 6152 | tf_op jit(solution)/shard_map/ppermute | solution.py:487
  42.2 1.1 %collective-permute-start.14 = (f32[8,64]{1,0:T(8,128)S(1)}, f32[8,64]{1,0:T(8,128)S(1)}, u32[]{:S(2)}, u32[]{:S(2)}) collective-permute-start(f32[8,64]{1,0:T(8,128)S(1)} %get-tuple-element.29.refs_0_), channel_id=1, source_target_pairs={{0,2},{1,3},{2,0},{3,1},{4,6},{5,7},{6,4},{7,5},{8,10},{9,11},{10,... | collective-permute-start | bytes 6152 | tf_op jit(solution)/shard_map/ppermute | solution.py:487
  43.3 1.0 %collective-permute-done.15.refs_3_ = f32[8,64]{1,0:T(8,128)S(1)} collective-permute-done((f32[8,64]{1,0:T(8,128)S(1)}, f32[8,64]{1,0:T(8,128)S(1)}, u32[]{:S(2)}, u32[]{:S(2)}) %collective-permute-start.15) | collective-permute-done | bytes 2080 | tf_op jit(solution)/shard_map/ppermute | solution.py:487
  44.3 1.5 %collective-permute-done.14.refs_2_ = f32[8,64]{1,0:T(8,128)S(1)} collective-permute-done((f32[8,64]{1,0:T(8,128)S(1)}, f32[8,64]{1,0:T(8,128)S(1)}, u32[]{:S(2)}, u32[]{:S(2)}) %collective-permute-start.14) | collective-permute-done | bytes 2080 | tf_op jit(solution)/shard_map/ppermute | solution.py:487
  45.8 0.8 %weight_step.1 = f32[1,16]{1,0:T(1,128)} custom-call(s32[1]{0:T(128)} %bitcast.tile, s32[1]{0:T(128)} %bitcast.1.place, f32[8,128]{1,0:T(8,128)S(1)} %get-tuple-element.20.info, f32[8,64]{1,0:T(8,128)S(1)} %get-tuple-element.29.refs_0_, f32[8,64]{1,0:T(8,128)S(1)} %collective-permute-done.13.refs_1_, f32[8,64]{1,0:T(8,128)S(1)} %collective-permute-done.14.refs_2_, ...), custom_call_target="tpu_custom_call" | custom-call | tf_op jit(solution)/shard_map/weight_step/pallas_call | solution.py:623
  (27 shorter events, 2.1 us)
Async XLA Ops:
  0.6 14.2 %copy-start.3 = (f32[256,256]{1,0:T(8,128)S(1)}, f32[256,256]{1,0:T(8,128)}, u32[]{:S(2)}) copy-start(f32[256,256]{1,0:T(8,128)} %refs_0_.1) | copy-start | bytes 786436
  0.6 14.6 %collective-permute-start = (f32[256,256]{1,0:T(8,128)}, f32[256,256]{1,0:T(8,128)S(1)}, u32[]{:S(2)}, u32[]{:S(2)}) collective-permute-start(f32[256,256]{1,0:T(8,128)} %refs_0_.1), channel_id=1, source_target_pairs={{0,1},{1,0},{2,3},{3,2},{4,5},{5,4},{6,7},{7,6},{8,9},{9,8},{10,11... | collective-permute-start | bytes 786440 | tf_op jit(solution)/shard_map/ppermute | solution.py:487
  2.7 12.6 %collective-permute-start.1 = (f32[64,256]{1,0:T(8,128)}, f32[64,256]{1,0:T(8,128)S(1)}, u32[]{:S(2)}, u32[]{:S(2)}) collective-permute-start(f32[64,256]{1,0:T(8,128)} %edge_rows.1), channel_id=1, source_target_pairs={{1,2},{3,0},{2,1},{0,3},{5,6},{7,4},{6,5},{4,7},{9,10},{11,8},{10,... | collective-permute-start | bytes 196616 | tf_op jit(solution)/shard_map/ppermute | solution.py:543
  6.8 8.0 %collective-permute-start.4 = (f32[8,128]{1,0:T(8,128)}, f32[8,128]{1,0:T(8,128)S(1)}, u32[]{:S(2)}, u32[]{:S(2)}) collective-permute-start(f32[8,128]{1,0:T(8,128)} %pack_sources.1.refs_0_), channel_id=1, source_target_pairs={{0,12},{4,8},{8,4},{12,0},{1,13},{5,9},{9,5},{13,1},{2,14},{6,10},... | collective-permute-start | bytes 12296 | tf_op jit(solution)/shard_map/ppermute | solution.py:487
  10.4 4.8 %collective-permute-start.3 = (f32[8,128]{1,0:T(8,128)}, f32[8,128]{1,0:T(8,128)S(1)}, u32[]{:S(2)}, u32[]{:S(2)}) collective-permute-start(f32[8,128]{1,0:T(8,128)} %pack_sources.1.refs_0_), channel_id=1, source_target_pairs={{0,8},{4,12},{8,0},{12,4},{1,9},{5,13},{9,1},{13,5},{2,10},{6,14},... | collective-permute-start | bytes 12296 | tf_op jit(solution)/shard_map/ppermute | solution.py:487
  10.4 4.8 %collective-permute-start.2 = (f32[8,128]{1,0:T(8,128)}, f32[8,128]{1,0:T(8,128)S(1)}, u32[]{:S(2)}, u32[]{:S(2)}) collective-permute-start(f32[8,128]{1,0:T(8,128)} %pack_sources.1.refs_0_), channel_id=1, source_target_pairs={{0,4},{4,0},{8,12},{12,8},{1,5},{5,1},{9,13},{13,9},{2,6},{6,2},{1... | collective-permute-start | bytes 12296 | tf_op jit(solution)/shard_map/ppermute | solution.py:487
  11.2 1.5 %copy-start = (bf16[1856,512]{1,0:T(8,128)(2,1)S(1)}, bf16[1856,512]{1,0:T(8,128)(2,1)}, u32[]{:S(2)}) copy-start(bf16[1856,512]{1,0:T(8,128)(2,1)} %constant.9.clone.whole.table) | copy-start | bytes 5701636
  12.7 0.9 %copy-start.2 = (f32[256,256]{1,0:T(8,128)S(1)}, f32[256,256]{1,0:T(8,128)}, u32[]{:S(2)}) copy-start(f32[256,256]{1,0:T(8,128)} %target.1) | copy-start | bytes 786436
  13.7 0.8 %copy-start.4 = (f32[2,32,32]{2,1,0:T(8,128)S(1)}, f32[2,32,32]{2,1,0:T(8,128)}, u32[]{:S(2)}) copy-start(f32[2,32,32]{2,1,0:T(8,128)} %pupil.1) | copy-start | bytes 24580
  14.4 1.5 %copy-start.1 = (bf16[1856,512]{1,0:T(8,128)(2,1)S(1)}, bf16[1856,512]{1,0:T(8,128)(2,1)}, u32[]{:S(2)}) copy-start(bf16[1856,512]{1,0:T(8,128)(2,1)} %constant.9.clone.whole.table) | copy-start | bytes 5701636
  14.4 1.5 %copy-start.5 = (f32[8,128]{1,0:T(8,128)S(1)}, f32[8,128]{1,0:T(8,128)}, u32[]{:S(2)}) copy-start(f32[8,128]{1,0:T(8,128)} %pack_sources.1.refs_0_) | copy-start | bytes 12292
  14.8 7.6 %collective-permute-start.5 = (f32[256,256]{1,0:T(8,128)S(1)}, f32[256,256]{1,0:T(8,128)S(1)}, u32[]{:S(2)}, u32[]{:S(2)}) collective-permute-start(f32[256,256]{1,0:T(8,128)S(1)} %copy-done.3), channel_id=1, source_target_pairs={{0,2},{1,3},{2,0},{3,1},{4,6},{5,7},{6,4},{7,5},{8,10},{9,11},{10,... | collective-permute-start | bytes 786440 | tf_op jit(solution)/shard_map/ppermute | solution.py:487
  22.4 4.5 %collective-permute-start.6 = (f32[256,256]{1,0:T(8,128)S(1)}, f32[256,256]{1,0:T(8,128)S(1)}, u32[]{:S(2)}, u32[]{:S(2)}) collective-permute-start(f32[256,256]{1,0:T(8,128)S(1)} %collective-permute-done.5.refs_2_), channel_id=1, source_target_pairs={{0,1},{1,0},{2,3},{3,2},{4,5},{5,4},{6,7},{7,6},{8,9},{9,8},{10,11... | collective-permute-start | bytes 786440 | tf_op jit(solution)/shard_map/ppermute | solution.py:487
  22.4 3.3 %collective-permute-start.9 = (f32[64,128]{1,0:T(8,128)S(1)}, f32[64,128]{1,0:T(8,128)S(1)}, u32[]{:S(2)}, u32[]{:S(2)}) collective-permute-start(f32[64,128]{1,0:T(8,128)S(1)} %get-tuple-element.25.refs_4_), channel_id=1, source_target_pairs={{0,3},{1,2},{2,1},{3,0},{4,7},{5,6},{6,5},{7,4},{8,11},{9,10},{10,... | collective-permute-start | bytes 98312 | tf_op jit(solution)/shard_map/ppermute | solution.py:487
  23.0 3.9 %collective-permute-start.8 = (f32[64,128]{1,0:T(8,128)S(1)}, f32[64,128]{1,0:T(8,128)S(1)}, u32[]{:S(2)}, u32[]{:S(2)}) collective-permute-start(f32[64,128]{1,0:T(8,128)S(1)} %get-tuple-element.25.refs_4_), channel_id=1, source_target_pairs={{0,2},{1,3},{2,0},{3,1},{4,6},{5,7},{6,4},{7,5},{8,10},{9,11},{10,... | collective-permute-start | bytes 98312 | tf_op jit(solution)/shard_map/ppermute | solution.py:487
  24.5 2.4 %collective-permute-start.7 = (f32[64,128]{1,0:T(8,128)S(1)}, f32[64,128]{1,0:T(8,128)S(1)}, u32[]{:S(2)}, u32[]{:S(2)}) collective-permute-start(f32[64,128]{1,0:T(8,128)S(1)} %get-tuple-element.25.refs_4_), channel_id=1, source_target_pairs={{0,1},{1,0},{2,3},{3,2},{4,5},{5,4},{6,7},{7,6},{8,9},{9,8},{10,11... | collective-permute-start | bytes 98312 | tf_op jit(solution)/shard_map/ppermute | solution.py:487
  32.4 3.6 %collective-permute-start.12 = (f32[64,128]{1,0:T(8,128)S(1)}, f32[64,128]{1,0:T(8,128)S(1)}, u32[]{:S(2)}, u32[]{:S(2)}) collective-permute-start(f32[64,128]{1,0:T(8,128)S(1)} %get-tuple-element.27.refs_0_), channel_id=1, source_target_pairs={{0,3},{1,2},{2,1},{3,0},{4,7},{5,6},{6,5},{7,4},{8,11},{9,10},{10,... | collective-permute-start | bytes 98312 | tf_op jit(solution)/shard_map/ppermute | solution.py:487
  32.4 4.0 %collective-permute-start.11 = (f32[64,128]{1,0:T(8,128)S(1)}, f32[64,128]{1,0:T(8,128)S(1)}, u32[]{:S(2)}, u32[]{:S(2)}) collective-permute-start(f32[64,128]{1,0:T(8,128)S(1)} %get-tuple-element.27.refs_0_), channel_id=1, source_target_pairs={{0,2},{1,3},{2,0},{3,1},{4,6},{5,7},{6,4},{7,5},{8,10},{9,11},{10,... | collective-permute-start | bytes 98312 | tf_op jit(solution)/shard_map/ppermute | solution.py:487
  34.0 2.4 %collective-permute-start.10 = (f32[64,128]{1,0:T(8,128)S(1)}, f32[64,128]{1,0:T(8,128)S(1)}, u32[]{:S(2)}, u32[]{:S(2)}) collective-permute-start(f32[64,128]{1,0:T(8,128)S(1)} %get-tuple-element.27.refs_0_), channel_id=1, source_target_pairs={{0,1},{1,0},{2,3},{3,2},{4,5},{5,4},{6,7},{7,6},{8,9},{9,8},{10,11... | collective-permute-start | bytes 98312 | tf_op jit(solution)/shard_map/ppermute | solution.py:487
  41.2 3.0 %collective-permute-start.15 = (f32[8,64]{1,0:T(8,128)S(1)}, f32[8,64]{1,0:T(8,128)S(1)}, u32[]{:S(2)}, u32[]{:S(2)}) collective-permute-start(f32[8,64]{1,0:T(8,128)S(1)} %get-tuple-element.29.refs_0_), channel_id=1, source_target_pairs={{0,3},{1,2},{2,1},{3,0},{4,7},{5,6},{6,5},{7,4},{8,11},{9,10},{10,... | collective-permute-start | bytes 6152 | tf_op jit(solution)/shard_map/ppermute | solution.py:487
  42.2 3.6 %collective-permute-start.14 = (f32[8,64]{1,0:T(8,128)S(1)}, f32[8,64]{1,0:T(8,128)S(1)}, u32[]{:S(2)}, u32[]{:S(2)}) collective-permute-start(f32[8,64]{1,0:T(8,128)S(1)} %get-tuple-element.29.refs_0_), channel_id=1, source_target_pairs={{0,2},{1,3},{2,0},{3,1},{4,6},{5,7},{6,4},{7,5},{8,10},{9,11},{10,... | collective-permute-start | bytes 6152 | tf_op jit(solution)/shard_map/ppermute | solution.py:487
  43.2 2.5 %collective-permute-start.13 = (f32[8,64]{1,0:T(8,128)S(1)}, f32[8,64]{1,0:T(8,128)S(1)}, u32[]{:S(2)}, u32[]{:S(2)}) collective-permute-start(f32[8,64]{1,0:T(8,128)S(1)} %get-tuple-element.29.refs_0_), channel_id=1, source_target_pairs={{0,1},{1,0},{2,3},{3,2},{4,5},{5,4},{6,7},{7,6},{8,9},{9,8},{10,11... | collective-permute-start | bytes 6152 | tf_op jit(solution)/shard_map/ppermute | solution.py:487

commit v4 on v3

--- a/solution.py
+++ b/solution.py
@@ -17,6 +17,7 @@
 WEIGHT_RATE = 0.3
 TINY_EPS = 1e-06
 CHUNK = 16
+GROUP = 2
 
 
 bf16 = jnp.bfloat16
@@ -159,18 +160,32 @@
     return second(chunks - 1, stages[(chunks - 1) % 2], carry)
 
 
-def placed_pupils(shifts, roots, pupil_re, pupil_im, pr, pi):
+def turn_pupils(pupil, turned_re, turned_im):
+    count, size, lanes = turned_re.shape
+    grid = lanes // 2
+    turned_re[0] = jnp.zeros((size, lanes), f32)
+    turned_im[0] = jnp.zeros((size, lanes), f32)
+    turned_re[0, :, :size] = pupil[0]
+    turned_re[0, :, grid : grid + size] = pupil[0]
+    turned_im[0, :, :size] = -pupil[1]
+    turned_im[0, :, grid : grid + size] = pupil[1]
+    real, imag = turned_re[0], turned_im[0]
+    for by in range(1, count):
+        turned_re[by] = pltpu.roll(real, by, 1)
+        turned_im[by] = pltpu.roll(imag, by, 1)
+
+
+def placed_pupils(shifts, roots, turned_re, turned_im, pr, pi):
     def make(s):
         by = shifts[2, s] + MAX_SHIFT
-        real = pltpu.roll(pupil_re[...] * roots[3, s], by, 1)
-        imag = pltpu.roll(pupil_im[...] * roots[3, s], by, 1)
+        real, imag = turned_re[by] * roots[3, s], turned_im[by] * roots[3, s]
         pr[s], pi[s] = real, imag
         return real, imag
 
     return make
 
 
-def grid_fields(spec, shifts, t, pupils, work):
+def grid_fields(spec, shifts, t, pupils, work, squares=False):
     plain, crossed, fields, *stages = work
     count, grid, lanes = fields.shape
     box_len = t["row_fwd"].shape[1] // 6
@@ -189,16 +204,18 @@
         stage[...] = halves(dot(jnp.concatenate(rows, 0), t["lane_fwd"][...]))
 
     def second(c, stage, power):
-        stacks = []
-        for i in range(CHUNK):
-            part = stage[i * box_len : (i + 1) * box_len, :]
-            high, low = split(jnp.concatenate([part, sign * swap(part)], 0))
-            stacks.append(jnp.concatenate([high, low, high], 0))
-        out = dot(t["row_fwd"][...], jnp.concatenate(stacks, 1))
-        for i in range(CHUNK):
-            field = out[:, i * lanes : (i + 1) * lanes]
-            fields[c * CHUNK + i] = field
-            power = power + field * field
+        for base in range(0, CHUNK, GROUP):
+            stacks = []
+            for i in range(base, base + GROUP):
+                part = stage[i * box_len : (i + 1) * box_len, :]
+                high, low = split(jnp.concatenate([part, sign * swap(part)], 0))
+                stacks.append(jnp.concatenate([high, low, high], 0))
+            out = dot(t["row_fwd"][...], jnp.concatenate(stacks, 1))
+            for i in range(GROUP):
+                field = out[:, i * lanes : (i + 1) * lanes]
+                square = field * field
+                fields[c * CHUNK + base + i] = square if squares else field
+                power = power + square
         return power
 
     return skewed(count, stages, first, second, jnp.zeros((grid, lanes), f32))
@@ -219,16 +236,16 @@
     sign = lane_sign(box_len, lanes, 1.0)
 
     def first(c, stage):
-        stacks = []
-        for i in range(CHUNK):
-            high, low = split(fields[c * CHUNK + i] * misfit)
-            stacks.append(jnp.concatenate([high, low, high], 0))
-        both = dot(t["row_back"][...], jnp.concatenate(stacks, 1))
-        for i in range(CHUNK):
-            part = both[:, i * lanes : (i + 1) * lanes]
-            stage[i * box_len : (i + 1) * box_len, :] = part[:box_len] + sign * swap(
-                part[box_len:]
-            )
+        for base in range(0, CHUNK, GROUP):
+            stacks = []
+            for i in range(base, base + GROUP):
+                high, low = split(fields[c * CHUNK + i] * misfit)
+                stacks.append(jnp.concatenate([high, low, high], 0))
+            both = dot(t["row_back"][...], jnp.concatenate(stacks, 1))
+            for i in range(GROUP):
+                part = both[:, i * lanes : (i + 1) * lanes]
+                at = (base + i) * box_len
+                stage[at : at + box_len, :] = part[:box_len] + sign * swap(part[box_len:])
 
     def second(c, stage, carry):
         high, low = split(stage[...])
@@ -300,9 +317,13 @@
     return copies
 
 
-def pack_kernel(place, weights, shifts, packed, hold_w, hold_s, sems):
+def pack_kernel(tile, place, weights, shifts, mask, packed, edge, hold_w, hold_s, sems):
     local = weights.shape[1]
-    for copy in start_all(((weights, hold_w), (shifts, hold_s)), sems):
+    at = pl.multiple_of(lax.rem(tile[0], 2) * (mask.shape[0] - MARGIN), MARGIN)
+    copies = start_all(
+        ((weights, hold_w), (shifts, hold_s), (mask.at[pl.ds(at, MARGIN), :], edge)), sems
+    )
+    for copy in copies:
         copy.wait()
     packed[...] = jnp.zeros_like(packed)
     packed[0:1, :local] = hold_w[...]
@@ -311,26 +332,14 @@
     packed[...] = pltpu.roll(packed[...], place[0] * local, 1)
 
 
-def edge_kernel(tile, mask, edge, sems):
-    at = pl.multiple_of(lax.rem(tile[0], 2) * (mask.shape[0] - MARGIN), MARGIN)
-    for copy in start_all(((mask.at[pl.ds(at, MARGIN), :], edge),), sems):
-        copy.wait()
-
-
-def target_kernel(spots, target, pupil, whole, out, pupil_re, pupil_im):
-    grid, size = out.shape[0], pupil.shape[1]
-    pupil_re[...] = jnp.zeros_like(pupil_re)
-    pupil_im[...] = jnp.zeros_like(pupil_im)
-    pupil_re[:, :size] = pupil[0]
-    pupil_re[:, grid : grid + size] = pupil[0]
-    pupil_im[:, :size] = -pupil[1]
-    pupil_im[:, grid : grid + size] = pupil[1]
-    rows, cols = whole.at[spots["target_rows"]], whole.at[spots["target_cols"]]
-    high, low = split(target[...])
+def target_terms(target, t):
+    rows, cols = t["target_rows"], t["target_cols"]
+    grid = rows.shape[0] // 2
+    high, low = split(target)
     both = dot(rows[...], high)
     mid = both[:grid] + both[grid:] + dot(rows[:grid, :], low)
     high, low = split(mid)
-    out[...] = halves(dot(high, cols[...])) + dot(low, cols[:, : 2 * grid])
+    return halves(dot(high, cols[...])) + dot(low, cols[:, : 2 * grid])
 
 
 def doses(info, scale):
@@ -338,12 +347,12 @@
     return 1.0 / dose, scale / dose
 
 
-def first_kernel(spots, peers, tiles, scale, tile, table, pupil_re, pupil_im, target,
+def first_kernel(spots, peers, tiles, scale, tile, table, pupil, goal,
                  own, mate, cross, *refs):
     parts = refs[:peers]
     t = {n: table.at[spot] for n, spot in spots.items()}
-    back, pr, pi, info, whole = refs[peers : peers + 5]
-    *work, s0, s1, s2, s3, shifts, roots, sems = refs[peers + 5 :]
+    back, pr, pi, info, whole, target = refs[peers : peers + 6]
+    *work, s0, s1, s2, s3, turned_re, turned_im, shifts, roots, sems = refs[peers + 6 :]
     here = tile[0]
     total = parts[0][...]
     for part in parts[1:]:
@@ -365,9 +374,11 @@
         [sigmoid(before) * has_prev, sigmoid(own[...]), sigmoid(after) * has_next], 0
     )
     spec = window_spectrum(window, t)
+    target[...] = target_terms(goal[...], t)
+    turn_pupils(pupil, turned_re, turned_im)
     for copy in copies:
         copy.wait()
-    pupils = placed_pupils(shifts, roots, pupil_re, pupil_im, pr, pi)
+    pupils = placed_pupils(shifts, roots, turned_re, turned_im, pr, pi)
     power = grid_fields(spec, shifts, t, pupils, work)
     inv_dose, factor = doses(total, scale)
     misfit = grid_misfit(power, inv_dose, target[...], t)
@@ -433,15 +444,14 @@
         0,
     )
     spec = window_spectrum(window, t)
-    power = grid_fields(spec, shifts, t, lambda s: (pr[s], pi[s]), work)
+    power = grid_fields(spec, shifts, t, lambda s: (pr[s], pi[s]), work, squares=True)
     inv_dose, _ = doses(info[...], 1.0)
     misfit = grid_misfit(power, inv_dose, target[...], t)
 
     def chunk(c, carry):
         rows = []
         for i in range(CHUNK):
-            field = fields[c * CHUNK + i]
-            rows.append(jnp.sum(field * field * misfit, axis=0, keepdims=True))
+            rows.append(jnp.sum(fields[c * CHUNK + i] * misfit, axis=0, keepdims=True))
         terms[pl.ds(pl.multiple_of(c * CHUNK, CHUNK), CHUNK), :] = jnp.concatenate(rows, 0)
         return carry
 
@@ -517,28 +527,20 @@
     def cost(flops):
         return pl.CostEstimate(flops=flops, bytes_accessed=1 << 20, transcendentals=0)
 
-    packed = pl.pallas_call(
+    packed, edge = pl.pallas_call(
         pack_kernel,
-        out_shape=struct(8, 128),
-        in_specs=[smem, left, left],
-        out_specs=vmem,
+        out_shape=[struct(8, 128), struct(MARGIN, tile_len)],
+        in_specs=[smem, smem, left, left, left],
+        out_specs=[vmem] * 2,
         scratch_shapes=[
             pltpu.VMEM((1, local), f32),
             pltpu.VMEM((2, local), jnp.int32),
-            pltpu.SemaphoreType.DMA((2,)),
+            pltpu.SemaphoreType.DMA((3,)),
         ],
         name="pack_sources",
-    )(place, source_weights[None], source_shifts.T)
+    )(tile, place, source_weights[None], source_shifts.T, mask_param)
     packed = all_of(packed, "src")
 
-    edge = pl.pallas_call(
-        edge_kernel,
-        out_shape=struct(MARGIN, tile_len),
-        in_specs=[smem, left],
-        out_specs=vmem,
-        scratch_shapes=[pltpu.SemaphoreType.DMA((1,))],
-        name="edge_rows",
-    )(tile, mask_param)
     pairs = [(i, (i + 1) % tiles) for i in range(1, tiles, 2)]
     cross = lax.ppermute(edge, "tile", pairs + [(j, i) for i, j in pairs])
     mate = crossed(mask_param, "tile", 1)
@@ -546,16 +548,6 @@
 
     whole, spots = pack_tables(tables)
     table = jnp.asarray(whole)
-    target, pupil_re, pupil_im = pl.pallas_call(
-        functools.partial(target_kernel, spots),
-        out_shape=[struct(grid, lanes), struct(box_len, lanes), struct(box_len, lanes)],
-        in_specs=[vmem] * 3,
-        out_specs=[vmem] * 3,
-        compiler_params=params_of,
-        cost_estimate=cost(1 << 26),
-        name="target_terms",
-    )(target_image, pupil_map, table)
-
     work = [
         pltpu.VMEM((grid, lanes), f32),
         pltpu.VMEM((grid, lanes), f32),
@@ -572,13 +564,15 @@
     scale = 0.5 / (grid * grid * period * tile_len)
     source_len = struct(count, box_len, lanes)
 
-    back, pr, pi, info, whole = pl.pallas_call(
+    back, pr, pi, info, whole, target = pl.pallas_call(
         functools.partial(first_kernel, spots, peers, tiles, scale),
         out_shape=[struct(grid, lanes), source_len, source_len, struct(8, 128),
-                   struct(8, 128, kind=jnp.int32)],
-        in_specs=[smem] + [vmem] * (7 + peers),
-        out_specs=[vmem] * 5,
+                   struct(8, 128, kind=jnp.int32), struct(grid, lanes)],
+        in_specs=[smem] + [vmem] * (6 + peers),
+        out_specs=[vmem] * 6,
         scratch_shapes=work + hold + [
+            pltpu.VMEM((2 * MAX_SHIFT + 1, box_len, lanes), f32),
+            pltpu.VMEM((2 * MAX_SHIFT + 1, box_len, lanes), f32),
             pltpu.SMEM((8, 128), jnp.int32),
             pltpu.SMEM((8, 128), f32),
             pltpu.SemaphoreType.DMA((2,)),
@@ -586,7 +580,7 @@
         compiler_params=params_of,
         cost_estimate=cost(1 << 32),
         name="first_step",
-    )(tile, table, pupil_re, pupil_im, target, mask_param, mate, cross, *packed)
+    )(tile, table, pupil_map, target_image, mask_param, mate, cross, *packed)
 
     shared = (tile, table, whole, info, pr, pi, target)
     shared_specs = [smem, vmem, smem] + [vmem] * 4

time: 46.9 us -> 47.4 us (1.011)
  Pallas kernels: 18.3 us -> 16.7 us
  waiting for transfers between devices: 9.41 us -> 10.8 us
  local copies, waits for them, and re-layouts: 3.95 us -> 4.86 us
    pallas_call x3 -> x1, Pallas kernels: 3.19 us -> 1.57 us  [per_device(): pl.pallas_call(pack_kernel, out_shape=[struct(8, 128), struct(MARGIN, til...]
    ppermute x15, waiting for transfers between devices: 9.41 us -> 10.8 us  [crossed(): lax.ppermute(value, axis, [(i, i ^ k) for i in range(lax.axis_size(axis))])]
    unnamed x12, local copies, waits for them, and re-layouts: 3.95 us -> 4.86 us
  transfers between devices with their start and end apart: 16 -> 16, of which waited for: 7 -> 8; matrix products, arithmetic and copies ran while one was open for 0% -> 0% of each run, Pallas kernels for 16% -> 12%
where the time goes in v4:
time: 47.4 us; the launch traced here: 47 us
  Pallas kernels  16.7 us (35%)
  starting transfers between devices  14 us (30%)
  waiting for transfers between devices  10.8 us (23%)
  local copies, waits for them, and re-layouts  4.86 us (10%)
  between operations  0.7 us (1%)
    ppermute x15, starting transfers between devices, crossed(): lax.ppermute(value, axis, [(i, i ^ k) for i in range(lax.axis_size(axis))])  11.3 us
    ppermute x15, waiting for transfers between devices, crossed(): lax.ppermute(value, axis, [(i, i ^ k) for i in range(lax.axis_size(axis))])  10.8 us
    pallas_call x1, Pallas kernels, per_device(): pl.pallas_call(functools.partial(next_kernel, spots, tiles, scale), out_s...  5.42 us
    unnamed x12, local copies, waits for them, and re-layouts  4.86 us
    pallas_call x1, Pallas kernels, per_device(): pl.pallas_call(functools.partial(last_kernel, spots, tiles), out_shape=[s...  4.76 us
    pallas_call x1, Pallas kernels, per_device(): pl.pallas_call(functools.partial(first_kernel, spots, peers, tiles, scale...  4.15 us
    ppermute x1, starting transfers between devices, per_device(): cross = lax.ppermute(edge, 'tile', pairs + [(j, i) for i, j in pairs])  2.68 us
    pallas_call x1, Pallas kernels, per_device(): pl.pallas_call(pack_kernel, out_shape=[struct(8, 128), struct(MARGIN, til...  1.57 us
  transfers between devices with their start and end apart: 16, of which 8 were waited for; matrix products, arithmetic and copies ran while one was open for 0% of the time, Pallas kernels for 12%

profile of v4, /device:TPU:0, one launch (start us, length us, event | category | flops | bytes accessed | tf_op | source)
XLA Modules:
  0.0 47.0 jit_solution(13971261347117946009)
XLA Ops:
  1.2 1.6 %pack_sources.1 = (f32[8,128]{1,0:T(8,128)}, f32[64,256]{1,0:T(8,128)}) custom-call(s32[1]{0:T(128)} %bitcast.tile, s32[1]{0:T(128)} %bitcast.1.place, f32[1,16]{1,0:T(1,128)} %bitcast.6, s32[2,16]{1,0:T(2,128)} %bitcast.5, f32[256,256]{1,0:T(8,128)} %refs_0_.1), custom_call_target="tpu_custom_call" | custom-call | tf_op jit(solution)/shard_map/pack_sources/pallas_call | solution.py:530
  2.8 2.7 %collective-permute-start.1 = (f32[64,256]{1,0:T(8,128)}, f32[64,256]{1,0:T(8,128)S(1)}, u32[]{:S(2)}, u32[]{:S(2)}) collective-permute-start(f32[64,256]{1,0:T(8,128)} %get-tuple-element.16), channel_id=1, source_target_pairs={{1,2},{3,0},{2,1},{0,3},{5,6},{7,4},{6,5},{4,7},{9,10},{11,8},{10,... | collective-permute-start | bytes 196616 | tf_op jit(solution)/shard_map/ppermute | solution.py:545
  5.5 3.6 %collective-permute-start.4 = (f32[8,128]{1,0:T(8,128)}, f32[8,128]{1,0:T(8,128)S(1)}, u32[]{:S(2)}, u32[]{:S(2)}) collective-permute-start(f32[8,128]{1,0:T(8,128)} %get-tuple-element.17.refs_0_), channel_id=1, source_target_pairs={{0,12},{4,8},{8,4},{12,0},{1,13},{5,9},{9,5},{13,1},{2,14},{6,10},... | collective-permute-start | bytes 12296 | tf_op jit(solution)/shard_map/ppermute | solution.py:497
  9.1 0.8 %collective-permute-start.2 = (f32[8,128]{1,0:T(8,128)}, f32[8,128]{1,0:T(8,128)S(1)}, u32[]{:S(2)}, u32[]{:S(2)}) collective-permute-start(f32[8,128]{1,0:T(8,128)} %get-tuple-element.17.refs_0_), channel_id=1, source_target_pairs={{0,4},{4,0},{8,12},{12,8},{1,5},{5,1},{9,13},{13,9},{2,6},{6,2},{1... | collective-permute-start | bytes 12296 | tf_op jit(solution)/shard_map/ppermute | solution.py:497
  9.8 1.2 %collective-permute-done.4.refs_3_ = f32[8,128]{1,0:T(8,128)S(1)} collective-permute-done((f32[8,128]{1,0:T(8,128)}, f32[8,128]{1,0:T(8,128)S(1)}, u32[]{:S(2)}, u32[]{:S(2)}) %collective-permute-start.4) | collective-permute-done | bytes 4128 | tf_op jit(solution)/shard_map/ppermute | solution.py:497
  11.4 2.4 %collective-permute-done.3.refs_2_ = f32[8,128]{1,0:T(8,128)S(1)} collective-permute-done((f32[8,128]{1,0:T(8,128)}, f32[8,128]{1,0:T(8,128)S(1)}, u32[]{:S(2)}, u32[]{:S(2)}) %collective-permute-start.3) | collective-permute-done | bytes 4128 | tf_op jit(solution)/shard_map/ppermute | solution.py:497
  13.8 0.9 %copy-done = f32[256,256]{1,0:T(8,128)S(1)} copy-done((f32[256,256]{1,0:T(8,128)S(1)}, f32[256,256]{1,0:T(8,128)}, u32[]{:S(2)}) %copy-start) | copy-done | bytes 262168
  14.7 0.9 %copy-done.1 = f32[256,256]{1,0:T(8,128)S(1)} copy-done((f32[256,256]{1,0:T(8,128)S(1)}, f32[256,256]{1,0:T(8,128)}, u32[]{:S(2)}) %copy-start.1) | copy-done | bytes 262168
  15.7 0.8 %copy-done.2 = f32[2,32,32]{2,1,0:T(8,128)S(1)} copy-done((f32[2,32,32]{2,1,0:T(8,128)S(1)}, f32[2,32,32]{2,1,0:T(8,128)}, u32[]{:S(2)}) %copy-start.2) | copy-done | bytes 8216
  16.4 0.7 %copy-done.3 = f32[8,128]{1,0:T(8,128)S(1)} copy-done((f32[8,128]{1,0:T(8,128)S(1)}, f32[8,128]{1,0:T(8,128)}, u32[]{:S(2)}) %copy-start.3) | copy-done | bytes 4120
  17.1 1.5 %copy-done.4 = bf16[1856,512]{1,0:T(8,128)(2,1)S(1)} copy-done((bf16[1856,512]{1,0:T(8,128)(2,1)S(1)}, bf16[1856,512]{1,0:T(8,128)(2,1)}, u32[]{:S(2)}) %copy-start.4) | copy-done | bytes 1900568
  18.7 4.2 %first_step.1 = (f32[64,128]{1,0:T(8,128)S(1)}, f32[64,32,128]{2,1,0:T(8,128)S(1)}, f32[64,32,128]{2,1,0:T(8,128)S(1)}, f32[8,128]{1,0:T(8,128)S(1)}, s32[8,128]{1,0:T(8,128)S(1)}, /*index=5*/f32[64,128]{1,0:T(8,128)S(1)}) custom-call(s32[1]{0:T(128)} %bitcast.tile, bf16[1856,512]{1,0:T(8,128)(2,1)S(1)} %copy-done.4, f32[2,32,32]{2,1,0:T(8,128)S(1)} %copy-done.2, ...), custom_call_target="tpu_custom_call" | custom-call | flops 4294967296 | bytes 1048576 | tf_op jit(solution)/shard_map/first_step/pallas_call | solution.py:567
  23.5 1.5 %collective-permute-start.8 = (f32[64,128]{1,0:T(8,128)S(1)}, f32[64,128]{1,0:T(8,128)S(1)}, u32[]{:S(2)}, u32[]{:S(2)}) collective-permute-start(f32[64,128]{1,0:T(8,128)S(1)} %get-tuple-element.25.refs_4_), channel_id=1, source_target_pairs={{0,2},{1,3},{2,0},{3,1},{4,6},{5,7},{6,4},{7,5},{8,10},{9,11},{10,... | collective-permute-start | bytes 98312 | tf_op jit(solution)/shard_map/ppermute | solution.py:497
  25.0 1.3 %collective-permute-done.9.refs_7_ = f32[64,128]{1,0:T(8,128)S(1)} collective-permute-done((f32[64,128]{1,0:T(8,128)S(1)}, f32[64,128]{1,0:T(8,128)S(1)}, u32[]{:S(2)}, u32[]{:S(2)}) %collective-permute-start.9) | collective-permute-done | bytes 32800 | tf_op jit(solution)/shard_map/ppermute | solution.py:497
  26.3 1.1 %collective-permute-done.8.refs_6_ = f32[64,128]{1,0:T(8,128)S(1)} collective-permute-done((f32[64,128]{1,0:T(8,128)S(1)}, f32[64,128]{1,0:T(8,128)S(1)}, u32[]{:S(2)}, u32[]{:S(2)}) %collective-permute-start.8) | collective-permute-done | bytes 32800 | tf_op jit(solution)/shard_map/ppermute | solution.py:497
  27.4 5.4 %next_step.1 = (f32[1024,256]{1,0:T(8,128)S(1)}, f32[64,128]{1,0:T(8,128)S(1)}) custom-call(s32[1]{0:T(128)} %bitcast.tile, bf16[1856,512]{1,0:T(8,128)(2,1)S(1)} %copy-done.5, s32[8,128]{1,0:T(8,128)S(1)} %get-tuple-element.18.shifts, f32[8,128]{1,0:T(8,128)S(1)} %get-tuple-element.19.info, f32[64,32,128]{2,1,0:T(8,128)S(1)} %get-tuple-element.20.pr, ...), custom_call_target="tpu_custom_call" | custom-call | flops 4294967296 | bytes 1048576 | tf_op jit(solution)/shard_map/next_step/pallas_call | solution.py:593
  32.9 1.5 %collective-permute-start.11 = (f32[64,128]{1,0:T(8,128)S(1)}, f32[64,128]{1,0:T(8,128)S(1)}, u32[]{:S(2)}, u32[]{:S(2)}) collective-permute-start(f32[64,128]{1,0:T(8,128)S(1)} %get-tuple-element.27.refs_0_), channel_id=1, source_target_pairs={{0,2},{1,3},{2,0},{3,1},{4,6},{5,7},{6,4},{7,5},{8,10},{9,11},{10,... | collective-permute-start | bytes 98312 | tf_op jit(solution)/shard_map/ppermute | solution.py:497
  34.7 1.7 %collective-permute-done.12.refs_3_ = f32[64,128]{1,0:T(8,128)S(1)} collective-permute-done((f32[64,128]{1,0:T(8,128)S(1)}, f32[64,128]{1,0:T(8,128)S(1)}, u32[]{:S(2)}, u32[]{:S(2)}) %collective-permute-start.12) | collective-permute-done | bytes 32800 | tf_op jit(solution)/shard_map/ppermute | solution.py:497
  36.9 4.8 %last_step.1 = (f32[256,256]{1,0:T(8,128)}, f32[8,64]{1,0:T(8,128)S(1)}) custom-call(s32[1]{0:T(128)} %bitcast.tile, bf16[1856,512]{1,0:T(8,128)(2,1)S(1)} %copy-done.5, s32[8,128]{1,0:T(8,128)S(1)} %get-tuple-element.18.shifts, f32[8,128]{1,0:T(8,128)S(1)} %get-tuple-element.19.info, f32[64,32,128]{2,1,0:T(8,128)S(1)} %get-tuple-element.20.pr, ...), custom_call_target="tpu_custom_call" | custom-call | flops 4294967296 | bytes 1048576 | tf_op jit(solution)/shard_map/last_step/pallas_call | solution.py:605
  41.7 0.9 %collective-permute-start.15 = (f32[8,64]{1,0:T(8,128)S(1)}, f32[8,64]{1,0:T(8,128)S(1)}, u32[]{:S(2)}, u32[]{:S(2)}) collective-permute-start(f32[8,64]{1,0:T(8,128)S(1)} %get-tuple-element.29.refs_0_), channel_id=1, source_target_pairs={{0,3},{1,2},{2,1},{3,0},{4,7},{5,6},{6,5},{7,4},{8,11},{9,10},{10,... | collective-permute-start | bytes 6152 | tf_op jit(solution)/shard_map/ppermute | solution.py:497
  42.6 1.1 %collective-permute-start.14 = (f32[8,64]{1,0:T(8,128)S(1)}, f32[8,64]{1,0:T(8,128)S(1)}, u32[]{:S(2)}, u32[]{:S(2)}) collective-permute-start(f32[8,64]{1,0:T(8,128)S(1)} %get-tuple-element.29.refs_0_), channel_id=1, source_target_pairs={{0,2},{1,3},{2,0},{3,1},{4,6},{5,7},{6,4},{7,5},{8,10},{9,11},{10,... | collective-permute-start | bytes 6152 | tf_op jit(solution)/shard_map/ppermute | solution.py:497
  43.7 1.0 %collective-permute-done.15.refs_3_ = f32[8,64]{1,0:T(8,128)S(1)} collective-permute-done((f32[8,64]{1,0:T(8,128)S(1)}, f32[8,64]{1,0:T(8,128)S(1)}, u32[]{:S(2)}, u32[]{:S(2)}) %collective-permute-start.15) | collective-permute-done | bytes 2080 | tf_op jit(solution)/shard_map/ppermute | solution.py:497
  44.7 1.5 %collective-permute-done.14.refs_2_ = f32[8,64]{1,0:T(8,128)S(1)} collective-permute-done((f32[8,64]{1,0:T(8,128)S(1)}, f32[8,64]{1,0:T(8,128)S(1)}, u32[]{:S(2)}, u32[]{:S(2)}) %collective-permute-start.14) | collective-permute-done | bytes 2080 | tf_op jit(solution)/shard_map/ppermute | solution.py:497
  46.2 0.8 %weight_step.1 = f32[1,16]{1,0:T(1,128)} custom-call(s32[1]{0:T(128)} %bitcast.tile, s32[1]{0:T(128)} %bitcast.1.place, f32[8,128]{1,0:T(8,128)S(1)} %get-tuple-element.19.info, f32[8,64]{1,0:T(8,128)S(1)} %get-tuple-element.29.refs_0_, f32[8,64]{1,0:T(8,128)S(1)} %collective-permute-done.13.refs_1_, f32[8,64]{1,0:T(8,128)S(1)} %collective-permute-done.14.refs_2_, ...), custom_call_target="tpu_custom_call" | custom-call | tf_op jit(solution)/shard_map/weight_step/pallas_call | solution.py:617
  (25 shorter events, 2.3 us)
Async XLA Ops:
  0.6 13.1 %collective-permute-start = (f32[256,256]{1,0:T(8,128)}, f32[256,256]{1,0:T(8,128)S(1)}, u32[]{:S(2)}, u32[]{:S(2)}) collective-permute-start(f32[256,256]{1,0:T(8,128)} %refs_0_.1), channel_id=1, source_target_pairs={{0,1},{1,0},{2,3},{3,2},{4,5},{5,4},{6,7},{7,6},{8,9},{9,8},{10,11... | collective-permute-start | bytes 786440 | tf_op jit(solution)/shard_map/ppermute | solution.py:497
  2.8 11.0 %collective-permute-start.1 = (f32[64,256]{1,0:T(8,128)}, f32[64,256]{1,0:T(8,128)S(1)}, u32[]{:S(2)}, u32[]{:S(2)}) collective-permute-start(f32[64,256]{1,0:T(8,128)} %get-tuple-element.16), channel_id=1, source_target_pairs={{1,2},{3,0},{2,1},{0,3},{5,6},{7,4},{6,5},{4,7},{9,10},{11,8},{10,... | collective-permute-start | bytes 196616 | tf_op jit(solution)/shard_map/ppermute | solution.py:545
  5.5 5.6 %collective-permute-start.4 = (f32[8,128]{1,0:T(8,128)}, f32[8,128]{1,0:T(8,128)S(1)}, u32[]{:S(2)}, u32[]{:S(2)}) collective-permute-start(f32[8,128]{1,0:T(8,128)} %get-tuple-element.17.refs_0_), channel_id=1, source_target_pairs={{0,12},{4,8},{8,4},{12,0},{1,13},{5,9},{9,5},{13,1},{2,14},{6,10},... | collective-permute-start | bytes 12296 | tf_op jit(solution)/shard_map/ppermute | solution.py:497
  9.1 4.7 %collective-permute-start.3 = (f32[8,128]{1,0:T(8,128)}, f32[8,128]{1,0:T(8,128)S(1)}, u32[]{:S(2)}, u32[]{:S(2)}) collective-permute-start(f32[8,128]{1,0:T(8,128)} %get-tuple-element.17.refs_0_), channel_id=1, source_target_pairs={{0,8},{4,12},{8,0},{12,4},{1,9},{5,13},{9,1},{13,5},{2,10},{6,14},... | collective-permute-start | bytes 12296 | tf_op jit(solution)/shard_map/ppermute | solution.py:497
  9.1 4.7 %collective-permute-start.2 = (f32[8,128]{1,0:T(8,128)}, f32[8,128]{1,0:T(8,128)S(1)}, u32[]{:S(2)}, u32[]{:S(2)}) collective-permute-start(f32[8,128]{1,0:T(8,128)} %get-tuple-element.17.refs_0_), channel_id=1, source_target_pairs={{0,4},{4,0},{8,12},{12,8},{1,5},{5,1},{9,13},{13,9},{2,6},{6,2},{1... | collective-permute-start | bytes 12296 | tf_op jit(solution)/shard_map/ppermute | solution.py:497
  11.1 11.7 %collective-permute-start.5 = (f32[256,256]{1,0:T(8,128)}, f32[256,256]{1,0:T(8,128)S(1)}, u32[]{:S(2)}, u32[]{:S(2)}) collective-permute-start(f32[256,256]{1,0:T(8,128)} %refs_0_.1), channel_id=1, source_target_pairs={{0,2},{1,3},{2,0},{3,1},{4,6},{5,7},{6,4},{7,5},{8,10},{9,11},{10,... | collective-permute-start | bytes 786440 | tf_op jit(solution)/shard_map/ppermute | solution.py:497
  13.8 1.0 %copy-start = (f32[256,256]{1,0:T(8,128)S(1)}, f32[256,256]{1,0:T(8,128)}, u32[]{:S(2)}) copy-start(f32[256,256]{1,0:T(8,128)} %refs_0_.1) | copy-start | bytes 786436
  14.7 0.9 %copy-start.1 = (f32[256,256]{1,0:T(8,128)S(1)}, f32[256,256]{1,0:T(8,128)}, u32[]{:S(2)}) copy-start(f32[256,256]{1,0:T(8,128)} %goal.1) | copy-start | bytes 786436
  15.7 0.8 %copy-start.2 = (f32[2,32,32]{2,1,0:T(8,128)S(1)}, f32[2,32,32]{2,1,0:T(8,128)}, u32[]{:S(2)}) copy-start(f32[2,32,32]{2,1,0:T(8,128)} %pupil.1) | copy-start | bytes 24580
  16.4 0.7 %copy-start.3 = (f32[8,128]{1,0:T(8,128)S(1)}, f32[8,128]{1,0:T(8,128)}, u32[]{:S(2)}) copy-start(f32[8,128]{1,0:T(8,128)} %get-tuple-element.17.refs_0_) | copy-start | bytes 12292
  17.1 1.5 %copy-start.4 = (bf16[1856,512]{1,0:T(8,128)(2,1)S(1)}, bf16[1856,512]{1,0:T(8,128)(2,1)}, u32[]{:S(2)}) copy-start(bf16[1856,512]{1,0:T(8,128)(2,1)} %constant.9.clone.table) | copy-start | bytes 5701636
  18.6 8.8 %copy-start.5 = (bf16[1856,512]{1,0:T(8,128)(2,1)S(1)}, bf16[1856,512]{1,0:T(8,128)(2,1)}, u32[]{:S(2)}) copy-start(bf16[1856,512]{1,0:T(8,128)(2,1)} %constant.9.clone.table) | copy-start | bytes 5701636
  22.8 4.6 %collective-permute-start.6 = (f32[256,256]{1,0:T(8,128)S(1)}, f32[256,256]{1,0:T(8,128)S(1)}, u32[]{:S(2)}, u32[]{:S(2)}) collective-permute-start(f32[256,256]{1,0:T(8,128)S(1)} %collective-permute-done.5.refs_2_), channel_id=1, source_target_pairs={{0,1},{1,0},{2,3},{3,2},{4,5},{5,4},{6,7},{7,6},{8,9},{9,8},{10,11... | collective-permute-start | bytes 786440 | tf_op jit(solution)/shard_map/ppermute | solution.py:497
  22.9 3.4 %collective-permute-start.9 = (f32[64,128]{1,0:T(8,128)S(1)}, f32[64,128]{1,0:T(8,128)S(1)}, u32[]{:S(2)}, u32[]{:S(2)}) collective-permute-start(f32[64,128]{1,0:T(8,128)S(1)} %get-tuple-element.25.refs_4_), channel_id=1, source_target_pairs={{0,3},{1,2},{2,1},{3,0},{4,7},{5,6},{6,5},{7,4},{8,11},{9,10},{10,... | collective-permute-start | bytes 98312 | tf_op jit(solution)/shard_map/ppermute | solution.py:497
  23.5 3.9 %collective-permute-start.8 = (f32[64,128]{1,0:T(8,128)S(1)}, f32[64,128]{1,0:T(8,128)S(1)}, u32[]{:S(2)}, u32[]{:S(2)}) collective-permute-start(f32[64,128]{1,0:T(8,128)S(1)} %get-tuple-element.25.refs_4_), channel_id=1, source_target_pairs={{0,2},{1,3},{2,0},{3,1},{4,6},{5,7},{6,4},{7,5},{8,10},{9,11},{10,... | collective-permute-start | bytes 98312 | tf_op jit(solution)/shard_map/ppermute | solution.py:497
  25.0 2.4 %collective-permute-start.7 = (f32[64,128]{1,0:T(8,128)S(1)}, f32[64,128]{1,0:T(8,128)S(1)}, u32[]{:S(2)}, u32[]{:S(2)}) collective-permute-start(f32[64,128]{1,0:T(8,128)S(1)} %get-tuple-element.25.refs_4_), channel_id=1, source_target_pairs={{0,1},{1,0},{2,3},{3,2},{4,5},{5,4},{6,7},{7,6},{8,9},{9,8},{10,11... | collective-permute-start | bytes 98312 | tf_op jit(solution)/shard_map/ppermute | solution.py:497
  32.8 3.6 %collective-permute-start.12 = (f32[64,128]{1,0:T(8,128)S(1)}, f32[64,128]{1,0:T(8,128)S(1)}, u32[]{:S(2)}, u32[]{:S(2)}) collective-permute-start(f32[64,128]{1,0:T(8,128)S(1)} %get-tuple-element.27.refs_0_), channel_id=1, source_target_pairs={{0,3},{1,2},{2,1},{3,0},{4,7},{5,6},{6,5},{7,4},{8,11},{9,10},{10,... | collective-permute-start | bytes 98312 | tf_op jit(solution)/shard_map/ppermute | solution.py:497
  32.9 4.0 %collective-permute-start.11 = (f32[64,128]{1,0:T(8,128)S(1)}, f32[64,128]{1,0:T(8,128)S(1)}, u32[]{:S(2)}, u32[]{:S(2)}) collective-permute-start(f32[64,128]{1,0:T(8,128)S(1)} %get-tuple-element.27.refs_0_), channel_id=1, source_target_pairs={{0,2},{1,3},{2,0},{3,1},{4,6},{5,7},{6,4},{7,5},{8,10},{9,11},{10,... | collective-permute-start | bytes 98312 | tf_op jit(solution)/shard_map/ppermute | solution.py:497
  34.5 2.4 %collective-permute-start.10 = (f32[64,128]{1,0:T(8,128)S(1)}, f32[64,128]{1,0:T(8,128)S(1)}, u32[]{:S(2)}, u32[]{:S(2)}) collective-permute-start(f32[64,128]{1,0:T(8,128)S(1)} %get-tuple-element.27.refs_0_), channel_id=1, source_target_pairs={{0,1},{1,0},{2,3},{3,2},{4,5},{5,4},{6,7},{7,6},{8,9},{9,8},{10,11... | collective-permute-start | bytes 98312 | tf_op jit(solution)/shard_map/ppermute | solution.py:497
  41.7 3.0 %collective-permute-start.15 = (f32[8,64]{1,0:T(8,128)S(1)}, f32[8,64]{1,0:T(8,128)S(1)}, u32[]{:S(2)}, u32[]{:S(2)}) collective-permute-start(f32[8,64]{1,0:T(8,128)S(1)} %get-tuple-element.29.refs_0_), channel_id=1, source_target_pairs={{0,3},{1,2},{2,1},{3,0},{4,7},{5,6},{6,5},{7,4},{8,11},{9,10},{10,... | collective-permute-start | bytes 6152 | tf_op jit(solution)/shard_map/ppermute | solution.py:497
  42.6 3.6 %collective-permute-start.14 = (f32[8,64]{1,0:T(8,128)S(1)}, f32[8,64]{1,0:T(8,128)S(1)}, u32[]{:S(2)}, u32[]{:S(2)}) collective-permute-start(f32[8,64]{1,0:T(8,128)S(1)} %get-tuple-element.29.refs_0_), channel_id=1, source_target_pairs={{0,2},{1,3},{2,0},{3,1},{4,6},{5,7},{6,4},{7,5},{8,10},{9,11},{10,... | collective-permute-start | bytes 6152 | tf_op jit(solution)/shard_map/ppermute | solution.py:497
  43.7 2.6 %collective-permute-start.13 = (f32[8,64]{1,0:T(8,128)S(1)}, f32[8,64]{1,0:T(8,128)S(1)}, u32[]{:S(2)}, u32[]{:S(2)}) collective-permute-start(f32[8,64]{1,0:T(8,128)S(1)} %get-tuple-element.29.refs_0_), channel_id=1, source_target_pairs={{0,1},{1,0},{2,3},{3,2},{4,5},{5,4},{6,7},{7,6},{8,9},{9,8},{10,11... | collective-permute-start | bytes 6152 | tf_op jit(solution)/shard_map/ppermute | solution.py:497

commit v5 on v4

--- a/solution.py
+++ b/solution.py
@@ -318,17 +318,21 @@
 
 
 def pack_kernel(tile, place, weights, shifts, mask, packed, edge, hold_w, hold_s, sems):
-    local = weights.shape[1]
     at = pl.multiple_of(lax.rem(tile[0], 2) * (mask.shape[0] - MARGIN), MARGIN)
     copies = start_all(
         ((weights, hold_w), (shifts, hold_s), (mask.at[pl.ds(at, MARGIN), :], edge)), sems
     )
     for copy in copies:
         copy.wait()
+    fill_sources(packed, hold_w, hold_s, place)
+
+
+def fill_sources(packed, weights, shifts, place):
+    local = weights.shape[1]
     packed[...] = jnp.zeros_like(packed)
-    packed[0:1, :local] = hold_w[...]
-    packed[1:3, :local] = hold_s[...].astype(f32)
-    packed[3:4, :local] = jnp.sqrt(hold_w[...])
+    packed[0:1, :local] = weights[...]
+    packed[1:3, :local] = shifts[...].astype(f32)
+    packed[3:4, :local] = jnp.sqrt(weights[...])
     packed[...] = pltpu.roll(packed[...], place[0] * local, 1)
 
 
@@ -347,15 +351,16 @@
     return 1.0 / dose, scale / dose
 
 
-def first_kernel(spots, peers, tiles, scale, tile, table, pupil, goal,
+def first_kernel(spots, peers, tiles, scale, tile, place, table, pupil, goal, weights, turns,
                  own, mate, cross, *refs):
-    parts = refs[:peers]
+    parts = refs[: peers - 1]
     t = {n: table.at[spot] for n, spot in spots.items()}
-    back, pr, pi, info, whole, target = refs[peers : peers + 6]
-    *work, s0, s1, s2, s3, turned_re, turned_im, shifts, roots, sems = refs[peers + 6 :]
+    back, pr, pi, info, whole, target = refs[peers - 1 : peers + 5]
+    *work, s0, s1, s2, s3, turned_re, turned_im, shifts, roots, sems = refs[peers + 5 :]
     here = tile[0]
-    total = parts[0][...]
-    for part in parts[1:]:
+    fill_sources(info, weights, turns, place)
+    total = info[...]
+    for part in parts:
         total = total + part[...]
     info[...] = total
     whole[...] = total.astype(jnp.int32)
@@ -537,9 +542,10 @@
             pltpu.VMEM((2, local), jnp.int32),
             pltpu.SemaphoreType.DMA((3,)),
         ],
+        cost_estimate=cost(1 << 34),
         name="pack_sources",
     )(tile, place, source_weights[None], source_shifts.T, mask_param)
-    packed = all_of(packed, "src")
+    packed = all_of(packed, "src")[1:]
 
     pairs = [(i, (i + 1) % tiles) for i in range(1, tiles, 2)]
     cross = lax.ppermute(edge, "tile", pairs + [(j, i) for i, j in pairs])
@@ -568,7 +574,7 @@
         functools.partial(first_kernel, spots, peers, tiles, scale),
         out_shape=[struct(grid, lanes), source_len, source_len, struct(8, 128),
                    struct(8, 128, kind=jnp.int32), struct(grid, lanes)],
-        in_specs=[smem] + [vmem] * (6 + peers),
+        in_specs=[smem] * 2 + [vmem] * (7 + peers),
         out_specs=[vmem] * 6,
         scratch_shapes=work + hold + [
             pltpu.VMEM((2 * MAX_SHIFT + 1, box_len, lanes), f32),
@@ -580,7 +586,8 @@
         compiler_params=params_of,
         cost_estimate=cost(1 << 32),
         name="first_step",
-    )(tile, table, pupil_map, target_image, mask_param, mate, cross, *packed)
+    )(tile, place, table, pupil_map, target_image, source_weights[None], source_shifts.T,
+      mask_param, mate, cross, *packed)
 
     shared = (tile, table, whole, info, pr, pi, target)
     shared_specs = [smem, vmem, smem] + [vmem] * 4

time: 47.4 us -> 42.7 us (0.901)
  local copies, waits for them, and re-layouts: 4.86 us -> 0.03 us
    unnamed x12, local copies, waits for them, and re-layouts: 4.86 us -> 0.03 us
  transfers between devices with their start and end apart: 16 -> 16, of which waited for: 8 -> 9; matrix products, arithmetic and copies ran while one was open for 0% -> 0% of each run, Pallas kernels for 12% -> 14%
where the time goes in v5:
time: 42.7 us; the launch traced here: 42.6 us
  Pallas kernels  16.7 us (39%)
  starting transfers between devices  13.9 us (33%)
  waiting for transfers between devices  11.1 us (26%)
  between operations  0.74 us (2%)
    ppermute x15, starting transfers between devices, crossed(): lax.ppermute(value, axis, [(i, i ^ k) for i in range(lax.axis_size(axis))])  11.2 us
    ppermute x15, waiting for transfers between devices, crossed(): lax.ppermute(value, axis, [(i, i ^ k) for i in range(lax.axis_size(axis))])  11.1 us
    pallas_call x1, Pallas kernels, per_device(): pl.pallas_call(functools.partial(next_kernel, spots, tiles, scale), out_s...  5.44 us
    pallas_call x1, Pallas kernels, per_device(): pl.pallas_call(functools.partial(last_kernel, spots, tiles), out_shape=[s...  4.76 us
    pallas_call x1, Pallas kernels, per_device(): pl.pallas_call(functools.partial(first_kernel, spots, peers, tiles, scale...  4.04 us
    ppermute x1, starting transfers between devices, per_device(): cross = lax.ppermute(edge, 'tile', pairs + [(j, i) for i, j in pairs])  2.68 us
    pallas_call x1, Pallas kernels, per_device(): pl.pallas_call(pack_kernel, out_shape=[struct(8, 128), struct(MARGIN, til...  1.72 us
  transfers between devices with their start and end apart: 16, of which 9 were waited for; matrix products, arithmetic and copies ran while one was open for 0% of the time, Pallas kernels for 14%

profile of v5, /device:TPU:0, one launch (start us, length us, event | category | flops | bytes accessed | tf_op | source)
XLA Modules:
  0.0 42.6 jit_solution(16704917822888687616)
XLA Ops:
  0.6 0.6 %collective-permute-start = (f32[256,256]{1,0:T(8,128)}, f32[256,256]{1,0:T(8,128)S(1)}, u32[]{:S(2)}, u32[]{:S(2)}) collective-permute-start(f32[256,256]{1,0:T(8,128)} %refs_0_.1), channel_id=1, source_target_pairs={{0,1},{1,0},{2,3},{3,2},{4,5},{5,4},{6,7},{7,6},{8,9},{9,8},{10,11... | collective-permute-start | bytes 786440 | tf_op jit(solution)/shard_map/ppermute | solution.py:502
  1.2 1.7 %pack_sources.1 = (f32[8,128]{1,0:T(8,128)}, f32[64,256]{1,0:T(8,128)}) custom-call(s32[1]{0:T(128)} %bitcast.tile, s32[1]{0:T(128)} %bitcast.1.place, f32[1,16]{1,0:T(1,128)} %bitcast.7, s32[2,16]{1,0:T(2,128)} %bitcast.5, f32[256,256]{1,0:T(8,128)} %refs_0_.1), custom_call_target="tpu_custom_call" | custom-call | flops 17179869184 | bytes 1048576 | tf_op jit(solution)/shard_map/pack_sources/pallas_call | solution.py:535
  3.0 2.7 %collective-permute-start.1 = (f32[64,256]{1,0:T(8,128)}, f32[64,256]{1,0:T(8,128)S(1)}, u32[]{:S(2)}, u32[]{:S(2)}) collective-permute-start(f32[64,256]{1,0:T(8,128)} %get-tuple-element.16), channel_id=1, source_target_pairs={{1,2},{3,0},{2,1},{0,3},{5,6},{7,4},{6,5},{4,7},{9,10},{11,8},{10,... | collective-permute-start | bytes 196616 | tf_op jit(solution)/shard_map/ppermute | solution.py:551
  5.6 3.6 %collective-permute-start.4 = (f32[8,128]{1,0:T(8,128)}, f32[8,128]{1,0:T(8,128)S(1)}, u32[]{:S(2)}, u32[]{:S(2)}) collective-permute-start(f32[8,128]{1,0:T(8,128)} %get-tuple-element.17), channel_id=1, source_target_pairs={{0,12},{4,8},{8,4},{12,0},{1,13},{5,9},{9,5},{13,1},{2,14},{6,10},... | collective-permute-start | bytes 12296 | tf_op jit(solution)/shard_map/ppermute | solution.py:502
  9.2 0.8 %collective-permute-start.2 = (f32[8,128]{1,0:T(8,128)}, f32[8,128]{1,0:T(8,128)S(1)}, u32[]{:S(2)}, u32[]{:S(2)}) collective-permute-start(f32[8,128]{1,0:T(8,128)} %get-tuple-element.17), channel_id=1, source_target_pairs={{0,4},{4,0},{8,12},{12,8},{1,5},{5,1},{9,13},{13,9},{2,6},{6,2},{1... | collective-permute-start | bytes 12296 | tf_op jit(solution)/shard_map/ppermute | solution.py:502
  10.0 1.2 %collective-permute-done.4.refs_2_ = f32[8,128]{1,0:T(8,128)S(1)} collective-permute-done((f32[8,128]{1,0:T(8,128)}, f32[8,128]{1,0:T(8,128)S(1)}, u32[]{:S(2)}, u32[]{:S(2)}) %collective-permute-start.4) | collective-permute-done | bytes 4128 | tf_op jit(solution)/shard_map/ppermute | solution.py:502
  11.3 0.3 collective-permute-start.5
  11.5 2.4 %collective-permute-done.3.refs_1_ = f32[8,128]{1,0:T(8,128)S(1)} collective-permute-done((f32[8,128]{1,0:T(8,128)}, f32[8,128]{1,0:T(8,128)S(1)}, u32[]{:S(2)}, u32[]{:S(2)}) %collective-permute-start.3) | collective-permute-done | bytes 4128 | tf_op jit(solution)/shard_map/ppermute | solution.py:502
  14.0 4.0 %first_step.1 = (f32[64,128]{1,0:T(8,128)S(1)}, f32[64,32,128]{2,1,0:T(8,128)S(1)}, f32[64,32,128]{2,1,0:T(8,128)S(1)}, f32[8,128]{1,0:T(8,128)S(1)}, s32[8,128]{1,0:T(8,128)S(1)}, /*index=5*/f32[64,128]{1,0:T(8,128)S(1)}) custom-call(s32[1]{0:T(128)} %bitcast.tile, s32[1]{0:T(128)} %bitcast.1.place, bf16[1856,512]{1,0:T(8,128)(2,1)S(1)} %copy-done.5, ...), custom_call_target="tpu_custom_call" | custom-call | flops 4294967296 | bytes 1048576 | tf_op jit(solution)/shard_map/first_step/pallas_call | solution.py:573
  18.1 0.4 collective-permute-done.5.refs_2_
  18.4 0.6 %collective-permute-start.9 = (f32[64,128]{1,0:T(8,128)S(1)}, f32[64,128]{1,0:T(8,128)S(1)}, u32[]{:S(2)}, u32[]{:S(2)}) collective-permute-start(f32[64,128]{1,0:T(8,128)S(1)} %get-tuple-element.25.refs_4_), channel_id=1, source_target_pairs={{0,3},{1,2},{2,1},{3,0},{4,7},{5,6},{6,5},{7,4},{8,11},{9,10},{10,... | collective-permute-start | bytes 98312 | tf_op jit(solution)/shard_map/ppermute | solution.py:502
  19.0 1.5 %collective-permute-start.8 = (f32[64,128]{1,0:T(8,128)S(1)}, f32[64,128]{1,0:T(8,128)S(1)}, u32[]{:S(2)}, u32[]{:S(2)}) collective-permute-start(f32[64,128]{1,0:T(8,128)S(1)} %get-tuple-element.25.refs_4_), channel_id=1, source_target_pairs={{0,2},{1,3},{2,0},{3,1},{4,6},{5,7},{6,4},{7,5},{8,10},{9,11},{10,... | collective-permute-start | bytes 98312 | tf_op jit(solution)/shard_map/ppermute | solution.py:502
  20.6 1.2 %collective-permute-done.9.refs_7_ = f32[64,128]{1,0:T(8,128)S(1)} collective-permute-done((f32[64,128]{1,0:T(8,128)S(1)}, f32[64,128]{1,0:T(8,128)S(1)}, u32[]{:S(2)}, u32[]{:S(2)}) %collective-permute-start.9) | collective-permute-done | bytes 32800 | tf_op jit(solution)/shard_map/ppermute | solution.py:502
  21.8 1.2 %collective-permute-done.8.refs_6_ = f32[64,128]{1,0:T(8,128)S(1)} collective-permute-done((f32[64,128]{1,0:T(8,128)S(1)}, f32[64,128]{1,0:T(8,128)S(1)}, u32[]{:S(2)}, u32[]{:S(2)}) %collective-permute-start.8) | collective-permute-done | bytes 32800 | tf_op jit(solution)/shard_map/ppermute | solution.py:502
  23.0 5.4 %next_step.1 = (f32[1024,256]{1,0:T(8,128)S(1)}, f32[64,128]{1,0:T(8,128)S(1)}) custom-call(s32[1]{0:T(128)} %bitcast.tile, bf16[1856,512]{1,0:T(8,128)(2,1)S(1)} %copy-done.5, s32[8,128]{1,0:T(8,128)S(1)} %get-tuple-element.18.shifts, f32[8,128]{1,0:T(8,128)S(1)} %get-tuple-element.19.info, f32[64,32,128]{2,1,0:T(8,128)S(1)} %get-tuple-element.20.pr, ...), custom_call_target="tpu_custom_call" | custom-call | flops 4294967296 | bytes 1048576 | tf_op jit(solution)/shard_map/next_step/pallas_call | solution.py:600
  28.4 1.6 %collective-permute-start.11 = (f32[64,128]{1,0:T(8,128)S(1)}, f32[64,128]{1,0:T(8,128)S(1)}, u32[]{:S(2)}, u32[]{:S(2)}) collective-permute-start(f32[64,128]{1,0:T(8,128)S(1)} %get-tuple-element.27.refs_0_), channel_id=1, source_target_pairs={{0,2},{1,3},{2,0},{3,1},{4,6},{5,7},{6,4},{7,5},{8,10},{9,11},{10,... | collective-permute-start | bytes 98312 | tf_op jit(solution)/shard_map/ppermute | solution.py:502
  30.3 1.7 %collective-permute-done.12.refs_3_ = f32[64,128]{1,0:T(8,128)S(1)} collective-permute-done((f32[64,128]{1,0:T(8,128)S(1)}, f32[64,128]{1,0:T(8,128)S(1)}, u32[]{:S(2)}, u32[]{:S(2)}) %collective-permute-start.12) | collective-permute-done | bytes 32800 | tf_op jit(solution)/shard_map/ppermute | solution.py:502
  32.0 0.4 %collective-permute-done.11.refs_2_ = f32[64,128]{1,0:T(8,128)S(1)} collective-permute-done((f32[64,128]{1,0:T(8,128)S(1)}, f32[64,128]{1,0:T(8,128)S(1)}, u32[]{:S(2)}, u32[]{:S(2)}) %collective-permute-start.11) | collective-permute-done | bytes 32800 | tf_op jit(solution)/shard_map/ppermute | solution.py:502
  32.5 4.8 %last_step.1 = (f32[256,256]{1,0:T(8,128)}, f32[8,64]{1,0:T(8,128)S(1)}) custom-call(s32[1]{0:T(128)} %bitcast.tile, bf16[1856,512]{1,0:T(8,128)(2,1)S(1)} %copy-done.5, s32[8,128]{1,0:T(8,128)S(1)} %get-tuple-element.18.shifts, f32[8,128]{1,0:T(8,128)S(1)} %get-tuple-element.19.info, f32[64,32,128]{2,1,0:T(8,128)S(1)} %get-tuple-element.20.pr, ...), custom_call_target="tpu_custom_call" | custom-call | flops 4294967296 | bytes 1048576 | tf_op jit(solution)/shard_map/last_step/pallas_call | solution.py:612
  37.2 0.9 %collective-permute-start.15 = (f32[8,64]{1,0:T(8,128)S(1)}, f32[8,64]{1,0:T(8,128)S(1)}, u32[]{:S(2)}, u32[]{:S(2)}) collective-permute-start(f32[8,64]{1,0:T(8,128)S(1)} %get-tuple-element.29.refs_0_), channel_id=1, source_target_pairs={{0,3},{1,2},{2,1},{3,0},{4,7},{5,6},{6,5},{7,4},{8,11},{9,10},{10,... | collective-permute-start | bytes 6152 | tf_op jit(solution)/shard_map/ppermute | solution.py:502
  38.2 1.1 %collective-permute-start.14 = (f32[8,64]{1,0:T(8,128)S(1)}, f32[8,64]{1,0:T(8,128)S(1)}, u32[]{:S(2)}, u32[]{:S(2)}) collective-permute-start(f32[8,64]{1,0:T(8,128)S(1)} %get-tuple-element.29.refs_0_), channel_id=1, source_target_pairs={{0,2},{1,3},{2,0},{3,1},{4,6},{5,7},{6,4},{7,5},{8,10},{9,11},{10,... | collective-permute-start | bytes 6152 | tf_op jit(solution)/shard_map/ppermute | solution.py:502
  39.2 1.0 %collective-permute-done.15.refs_3_ = f32[8,64]{1,0:T(8,128)S(1)} collective-permute-done((f32[8,64]{1,0:T(8,128)S(1)}, f32[8,64]{1,0:T(8,128)S(1)}, u32[]{:S(2)}, u32[]{:S(2)}) %collective-permute-start.15) | collective-permute-done | bytes 2080 | tf_op jit(solution)/shard_map/ppermute | solution.py:502
  40.3 1.5 %collective-permute-done.14.refs_2_ = f32[8,64]{1,0:T(8,128)S(1)} collective-permute-done((f32[8,64]{1,0:T(8,128)S(1)}, f32[8,64]{1,0:T(8,128)S(1)}, u32[]{:S(2)}, u32[]{:S(2)}) %collective-permute-start.14) | collective-permute-done | bytes 2080 | tf_op jit(solution)/shard_map/ppermute | solution.py:502
  41.8 0.8 %weight_step.1 = f32[1,16]{1,0:T(1,128)} custom-call(s32[1]{0:T(128)} %bitcast.tile, s32[1]{0:T(128)} %bitcast.1.place, f32[8,128]{1,0:T(8,128)S(1)} %get-tuple-element.19.info, f32[8,64]{1,0:T(8,128)S(1)} %get-tuple-element.29.refs_0_, f32[8,64]{1,0:T(8,128)S(1)} %collective-permute-done.13.refs_1_, f32[8,64]{1,0:T(8,128)S(1)} %collective-permute-done.14.refs_2_, ...), custom_call_target="tpu_custom_call" | custom-call | tf_op jit(solution)/shard_map/weight_step/pallas_call | solution.py:624
  (25 shorter events, 0.3 us)
Async XLA Ops:
  0.6 13.3 %collective-permute-start = (f32[256,256]{1,0:T(8,128)}, f32[256,256]{1,0:T(8,128)S(1)}, u32[]{:S(2)}, u32[]{:S(2)}) collective-permute-start(f32[256,256]{1,0:T(8,128)} %refs_0_.1), channel_id=1, source_target_pairs={{0,1},{1,0},{2,3},{3,2},{4,5},{5,4},{6,7},{7,6},{8,9},{9,8},{10,11... | collective-permute-start | bytes 786440 | tf_op jit(solution)/shard_map/ppermute | solution.py:502
  1.2 10.1 %copy-start.1 = (f32[256,256]{1,0:T(8,128)S(1)}, f32[256,256]{1,0:T(8,128)}, u32[]{:S(2)}) copy-start(f32[256,256]{1,0:T(8,128)} %refs_0_.1) | copy-start | bytes 786436
  1.2 12.8 %copy-start = (f32[256,256]{1,0:T(8,128)S(1)}, f32[256,256]{1,0:T(8,128)}, u32[]{:S(2)}) copy-start(f32[256,256]{1,0:T(8,128)} %goal.1) | copy-start | bytes 786436
  1.2 12.8 %copy-start.2 = (f32[2,32,32]{2,1,0:T(8,128)S(1)}, f32[2,32,32]{2,1,0:T(8,128)}, u32[]{:S(2)}) copy-start(f32[2,32,32]{2,1,0:T(8,128)} %pupil.1) | copy-start | bytes 24580
  1.2 12.8 %copy-start.3 = (s32[16,2]{0,1:T(2,128)S(1)}, s32[16,2]{0,1:T(2,128)}, u32[]{:S(2)}) copy-start(s32[16,2]{0,1:T(2,128)} %param.9) | copy-start | bytes 388
  1.2 12.8 %copy-start.4 = (f32[16]{0:T(128)S(1)}, f32[16]{0:T(128)}, u32[]{:S(2)}) copy-start(f32[16]{0:T(128)} %param.8) | copy-start | bytes 196
  1.2 12.8 %copy-start.5 = (bf16[1856,512]{1,0:T(8,128)(2,1)S(1)}, bf16[1856,512]{1,0:T(8,128)(2,1)}, u32[]{:S(2)}) copy-start(bf16[1856,512]{1,0:T(8,128)(2,1)} %constant.9.clone.table) | copy-start | bytes 5701636
  3.0 11.0 %collective-permute-start.1 = (f32[64,256]{1,0:T(8,128)}, f32[64,256]{1,0:T(8,128)S(1)}, u32[]{:S(2)}, u32[]{:S(2)}) collective-permute-start(f32[64,256]{1,0:T(8,128)} %get-tuple-element.16), channel_id=1, source_target_pairs={{1,2},{3,0},{2,1},{0,3},{5,6},{7,4},{6,5},{4,7},{9,10},{11,8},{10,... | collective-permute-start | bytes 196616 | tf_op jit(solution)/shard_map/ppermute | solution.py:551
  5.6 5.6 %collective-permute-start.4 = (f32[8,128]{1,0:T(8,128)}, f32[8,128]{1,0:T(8,128)S(1)}, u32[]{:S(2)}, u32[]{:S(2)}) collective-permute-start(f32[8,128]{1,0:T(8,128)} %get-tuple-element.17), channel_id=1, source_target_pairs={{0,12},{4,8},{8,4},{12,0},{1,13},{5,9},{9,5},{13,1},{2,14},{6,10},... | collective-permute-start | bytes 12296 | tf_op jit(solution)/shard_map/ppermute | solution.py:502
  9.2 4.7 %collective-permute-start.3 = (f32[8,128]{1,0:T(8,128)}, f32[8,128]{1,0:T(8,128)S(1)}, u32[]{:S(2)}, u32[]{:S(2)}) collective-permute-start(f32[8,128]{1,0:T(8,128)} %get-tuple-element.17), channel_id=1, source_target_pairs={{0,8},{4,12},{8,0},{12,4},{1,9},{5,13},{9,1},{13,5},{2,10},{6,14},... | collective-permute-start | bytes 12296 | tf_op jit(solution)/shard_map/ppermute | solution.py:502
  9.2 4.7 %collective-permute-start.2 = (f32[8,128]{1,0:T(8,128)}, f32[8,128]{1,0:T(8,128)S(1)}, u32[]{:S(2)}, u32[]{:S(2)}) collective-permute-start(f32[8,128]{1,0:T(8,128)} %get-tuple-element.17), channel_id=1, source_target_pairs={{0,4},{4,0},{8,12},{12,8},{1,5},{5,1},{9,13},{13,9},{2,6},{6,2},{1... | collective-permute-start | bytes 12296 | tf_op jit(solution)/shard_map/ppermute | solution.py:502
  11.3 7.2 %collective-permute-start.5 = (f32[256,256]{1,0:T(8,128)S(1)}, f32[256,256]{1,0:T(8,128)S(1)}, u32[]{:S(2)}, u32[]{:S(2)}) collective-permute-start(f32[256,256]{1,0:T(8,128)S(1)} %copy-done.1), channel_id=1, source_target_pairs={{0,2},{1,3},{2,0},{3,1},{4,6},{5,7},{6,4},{7,5},{8,10},{9,11},{10,... | collective-permute-start | bytes 786440 | tf_op jit(solution)/shard_map/ppermute | solution.py:502
  18.4 4.5 %collective-permute-start.6 = (f32[256,256]{1,0:T(8,128)S(1)}, f32[256,256]{1,0:T(8,128)S(1)}, u32[]{:S(2)}, u32[]{:S(2)}) collective-permute-start(f32[256,256]{1,0:T(8,128)S(1)} %collective-permute-done.5.refs_2_), channel_id=1, source_target_pairs={{0,1},{1,0},{2,3},{3,2},{4,5},{5,4},{6,7},{7,6},{8,9},{9,8},{10,11... | collective-permute-start | bytes 786440 | tf_op jit(solution)/shard_map/ppermute | solution.py:502
  18.4 3.3 %collective-permute-start.9 = (f32[64,128]{1,0:T(8,128)S(1)}, f32[64,128]{1,0:T(8,128)S(1)}, u32[]{:S(2)}, u32[]{:S(2)}) collective-permute-start(f32[64,128]{1,0:T(8,128)S(1)} %get-tuple-element.25.refs_4_), channel_id=1, source_target_pairs={{0,3},{1,2},{2,1},{3,0},{4,7},{5,6},{6,5},{7,4},{8,11},{9,10},{10,... | collective-permute-start | bytes 98312 | tf_op jit(solution)/shard_map/ppermute | solution.py:502
  19.0 3.9 %collective-permute-start.8 = (f32[64,128]{1,0:T(8,128)S(1)}, f32[64,128]{1,0:T(8,128)S(1)}, u32[]{:S(2)}, u32[]{:S(2)}) collective-permute-start(f32[64,128]{1,0:T(8,128)S(1)} %get-tuple-element.25.refs_4_), channel_id=1, source_target_pairs={{0,2},{1,3},{2,0},{3,1},{4,6},{5,7},{6,4},{7,5},{8,10},{9,11},{10,... | collective-permute-start | bytes 98312 | tf_op jit(solution)/shard_map/ppermute | solution.py:502
  20.6 2.4 %collective-permute-start.7 = (f32[64,128]{1,0:T(8,128)S(1)}, f32[64,128]{1,0:T(8,128)S(1)}, u32[]{:S(2)}, u32[]{:S(2)}) collective-permute-start(f32[64,128]{1,0:T(8,128)S(1)} %get-tuple-element.25.refs_4_), channel_id=1, source_target_pairs={{0,1},{1,0},{2,3},{3,2},{4,5},{5,4},{6,7},{7,6},{8,9},{9,8},{10,11... | collective-permute-start | bytes 98312 | tf_op jit(solution)/shard_map/ppermute | solution.py:502
  28.4 3.6 %collective-permute-start.12 = (f32[64,128]{1,0:T(8,128)S(1)}, f32[64,128]{1,0:T(8,128)S(1)}, u32[]{:S(2)}, u32[]{:S(2)}) collective-permute-start(f32[64,128]{1,0:T(8,128)S(1)} %get-tuple-element.27.refs_0_), channel_id=1, source_target_pairs={{0,3},{1,2},{2,1},{3,0},{4,7},{5,6},{6,5},{7,4},{8,11},{9,10},{10,... | collective-permute-start | bytes 98312 | tf_op jit(solution)/shard_map/ppermute | solution.py:502
  28.4 4.0 %collective-permute-start.11 = (f32[64,128]{1,0:T(8,128)S(1)}, f32[64,128]{1,0:T(8,128)S(1)}, u32[]{:S(2)}, u32[]{:S(2)}) collective-permute-start(f32[64,128]{1,0:T(8,128)S(1)} %get-tuple-element.27.refs_0_), channel_id=1, source_target_pairs={{0,2},{1,3},{2,0},{3,1},{4,6},{5,7},{6,4},{7,5},{8,10},{9,11},{10,... | collective-permute-start | bytes 98312 | tf_op jit(solution)/shard_map/ppermute | solution.py:502
  30.0 2.4 %collective-permute-start.10 = (f32[64,128]{1,0:T(8,128)S(1)}, f32[64,128]{1,0:T(8,128)S(1)}, u32[]{:S(2)}, u32[]{:S(2)}) collective-permute-start(f32[64,128]{1,0:T(8,128)S(1)} %get-tuple-element.27.refs_0_), channel_id=1, source_target_pairs={{0,1},{1,0},{2,3},{3,2},{4,5},{5,4},{6,7},{7,6},{8,9},{9,8},{10,11... | collective-permute-start | bytes 98312 | tf_op jit(solution)/shard_map/ppermute | solution.py:502
  37.2 3.0 %collective-permute-start.15 = (f32[8,64]{1,0:T(8,128)S(1)}, f32[8,64]{1,0:T(8,128)S(1)}, u32[]{:S(2)}, u32[]{:S(2)}) collective-permute-start(f32[8,64]{1,0:T(8,128)S(1)} %get-tuple-element.29.refs_0_), channel_id=1, source_target_pairs={{0,3},{1,2},{2,1},{3,0},{4,7},{5,6},{6,5},{7,4},{8,11},{9,10},{10,... | collective-permute-start | bytes 6152 | tf_op jit(solution)/shard_map/ppermute | solution.py:502
  38.2 3.6 %collective-permute-start.14 = (f32[8,64]{1,0:T(8,128)S(1)}, f32[8,64]{1,0:T(8,128)S(1)}, u32[]{:S(2)}, u32[]{:S(2)}) collective-permute-start(f32[8,64]{1,0:T(8,128)S(1)} %get-tuple-element.29.refs_0_), channel_id=1, source_target_pairs={{0,2},{1,3},{2,0},{3,1},{4,6},{5,7},{6,4},{7,5},{8,10},{9,11},{10,... | collective-permute-start | bytes 6152 | tf_op jit(solution)/shard_map/ppermute | solution.py:502
  39.2 2.6 %collective-permute-start.13 = (f32[8,64]{1,0:T(8,128)S(1)}, f32[8,64]{1,0:T(8,128)S(1)}, u32[]{:S(2)}, u32[]{:S(2)}) collective-permute-start(f32[8,64]{1,0:T(8,128)S(1)} %get-tuple-element.29.refs_0_), channel_id=1, source_target_pairs={{0,1},{1,0},{2,3},{3,2},{4,5},{5,4},{6,7},{7,6},{8,9},{9,8},{10,11... | collective-permute-start | bytes 6152 | tf_op jit(solution)/shard_map/ppermute | solution.py:502

commit v6 on v4

--- a/solution.py
+++ b/solution.py
@@ -189,8 +189,9 @@
     plain, crossed, fields, *stages = work
     count, grid, lanes = fields.shape
     box_len = t["row_fwd"].shape[1] // 6
-    plain[...] = spec
-    crossed[...] = swap(spec)
+    if spec is not None:
+        plain[...] = spec
+        crossed[...] = swap(spec)
     sign = lane_sign(box_len, lanes, -1.0)
 
     def first(c, stage):
@@ -317,18 +318,18 @@
     return copies
 
 
-def pack_kernel(tile, place, weights, shifts, mask, packed, edge, hold_w, hold_s, sems):
+def head_kernel(out):
+    out[...] = jnp.zeros_like(out)
+
+
+def pack_kernel(tile, place, head, weights, shifts, mask, packed, edge):
+    at = pl.multiple_of(lax.rem(tile[0], 2) * (mask.shape[0] - MARGIN), MARGIN)
+    edge[...] = mask[pl.ds(at, MARGIN), :]
     local = weights.shape[1]
-    at = pl.multiple_of(lax.rem(tile[0], 2) * (mask.shape[0] - MARGIN), MARGIN)
-    copies = start_all(
-        ((weights, hold_w), (shifts, hold_s), (mask.at[pl.ds(at, MARGIN), :], edge)), sems
-    )
-    for copy in copies:
-        copy.wait()
-    packed[...] = jnp.zeros_like(packed)
-    packed[0:1, :local] = hold_w[...]
-    packed[1:3, :local] = hold_s[...].astype(f32)
-    packed[3:4, :local] = jnp.sqrt(hold_w[...])
+    packed[...] = head[...]
+    packed[0:1, :local] = weights[...]
+    packed[1:3, :local] = shifts[...].astype(f32)
+    packed[3:4, :local] = jnp.sqrt(weights[...])
     packed[...] = pltpu.roll(packed[...], place[0] * local, 1)
 
 
@@ -347,24 +348,10 @@
     return 1.0 / dose, scale / dose
 
 
-def first_kernel(spots, peers, tiles, scale, tile, table, pupil, goal,
-                 own, mate, cross, *refs):
-    parts = refs[:peers]
+def ready_kernel(spots, tiles, tile, table, pupil, goal, own, mate, cross,
+                 plain, crossed, target, turned_re, turned_im):
     t = {n: table.at[spot] for n, spot in spots.items()}
-    back, pr, pi, info, whole, target = refs[peers : peers + 6]
-    *work, s0, s1, s2, s3, turned_re, turned_im, shifts, roots, sems = refs[peers + 6 :]
     here = tile[0]
-    total = parts[0][...]
-    for part in parts[1:]:
-        total = total + part[...]
-    info[...] = total
-    whole[...] = total.astype(jnp.int32)
-    copies = (
-        pltpu.make_async_copy(whole, shifts, sems.at[0]),
-        pltpu.make_async_copy(info, roots, sems.at[1]),
-    )
-    for copy in copies:
-        copy.start()
     has_prev = (here > 0).astype(f32)
     has_next = (here < tiles - 1).astype(f32)
     odd = lax.rem(here, 2) > 0
@@ -373,13 +360,28 @@
     window = jnp.concatenate(
         [sigmoid(before) * has_prev, sigmoid(own[...]), sigmoid(after) * has_next], 0
     )
+    turn_pupils(pupil, turned_re, turned_im)
     spec = window_spectrum(window, t)
+    plain[...] = spec
+    crossed[...] = swap(spec)
     target[...] = target_terms(goal[...], t)
-    turn_pupils(pupil, turned_re, turned_im)
-    for copy in copies:
+
+
+def first_kernel(spots, peers, scale, table, plain, crossed, target, turned_re, turned_im, *refs):
+    parts = refs[:peers]
+    t = {n: table.at[spot] for n, spot in spots.items()}
+    back, pr, pi, info, whole = refs[peers : peers + 5]
+    *work, s0, s1, s2, s3, shifts, roots, sems = refs[peers + 5 :]
+    total = parts[0][...]
+    for part in parts[1:]:
+        total = total + part[...]
+    info[...] = total
+    whole[...] = total.astype(jnp.int32)
+    for copy in start_all(((whole, shifts), (info, roots)), sems):
         copy.wait()
     pupils = placed_pupils(shifts, roots, turned_re, turned_im, pr, pi)
-    power = grid_fields(spec, shifts, t, pupils, work)
+    work = [plain, crossed, *work]
+    power = grid_fields(None, shifts, t, pupils, work)
     inv_dose, factor = doses(total, scale)
     misfit = grid_misfit(power, inv_dose, target[...], t)
     sums = (s0, s1, s2, s3)
@@ -421,23 +423,24 @@
 def last_kernel(spots, tiles, tile, table, shifts, info, pr, pi, target, params, *refs):
     backs = refs[:tiles]
     t = {n: table.at[spot] for n, spot in spots.items()}
-    final, row, *work, terms, wins, grads = refs[tiles:]
+    final, row, *work, terms, wins, grads, fresh, sems = refs[tiles:]
     fields = work[2]
     here = tile[0]
-    tile_len = final.shape[0]
+    tile_len = fresh.shape[0]
     rate = mask_grads(
         lambda k, low, high: params[k * tile_len + low : k * tile_len + high, :],
         list(range(tiles)), backs, t, here, tiles, wins, grads,
     )
     above, below, has_prev, has_next = edge_rows(here, tiles, tile_len)
     own = pl.ds(pl.multiple_of(here * tile_len, tile_len), tile_len)
-    final[...] = params[own, :] - grads[here] * rate
+    fresh[...] = params[own, :] - grads[here] * rate
+    (leave,) = start_all(((fresh, final),), sems)
     prev, follow = jnp.maximum(here - 1, 0), jnp.minimum(here + 1, tiles - 1)
     window = jnp.concatenate(
         [
             sigmoid(params[pl.ds(above, MARGIN), :] - grads[prev, tile_len - MARGIN :, :] * rate)
             * has_prev,
-            sigmoid(final[...]),
+            sigmoid(fresh[...]),
             sigmoid(params[pl.ds(below, MARGIN), :] - grads[follow, :MARGIN, :] * rate)
             * has_next,
         ],
@@ -466,6 +469,7 @@
             ones, part, (((1,), (1,)), ((), ())), preferred_element_type=f32
         )
     row[...] = total
+    leave.wait()
 
 
 def weight_kernel(tiles, scale, tile, place, info, *refs):
@@ -527,18 +531,23 @@
     def cost(flops):
         return pl.CostEstimate(flops=flops, bytes_accessed=1 << 20, transcendentals=0)
 
+    head = pl.pallas_call(
+        head_kernel,
+        out_shape=struct(8, 128),
+        out_specs=vmem,
+        compiler_params=params_of,
+        cost_estimate=cost(1 << 34),
+        name="head_step",
+    )()
     packed, edge = pl.pallas_call(
         pack_kernel,
         out_shape=[struct(8, 128), struct(MARGIN, tile_len)],
-        in_specs=[smem, smem, left, left, left],
+        in_specs=[smem, smem] + [vmem] * 4,
         out_specs=[vmem] * 2,
-        scratch_shapes=[
-            pltpu.VMEM((1, local), f32),
-            pltpu.VMEM((2, local), jnp.int32),
-            pltpu.SemaphoreType.DMA((3,)),
-        ],
+        compiler_params=params_of,
+        cost_estimate=cost(1 << 20),
         name="pack_sources",
-    )(tile, place, source_weights[None], source_shifts.T, mask_param)
+    )(tile, place, head, source_weights[None], source_shifts.T, mask_param)
     packed = all_of(packed, "src")
 
     pairs = [(i, (i + 1) % tiles) for i in range(1, tiles, 2)]
@@ -564,15 +573,23 @@
     scale = 0.5 / (grid * grid * period * tile_len)
     source_len = struct(count, box_len, lanes)
 
-    back, pr, pi, info, whole, target = pl.pallas_call(
-        functools.partial(first_kernel, spots, peers, tiles, scale),
+    plain, crossed_spec, target, *turned = pl.pallas_call(
+        functools.partial(ready_kernel, spots, tiles),
+        out_shape=[struct(grid, lanes)] * 3 + [struct(2 * MAX_SHIFT + 1, box_len, lanes)] * 2,
+        in_specs=[smem] + [vmem] * 6,
+        out_specs=[vmem] * 5,
+        compiler_params=params_of,
+        cost_estimate=cost(1 << 30),
+        name="ready_step",
+    )(tile, table, pupil_map, target_image, mask_param, mate, cross)
+
+    back, pr, pi, info, whole = pl.pallas_call(
+        functools.partial(first_kernel, spots, peers, scale),
         out_shape=[struct(grid, lanes), source_len, source_len, struct(8, 128),
-                   struct(8, 128, kind=jnp.int32), struct(grid, lanes)],
-        in_specs=[smem] + [vmem] * (6 + peers),
-        out_specs=[vmem] * 6,
-        scratch_shapes=work + hold + [
-            pltpu.VMEM((2 * MAX_SHIFT + 1, box_len, lanes), f32),
-            pltpu.VMEM((2 * MAX_SHIFT + 1, box_len, lanes), f32),
+                   struct(8, 128, kind=jnp.int32)],
+        in_specs=[vmem] * (6 + peers),
+        out_specs=[vmem] * 5,
+        scratch_shapes=work[2:] + hold + [
             pltpu.SMEM((8, 128), jnp.int32),
             pltpu.SMEM((8, 128), f32),
             pltpu.SemaphoreType.DMA((2,)),
@@ -580,7 +597,7 @@
         compiler_params=params_of,
         cost_estimate=cost(1 << 32),
         name="first_step",
-    )(tile, table, pupil_map, target_image, mask_param, mate, cross, *packed)
+    )(table, plain, crossed_spec, target, *turned, *packed)
 
     shared = (tile, table, whole, info, pr, pi, target)
     shared_specs = [smem, vmem, smem] + [vmem] * 4
@@ -606,8 +623,11 @@
         functools.partial(last_kernel, spots, tiles),
         out_shape=[struct(tile_len, tile_len), struct(8, count)],
         in_specs=shared_specs + [vmem] * (1 + tiles),
-        out_specs=[vmem] * 2,
-        scratch_shapes=work + [pltpu.VMEM((count, lanes), f32)] + steps,
+        out_specs=[left, vmem],
+        scratch_shapes=work + [pltpu.VMEM((count, lanes), f32)] + steps + [
+            pltpu.VMEM((tile_len, tile_len), f32),
+            pltpu.SemaphoreType.DMA((1,)),
+        ],
         compiler_params=params_of,
         cost_estimate=cost(1 << 32),
         name="last_step",

time: 47.4 us -> 40.9 us (0.86)
  local copies, waits for them, and re-layouts: 4.86 us -> 0.5 us
  Pallas kernels: 16.7 us -> 14.8 us
    unnamed x12, local copies, waits for them, and re-layouts: 4.86 us -> 0.5 us
    pallas_call x1, Pallas kernels: 1.57 us -> 0.08 us  [per_device(): pl.pallas_call(pack_kernel, out_shape=[struct(8, 128), struct(MARGIN, til...]
    pallas_call x1, Pallas kernels: 4.76 us -> 4.29 us  [per_device(): pl.pallas_call(functools.partial(last_kernel, spots, tiles), out_shape=[s...]
    pallas_call x1 -> x3, Pallas kernels: 4.15 us -> 4.26 us  [the longest x1 3.61 us: per_device(): pl.pallas_call(functools.partial(first_kernel, spots, peers, scale), out_...]
  transfers between devices with their start and end apart: 16 -> 16, of which waited for: 8 -> 8; matrix products, arithmetic and copies ran while one was open for 0% -> 0% of each run, Pallas kernels for 12% -> 11%
where the time goes in v6:
time: 40.9 us; the launch traced here: 40.7 us
  Pallas kernels  14.8 us (36%)
  starting transfers between devices  14 us (34%)
  waiting for transfers between devices  10.7 us (26%)
  between operations  0.75 us (2%)
  local copies, waits for them, and re-layouts  0.5 us (1%)
    ppermute x15, starting transfers between devices, crossed(): lax.ppermute(value, axis, [(i, i ^ k) for i in range(lax.axis_size(axis))])  11.5 us
    ppermute x15, waiting for transfers between devices, crossed(): lax.ppermute(value, axis, [(i, i ^ k) for i in range(lax.axis_size(axis))])  10.7 us
    pallas_call x1, Pallas kernels, per_device(): pl.pallas_call(functools.partial(next_kernel, spots, tiles, scale), out_s...  5.45 us
    pallas_call x1, Pallas kernels, per_device(): pl.pallas_call(functools.partial(last_kernel, spots, tiles), out_shape=[s...  4.29 us
    pallas_call x1, Pallas kernels, per_device(): pl.pallas_call(functools.partial(first_kernel, spots, peers, scale), out_...  3.61 us
    ppermute x1, starting transfers between devices, per_device(): cross = lax.ppermute(edge, 'tile', pairs + [(j, i) for i, j in pairs])  2.44 us
  transfers between devices with their start and end apart: 16, of which 8 were waited for; matrix products, arithmetic and copies ran while one was open for 0% of the time, Pallas kernels for 11%

profile of v6, /device:TPU:0, one launch (start us, length us, event | category | flops | bytes accessed | tf_op | source)
XLA Modules:
  0.0 40.7 jit_solution(10038536547193165459)
XLA Ops:
  0.7 0.6 %collective-permute-start = (f32[256,256]{1,0:T(8,128)}, f32[256,256]{1,0:T(8,128)S(1)}, u32[]{:S(2)}, u32[]{:S(2)}) collective-permute-start(f32[256,256]{1,0:T(8,128)} %refs_0_.1), channel_id=1, source_target_pairs={{0,1},{1,0},{2,3},{3,2},{4,5},{5,4},{6,7},{7,6},{8,9},{9,8},{10,11... | collective-permute-start | bytes 786440 | tf_op jit(solution)/shard_map/ppermute | solution.py:501
  1.8 2.4 %collective-permute-start.1 = (f32[64,256]{1,0:T(8,128)S(1)}, f32[64,256]{1,0:T(8,128)S(1)}, u32[]{:S(2)}, u32[]{:S(2)}) collective-permute-start(f32[64,256]{1,0:T(8,128)S(1)} %get-tuple-element.20), channel_id=1, source_target_pairs={{1,2},{3,0},{2,1},{0,3},{5,6},{7,4},{6,5},{4,7},{9,10},{11,8},{10,... | collective-permute-start | bytes 196616 | tf_op jit(solution)/shard_map/ppermute | solution.py:554
  4.3 3.6 %collective-permute-start.4 = (f32[8,128]{1,0:T(8,128)S(1)}, f32[8,128]{1,0:T(8,128)S(1)}, u32[]{:S(2)}, u32[]{:S(2)}) collective-permute-start(f32[8,128]{1,0:T(8,128)S(1)} %get-tuple-element.26.refs_0_), channel_id=1, source_target_pairs={{0,12},{4,8},{8,4},{12,0},{1,13},{5,9},{9,5},{13,1},{2,14},{6,10},... | collective-permute-start | bytes 12296 | tf_op jit(solution)/shard_map/ppermute | solution.py:501
  7.9 0.8 %collective-permute-start.2 = (f32[8,128]{1,0:T(8,128)S(1)}, f32[8,128]{1,0:T(8,128)S(1)}, u32[]{:S(2)}, u32[]{:S(2)}) collective-permute-start(f32[8,128]{1,0:T(8,128)S(1)} %get-tuple-element.26.refs_0_), channel_id=1, source_target_pairs={{0,4},{4,0},{8,12},{12,8},{1,5},{5,1},{9,13},{13,9},{2,6},{6,2},{1... | collective-permute-start | bytes 12296 | tf_op jit(solution)/shard_map/ppermute | solution.py:501
  8.7 0.6 %collective-permute-start.5 = (f32[256,256]{1,0:T(8,128)S(1)}, f32[256,256]{1,0:T(8,128)S(1)}, u32[]{:S(2)}, u32[]{:S(2)}) collective-permute-start(f32[256,256]{1,0:T(8,128)S(1)} %copy-done), channel_id=1, source_target_pairs={{0,2},{1,3},{2,0},{3,1},{4,6},{5,7},{6,4},{7,5},{8,10},{9,11},{10,... | collective-permute-start | bytes 786440 | tf_op jit(solution)/shard_map/ppermute | solution.py:501
  9.3 0.6 %ready_step.1 = (f32[64,128]{1,0:T(8,128)S(1)}, f32[64,128]{1,0:T(8,128)S(1)}, f32[64,128]{1,0:T(8,128)S(1)}, f32[33,32,128]{2,1,0:T(8,128)S(1)}, f32[33,32,128]{2,1,0:T(8,128)S(1)}) custom-call(s32[1]{0:T(128)} %bitcast.tile, bf16[1856,512]{1,0:T(8,128)(2,1)S(1)} %copy-done.5, f32[2,32,32]{2,1,0:T(8,128)S(1)} %copy-done.4, f32[256,256]{1,0:T(8,128)S(1)} %copy-done.3, ...), custom_call_target="tpu_custom_call" | custom-call | flops 1073741824 | bytes 1048576 | tf_op jit(solution)/shard_map/ready_step/pallas_call | solution.py:576
  10.0 2.4 %collective-permute-done.3.refs_2_ = f32[8,128]{1,0:T(8,128)S(1)} collective-permute-done((f32[8,128]{1,0:T(8,128)S(1)}, f32[8,128]{1,0:T(8,128)S(1)}, u32[]{:S(2)}, u32[]{:S(2)}) %collective-permute-start.3) | collective-permute-done | bytes 4128 | tf_op jit(solution)/shard_map/ppermute | solution.py:501
  12.4 3.6 %first_step.1 = (f32[64,128]{1,0:T(8,128)S(1)}, f32[64,32,128]{2,1,0:T(8,128)S(1)}, f32[64,32,128]{2,1,0:T(8,128)S(1)}, f32[8,128]{1,0:T(8,128)S(1)}, s32[8,128]{1,0:T(8,128)S(1)}) custom-call(bf16[1856,512]{1,0:T(8,128)(2,1)S(1)} %copy-done.5, f32[64,128]{1,0:T(8,128)S(1)} %get-tuple-element.21.plain, f32[64,128]{1,0:T(8,128)S(1)} %get-tuple-element.22.crossed, ...), custom_call_target="tpu_custom_call" | custom-call | flops 4294967296 | bytes 1048576 | tf_op jit(solution)/shard_map/first_step/pallas_call | solution.py:586
  16.0 0.8 %collective-permute-done.5.refs_2_ = f32[256,256]{1,0:T(8,128)S(1)} collective-permute-done((f32[256,256]{1,0:T(8,128)S(1)}, f32[256,256]{1,0:T(8,128)S(1)}, u32[]{:S(2)}, u32[]{:S(2)}) %collective-permute-start.5) | collective-permute-done | bytes 262176 | tf_op jit(solution)/shard_map/ppermute | solution.py:501
  16.8 0.9 %collective-permute-start.9 = (f32[64,128]{1,0:T(8,128)S(1)}, f32[64,128]{1,0:T(8,128)S(1)}, u32[]{:S(2)}, u32[]{:S(2)}) collective-permute-start(f32[64,128]{1,0:T(8,128)S(1)} %get-tuple-element.33.refs_4_), channel_id=1, source_target_pairs={{0,3},{1,2},{2,1},{3,0},{4,7},{5,6},{6,5},{7,4},{8,11},{9,10},{10,... | collective-permute-start | bytes 98312 | tf_op jit(solution)/shard_map/ppermute | solution.py:501
  17.6 1.3 %collective-permute-start.8 = (f32[64,128]{1,0:T(8,128)S(1)}, f32[64,128]{1,0:T(8,128)S(1)}, u32[]{:S(2)}, u32[]{:S(2)}) collective-permute-start(f32[64,128]{1,0:T(8,128)S(1)} %get-tuple-element.33.refs_4_), channel_id=1, source_target_pairs={{0,2},{1,3},{2,0},{3,1},{4,6},{5,7},{6,4},{7,5},{8,10},{9,11},{10,... | collective-permute-start | bytes 98312 | tf_op jit(solution)/shard_map/ppermute | solution.py:501
  18.9 1.2 %collective-permute-done.9.refs_7_ = f32[64,128]{1,0:T(8,128)S(1)} collective-permute-done((f32[64,128]{1,0:T(8,128)S(1)}, f32[64,128]{1,0:T(8,128)S(1)}, u32[]{:S(2)}, u32[]{:S(2)}) %collective-permute-start.9) | collective-permute-done | bytes 32800 | tf_op jit(solution)/shard_map/ppermute | solution.py:501
  20.1 1.4 %collective-permute-done.8.refs_6_ = f32[64,128]{1,0:T(8,128)S(1)} collective-permute-done((f32[64,128]{1,0:T(8,128)S(1)}, f32[64,128]{1,0:T(8,128)S(1)}, u32[]{:S(2)}, u32[]{:S(2)}) %collective-permute-start.8) | collective-permute-done | bytes 32800 | tf_op jit(solution)/shard_map/ppermute | solution.py:501
  21.6 5.4 %next_step.1 = (f32[1024,256]{1,0:T(8,128)S(1)}, f32[64,128]{1,0:T(8,128)S(1)}) custom-call(s32[1]{0:T(128)} %bitcast.tile, bf16[1856,512]{1,0:T(8,128)(2,1)S(1)} %copy-done.5, s32[8,128]{1,0:T(8,128)S(1)} %get-tuple-element.27.shifts, f32[8,128]{1,0:T(8,128)S(1)} %get-tuple-element.28.info, f32[64,32,128]{2,1,0:T(8,128)S(1)} %get-tuple-element.29.pr, ...), custom_call_target="tpu_custom_call" | custom-call | flops 4294967296 | bytes 1048576 | tf_op jit(solution)/shard_map/next_step/pallas_call | solution.py:610
  27.0 1.3 %collective-permute-start.11 = (f32[64,128]{1,0:T(8,128)S(1)}, f32[64,128]{1,0:T(8,128)S(1)}, u32[]{:S(2)}, u32[]{:S(2)}) collective-permute-start(f32[64,128]{1,0:T(8,128)S(1)} %get-tuple-element.35.refs_0_), channel_id=1, source_target_pairs={{0,2},{1,3},{2,0},{3,1},{4,6},{5,7},{6,4},{7,5},{8,10},{9,11},{10,... | collective-permute-start | bytes 98312 | tf_op jit(solution)/shard_map/ppermute | solution.py:501
  28.4 0.5 %collective-permute-start.10 = (f32[64,128]{1,0:T(8,128)S(1)}, f32[64,128]{1,0:T(8,128)S(1)}, u32[]{:S(2)}, u32[]{:S(2)}) collective-permute-start(f32[64,128]{1,0:T(8,128)S(1)} %get-tuple-element.35.refs_0_), channel_id=1, source_target_pairs={{0,1},{1,0},{2,3},{3,2},{4,5},{5,4},{6,7},{7,6},{8,9},{9,8},{10,11... | collective-permute-start | bytes 98312 | tf_op jit(solution)/shard_map/ppermute | solution.py:501
  28.9 1.6 %collective-permute-done.12.refs_3_ = f32[64,128]{1,0:T(8,128)S(1)} collective-permute-done((f32[64,128]{1,0:T(8,128)S(1)}, f32[64,128]{1,0:T(8,128)S(1)}, u32[]{:S(2)}, u32[]{:S(2)}) %collective-permute-start.12) | collective-permute-done | bytes 32800 | tf_op jit(solution)/shard_map/ppermute | solution.py:501
  30.5 0.5 %collective-permute-done.11.refs_2_ = f32[64,128]{1,0:T(8,128)S(1)} collective-permute-done((f32[64,128]{1,0:T(8,128)S(1)}, f32[64,128]{1,0:T(8,128)S(1)}, u32[]{:S(2)}, u32[]{:S(2)}) %collective-permute-start.11) | collective-permute-done | bytes 32800 | tf_op jit(solution)/shard_map/ppermute | solution.py:501
  31.0 4.3 %last_step.1 = (f32[256,256]{1,0:T(8,128)}, f32[8,64]{1,0:T(8,128)S(1)}) custom-call(s32[1]{0:T(128)} %bitcast.tile, bf16[1856,512]{1,0:T(8,128)(2,1)S(1)} %copy-done.5, s32[8,128]{1,0:T(8,128)S(1)} %get-tuple-element.27.shifts, f32[8,128]{1,0:T(8,128)S(1)} %get-tuple-element.28.info, f32[64,32,128]{2,1,0:T(8,128)S(1)} %get-tuple-element.29.pr, ...), custom_call_target="tpu_custom_call" | custom-call | flops 4294967296 | bytes 1048576 | tf_op jit(solution)/shard_map/last_step/pallas_call | solution.py:622
  35.3 1.0 %collective-permute-start.15 = (f32[8,64]{1,0:T(8,128)S(1)}, f32[8,64]{1,0:T(8,128)S(1)}, u32[]{:S(2)}, u32[]{:S(2)}) collective-permute-start(f32[8,64]{1,0:T(8,128)S(1)} %get-tuple-element.37.refs_0_), channel_id=1, source_target_pairs={{0,3},{1,2},{2,1},{3,0},{4,7},{5,6},{6,5},{7,4},{8,11},{9,10},{10,... | collective-permute-start | bytes 6152 | tf_op jit(solution)/shard_map/ppermute | solution.py:501
  36.4 0.8 %collective-permute-start.14 = (f32[8,64]{1,0:T(8,128)S(1)}, f32[8,64]{1,0:T(8,128)S(1)}, u32[]{:S(2)}, u32[]{:S(2)}) collective-permute-start(f32[8,64]{1,0:T(8,128)S(1)} %get-tuple-element.37.refs_0_), channel_id=1, source_target_pairs={{0,2},{1,3},{2,0},{3,1},{4,6},{5,7},{6,4},{7,5},{8,10},{9,11},{10,... | collective-permute-start | bytes 6152 | tf_op jit(solution)/shard_map/ppermute | solution.py:501
  37.3 1.2 %collective-permute-done.15.refs_3_ = f32[8,64]{1,0:T(8,128)S(1)} collective-permute-done((f32[8,64]{1,0:T(8,128)S(1)}, f32[8,64]{1,0:T(8,128)S(1)}, u32[]{:S(2)}, u32[]{:S(2)}) %collective-permute-start.15) | collective-permute-done | bytes 2080 | tf_op jit(solution)/shard_map/ppermute | solution.py:501
  38.4 1.5 %collective-permute-done.14.refs_2_ = f32[8,64]{1,0:T(8,128)S(1)} collective-permute-done((f32[8,64]{1,0:T(8,128)S(1)}, f32[8,64]{1,0:T(8,128)S(1)}, u32[]{:S(2)}, u32[]{:S(2)}) %collective-permute-start.14) | collective-permute-done | bytes 2080 | tf_op jit(solution)/shard_map/ppermute | solution.py:501
  40.0 0.8 %weight_step.1 = f32[1,16]{1,0:T(1,128)} custom-call(s32[1]{0:T(128)} %bitcast.tile, s32[1]{0:T(128)} %bitcast.1.place, f32[8,128]{1,0:T(8,128)S(1)} %get-tuple-element.28.info, f32[8,64]{1,0:T(8,128)S(1)} %get-tuple-element.37.refs_0_, f32[8,64]{1,0:T(8,128)S(1)} %collective-permute-done.13.refs_1_, f32[8,64]{1,0:T(8,128)S(1)} %collective-permute-done.14.refs_2_, ...), custom_call_target="tpu_custom_call" | custom-call | tf_op jit(solution)/shard_map/weight_step/pallas_call | solution.py:637
  (27 shorter events, 0.7 us)
Async XLA Ops:
  0.6 8.7 %copy-start.5 = (bf16[1856,512]{1,0:T(8,128)(2,1)S(1)}, bf16[1856,512]{1,0:T(8,128)(2,1)}, u32[]{:S(2)}) copy-start(bf16[1856,512]{1,0:T(8,128)(2,1)} %constant.9.clone.table) | copy-start | bytes 5701636
  0.6 1.1 %copy-start = (f32[256,256]{1,0:T(8,128)S(1)}, f32[256,256]{1,0:T(8,128)}, u32[]{:S(2)}) copy-start(f32[256,256]{1,0:T(8,128)} %refs_0_.1) | copy-start | bytes 786436
  0.7 1.1 %copy-start.1 = (s32[16,2]{0,1:T(2,128)S(1)}, s32[16,2]{0,1:T(2,128)}, u32[]{:S(2)}) copy-start(s32[16,2]{0,1:T(2,128)} %param.9) | copy-start | bytes 388
  0.7 1.1 %copy-start.2 = (f32[16]{0:T(128)S(1)}, f32[16]{0:T(128)}, u32[]{:S(2)}) copy-start(f32[16]{0:T(128)} %param.8) | copy-start | bytes 196
  0.7 8.6 %copy-start.4 = (f32[2,32,32]{2,1,0:T(8,128)S(1)}, f32[2,32,32]{2,1,0:T(8,128)}, u32[]{:S(2)}) copy-start(f32[2,32,32]{2,1,0:T(8,128)} %pupil.1) | copy-start | bytes 24580
  0.7 8.6 %copy-start.3 = (f32[256,256]{1,0:T(8,128)S(1)}, f32[256,256]{1,0:T(8,128)}, u32[]{:S(2)}) copy-start(f32[256,256]{1,0:T(8,128)} %goal.1) | copy-start | bytes 786436
  0.7 8.6 %collective-permute-start = (f32[256,256]{1,0:T(8,128)}, f32[256,256]{1,0:T(8,128)S(1)}, u32[]{:S(2)}, u32[]{:S(2)}) collective-permute-start(f32[256,256]{1,0:T(8,128)} %refs_0_.1), channel_id=1, source_target_pairs={{0,1},{1,0},{2,3},{3,2},{4,5},{5,4},{6,7},{7,6},{8,9},{9,8},{10,11... | collective-permute-start | bytes 786440 | tf_op jit(solution)/shard_map/ppermute | solution.py:501
  1.8 6.8 %collective-permute-start.1 = (f32[64,256]{1,0:T(8,128)S(1)}, f32[64,256]{1,0:T(8,128)S(1)}, u32[]{:S(2)}, u32[]{:S(2)}) collective-permute-start(f32[64,256]{1,0:T(8,128)S(1)} %get-tuple-element.20), channel_id=1, source_target_pairs={{1,2},{3,0},{2,1},{0,3},{5,6},{7,4},{6,5},{4,7},{9,10},{11,8},{10,... | collective-permute-start | bytes 196616 | tf_op jit(solution)/shard_map/ppermute | solution.py:554
  4.3 5.7 %collective-permute-start.4 = (f32[8,128]{1,0:T(8,128)S(1)}, f32[8,128]{1,0:T(8,128)S(1)}, u32[]{:S(2)}, u32[]{:S(2)}) collective-permute-start(f32[8,128]{1,0:T(8,128)S(1)} %get-tuple-element.26.refs_0_), channel_id=1, source_target_pairs={{0,12},{4,8},{8,4},{12,0},{1,13},{5,9},{9,5},{13,1},{2,14},{6,10},... | collective-permute-start | bytes 12296 | tf_op jit(solution)/shard_map/ppermute | solution.py:501
  7.9 4.5 %collective-permute-start.3 = (f32[8,128]{1,0:T(8,128)S(1)}, f32[8,128]{1,0:T(8,128)S(1)}, u32[]{:S(2)}, u32[]{:S(2)}) collective-permute-start(f32[8,128]{1,0:T(8,128)S(1)} %get-tuple-element.26.refs_0_), channel_id=1, source_target_pairs={{0,8},{4,12},{8,0},{12,4},{1,9},{5,13},{9,1},{13,5},{2,10},{6,14},... | collective-permute-start | bytes 12296 | tf_op jit(solution)/shard_map/ppermute | solution.py:501
  7.9 4.5 %collective-permute-start.2 = (f32[8,128]{1,0:T(8,128)S(1)}, f32[8,128]{1,0:T(8,128)S(1)}, u32[]{:S(2)}, u32[]{:S(2)}) collective-permute-start(f32[8,128]{1,0:T(8,128)S(1)} %get-tuple-element.26.refs_0_), channel_id=1, source_target_pairs={{0,4},{4,0},{8,12},{12,8},{1,5},{5,1},{9,13},{13,9},{2,6},{6,2},{1... | collective-permute-start | bytes 12296 | tf_op jit(solution)/shard_map/ppermute | solution.py:501
  8.7 8.1 %collective-permute-start.5 = (f32[256,256]{1,0:T(8,128)S(1)}, f32[256,256]{1,0:T(8,128)S(1)}, u32[]{:S(2)}, u32[]{:S(2)}) collective-permute-start(f32[256,256]{1,0:T(8,128)S(1)} %copy-done), channel_id=1, source_target_pairs={{0,2},{1,3},{2,0},{3,1},{4,6},{5,7},{6,4},{7,5},{8,10},{9,11},{10,... | collective-permute-start | bytes 786440 | tf_op jit(solution)/shard_map/ppermute | solution.py:501
  16.8 4.8 %collective-permute-start.6 = (f32[256,256]{1,0:T(8,128)S(1)}, f32[256,256]{1,0:T(8,128)S(1)}, u32[]{:S(2)}, u32[]{:S(2)}) collective-permute-start(f32[256,256]{1,0:T(8,128)S(1)} %collective-permute-done.5.refs_2_), channel_id=1, source_target_pairs={{0,1},{1,0},{2,3},{3,2},{4,5},{5,4},{6,7},{7,6},{8,9},{9,8},{10,11... | collective-permute-start | bytes 786440 | tf_op jit(solution)/shard_map/ppermute | solution.py:501
  16.8 3.3 %collective-permute-start.9 = (f32[64,128]{1,0:T(8,128)S(1)}, f32[64,128]{1,0:T(8,128)S(1)}, u32[]{:S(2)}, u32[]{:S(2)}) collective-permute-start(f32[64,128]{1,0:T(8,128)S(1)} %get-tuple-element.33.refs_4_), channel_id=1, source_target_pairs={{0,3},{1,2},{2,1},{3,0},{4,7},{5,6},{6,5},{7,4},{8,11},{9,10},{10,... | collective-permute-start | bytes 98312 | tf_op jit(solution)/shard_map/ppermute | solution.py:501
  17.6 3.9 %collective-permute-start.8 = (f32[64,128]{1,0:T(8,128)S(1)}, f32[64,128]{1,0:T(8,128)S(1)}, u32[]{:S(2)}, u32[]{:S(2)}) collective-permute-start(f32[64,128]{1,0:T(8,128)S(1)} %get-tuple-element.33.refs_4_), channel_id=1, source_target_pairs={{0,2},{1,3},{2,0},{3,1},{4,6},{5,7},{6,4},{7,5},{8,10},{9,11},{10,... | collective-permute-start | bytes 98312 | tf_op jit(solution)/shard_map/ppermute | solution.py:501
  18.9 2.7 %collective-permute-start.7 = (f32[64,128]{1,0:T(8,128)S(1)}, f32[64,128]{1,0:T(8,128)S(1)}, u32[]{:S(2)}, u32[]{:S(2)}) collective-permute-start(f32[64,128]{1,0:T(8,128)S(1)} %get-tuple-element.33.refs_4_), channel_id=1, source_target_pairs={{0,1},{1,0},{2,3},{3,2},{4,5},{5,4},{6,7},{7,6},{8,9},{9,8},{10,11... | collective-permute-start | bytes 98312 | tf_op jit(solution)/shard_map/ppermute | solution.py:501
  27.0 3.5 %collective-permute-start.12 = (f32[64,128]{1,0:T(8,128)S(1)}, f32[64,128]{1,0:T(8,128)S(1)}, u32[]{:S(2)}, u32[]{:S(2)}) collective-permute-start(f32[64,128]{1,0:T(8,128)S(1)} %get-tuple-element.35.refs_0_), channel_id=1, source_target_pairs={{0,3},{1,2},{2,1},{3,0},{4,7},{5,6},{6,5},{7,4},{8,11},{9,10},{10,... | collective-permute-start | bytes 98312 | tf_op jit(solution)/shard_map/ppermute | solution.py:501
  27.0 4.0 %collective-permute-start.11 = (f32[64,128]{1,0:T(8,128)S(1)}, f32[64,128]{1,0:T(8,128)S(1)}, u32[]{:S(2)}, u32[]{:S(2)}) collective-permute-start(f32[64,128]{1,0:T(8,128)S(1)} %get-tuple-element.35.refs_0_), channel_id=1, source_target_pairs={{0,2},{1,3},{2,0},{3,1},{4,6},{5,7},{6,4},{7,5},{8,10},{9,11},{10,... | collective-permute-start | bytes 98312 | tf_op jit(solution)/shard_map/ppermute | solution.py:501
  28.4 2.7 %collective-permute-start.10 = (f32[64,128]{1,0:T(8,128)S(1)}, f32[64,128]{1,0:T(8,128)S(1)}, u32[]{:S(2)}, u32[]{:S(2)}) collective-permute-start(f32[64,128]{1,0:T(8,128)S(1)} %get-tuple-element.35.refs_0_), channel_id=1, source_target_pairs={{0,1},{1,0},{2,3},{3,2},{4,5},{5,4},{6,7},{7,6},{8,9},{9,8},{10,11... | collective-permute-start | bytes 98312 | tf_op jit(solution)/shard_map/ppermute | solution.py:501
  35.3 3.1 %collective-permute-start.15 = (f32[8,64]{1,0:T(8,128)S(1)}, f32[8,64]{1,0:T(8,128)S(1)}, u32[]{:S(2)}, u32[]{:S(2)}) collective-permute-start(f32[8,64]{1,0:T(8,128)S(1)} %get-tuple-element.37.refs_0_), channel_id=1, source_target_pairs={{0,3},{1,2},{2,1},{3,0},{4,7},{5,6},{6,5},{7,4},{8,11},{9,10},{10,... | collective-permute-start | bytes 6152 | tf_op jit(solution)/shard_map/ppermute | solution.py:501
  36.4 3.6 %collective-permute-start.14 = (f32[8,64]{1,0:T(8,128)S(1)}, f32[8,64]{1,0:T(8,128)S(1)}, u32[]{:S(2)}, u32[]{:S(2)}) collective-permute-start(f32[8,64]{1,0:T(8,128)S(1)} %get-tuple-element.37.refs_0_), channel_id=1, source_target_pairs={{0,2},{1,3},{2,0},{3,1},{4,6},{5,7},{6,4},{7,5},{8,10},{9,11},{10,... | collective-permute-start | bytes 6152 | tf_op jit(solution)/shard_map/ppermute | solution.py:501
  37.2 2.8 %collective-permute-start.13 = (f32[8,64]{1,0:T(8,128)S(1)}, f32[8,64]{1,0:T(8,128)S(1)}, u32[]{:S(2)}, u32[]{:S(2)}) collective-permute-start(f32[8,64]{1,0:T(8,128)S(1)} %get-tuple-element.37.refs_0_), channel_id=1, source_target_pairs={{0,1},{1,0},{2,3},{3,2},{4,5},{5,4},{6,7},{7,6},{8,9},{9,8},{10,11... | collective-permute-start | bytes 6152 | tf_op jit(solution)/shard_map/ppermute | solution.py:501

commit v7 on v6

--- a/solution.py
+++ b/solution.py
@@ -81,9 +81,10 @@
     out["target_cols"] = np.concatenate([high, low], 1)
     ang = phases(wide, pix, period)
     cos, sin = np.cos(ang), np.sin(ang)
-    high, low = np_split(np.block([[cos, sin], [-sin, cos]]))
+    high, low = np_split(np.block([[cos, -sin], [-sin, -cos]]))
     out["grad_cols"] = np.concatenate([high, high, low], 0)
-    high, low = np_split(np.concatenate([np.cos(ang_rows).T, -np.sin(ang_rows).T], 1))
+    ang = phases(full, np.arange(grid // 2), period)
+    high, low = np_split(np.concatenate([np.cos(ang), np.sin(ang)], 1))
     out["grad_rows"] = np.concatenate([high, high, low], 1)
     return out
 
@@ -232,6 +233,7 @@
 
 def gather_back(misfit, shifts, scale, t, pr, pi, fields, stages, sums):
     count, box_len, lanes = pr.shape
+    grid = lanes // 2
     for ref in sums:
         ref[...] = jnp.zeros_like(ref)
     sign = lane_sign(box_len, lanes, 1.0)
@@ -261,54 +263,95 @@
         return carry
 
     skewed(count, stages, first, second, 0)
-    return (sums[0][...] + sums[2][...] + swap(sums[1][...] + sums[3][...])) * scale
+    whole, turned = sums[0], sums[1]
+    whole[...] = (whole[...] + sums[2][...] + swap(turned[...] + sums[3][...])) * scale
+    middle = grid // 2
+    turned[0:1, :] = jnp.zeros((1, lanes), f32)
+    for a in range(1, middle):
+        turned[a : a + 1, :] = whole[middle - a : middle - a + 1, :]
+    ahead, behind = whole[middle:, :], turned[:middle, :]
+    return jnp.concatenate([ahead + behind, ahead - behind], 0)
 
 
 def tile_of(k, tile):
     return lax.bitwise_xor(tile, jnp.int32(k))
 
 
-def mask_grads(params, ids, backs, t, tile, tiles, wins, grads):
-    grid = backs[0].shape[0]
+def fill_windows(backs, t, tile, tiles, wins):
+    half = backs[0].shape[0] // 2
     tile_len = wins.shape[2]
-    rows = []
-    for back in backs:
-        high, low = split(back[...])
-        rows.append(jnp.concatenate([high, low, high], 1))
-    mid = dot(jnp.concatenate(rows, 0), t["grad_cols"][...])
+    stacks = []
+    for rows in (slice(0, half), slice(half, 2 * half)):
+        parts = []
+        for back in backs:
+            high, low = split(back[rows, :])
+            parts.append(jnp.concatenate([high, low, high], 1))
+        stacks.append(jnp.concatenate(parts, 0))
+    even = dot(stacks[0], t["grad_cols"][:, :tile_len])
+    odd = dot(stacks[1], t["grad_cols"][:, tile_len:])
     wins[0, MARGIN + tile_len :, :] = jnp.zeros((MARGIN, tile_len), f32)
     wins[tiles + 1, :MARGIN, :] = jnp.zeros((MARGIN, tile_len), f32)
     for k in range(tiles):
-        part = mid[k * grid : (k + 1) * grid]
-        high, low = split(jnp.concatenate([part[:, :tile_len], part[:, tile_len:]], 0))
+        at = slice(k * half, (k + 1) * half)
+        high, low = split(jnp.concatenate([even[at], odd[at]], 0))
         out = dot(t["grad_rows"][...], jnp.concatenate([high, low, high], 0))
         wins[tile_of(k, tile) + 1] = out
-    square = jnp.zeros((8, tile_len), f32)
-    for k in range(tiles):
-        own = ids[k]
-        for low_row, high_row, near, shift in (
-            (0, MARGIN, 0, tile_len),
-            (MARGIN, tile_len - MARGIN, 1, 0),
-            (tile_len - MARGIN, tile_len, 2, -tile_len),
-        ):
-            total = wins[own + 1, MARGIN + low_row : MARGIN + high_row, :]
-            if near != 1:
-                at = MARGIN + low_row + shift
-                total = total + wins[own + near, at : at + MARGIN, :]
-            lean = half_tanh(params(k, low_row, high_row))
-            grad = total * (1.0 - lean * lean)
-            grads[own, low_row:high_row, :] = grad
-            square = square + jnp.sum((grad * grad).reshape(-1, 8, tile_len), axis=0)
+
+
+def pieces(tile_len):
+    return (
+        (0, MARGIN, 0, tile_len),
+        (MARGIN, tile_len - MARGIN, 1, 0),
+        (tile_len - MARGIN, tile_len, 2, -tile_len),
+    )
+
+
+def piece_total(own, piece, wins):
+    low, high, near, shift = piece
+    total = wins[own + 1, MARGIN + low : MARGIN + high, :]
+    if near != 1:
+        at = MARGIN + low + shift
+        total = total + wins[own + near, at : at + MARGIN, :]
+    return total
+
+
+def squares_of(grad):
+    return jnp.sum((grad * grad).reshape(-1, 8, grad.shape[1]), axis=0)
+
+
+def step_rate(square, tiles):
+    tile_len = square.shape[1]
     total = jnp.sum(jnp.sum(square, axis=0, keepdims=True), axis=1, keepdims=True)
-    pixels = tiles * tile_len * tile_len
-    return MASK_RATE / jnp.sqrt(total / pixels + TINY_EPS)
-
-
-def edge_rows(tile, tiles, tile_len):
-    above = pl.multiple_of(jnp.maximum(tile * tile_len - MARGIN, 0), MARGIN)
-    below = jnp.minimum((tile + 1) * tile_len, tiles * tile_len - MARGIN)
-    below = pl.multiple_of(below, MARGIN)
-    return above, below, (tile > 0).astype(f32), (tile < tiles - 1).astype(f32)
+    return MASK_RATE / jnp.sqrt(total / (tiles * tile_len * tile_len) + TINY_EPS)
+
+
+def slope_of(params):
+    lean = half_tanh(params)
+    return 1.0 - lean * lean
+
+
+def near_tiles(tile, tiles):
+    prev, follow = jnp.maximum(tile - 1, 0), jnp.minimum(tile + 1, tiles - 1)
+    return prev, follow, (tile > 0).astype(f32), (tile < tiles - 1).astype(f32)
+
+
+def edge_params(tile, mate, cross):
+    odd = lax.rem(tile, 2) > 0
+    before = jnp.where(odd, mate[-MARGIN:, :], cross[...])
+    after = jnp.where(odd, cross[...], mate[:MARGIN, :])
+    return before, after
+
+
+def mask_window(near, has_prev, has_next):
+    rows = near.shape[0]
+    return jnp.concatenate(
+        [
+            sigmoid(near[:MARGIN, :]) * has_prev,
+            sigmoid(near[MARGIN : rows - MARGIN, :]),
+            sigmoid(near[rows - MARGIN :, :]) * has_next,
+        ],
+        0,
+    )
 
 
 def start_all(pairs, sems):
@@ -349,22 +392,22 @@
 
 
 def ready_kernel(spots, tiles, tile, table, pupil, goal, own, mate, cross,
-                 plain, crossed, target, turned_re, turned_im):
+                 plain, crossed, target, turned_re, turned_im, slopes, near):
     t = {n: table.at[spot] for n, spot in spots.items()}
     here = tile[0]
-    has_prev = (here > 0).astype(f32)
-    has_next = (here < tiles - 1).astype(f32)
-    odd = lax.rem(here, 2) > 0
-    before = jnp.where(odd, mate[-MARGIN:, :], cross[...])
-    after = jnp.where(odd, cross[...], mate[:MARGIN, :])
-    window = jnp.concatenate(
-        [sigmoid(before) * has_prev, sigmoid(own[...]), sigmoid(after) * has_next], 0
-    )
+    tile_len = own.shape[0]
+    _, _, has_prev, has_next = near_tiles(here, tiles)
+    before, after = edge_params(here, mate, cross)
+    near[:MARGIN, :] = before
+    near[MARGIN : MARGIN + tile_len, :] = own[...]
+    near[MARGIN + tile_len :, :] = after
     turn_pupils(pupil, turned_re, turned_im)
-    spec = window_spectrum(window, t)
+    spec = window_spectrum(mask_window(near, has_prev, has_next), t)
     plain[...] = spec
     crossed[...] = swap(spec)
     target[...] = target_terms(goal[...], t)
+    slopes[0] = slope_of(own[...])
+    slopes[1] = slope_of(mate[...])
 
 
 def first_kernel(spots, peers, scale, table, plain, crossed, target, turned_re, turned_im, *refs):
@@ -388,31 +431,30 @@
     back[...] = gather_back(misfit, shifts, factor, t, pr, pi, work[2], work[3:], sums)
 
 
-def next_kernel(spots, tiles, scale, tile, table, shifts, info, pr, pi, target, *refs):
-    params, backs = refs[:tiles], refs[tiles : 2 * tiles]
+def next_kernel(spots, tiles, scale, tile, table, shifts, info, pr, pi, target, near, slopes, *refs):
+    params, backs = refs[: tiles - 2], refs[tiles - 2 : 2 * tiles - 2]
     t = {n: table.at[spot] for n, spot in spots.items()}
-    new, back, *work, s0, s1, s2, s3, wins, grads = refs[2 * tiles :]
+    new, grads, rates, back, *work, s0, s1, s2, s3, wins = refs[2 * tiles - 2 :]
     here = tile[0]
-    tile_len = params[0].shape[0]
-    ids = [tile_of(k, here) for k in range(tiles)]
-    rate = mask_grads(
-        lambda k, low, high: params[k][low:high, :], ids, backs, t, here, tiles, wins, grads
-    )
+    tile_len = wins.shape[2]
+    fill_windows(backs, t, here, tiles, wins)
+    square = jnp.zeros((8, tile_len), f32)
     for k in range(tiles):
-        own = ids[k]
-        at = pl.ds(pl.multiple_of(own * tile_len, tile_len), tile_len)
-        new[at, :] = params[k][...] - grads[own] * rate
-    above, below, has_prev, has_next = edge_rows(here, tiles, tile_len)
-    own = pl.ds(pl.multiple_of(here * tile_len, tile_len), tile_len)
-    window = jnp.concatenate(
-        [
-            sigmoid(new[pl.ds(above, MARGIN), :]) * has_prev,
-            sigmoid(new[own, :]),
-            sigmoid(new[pl.ds(below, MARGIN), :]) * has_next,
-        ],
-        0,
-    )
-    spec = window_spectrum(window, t)
+        own = tile_of(k, here)
+        for piece in pieces(tile_len):
+            low, high = piece[:2]
+            slope = slopes[k, low:high, :] if k < 2 else slope_of(params[k - 2][low:high, :])
+            grad = piece_total(own, piece, wins) * slope
+            grads[own, low:high, :] = grad
+            square = square + squares_of(grad)
+    rate = step_rate(square, tiles)
+    rates[...] = jnp.broadcast_to(rate, rates.shape)
+    prev, follow, has_prev, has_next = near_tiles(here, tiles)
+    inner = slice(MARGIN, MARGIN + tile_len)
+    new[:MARGIN, :] = near[:MARGIN, :] - grads[prev, tile_len - MARGIN :, :] * rate
+    new[inner, :] = near[inner, :] - grads[here] * rate
+    new[MARGIN + tile_len :, :] = near[MARGIN + tile_len :, :] - grads[follow, :MARGIN, :] * rate
+    spec = window_spectrum(mask_window(new, has_prev, has_next), t)
     power = grid_fields(spec, shifts, t, lambda s: (pr[s], pi[s]), work)
     inv_dose, factor = doses(info[...], scale)
     misfit = grid_misfit(power, inv_dose, target[...], t)
@@ -420,34 +462,43 @@
     back[...] = gather_back(misfit, shifts, factor, t, pr, pi, work[2], work[3:], sums)
 
 
-def last_kernel(spots, tiles, tile, table, shifts, info, pr, pi, target, params, *refs):
+def slope_kernel(tiles, tile, grads, rates, *refs):
+    params, slopes = refs[:tiles], refs[tiles]
+    rate = rates[0:1, 0:1]
+    for k in range(tiles):
+        own = tile_of(k, tile[0])
+        slopes[own] = slope_of(params[k][...] - grads[own] * rate)
+
+
+def last_kernel(spots, tiles, tile, table, shifts, info, pr, pi, target, near, slopes, *refs):
     backs = refs[:tiles]
     t = {n: table.at[spot] for n, spot in spots.items()}
-    final, row, *work, terms, wins, grads, fresh, sems = refs[tiles:]
+    final, row, *work, terms, wins, fresh, sems = refs[tiles:]
     fields = work[2]
     here = tile[0]
-    tile_len = fresh.shape[0]
-    rate = mask_grads(
-        lambda k, low, high: params[k * tile_len + low : k * tile_len + high, :],
-        list(range(tiles)), backs, t, here, tiles, wins, grads,
+    tile_len = wins.shape[2]
+    fill_windows(backs, t, here, tiles, wins)
+
+    def grad_of(own, piece):
+        return piece_total(own, piece, wins) * slopes[own, piece[0] : piece[1], :]
+
+    square = jnp.zeros((8, tile_len), f32)
+    for own in range(tiles):
+        for piece in pieces(tile_len):
+            square = square + squares_of(grad_of(own, piece))
+    rate = step_rate(square, tiles)
+    prev, follow, has_prev, has_next = near_tiles(here, tiles)
+    first, *_, end = pieces(tile_len)
+    fresh[:MARGIN, :] = near[:MARGIN, :] - grad_of(prev, end) * rate
+    for piece in pieces(tile_len):
+        at = slice(MARGIN + piece[0], MARGIN + piece[1])
+        fresh[at, :] = near[at, :] - grad_of(here, piece) * rate
+    fresh[MARGIN + tile_len :, :] = near[MARGIN + tile_len :, :] - grad_of(follow, first) * rate
+    (leave,) = start_all(((fresh.at[pl.ds(MARGIN, tile_len), :], final),), sems)
+    spec = window_spectrum(mask_window(fresh, has_prev, has_next), t)
+    power = grid_fields(
+        spec, shifts, t, lambda s: (pr[s], pi[s]), work, squares=True
     )
-    above, below, has_prev, has_next = edge_rows(here, tiles, tile_len)
-    own = pl.ds(pl.multiple_of(here * tile_len, tile_len), tile_len)
-    fresh[...] = params[own, :] - grads[here] * rate
-    (leave,) = start_all(((fresh, final),), sems)
-    prev, follow = jnp.maximum(here - 1, 0), jnp.minimum(here + 1, tiles - 1)
-    window = jnp.concatenate(
-        [
-            sigmoid(params[pl.ds(above, MARGIN), :] - grads[prev, tile_len - MARGIN :, :] * rate)
-            * has_prev,
-            sigmoid(fresh[...]),
-            sigmoid(params[pl.ds(below, MARGIN), :] - grads[follow, :MARGIN, :] * rate)
-            * has_next,
-        ],
-        0,
-    )
-    spec = window_spectrum(window, t)
-    power = grid_fields(spec, shifts, t, lambda s: (pr[s], pi[s]), work, squares=True)
     inv_dose, _ = doses(info[...], 1.0)
     misfit = grid_misfit(power, inv_dose, target[...], t)
 
@@ -565,19 +616,18 @@
         pltpu.VMEM((CHUNK * box_len, lanes), f32),
     ]
     hold = [pltpu.VMEM((grid, lanes), f32)] * 4
-    steps = [
-        pltpu.VMEM((tiles + 2, tile_len + 2 * MARGIN, tile_len), f32),
-        pltpu.VMEM((tiles, tile_len, tile_len), f32),
-    ]
     period = tile_len + 2 * MARGIN
+    steps = [pltpu.VMEM((tiles + 2, period, tile_len), f32)]
     scale = 0.5 / (grid * grid * period * tile_len)
     source_len = struct(count, box_len, lanes)
 
-    plain, crossed_spec, target, *turned = pl.pallas_call(
+    plain, crossed_spec, target, *turned, slopes, near = pl.pallas_call(
         functools.partial(ready_kernel, spots, tiles),
-        out_shape=[struct(grid, lanes)] * 3 + [struct(2 * MAX_SHIFT + 1, box_len, lanes)] * 2,
+        out_shape=[struct(grid, lanes)] * 3
+        + [struct(2 * MAX_SHIFT + 1, box_len, lanes)] * 2
+        + [struct(2, tile_len, tile_len), struct(period, tile_len)],
         in_specs=[smem] + [vmem] * 6,
-        out_specs=[vmem] * 5,
+        out_specs=[vmem] * 7,
         compiler_params=params_of,
         cost_estimate=cost(1 << 30),
         name="ready_step",
@@ -607,31 +657,41 @@
     entries = [mask_param, mate]
     for one in far:
         entries += [one, crossed(one, "tile", 1)]
-    params, back = pl.pallas_call(
+    near, grads, rates, back = pl.pallas_call(
         functools.partial(next_kernel, spots, tiles, scale),
-        out_shape=[struct(tiles * tile_len, tile_len), struct(grid, lanes)],
+        out_shape=[struct(period, tile_len), struct(tiles, tile_len, tile_len),
+                   struct(8, 128), struct(grid, lanes)],
         in_specs=shared_specs + [vmem] * (2 * tiles),
-        out_specs=[vmem] * 2,
+        out_specs=[vmem] * 4,
         scratch_shapes=work + hold + steps,
         compiler_params=params_of,
         cost_estimate=cost(1 << 32),
         name="next_step",
-    )(*shared, *entries, *backs)
+    )(*shared, near, slopes, *entries[2:], *backs)
 
     backs = all_of(back, "tile")
+    slopes = pl.pallas_call(
+        functools.partial(slope_kernel, tiles),
+        out_shape=struct(tiles, tile_len, tile_len),
+        in_specs=[smem] + [vmem] * (2 + tiles),
+        out_specs=vmem,
+        compiler_params=params_of,
+        cost_estimate=cost(1 << 28),
+        name="slope_step",
+    )(tile, grads, rates, *entries)
     final, row = pl.pallas_call(
         functools.partial(last_kernel, spots, tiles),
         out_shape=[struct(tile_len, tile_len), struct(8, count)],
-        in_specs=shared_specs + [vmem] * (1 + tiles),
+        in_specs=shared_specs + [vmem] * (2 + tiles),
         out_specs=[left, vmem],
         scratch_shapes=work + [pltpu.VMEM((count, lanes), f32)] + steps + [
-            pltpu.VMEM((tile_len, tile_len), f32),
+            pltpu.VMEM((period, tile_len), f32),
             pltpu.SemaphoreType.DMA((1,)),
         ],
         compiler_params=params_of,
         cost_estimate=cost(1 << 32),
         name="last_step",
-    )(*shared, params, *backs)
+    )(*shared, near, slopes, *backs)
 
     rows = all_of(row, "tile")
     out = pl.pallas_call(

time: 40.9 us -> 41.4 us (1.012)
  waiting for transfers between devices: 10.7 us -> 11.7 us
    ppermute x15, waiting for transfers between devices: 10.7 us -> 11.7 us  [crossed(): lax.ppermute(value, axis, [(i, i ^ k) for i in range(lax.axis_size(axis))])]
where the time goes in v7:
time: 41.4 us; the launch traced here: 41.3 us
  Pallas kernels  14.5 us (35%)
  starting transfers between devices  13.9 us (34%)
  waiting for transfers between devices  11.7 us (28%)
  between operations  0.77 us (2%)
  local copies, waits for them, and re-layouts  0.49 us (1%)
    ppermute x15, waiting for transfers between devices, crossed(): lax.ppermute(value, axis, [(i, i ^ k) for i in range(lax.axis_size(axis))])  11.7 us
    ppermute x15, starting transfers between devices, crossed(): lax.ppermute(value, axis, [(i, i ^ k) for i in range(lax.axis_size(axis))])  11.4 us
    pallas_call x1, Pallas kernels, per_device(): pl.pallas_call(functools.partial(next_kernel, spots, tiles, scale), out_s...  5.06 us
    pallas_call x1, Pallas kernels, per_device(): pl.pallas_call(functools.partial(last_kernel, spots, tiles), out_shape=[s...  3.95 us
    pallas_call x1, Pallas kernels, per_device(): pl.pallas_call(functools.partial(first_kernel, spots, peers, scale), out_...  3.63 us
    ppermute x1, starting transfers between devices, per_device(): cross = lax.ppermute(edge, 'tile', pairs + [(j, i) for i, j in pairs])  2.44 us
  transfers between devices with their start and end apart: 16, of which 8 were waited for; matrix products, arithmetic and copies ran while one was open for 0% of the time, Pallas kernels for 11%

profile of v7, /device:TPU:0, one launch (start us, length us, event | category | flops | bytes accessed | tf_op | source)
XLA Modules:
  0.0 41.3 jit_solution(9193992268838870235)
XLA Ops:
  0.7 0.6 %collective-permute-start = (f32[256,256]{1,0:T(8,128)}, f32[256,256]{1,0:T(8,128)S(1)}, u32[]{:S(2)}, u32[]{:S(2)}) collective-permute-start(f32[256,256]{1,0:T(8,128)} %refs_0_.1), channel_id=1, source_target_pairs={{0,1},{1,0},{2,3},{3,2},{4,5},{5,4},{6,7},{7,6},{8,9},{9,8},{10,11... | collective-permute-start | bytes 786440 | tf_op jit(solution)/shard_map/ppermute | solution.py:552
  1.3 0.5 %copy-done = f32[256,256]{1,0:T(8,128)S(1)} copy-done((f32[256,256]{1,0:T(8,128)S(1)}, f32[256,256]{1,0:T(8,128)}, u32[]{:S(2)}) %copy-start) | copy-done | bytes 262168
  1.8 2.4 %collective-permute-start.1 = (f32[64,256]{1,0:T(8,128)S(1)}, f32[64,256]{1,0:T(8,128)S(1)}, u32[]{:S(2)}, u32[]{:S(2)}) collective-permute-start(f32[64,256]{1,0:T(8,128)S(1)} %get-tuple-element.24), channel_id=1, source_target_pairs={{1,2},{3,0},{2,1},{0,3},{5,6},{7,4},{6,5},{4,7},{9,10},{11,8},{10,... | collective-permute-start | bytes 196616 | tf_op jit(solution)/shard_map/ppermute | solution.py:605
  4.2 1.6 %collective-permute-start.2 = (f32[8,128]{1,0:T(8,128)S(1)}, f32[8,128]{1,0:T(8,128)S(1)}, u32[]{:S(2)}, u32[]{:S(2)}) collective-permute-start(f32[8,128]{1,0:T(8,128)S(1)} %get-tuple-element.30.refs_0_), channel_id=1, source_target_pairs={{0,4},{4,0},{8,12},{12,8},{1,5},{5,1},{9,13},{13,9},{2,6},{6,2},{1... | collective-permute-start | bytes 12296 | tf_op jit(solution)/shard_map/ppermute | solution.py:552
  5.8 2.6 %collective-permute-start.3 = (f32[8,128]{1,0:T(8,128)S(1)}, f32[8,128]{1,0:T(8,128)S(1)}, u32[]{:S(2)}, u32[]{:S(2)}) collective-permute-start(f32[8,128]{1,0:T(8,128)S(1)} %get-tuple-element.30.refs_0_), channel_id=1, source_target_pairs={{0,8},{4,12},{8,0},{12,4},{1,9},{5,13},{9,1},{13,5},{2,10},{6,14},... | collective-permute-start | bytes 12296 | tf_op jit(solution)/shard_map/ppermute | solution.py:552
  8.6 0.6 %collective-permute-start.5 = (f32[256,256]{1,0:T(8,128)S(1)}, f32[256,256]{1,0:T(8,128)S(1)}, u32[]{:S(2)}, u32[]{:S(2)}) collective-permute-start(f32[256,256]{1,0:T(8,128)S(1)} %copy-done), channel_id=1, source_target_pairs={{0,2},{1,3},{2,0},{3,1},{4,6},{5,7},{6,4},{7,5},{8,10},{9,11},{10,... | collective-permute-start | bytes 786440 | tf_op jit(solution)/shard_map/ppermute | solution.py:552
  9.3 0.7 %ready_step.1 = (f32[64,128]{1,0:T(8,128)S(1)}, f32[64,128]{1,0:T(8,128)S(1)}, f32[64,128]{1,0:T(8,128)S(1)}, f32[33,32,128]{2,1,0:T(8,128)S(1)}, f32[33,32,128]...) custom-call(s32[1]{0:T(128)} %bitcast.tile, bf16[1664,512]{1,0:T(8,128)(2,1)S(1)} %copy-done.5, ...), custom_call_target="tpu_custom_call" | custom-call | flops 1073741824 | bytes 1048576 | tf_op jit(solution)/shard_map/ready_step/pallas_call | solution.py:624
  10.3 3.5 %collective-permute-done.4.refs_3_ = f32[8,128]{1,0:T(8,128)S(1)} collective-permute-done((f32[8,128]{1,0:T(8,128)S(1)}, f32[8,128]{1,0:T(8,128)S(1)}, u32[]{:S(2)}, u32[]{:S(2)}) %collective-permute-start.4) | collective-permute-done | bytes 4128 | tf_op jit(solution)/shard_map/ppermute | solution.py:552
  13.8 3.6 %first_step.1 = (f32[64,128]{1,0:T(8,128)S(1)}, f32[64,32,128]{2,1,0:T(8,128)S(1)}, f32[64,32,128]{2,1,0:T(8,128)S(1)}, f32[8,128]{1,0:T(8,128)S(1)}, s32[8,128]{1,0:T(8,128)S(1)}) custom-call(bf16[1664,512]{1,0:T(8,128)(2,1)S(1)} %copy-done.5, f32[64,128]{1,0:T(8,128)S(1)} %get-tuple-element.25.plain, f32[64,128]{1,0:T(8,128)S(1)} %get-tuple-element.26.crossed, ...), custom_call_target="tpu_custom_call" | custom-call | flops 4294967296 | bytes 1048576 | tf_op jit(solution)/shard_map/first_step/pallas_call | solution.py:636
  17.5 0.5 %collective-permute-start.7 = (f32[64,128]{1,0:T(8,128)S(1)}, f32[64,128]{1,0:T(8,128)S(1)}, u32[]{:S(2)}, u32[]{:S(2)}) collective-permute-start(f32[64,128]{1,0:T(8,128)S(1)} %get-tuple-element.39.refs_2_), channel_id=1, source_target_pairs={{0,1},{1,0},{2,3},{3,2},{4,5},{5,4},{6,7},{7,6},{8,9},{9,8},{10,11... | collective-permute-start | bytes 98312 | tf_op jit(solution)/shard_map/ppermute | solution.py:552
  18.0 0.6 %collective-permute-start.8 = (f32[64,128]{1,0:T(8,128)S(1)}, f32[64,128]{1,0:T(8,128)S(1)}, u32[]{:S(2)}, u32[]{:S(2)}) collective-permute-start(f32[64,128]{1,0:T(8,128)S(1)} %get-tuple-element.39.refs_2_), channel_id=1, source_target_pairs={{0,2},{1,3},{2,0},{3,1},{4,6},{5,7},{6,4},{7,5},{8,10},{9,11},{10,... | collective-permute-start | bytes 98312 | tf_op jit(solution)/shard_map/ppermute | solution.py:552
  18.7 0.8 %collective-permute-start.9 = (f32[64,128]{1,0:T(8,128)S(1)}, f32[64,128]{1,0:T(8,128)S(1)}, u32[]{:S(2)}, u32[]{:S(2)}) collective-permute-start(f32[64,128]{1,0:T(8,128)S(1)} %get-tuple-element.39.refs_2_), channel_id=1, source_target_pairs={{0,3},{1,2},{2,1},{3,0},{4,7},{5,6},{6,5},{7,4},{8,11},{9,10},{10,... | collective-permute-start | bytes 98312 | tf_op jit(solution)/shard_map/ppermute | solution.py:552
  19.5 2.8 %collective-permute-done.8.refs_4_ = f32[64,128]{1,0:T(8,128)S(1)} collective-permute-done((f32[64,128]{1,0:T(8,128)S(1)}, f32[64,128]{1,0:T(8,128)S(1)}, u32[]{:S(2)}, u32[]{:S(2)}) %collective-permute-start.8) | collective-permute-done | bytes 32800 | tf_op jit(solution)/shard_map/ppermute | solution.py:552
  22.4 5.1 %next_step.1 = (f32[384,256]{1,0:T(8,128)S(1)}, f32[4,256,256]{2,1,0:T(8,128)S(1)}, f32[8,128]{1,0:T(8,128)S(1)}, f32[64,128]{1,0:T(8,128)S(1)}) custom-call(s32[1]{0:T(128)} %bitcast.tile, bf16[1664,512]{1,0:T(8,128)(2,1)S(1)} %copy-done.5, s32[8,128]{1,0:T(8,128)S(1)} %get-tuple-element.31.shifts, f32[8,128]{1,0:T(8,128)S(1)} %get-tuple-element.32.info, ...), custom_call_target="tpu_custom_call" | custom-call | flops 4294967296 | bytes 1048576 | tf_op jit(solution)/shard_map/next_step/pallas_call | solution.py:660
  27.6 1.3 %collective-permute-start.11 = (f32[64,128]{1,0:T(8,128)S(1)}, f32[64,128]{1,0:T(8,128)S(1)}, u32[]{:S(2)}, u32[]{:S(2)}) collective-permute-start(f32[64,128]{1,0:T(8,128)S(1)} %get-tuple-element.43.refs_0_), channel_id=1, source_target_pairs={{0,2},{1,3},{2,0},{3,1},{4,6},{5,7},{6,4},{7,5},{8,10},{9,11},{10,... | collective-permute-start | bytes 98312 | tf_op jit(solution)/shard_map/ppermute | solution.py:552
  29.0 0.4 %collective-permute-start.12 = (f32[64,128]{1,0:T(8,128)S(1)}, f32[64,128]{1,0:T(8,128)S(1)}, u32[]{:S(2)}, u32[]{:S(2)}) collective-permute-start(f32[64,128]{1,0:T(8,128)S(1)} %get-tuple-element.43.refs_0_), channel_id=1, source_target_pairs={{0,3},{1,2},{2,1},{3,0},{4,7},{5,6},{6,5},{7,4},{8,11},{9,10},{10,... | collective-permute-start | bytes 98312 | tf_op jit(solution)/shard_map/ppermute | solution.py:552
  29.7 1.9 %collective-permute-done.11.refs_2_ = f32[64,128]{1,0:T(8,128)S(1)} collective-permute-done((f32[64,128]{1,0:T(8,128)S(1)}, f32[64,128]{1,0:T(8,128)S(1)}, u32[]{:S(2)}, u32[]{:S(2)}) %collective-permute-start.11) | collective-permute-done | bytes 32800 | tf_op jit(solution)/shard_map/ppermute | solution.py:552
  31.5 0.8 %collective-permute-done.12.refs_3_ = f32[64,128]{1,0:T(8,128)S(1)} collective-permute-done((f32[64,128]{1,0:T(8,128)S(1)}, f32[64,128]{1,0:T(8,128)S(1)}, u32[]{:S(2)}, u32[]{:S(2)}) %collective-permute-start.12) | collective-permute-done | bytes 32800 | tf_op jit(solution)/shard_map/ppermute | solution.py:552
  32.3 4.0 %last_step.1 = (f32[256,256]{1,0:T(8,128)}, f32[8,64]{1,0:T(8,128)S(1)}) custom-call(s32[1]{0:T(128)} %bitcast.tile, bf16[1664,512]{1,0:T(8,128)(2,1)S(1)} %copy-done.5, s32[8,128]{1,0:T(8,128)S(1)} %get-tuple-element.31.shifts, f32[8,128]{1,0:T(8,128)S(1)} %get-tuple-element.32.info, f32[64,32,128]{2,1,0:T(8,128)S(1)} %get-tuple-element.33.pr, ...), custom_call_target="tpu_custom_call" | custom-call | flops 4294967296 | bytes 1048576 | tf_op jit(solution)/shard_map/last_step/pallas_call | solution.py:682
  36.5 1.0 %collective-permute-start.14 = (f32[8,64]{1,0:T(8,128)S(1)}, f32[8,64]{1,0:T(8,128)S(1)}, u32[]{:S(2)}, u32[]{:S(2)}) collective-permute-start(f32[8,64]{1,0:T(8,128)S(1)} %get-tuple-element.45.refs_0_), channel_id=1, source_target_pairs={{0,2},{1,3},{2,0},{3,1},{4,6},{5,7},{6,4},{7,5},{8,10},{9,11},{10,... | collective-permute-start | bytes 6152 | tf_op jit(solution)/shard_map/ppermute | solution.py:552
  37.5 0.7 %collective-permute-start.15 = (f32[8,64]{1,0:T(8,128)S(1)}, f32[8,64]{1,0:T(8,128)S(1)}, u32[]{:S(2)}, u32[]{:S(2)}) collective-permute-start(f32[8,64]{1,0:T(8,128)S(1)} %get-tuple-element.45.refs_0_), channel_id=1, source_target_pairs={{0,3},{1,2},{2,1},{3,0},{4,7},{5,6},{6,5},{7,4},{8,11},{9,10},{10,... | collective-permute-start | bytes 6152 | tf_op jit(solution)/shard_map/ppermute | solution.py:552
  38.2 1.9 %collective-permute-done.14.refs_2_ = f32[8,64]{1,0:T(8,128)S(1)} collective-permute-done((f32[8,64]{1,0:T(8,128)S(1)}, f32[8,64]{1,0:T(8,128)S(1)}, u32[]{:S(2)}, u32[]{:S(2)}) %collective-permute-start.14) | collective-permute-done | bytes 2080 | tf_op jit(solution)/shard_map/ppermute | solution.py:552
  40.1 0.4 collective-permute-done.15.refs_3_
  40.5 0.8 %weight_step.1 = f32[1,16]{1,0:T(1,128)} custom-call(s32[1]{0:T(128)} %bitcast.tile, s32[1]{0:T(128)} %bitcast.1.place, f32[8,128]{1,0:T(8,128)S(1)} %get-tuple-element.32.info, f32[8,64]{1,0:T(8,128)S(1)} %get-tuple-element.45.refs_0_, f32[8,64]{1,0:T(8,128)S(1)} %collective-permute-done.13.refs_1_, f32[8,64]{1,0:T(8,128)S(1)} %collective-permute-done.14.refs_2_, ...), custom_call_target="tpu_custom_call" | custom-call | tf_op jit(solution)/shard_map/weight_step/pallas_call | solution.py:697
  (28 shorter events, 1.6 us)
Async XLA Ops:
  0.6 8.6 %copy-start.5 = (bf16[1664,512]{1,0:T(8,128)(2,1)S(1)}, bf16[1664,512]{1,0:T(8,128)(2,1)}, u32[]{:S(2)}) copy-start(bf16[1664,512]{1,0:T(8,128)(2,1)} %constant.9.clone.table) | copy-start | bytes 5111812
  0.6 1.1 %copy-start = (f32[256,256]{1,0:T(8,128)S(1)}, f32[256,256]{1,0:T(8,128)}, u32[]{:S(2)}) copy-start(f32[256,256]{1,0:T(8,128)} %refs_0_.1) | copy-start | bytes 786436
  0.7 1.1 %copy-start.2 = (f32[16]{0:T(128)S(1)}, f32[16]{0:T(128)}, u32[]{:S(2)}) copy-start(f32[16]{0:T(128)} %param.8) | copy-start | bytes 196
  0.7 1.1 %copy-start.1 = (s32[16,2]{0,1:T(2,128)S(1)}, s32[16,2]{0,1:T(2,128)}, u32[]{:S(2)}) copy-start(s32[16,2]{0,1:T(2,128)} %param.9) | copy-start | bytes 388
  0.7 8.6 %copy-start.4 = (f32[2,32,32]{2,1,0:T(8,128)S(1)}, f32[2,32,32]{2,1,0:T(8,128)}, u32[]{:S(2)}) copy-start(f32[2,32,32]{2,1,0:T(8,128)} %pupil.1) | copy-start | bytes 24580
  0.7 8.6 %copy-start.3 = (f32[256,256]{1,0:T(8,128)S(1)}, f32[256,256]{1,0:T(8,128)}, u32[]{:S(2)}) copy-start(f32[256,256]{1,0:T(8,128)} %goal.1) | copy-start | bytes 786436
  0.7 8.6 %collective-permute-start = (f32[256,256]{1,0:T(8,128)}, f32[256,256]{1,0:T(8,128)S(1)}, u32[]{:S(2)}, u32[]{:S(2)}) collective-permute-start(f32[256,256]{1,0:T(8,128)} %refs_0_.1), channel_id=1, source_target_pairs={{0,1},{1,0},{2,3},{3,2},{4,5},{5,4},{6,7},{7,6},{8,9},{9,8},{10,11... | collective-permute-start | bytes 786440 | tf_op jit(solution)/shard_map/ppermute | solution.py:552
  1.8 6.8 %collective-permute-start.1 = (f32[64,256]{1,0:T(8,128)S(1)}, f32[64,256]{1,0:T(8,128)S(1)}, u32[]{:S(2)}, u32[]{:S(2)}) collective-permute-start(f32[64,256]{1,0:T(8,128)S(1)} %get-tuple-element.24), channel_id=1, source_target_pairs={{1,2},{3,0},{2,1},{0,3},{5,6},{7,4},{6,5},{4,7},{9,10},{11,8},{10,... | collective-permute-start | bytes 196616 | tf_op jit(solution)/shard_map/ppermute | solution.py:605
  4.2 5.7 %collective-permute-start.2 = (f32[8,128]{1,0:T(8,128)S(1)}, f32[8,128]{1,0:T(8,128)S(1)}, u32[]{:S(2)}, u32[]{:S(2)}) collective-permute-start(f32[8,128]{1,0:T(8,128)S(1)} %get-tuple-element.30.refs_0_), channel_id=1, source_target_pairs={{0,4},{4,0},{8,12},{12,8},{1,5},{5,1},{9,13},{13,9},{2,6},{6,2},{1... | collective-permute-start | bytes 12296 | tf_op jit(solution)/shard_map/ppermute | solution.py:552
  5.8 4.5 %collective-permute-start.3 = (f32[8,128]{1,0:T(8,128)S(1)}, f32[8,128]{1,0:T(8,128)S(1)}, u32[]{:S(2)}, u32[]{:S(2)}) collective-permute-start(f32[8,128]{1,0:T(8,128)S(1)} %get-tuple-element.30.refs_0_), channel_id=1, source_target_pairs={{0,8},{4,12},{8,0},{12,4},{1,9},{5,13},{9,1},{13,5},{2,10},{6,14},... | collective-permute-start | bytes 12296 | tf_op jit(solution)/shard_map/ppermute | solution.py:552
  8.4 5.4 %collective-permute-start.4 = (f32[8,128]{1,0:T(8,128)S(1)}, f32[8,128]{1,0:T(8,128)S(1)}, u32[]{:S(2)}, u32[]{:S(2)}) collective-permute-start(f32[8,128]{1,0:T(8,128)S(1)} %get-tuple-element.30.refs_0_), channel_id=1, source_target_pairs={{0,12},{4,8},{8,4},{12,0},{1,13},{5,9},{9,5},{13,1},{2,14},{6,10},... | collective-permute-start | bytes 12296 | tf_op jit(solution)/shard_map/ppermute | solution.py:552
  8.6 8.8 %collective-permute-start.5 = (f32[256,256]{1,0:T(8,128)S(1)}, f32[256,256]{1,0:T(8,128)S(1)}, u32[]{:S(2)}, u32[]{:S(2)}) collective-permute-start(f32[256,256]{1,0:T(8,128)S(1)} %copy-done), channel_id=1, source_target_pairs={{0,2},{1,3},{2,0},{3,1},{4,6},{5,7},{6,4},{7,5},{8,10},{9,11},{10,... | collective-permute-start | bytes 786440 | tf_op jit(solution)/shard_map/ppermute | solution.py:552
  17.5 4.9 %collective-permute-start.6 = (f32[256,256]{1,0:T(8,128)S(1)}, f32[256,256]{1,0:T(8,128)S(1)}, u32[]{:S(2)}, u32[]{:S(2)}) collective-permute-start(f32[256,256]{1,0:T(8,128)S(1)} %collective-permute-done.5.refs_0_.refs_2_), channel_id=1, source_target_pairs={{0,1},{1,0},{2,3},{3,2},{4,5},{5,4},{6,7},{7,6},{8,9},{9,8},{10,11... | collective-permute-start | bytes 786440 | tf_op jit(solution)/shard_map/ppermute | solution.py:552
  17.5 1.9 %collective-permute-start.7 = (f32[64,128]{1,0:T(8,128)S(1)}, f32[64,128]{1,0:T(8,128)S(1)}, u32[]{:S(2)}, u32[]{:S(2)}) collective-permute-start(f32[64,128]{1,0:T(8,128)S(1)} %get-tuple-element.39.refs_2_), channel_id=1, source_target_pairs={{0,1},{1,0},{2,3},{3,2},{4,5},{5,4},{6,7},{7,6},{8,9},{9,8},{10,11... | collective-permute-start | bytes 98312 | tf_op jit(solution)/shard_map/ppermute | solution.py:552
  18.0 4.2 %collective-permute-start.8 = (f32[64,128]{1,0:T(8,128)S(1)}, f32[64,128]{1,0:T(8,128)S(1)}, u32[]{:S(2)}, u32[]{:S(2)}) collective-permute-start(f32[64,128]{1,0:T(8,128)S(1)} %get-tuple-element.39.refs_2_), channel_id=1, source_target_pairs={{0,2},{1,3},{2,0},{3,1},{4,6},{5,7},{6,4},{7,5},{8,10},{9,11},{10,... | collective-permute-start | bytes 98312 | tf_op jit(solution)/shard_map/ppermute | solution.py:552
  18.7 3.7 %collective-permute-start.9 = (f32[64,128]{1,0:T(8,128)S(1)}, f32[64,128]{1,0:T(8,128)S(1)}, u32[]{:S(2)}, u32[]{:S(2)}) collective-permute-start(f32[64,128]{1,0:T(8,128)S(1)} %get-tuple-element.39.refs_2_), channel_id=1, source_target_pairs={{0,3},{1,2},{2,1},{3,0},{4,7},{5,6},{6,5},{7,4},{8,11},{9,10},{10,... | collective-permute-start | bytes 98312 | tf_op jit(solution)/shard_map/ppermute | solution.py:552
  27.4 2.2 %collective-permute-start.10 = (f32[64,128]{1,0:T(8,128)S(1)}, f32[64,128]{1,0:T(8,128)S(1)}, u32[]{:S(2)}, u32[]{:S(2)}) collective-permute-start(f32[64,128]{1,0:T(8,128)S(1)} %get-tuple-element.43.refs_0_), channel_id=1, source_target_pairs={{0,1},{1,0},{2,3},{3,2},{4,5},{5,4},{6,7},{7,6},{8,9},{9,8},{10,11... | collective-permute-start | bytes 98312 | tf_op jit(solution)/shard_map/ppermute | solution.py:552
  27.6 3.9 %collective-permute-start.11 = (f32[64,128]{1,0:T(8,128)S(1)}, f32[64,128]{1,0:T(8,128)S(1)}, u32[]{:S(2)}, u32[]{:S(2)}) collective-permute-start(f32[64,128]{1,0:T(8,128)S(1)} %get-tuple-element.43.refs_0_), channel_id=1, source_target_pairs={{0,2},{1,3},{2,0},{3,1},{4,6},{5,7},{6,4},{7,5},{8,10},{9,11},{10,... | collective-permute-start | bytes 98312 | tf_op jit(solution)/shard_map/ppermute | solution.py:552
  29.0 3.4 %collective-permute-start.12 = (f32[64,128]{1,0:T(8,128)S(1)}, f32[64,128]{1,0:T(8,128)S(1)}, u32[]{:S(2)}, u32[]{:S(2)}) collective-permute-start(f32[64,128]{1,0:T(8,128)S(1)} %get-tuple-element.43.refs_0_), channel_id=1, source_target_pairs={{0,3},{1,2},{2,1},{3,0},{4,7},{5,6},{6,5},{7,4},{8,11},{9,10},{10,... | collective-permute-start | bytes 98312 | tf_op jit(solution)/shard_map/ppermute | solution.py:552
  36.3 1.9 %collective-permute-start.13 = (f32[8,64]{1,0:T(8,128)S(1)}, f32[8,64]{1,0:T(8,128)S(1)}, u32[]{:S(2)}, u32[]{:S(2)}) collective-permute-start(f32[8,64]{1,0:T(8,128)S(1)} %get-tuple-element.45.refs_0_), channel_id=1, source_target_pairs={{0,1},{1,0},{2,3},{3,2},{4,5},{5,4},{6,7},{7,6},{8,9},{9,8},{10,11... | collective-permute-start | bytes 6152 | tf_op jit(solution)/shard_map/ppermute | solution.py:552
  36.5 3.6 %collective-permute-start.14 = (f32[8,64]{1,0:T(8,128)S(1)}, f32[8,64]{1,0:T(8,128)S(1)}, u32[]{:S(2)}, u32[]{:S(2)}) collective-permute-start(f32[8,64]{1,0:T(8,128)S(1)} %get-tuple-element.45.refs_0_), channel_id=1, source_target_pairs={{0,2},{1,3},{2,0},{3,1},{4,6},{5,7},{6,4},{7,5},{8,10},{9,11},{10,... | collective-permute-start | bytes 6152 | tf_op jit(solution)/shard_map/ppermute | solution.py:552
  37.5 3.0 %collective-permute-start.15 = (f32[8,64]{1,0:T(8,128)S(1)}, f32[8,64]{1,0:T(8,128)S(1)}, u32[]{:S(2)}, u32[]{:S(2)}) collective-permute-start(f32[8,64]{1,0:T(8,128)S(1)} %get-tuple-element.45.refs_0_), channel_id=1, source_target_pairs={{0,3},{1,2},{2,1},{3,0},{4,7},{5,6},{6,5},{7,4},{8,11},{9,10},{10,... | collective-permute-start | bytes 6152 | tf_op jit(solution)/shard_map/ppermute | solution.py:552

commit v8 on v7

--- a/solution.py
+++ b/solution.py
@@ -553,7 +553,10 @@
 
 
 def all_of(value, axis):
-    return [value] + [crossed(value, axis, k) for k in range(1, lax.axis_size(axis))]
+    got = [value]
+    for k in range(1, lax.axis_size(axis)):
+        got.append(crossed(value, axis, k))
+    return got
 
 
 def per_device(mask_param, target_image, source_weights, source_shifts, pupil_map):

time: 41.4 us -> 41.4 us (level)
  no operation moved by 1% of the time
where the time goes in v8:
time: 41.4 us; the launch traced here: 41.3 us
  Pallas kernels  14.5 us (35%)
  starting transfers between devices  13.9 us (34%)
  waiting for transfers between devices  11.7 us (28%)
  between operations  0.77 us (2%)
  local copies, waits for them, and re-layouts  0.49 us (1%)
    ppermute x15, waiting for transfers between devices, crossed(): lax.ppermute(value, axis, [(i, i ^ k) for i in range(lax.axis_size(axis))])  11.7 us
    ppermute x15, starting transfers between devices, crossed(): lax.ppermute(value, axis, [(i, i ^ k) for i in range(lax.axis_size(axis))])  11.4 us
    pallas_call x1, Pallas kernels, per_device(): pl.pallas_call(functools.partial(next_kernel, spots, tiles, scale), out_s...  5.06 us
    pallas_call x1, Pallas kernels, per_device(): pl.pallas_call(functools.partial(last_kernel, spots, tiles), out_shape=[s...  3.95 us
    pallas_call x1, Pallas kernels, per_device(): pl.pallas_call(functools.partial(first_kernel, spots, peers, scale), out_...  3.63 us
    ppermute x1, starting transfers between devices, per_device(): cross = lax.ppermute(edge, 'tile', pairs + [(j, i) for i, j in pairs])  2.44 us
  transfers between devices with their start and end apart: 16, of which 8 were waited for; matrix products, arithmetic and copies ran while one was open for 0% of the time, Pallas kernels for 11%

profile of v8, /device:TPU:0, one launch (start us, length us, event | category | flops | bytes accessed | tf_op | source)
XLA Modules:
  0.0 41.3 jit_solution(9193992268838870235)
XLA Ops:
  0.7 0.6 %collective-permute-start = (f32[256,256]{1,0:T(8,128)}, f32[256,256]{1,0:T(8,128)S(1)}, u32[]{:S(2)}, u32[]{:S(2)}) collective-permute-start(f32[256,256]{1,0:T(8,128)} %refs_0_.1), channel_id=1, source_target_pairs={{0,1},{1,0},{2,3},{3,2},{4,5},{5,4},{6,7},{7,6},{8,9},{9,8},{10,11... | collective-permute-start | bytes 786440 | tf_op jit(solution)/shard_map/ppermute | solution.py:552
  1.3 0.5 %copy-done = f32[256,256]{1,0:T(8,128)S(1)} copy-done((f32[256,256]{1,0:T(8,128)S(1)}, f32[256,256]{1,0:T(8,128)}, u32[]{:S(2)}) %copy-start) | copy-done | bytes 262168
  1.8 2.4 %collective-permute-start.1 = (f32[64,256]{1,0:T(8,128)S(1)}, f32[64,256]{1,0:T(8,128)S(1)}, u32[]{:S(2)}, u32[]{:S(2)}) collective-permute-start(f32[64,256]{1,0:T(8,128)S(1)} %get-tuple-element.24), channel_id=1, source_target_pairs={{1,2},{3,0},{2,1},{0,3},{5,6},{7,4},{6,5},{4,7},{9,10},{11,8},{10,... | collective-permute-start | bytes 196616 | tf_op jit(solution)/shard_map/ppermute | solution.py:608
  4.2 1.6 %collective-permute-start.2 = (f32[8,128]{1,0:T(8,128)S(1)}, f32[8,128]{1,0:T(8,128)S(1)}, u32[]{:S(2)}, u32[]{:S(2)}) collective-permute-start(f32[8,128]{1,0:T(8,128)S(1)} %get-tuple-element.30.refs_0_), channel_id=1, source_target_pairs={{0,4},{4,0},{8,12},{12,8},{1,5},{5,1},{9,13},{13,9},{2,6},{6,2},{1... | collective-permute-start | bytes 12296 | tf_op jit(solution)/shard_map/ppermute | solution.py:552
  5.8 2.6 %collective-permute-start.3 = (f32[8,128]{1,0:T(8,128)S(1)}, f32[8,128]{1,0:T(8,128)S(1)}, u32[]{:S(2)}, u32[]{:S(2)}) collective-permute-start(f32[8,128]{1,0:T(8,128)S(1)} %get-tuple-element.30.refs_0_), channel_id=1, source_target_pairs={{0,8},{4,12},{8,0},{12,4},{1,9},{5,13},{9,1},{13,5},{2,10},{6,14},... | collective-permute-start | bytes 12296 | tf_op jit(solution)/shard_map/ppermute | solution.py:552
  8.6 0.6 %collective-permute-start.5 = (f32[256,256]{1,0:T(8,128)S(1)}, f32[256,256]{1,0:T(8,128)S(1)}, u32[]{:S(2)}, u32[]{:S(2)}) collective-permute-start(f32[256,256]{1,0:T(8,128)S(1)} %copy-done), channel_id=1, source_target_pairs={{0,2},{1,3},{2,0},{3,1},{4,6},{5,7},{6,4},{7,5},{8,10},{9,11},{10,... | collective-permute-start | bytes 786440 | tf_op jit(solution)/shard_map/ppermute | solution.py:552
  9.3 0.7 %ready_step.1 = (f32[64,128]{1,0:T(8,128)S(1)}, f32[64,128]{1,0:T(8,128)S(1)}, f32[64,128]{1,0:T(8,128)S(1)}, f32[33,32,128]{2,1,0:T(8,128)S(1)}, f32[33,32,128]...) custom-call(s32[1]{0:T(128)} %bitcast.tile, bf16[1664,512]{1,0:T(8,128)(2,1)S(1)} %copy-done.5, ...), custom_call_target="tpu_custom_call" | custom-call | flops 1073741824 | bytes 1048576 | tf_op jit(solution)/shard_map/ready_step/pallas_call | solution.py:627
  10.3 3.5 %collective-permute-done.4.refs_3_ = f32[8,128]{1,0:T(8,128)S(1)} collective-permute-done((f32[8,128]{1,0:T(8,128)S(1)}, f32[8,128]{1,0:T(8,128)S(1)}, u32[]{:S(2)}, u32[]{:S(2)}) %collective-permute-start.4) | collective-permute-done | bytes 4128 | tf_op jit(solution)/shard_map/ppermute | solution.py:552
  13.8 3.6 %first_step.1 = (f32[64,128]{1,0:T(8,128)S(1)}, f32[64,32,128]{2,1,0:T(8,128)S(1)}, f32[64,32,128]{2,1,0:T(8,128)S(1)}, f32[8,128]{1,0:T(8,128)S(1)}, s32[8,128]{1,0:T(8,128)S(1)}) custom-call(bf16[1664,512]{1,0:T(8,128)(2,1)S(1)} %copy-done.5, f32[64,128]{1,0:T(8,128)S(1)} %get-tuple-element.25.plain, f32[64,128]{1,0:T(8,128)S(1)} %get-tuple-element.26.crossed, ...), custom_call_target="tpu_custom_call" | custom-call | flops 4294967296 | bytes 1048576 | tf_op jit(solution)/shard_map/first_step/pallas_call | solution.py:639
  17.5 0.5 %collective-permute-start.7 = (f32[64,128]{1,0:T(8,128)S(1)}, f32[64,128]{1,0:T(8,128)S(1)}, u32[]{:S(2)}, u32[]{:S(2)}) collective-permute-start(f32[64,128]{1,0:T(8,128)S(1)} %get-tuple-element.39.refs_2_), channel_id=1, source_target_pairs={{0,1},{1,0},{2,3},{3,2},{4,5},{5,4},{6,7},{7,6},{8,9},{9,8},{10,11... | collective-permute-start | bytes 98312 | tf_op jit(solution)/shard_map/ppermute | solution.py:552
  18.0 0.6 %collective-permute-start.8 = (f32[64,128]{1,0:T(8,128)S(1)}, f32[64,128]{1,0:T(8,128)S(1)}, u32[]{:S(2)}, u32[]{:S(2)}) collective-permute-start(f32[64,128]{1,0:T(8,128)S(1)} %get-tuple-element.39.refs_2_), channel_id=1, source_target_pairs={{0,2},{1,3},{2,0},{3,1},{4,6},{5,7},{6,4},{7,5},{8,10},{9,11},{10,... | collective-permute-start | bytes 98312 | tf_op jit(solution)/shard_map/ppermute | solution.py:552
  18.7 0.8 %collective-permute-start.9 = (f32[64,128]{1,0:T(8,128)S(1)}, f32[64,128]{1,0:T(8,128)S(1)}, u32[]{:S(2)}, u32[]{:S(2)}) collective-permute-start(f32[64,128]{1,0:T(8,128)S(1)} %get-tuple-element.39.refs_2_), channel_id=1, source_target_pairs={{0,3},{1,2},{2,1},{3,0},{4,7},{5,6},{6,5},{7,4},{8,11},{9,10},{10,... | collective-permute-start | bytes 98312 | tf_op jit(solution)/shard_map/ppermute | solution.py:552
  19.5 2.8 %collective-permute-done.8.refs_4_ = f32[64,128]{1,0:T(8,128)S(1)} collective-permute-done((f32[64,128]{1,0:T(8,128)S(1)}, f32[64,128]{1,0:T(8,128)S(1)}, u32[]{:S(2)}, u32[]{:S(2)}) %collective-permute-start.8) | collective-permute-done | bytes 32800 | tf_op jit(solution)/shard_map/ppermute | solution.py:552
  22.4 5.1 %next_step.1 = (f32[384,256]{1,0:T(8,128)S(1)}, f32[4,256,256]{2,1,0:T(8,128)S(1)}, f32[8,128]{1,0:T(8,128)S(1)}, f32[64,128]{1,0:T(8,128)S(1)}) custom-call(s32[1]{0:T(128)} %bitcast.tile, bf16[1664,512]{1,0:T(8,128)(2,1)S(1)} %copy-done.5, s32[8,128]{1,0:T(8,128)S(1)} %get-tuple-element.31.shifts, f32[8,128]{1,0:T(8,128)S(1)} %get-tuple-element.32.info, ...), custom_call_target="tpu_custom_call" | custom-call | flops 4294967296 | bytes 1048576 | tf_op jit(solution)/shard_map/next_step/pallas_call | solution.py:663
  27.6 1.3 %collective-permute-start.11 = (f32[64,128]{1,0:T(8,128)S(1)}, f32[64,128]{1,0:T(8,128)S(1)}, u32[]{:S(2)}, u32[]{:S(2)}) collective-permute-start(f32[64,128]{1,0:T(8,128)S(1)} %get-tuple-element.43.refs_0_), channel_id=1, source_target_pairs={{0,2},{1,3},{2,0},{3,1},{4,6},{5,7},{6,4},{7,5},{8,10},{9,11},{10,... | collective-permute-start | bytes 98312 | tf_op jit(solution)/shard_map/ppermute | solution.py:552
  29.0 0.4 %collective-permute-start.12 = (f32[64,128]{1,0:T(8,128)S(1)}, f32[64,128]{1,0:T(8,128)S(1)}, u32[]{:S(2)}, u32[]{:S(2)}) collective-permute-start(f32[64,128]{1,0:T(8,128)S(1)} %get-tuple-element.43.refs_0_), channel_id=1, source_target_pairs={{0,3},{1,2},{2,1},{3,0},{4,7},{5,6},{6,5},{7,4},{8,11},{9,10},{10,... | collective-permute-start | bytes 98312 | tf_op jit(solution)/shard_map/ppermute | solution.py:552
  29.7 1.9 %collective-permute-done.11.refs_2_ = f32[64,128]{1,0:T(8,128)S(1)} collective-permute-done((f32[64,128]{1,0:T(8,128)S(1)}, f32[64,128]{1,0:T(8,128)S(1)}, u32[]{:S(2)}, u32[]{:S(2)}) %collective-permute-start.11) | collective-permute-done | bytes 32800 | tf_op jit(solution)/shard_map/ppermute | solution.py:552
  31.5 0.8 %collective-permute-done.12.refs_3_ = f32[64,128]{1,0:T(8,128)S(1)} collective-permute-done((f32[64,128]{1,0:T(8,128)S(1)}, f32[64,128]{1,0:T(8,128)S(1)}, u32[]{:S(2)}, u32[]{:S(2)}) %collective-permute-start.12) | collective-permute-done | bytes 32800 | tf_op jit(solution)/shard_map/ppermute | solution.py:552
  32.3 4.0 %last_step.1 = (f32[256,256]{1,0:T(8,128)}, f32[8,64]{1,0:T(8,128)S(1)}) custom-call(s32[1]{0:T(128)} %bitcast.tile, bf16[1664,512]{1,0:T(8,128)(2,1)S(1)} %copy-done.5, s32[8,128]{1,0:T(8,128)S(1)} %get-tuple-element.31.shifts, f32[8,128]{1,0:T(8,128)S(1)} %get-tuple-element.32.info, f32[64,32,128]{2,1,0:T(8,128)S(1)} %get-tuple-element.33.pr, ...), custom_call_target="tpu_custom_call" | custom-call | flops 4294967296 | bytes 1048576 | tf_op jit(solution)/shard_map/last_step/pallas_call | solution.py:685
  36.5 1.0 %collective-permute-start.14 = (f32[8,64]{1,0:T(8,128)S(1)}, f32[8,64]{1,0:T(8,128)S(1)}, u32[]{:S(2)}, u32[]{:S(2)}) collective-permute-start(f32[8,64]{1,0:T(8,128)S(1)} %get-tuple-element.45.refs_0_), channel_id=1, source_target_pairs={{0,2},{1,3},{2,0},{3,1},{4,6},{5,7},{6,4},{7,5},{8,10},{9,11},{10,... | collective-permute-start | bytes 6152 | tf_op jit(solution)/shard_map/ppermute | solution.py:552
  37.5 0.7 %collective-permute-start.15 = (f32[8,64]{1,0:T(8,128)S(1)}, f32[8,64]{1,0:T(8,128)S(1)}, u32[]{:S(2)}, u32[]{:S(2)}) collective-permute-start(f32[8,64]{1,0:T(8,128)S(1)} %get-tuple-element.45.refs_0_), channel_id=1, source_target_pairs={{0,3},{1,2},{2,1},{3,0},{4,7},{5,6},{6,5},{7,4},{8,11},{9,10},{10,... | collective-permute-start | bytes 6152 | tf_op jit(solution)/shard_map/ppermute | solution.py:552
  38.2 1.9 %collective-permute-done.14.refs_2_ = f32[8,64]{1,0:T(8,128)S(1)} collective-permute-done((f32[8,64]{1,0:T(8,128)S(1)}, f32[8,64]{1,0:T(8,128)S(1)}, u32[]{:S(2)}, u32[]{:S(2)}) %collective-permute-start.14) | collective-permute-done | bytes 2080 | tf_op jit(solution)/shard_map/ppermute | solution.py:552
  40.1 0.4 collective-permute-done.15.refs_3_
  40.5 0.8 %weight_step.1 = f32[1,16]{1,0:T(1,128)} custom-call(s32[1]{0:T(128)} %bitcast.tile, s32[1]{0:T(128)} %bitcast.1.place, f32[8,128]{1,0:T(8,128)S(1)} %get-tuple-element.32.info, f32[8,64]{1,0:T(8,128)S(1)} %get-tuple-element.45.refs_0_, f32[8,64]{1,0:T(8,128)S(1)} %collective-permute-done.13.refs_1_, f32[8,64]{1,0:T(8,128)S(1)} %collective-permute-done.14.refs_2_, ...), custom_call_target="tpu_custom_call" | custom-call | tf_op jit(solution)/shard_map/weight_step/pallas_call | solution.py:700
  (28 shorter events, 1.6 us)
Async XLA Ops:
  0.6 8.6 %copy-start.5 = (bf16[1664,512]{1,0:T(8,128)(2,1)S(1)}, bf16[1664,512]{1,0:T(8,128)(2,1)}, u32[]{:S(2)}) copy-start(bf16[1664,512]{1,0:T(8,128)(2,1)} %constant.9.clone.table) | copy-start | bytes 5111812
  0.6 1.1 %copy-start = (f32[256,256]{1,0:T(8,128)S(1)}, f32[256,256]{1,0:T(8,128)}, u32[]{:S(2)}) copy-start(f32[256,256]{1,0:T(8,128)} %refs_0_.1) | copy-start | bytes 786436
  0.7 1.1 %copy-start.2 = (f32[16]{0:T(128)S(1)}, f32[16]{0:T(128)}, u32[]{:S(2)}) copy-start(f32[16]{0:T(128)} %param.8) | copy-start | bytes 196
  0.7 1.1 %copy-start.1 = (s32[16,2]{0,1:T(2,128)S(1)}, s32[16,2]{0,1:T(2,128)}, u32[]{:S(2)}) copy-start(s32[16,2]{0,1:T(2,128)} %param.9) | copy-start | bytes 388
  0.7 8.6 %copy-start.4 = (f32[2,32,32]{2,1,0:T(8,128)S(1)}, f32[2,32,32]{2,1,0:T(8,128)}, u32[]{:S(2)}) copy-start(f32[2,32,32]{2,1,0:T(8,128)} %pupil.1) | copy-start | bytes 24580
  0.7 8.6 %copy-start.3 = (f32[256,256]{1,0:T(8,128)S(1)}, f32[256,256]{1,0:T(8,128)}, u32[]{:S(2)}) copy-start(f32[256,256]{1,0:T(8,128)} %goal.1) | copy-start | bytes 786436
  0.7 8.6 %collective-permute-start = (f32[256,256]{1,0:T(8,128)}, f32[256,256]{1,0:T(8,128)S(1)}, u32[]{:S(2)}, u32[]{:S(2)}) collective-permute-start(f32[256,256]{1,0:T(8,128)} %refs_0_.1), channel_id=1, source_target_pairs={{0,1},{1,0},{2,3},{3,2},{4,5},{5,4},{6,7},{7,6},{8,9},{9,8},{10,11... | collective-permute-start | bytes 786440 | tf_op jit(solution)/shard_map/ppermute | solution.py:552
  1.8 6.8 %collective-permute-start.1 = (f32[64,256]{1,0:T(8,128)S(1)}, f32[64,256]{1,0:T(8,128)S(1)}, u32[]{:S(2)}, u32[]{:S(2)}) collective-permute-start(f32[64,256]{1,0:T(8,128)S(1)} %get-tuple-element.24), channel_id=1, source_target_pairs={{1,2},{3,0},{2,1},{0,3},{5,6},{7,4},{6,5},{4,7},{9,10},{11,8},{10,... | collective-permute-start | bytes 196616 | tf_op jit(solution)/shard_map/ppermute | solution.py:608
  4.2 5.7 %collective-permute-start.2 = (f32[8,128]{1,0:T(8,128)S(1)}, f32[8,128]{1,0:T(8,128)S(1)}, u32[]{:S(2)}, u32[]{:S(2)}) collective-permute-start(f32[8,128]{1,0:T(8,128)S(1)} %get-tuple-element.30.refs_0_), channel_id=1, source_target_pairs={{0,4},{4,0},{8,12},{12,8},{1,5},{5,1},{9,13},{13,9},{2,6},{6,2},{1... | collective-permute-start | bytes 12296 | tf_op jit(solution)/shard_map/ppermute | solution.py:552
  5.8 4.5 %collective-permute-start.3 = (f32[8,128]{1,0:T(8,128)S(1)}, f32[8,128]{1,0:T(8,128)S(1)}, u32[]{:S(2)}, u32[]{:S(2)}) collective-permute-start(f32[8,128]{1,0:T(8,128)S(1)} %get-tuple-element.30.refs_0_), channel_id=1, source_target_pairs={{0,8},{4,12},{8,0},{12,4},{1,9},{5,13},{9,1},{13,5},{2,10},{6,14},... | collective-permute-start | bytes 12296 | tf_op jit(solution)/shard_map/ppermute | solution.py:552
  8.4 5.4 %collective-permute-start.4 = (f32[8,128]{1,0:T(8,128)S(1)}, f32[8,128]{1,0:T(8,128)S(1)}, u32[]{:S(2)}, u32[]{:S(2)}) collective-permute-start(f32[8,128]{1,0:T(8,128)S(1)} %get-tuple-element.30.refs_0_), channel_id=1, source_target_pairs={{0,12},{4,8},{8,4},{12,0},{1,13},{5,9},{9,5},{13,1},{2,14},{6,10},... | collective-permute-start | bytes 12296 | tf_op jit(solution)/shard_map/ppermute | solution.py:552
  8.6 8.8 %collective-permute-start.5 = (f32[256,256]{1,0:T(8,128)S(1)}, f32[256,256]{1,0:T(8,128)S(1)}, u32[]{:S(2)}, u32[]{:S(2)}) collective-permute-start(f32[256,256]{1,0:T(8,128)S(1)} %copy-done), channel_id=1, source_target_pairs={{0,2},{1,3},{2,0},{3,1},{4,6},{5,7},{6,4},{7,5},{8,10},{9,11},{10,... | collective-permute-start | bytes 786440 | tf_op jit(solution)/shard_map/ppermute | solution.py:552
  17.5 4.9 %collective-permute-start.6 = (f32[256,256]{1,0:T(8,128)S(1)}, f32[256,256]{1,0:T(8,128)S(1)}, u32[]{:S(2)}, u32[]{:S(2)}) collective-permute-start(f32[256,256]{1,0:T(8,128)S(1)} %collective-permute-done.5.refs_0_.refs_2_), channel_id=1, source_target_pairs={{0,1},{1,0},{2,3},{3,2},{4,5},{5,4},{6,7},{7,6},{8,9},{9,8},{10,11... | collective-permute-start | bytes 786440 | tf_op jit(solution)/shard_map/ppermute | solution.py:552
  17.5 1.9 %collective-permute-start.7 = (f32[64,128]{1,0:T(8,128)S(1)}, f32[64,128]{1,0:T(8,128)S(1)}, u32[]{:S(2)}, u32[]{:S(2)}) collective-permute-start(f32[64,128]{1,0:T(8,128)S(1)} %get-tuple-element.39.refs_2_), channel_id=1, source_target_pairs={{0,1},{1,0},{2,3},{3,2},{4,5},{5,4},{6,7},{7,6},{8,9},{9,8},{10,11... | collective-permute-start | bytes 98312 | tf_op jit(solution)/shard_map/ppermute | solution.py:552
  18.0 4.2 %collective-permute-start.8 = (f32[64,128]{1,0:T(8,128)S(1)}, f32[64,128]{1,0:T(8,128)S(1)}, u32[]{:S(2)}, u32[]{:S(2)}) collective-permute-start(f32[64,128]{1,0:T(8,128)S(1)} %get-tuple-element.39.refs_2_), channel_id=1, source_target_pairs={{0,2},{1,3},{2,0},{3,1},{4,6},{5,7},{6,4},{7,5},{8,10},{9,11},{10,... | collective-permute-start | bytes 98312 | tf_op jit(solution)/shard_map/ppermute | solution.py:552
  18.7 3.7 %collective-permute-start.9 = (f32[64,128]{1,0:T(8,128)S(1)}, f32[64,128]{1,0:T(8,128)S(1)}, u32[]{:S(2)}, u32[]{:S(2)}) collective-permute-start(f32[64,128]{1,0:T(8,128)S(1)} %get-tuple-element.39.refs_2_), channel_id=1, source_target_pairs={{0,3},{1,2},{2,1},{3,0},{4,7},{5,6},{6,5},{7,4},{8,11},{9,10},{10,... | collective-permute-start | bytes 98312 | tf_op jit(solution)/shard_map/ppermute | solution.py:552
  27.4 2.2 %collective-permute-start.10 = (f32[64,128]{1,0:T(8,128)S(1)}, f32[64,128]{1,0:T(8,128)S(1)}, u32[]{:S(2)}, u32[]{:S(2)}) collective-permute-start(f32[64,128]{1,0:T(8,128)S(1)} %get-tuple-element.43.refs_0_), channel_id=1, source_target_pairs={{0,1},{1,0},{2,3},{3,2},{4,5},{5,4},{6,7},{7,6},{8,9},{9,8},{10,11... | collective-permute-start | bytes 98312 | tf_op jit(solution)/shard_map/ppermute | solution.py:552
  27.6 3.9 %collective-permute-start.11 = (f32[64,128]{1,0:T(8,128)S(1)}, f32[64,128]{1,0:T(8,128)S(1)}, u32[]{:S(2)}, u32[]{:S(2)}) collective-permute-start(f32[64,128]{1,0:T(8,128)S(1)} %get-tuple-element.43.refs_0_), channel_id=1, source_target_pairs={{0,2},{1,3},{2,0},{3,1},{4,6},{5,7},{6,4},{7,5},{8,10},{9,11},{10,... | collective-permute-start | bytes 98312 | tf_op jit(solution)/shard_map/ppermute | solution.py:552
  29.0 3.4 %collective-permute-start.12 = (f32[64,128]{1,0:T(8,128)S(1)}, f32[64,128]{1,0:T(8,128)S(1)}, u32[]{:S(2)}, u32[]{:S(2)}) collective-permute-start(f32[64,128]{1,0:T(8,128)S(1)} %get-tuple-element.43.refs_0_), channel_id=1, source_target_pairs={{0,3},{1,2},{2,1},{3,0},{4,7},{5,6},{6,5},{7,4},{8,11},{9,10},{10,... | collective-permute-start | bytes 98312 | tf_op jit(solution)/shard_map/ppermute | solution.py:552
  36.3 1.9 %collective-permute-start.13 = (f32[8,64]{1,0:T(8,128)S(1)}, f32[8,64]{1,0:T(8,128)S(1)}, u32[]{:S(2)}, u32[]{:S(2)}) collective-permute-start(f32[8,64]{1,0:T(8,128)S(1)} %get-tuple-element.45.refs_0_), channel_id=1, source_target_pairs={{0,1},{1,0},{2,3},{3,2},{4,5},{5,4},{6,7},{7,6},{8,9},{9,8},{10,11... | collective-permute-start | bytes 6152 | tf_op jit(solution)/shard_map/ppermute | solution.py:552
  36.5 3.6 %collective-permute-start.14 = (f32[8,64]{1,0:T(8,128)S(1)}, f32[8,64]{1,0:T(8,128)S(1)}, u32[]{:S(2)}, u32[]{:S(2)}) collective-permute-start(f32[8,64]{1,0:T(8,128)S(1)} %get-tuple-element.45.refs_0_), channel_id=1, source_target_pairs={{0,2},{1,3},{2,0},{3,1},{4,6},{5,7},{6,4},{7,5},{8,10},{9,11},{10,... | collective-permute-start | bytes 6152 | tf_op jit(solution)/shard_map/ppermute | solution.py:552
  37.5 3.0 %collective-permute-start.15 = (f32[8,64]{1,0:T(8,128)S(1)}, f32[8,64]{1,0:T(8,128)S(1)}, u32[]{:S(2)}, u32[]{:S(2)}) collective-permute-start(f32[8,64]{1,0:T(8,128)S(1)} %get-tuple-element.45.refs_0_), channel_id=1, source_target_pairs={{0,3},{1,2},{2,1},{3,0},{4,7},{5,6},{6,5},{7,4},{8,11},{9,10},{10,... | collective-permute-start | bytes 6152 | tf_op jit(solution)/shard_map/ppermute | solution.py:552

commit v9 on v8

--- a/solution.py
+++ b/solution.py
@@ -363,6 +363,10 @@
 
 def head_kernel(out):
     out[...] = jnp.zeros_like(out)
+
+
+def mark_kernel(value, out):
+    out[...] = value[...]
 
 
 def pack_kernel(tile, place, head, weights, shifts, mask, packed, edge):
@@ -655,8 +659,17 @@
     shared = (tile, table, whole, info, pr, pi, target)
     shared_specs = [smem, vmem, smem] + [vmem] * 4
 
-    back, far = lax.optimization_barrier((back, far))
     backs = all_of(back, "tile")
+    backs[0] = pl.pallas_call(
+        mark_kernel,
+        out_shape=struct(grid, lanes),
+        in_specs=[vmem],
+        out_specs=vmem,
+        compiler_params=params_of,
+        cost_estimate=cost(1 << 20),
+        name="mark_step",
+    )(back)
+    far, backs[0] = lax.optimization_barrier((far, backs[0]))
     entries = [mask_param, mate]
     for one in far:
         entries += [one, crossed(one, "tile", 1)]

time: 41.4 us -> 41.4 us (level)
  no operation moved by 1% of the time
where the time goes in v9:
time: 41.4 us; the launch traced here: 41.3 us
  Pallas kernels  14.4 us (35%)
  starting transfers between devices  13.9 us (34%)
  waiting for transfers between devices  11.7 us (28%)
  between operations  0.78 us (2%)
  local copies, waits for them, and re-layouts  0.49 us (1%)
    ppermute x15, waiting for transfers between devices, crossed(): lax.ppermute(value, axis, [(i, i ^ k) for i in range(lax.axis_size(axis))])  11.7 us
    ppermute x15, starting transfers between devices, crossed(): lax.ppermute(value, axis, [(i, i ^ k) for i in range(lax.axis_size(axis))])  11.4 us
    pallas_call x1, Pallas kernels, per_device(): pl.pallas_call(functools.partial(next_kernel, spots, tiles, scale), out_s...  5.05 us
    pallas_call x1, Pallas kernels, per_device(): pl.pallas_call(functools.partial(last_kernel, spots, tiles), out_shape=[s...  3.95 us
    pallas_call x1, Pallas kernels, per_device(): pl.pallas_call(functools.partial(first_kernel, spots, peers, scale), out_...  3.63 us
    ppermute x1, starting transfers between devices, per_device(): cross = lax.ppermute(edge, 'tile', pairs + [(j, i) for i, j in pairs])  2.44 us
  transfers between devices with their start and end apart: 16, of which 8 were waited for; matrix products, arithmetic and copies ran while one was open for 0% of the time, Pallas kernels for 11%

profile of v9, /device:TPU:0, one launch (start us, length us, event | category | flops | bytes accessed | tf_op | source)
XLA Modules:
  0.0 41.3 jit_solution(9683025568427061063)
XLA Ops:
  0.7 0.6 %collective-permute-start = (f32[256,256]{1,0:T(8,128)}, f32[256,256]{1,0:T(8,128)S(1)}, u32[]{:S(2)}, u32[]{:S(2)}) collective-permute-start(f32[256,256]{1,0:T(8,128)} %refs_0_.1), channel_id=1, source_target_pairs={{0,1},{1,0},{2,3},{3,2},{4,5},{5,4},{6,7},{7,6},{8,9},{9,8},{10,11... | collective-permute-start | bytes 786440 | tf_op jit(solution)/shard_map/ppermute | solution.py:556
  1.3 0.5 %copy-done = f32[256,256]{1,0:T(8,128)S(1)} copy-done((f32[256,256]{1,0:T(8,128)S(1)}, f32[256,256]{1,0:T(8,128)}, u32[]{:S(2)}) %copy-start) | copy-done | bytes 262168
  1.8 2.4 %collective-permute-start.1 = (f32[64,256]{1,0:T(8,128)S(1)}, f32[64,256]{1,0:T(8,128)S(1)}, u32[]{:S(2)}, u32[]{:S(2)}) collective-permute-start(f32[64,256]{1,0:T(8,128)S(1)} %get-tuple-element.24), channel_id=1, source_target_pairs={{1,2},{3,0},{2,1},{0,3},{5,6},{7,4},{6,5},{4,7},{9,10},{11,8},{10,... | collective-permute-start | bytes 196616 | tf_op jit(solution)/shard_map/ppermute | solution.py:612
  4.2 1.6 %collective-permute-start.2 = (f32[8,128]{1,0:T(8,128)S(1)}, f32[8,128]{1,0:T(8,128)S(1)}, u32[]{:S(2)}, u32[]{:S(2)}) collective-permute-start(f32[8,128]{1,0:T(8,128)S(1)} %get-tuple-element.30.refs_0_), channel_id=1, source_target_pairs={{0,4},{4,0},{8,12},{12,8},{1,5},{5,1},{9,13},{13,9},{2,6},{6,2},{1... | collective-permute-start | bytes 12296 | tf_op jit(solution)/shard_map/ppermute | solution.py:556
  5.8 2.6 %collective-permute-start.3 = (f32[8,128]{1,0:T(8,128)S(1)}, f32[8,128]{1,0:T(8,128)S(1)}, u32[]{:S(2)}, u32[]{:S(2)}) collective-permute-start(f32[8,128]{1,0:T(8,128)S(1)} %get-tuple-element.30.refs_0_), channel_id=1, source_target_pairs={{0,8},{4,12},{8,0},{12,4},{1,9},{5,13},{9,1},{13,5},{2,10},{6,14},... | collective-permute-start | bytes 12296 | tf_op jit(solution)/shard_map/ppermute | solution.py:556
  8.6 0.6 %collective-permute-start.5 = (f32[256,256]{1,0:T(8,128)S(1)}, f32[256,256]{1,0:T(8,128)S(1)}, u32[]{:S(2)}, u32[]{:S(2)}) collective-permute-start(f32[256,256]{1,0:T(8,128)S(1)} %copy-done), channel_id=1, source_target_pairs={{0,2},{1,3},{2,0},{3,1},{4,6},{5,7},{6,4},{7,5},{8,10},{9,11},{10,... | collective-permute-start | bytes 786440 | tf_op jit(solution)/shard_map/ppermute | solution.py:556
  9.3 0.7 %ready_step.1 = (f32[64,128]{1,0:T(8,128)S(1)}, f32[64,128]{1,0:T(8,128)S(1)}, f32[64,128]{1,0:T(8,128)S(1)}, f32[33,32,128]{2,1,0:T(8,128)S(1)}, f32[33,32,128]...) custom-call(s32[1]{0:T(128)} %bitcast.tile, bf16[1664,512]{1,0:T(8,128)(2,1)S(1)} %copy-done.5, ...), custom_call_target="tpu_custom_call" | custom-call | flops 1073741824 | bytes 1048576 | tf_op jit(solution)/shard_map/ready_step/pallas_call | solution.py:631
  10.3 3.5 %collective-permute-done.4.refs_3_ = f32[8,128]{1,0:T(8,128)S(1)} collective-permute-done((f32[8,128]{1,0:T(8,128)S(1)}, f32[8,128]{1,0:T(8,128)S(1)}, u32[]{:S(2)}, u32[]{:S(2)}) %collective-permute-start.4) | collective-permute-done | bytes 4128 | tf_op jit(solution)/shard_map/ppermute | solution.py:556
  13.8 3.6 %first_step.1 = (f32[64,128]{1,0:T(8,128)S(1)}, f32[64,32,128]{2,1,0:T(8,128)S(1)}, f32[64,32,128]{2,1,0:T(8,128)S(1)}, f32[8,128]{1,0:T(8,128)S(1)}, s32[8,128]{1,0:T(8,128)S(1)}) custom-call(bf16[1664,512]{1,0:T(8,128)(2,1)S(1)} %copy-done.5, f32[64,128]{1,0:T(8,128)S(1)} %get-tuple-element.25.plain, f32[64,128]{1,0:T(8,128)S(1)} %get-tuple-element.26.crossed, ...), custom_call_target="tpu_custom_call" | custom-call | flops 4294967296 | bytes 1048576 | tf_op jit(solution)/shard_map/first_step/pallas_call | solution.py:643
  17.6 0.5 %collective-permute-start.7 = (f32[64,128]{1,0:T(8,128)S(1)}, f32[64,128]{1,0:T(8,128)S(1)}, u32[]{:S(2)}, u32[]{:S(2)}) collective-permute-start(f32[64,128]{1,0:T(8,128)S(1)} %get-tuple-element.37.value), channel_id=1, source_target_pairs={{0,1},{1,0},{2,3},{3,2},{4,5},{5,4},{6,7},{7,6},{8,9},{9,8},{10,11... | collective-permute-start | bytes 98312 | tf_op jit(solution)/shard_map/ppermute | solution.py:556
  18.1 0.6 %collective-permute-start.8 = (f32[64,128]{1,0:T(8,128)S(1)}, f32[64,128]{1,0:T(8,128)S(1)}, u32[]{:S(2)}, u32[]{:S(2)}) collective-permute-start(f32[64,128]{1,0:T(8,128)S(1)} %get-tuple-element.37.value), channel_id=1, source_target_pairs={{0,2},{1,3},{2,0},{3,1},{4,6},{5,7},{6,4},{7,5},{8,10},{9,11},{10,... | collective-permute-start | bytes 98312 | tf_op jit(solution)/shard_map/ppermute | solution.py:556
  18.7 0.8 %collective-permute-start.9 = (f32[64,128]{1,0:T(8,128)S(1)}, f32[64,128]{1,0:T(8,128)S(1)}, u32[]{:S(2)}, u32[]{:S(2)}) collective-permute-start(f32[64,128]{1,0:T(8,128)S(1)} %get-tuple-element.37.value), channel_id=1, source_target_pairs={{0,3},{1,2},{2,1},{3,0},{4,7},{5,6},{6,5},{7,4},{8,11},{9,10},{10,... | collective-permute-start | bytes 98312 | tf_op jit(solution)/shard_map/ppermute | solution.py:556
  19.5 2.8 %collective-permute-done.8.refs_4_ = f32[64,128]{1,0:T(8,128)S(1)} collective-permute-done((f32[64,128]{1,0:T(8,128)S(1)}, f32[64,128]{1,0:T(8,128)S(1)}, u32[]{:S(2)}, u32[]{:S(2)}) %collective-permute-start.8) | collective-permute-done | bytes 32800 | tf_op jit(solution)/shard_map/ppermute | solution.py:556
  22.4 5.1 %next_step.1 = (f32[384,256]{1,0:T(8,128)S(1)}, f32[4,256,256]{2,1,0:T(8,128)S(1)}, f32[8,128]{1,0:T(8,128)S(1)}, f32[64,128]{1,0:T(8,128)S(1)}) custom-call(s32[1]{0:T(128)} %bitcast.tile, bf16[1664,512]{1,0:T(8,128)(2,1)S(1)} %copy-done.5, s32[8,128]{1,0:T(8,128)S(1)} %get-tuple-element.31.shifts, f32[8,128]{1,0:T(8,128)S(1)} %get-tuple-element.32.info, ...), custom_call_target="tpu_custom_call" | custom-call | flops 4294967296 | bytes 1048576 | tf_op jit(solution)/shard_map/next_step/pallas_call | solution.py:676
  27.6 1.3 %collective-permute-start.11 = (f32[64,128]{1,0:T(8,128)S(1)}, f32[64,128]{1,0:T(8,128)S(1)}, u32[]{:S(2)}, u32[]{:S(2)}) collective-permute-start(f32[64,128]{1,0:T(8,128)S(1)} %get-tuple-element.43.refs_0_), channel_id=1, source_target_pairs={{0,2},{1,3},{2,0},{3,1},{4,6},{5,7},{6,4},{7,5},{8,10},{9,11},{10,... | collective-permute-start | bytes 98312 | tf_op jit(solution)/shard_map/ppermute | solution.py:556
  29.0 0.4 collective-permute-start.12
  29.7 1.9 %collective-permute-done.11.refs_2_ = f32[64,128]{1,0:T(8,128)S(1)} collective-permute-done((f32[64,128]{1,0:T(8,128)S(1)}, f32[64,128]{1,0:T(8,128)S(1)}, u32[]{:S(2)}, u32[]{:S(2)}) %collective-permute-start.11) | collective-permute-done | bytes 32800 | tf_op jit(solution)/shard_map/ppermute | solution.py:556
  31.5 0.8 %collective-permute-done.12.refs_3_ = f32[64,128]{1,0:T(8,128)S(1)} collective-permute-done((f32[64,128]{1,0:T(8,128)S(1)}, f32[64,128]{1,0:T(8,128)S(1)}, u32[]{:S(2)}, u32[]{:S(2)}) %collective-permute-start.12) | collective-permute-done | bytes 32800 | tf_op jit(solution)/shard_map/ppermute | solution.py:556
  32.4 4.0 %last_step.1 = (f32[256,256]{1,0:T(8,128)}, f32[8,64]{1,0:T(8,128)S(1)}) custom-call(s32[1]{0:T(128)} %bitcast.tile, bf16[1664,512]{1,0:T(8,128)(2,1)S(1)} %copy-done.5, s32[8,128]{1,0:T(8,128)S(1)} %get-tuple-element.31.shifts, f32[8,128]{1,0:T(8,128)S(1)} %get-tuple-element.32.info, f32[64,32,128]{2,1,0:T(8,128)S(1)} %get-tuple-element.33.pr, ...), custom_call_target="tpu_custom_call" | custom-call | flops 4294967296 | bytes 1048576 | tf_op jit(solution)/shard_map/last_step/pallas_call | solution.py:698
  36.5 1.0 %collective-permute-start.14 = (f32[8,64]{1,0:T(8,128)S(1)}, f32[8,64]{1,0:T(8,128)S(1)}, u32[]{:S(2)}, u32[]{:S(2)}) collective-permute-start(f32[8,64]{1,0:T(8,128)S(1)} %get-tuple-element.45.refs_0_), channel_id=1, source_target_pairs={{0,2},{1,3},{2,0},{3,1},{4,6},{5,7},{6,4},{7,5},{8,10},{9,11},{10,... | collective-permute-start | bytes 6152 | tf_op jit(solution)/shard_map/ppermute | solution.py:556
  37.5 0.8 %collective-permute-start.15 = (f32[8,64]{1,0:T(8,128)S(1)}, f32[8,64]{1,0:T(8,128)S(1)}, u32[]{:S(2)}, u32[]{:S(2)}) collective-permute-start(f32[8,64]{1,0:T(8,128)S(1)} %get-tuple-element.45.refs_0_), channel_id=1, source_target_pairs={{0,3},{1,2},{2,1},{3,0},{4,7},{5,6},{6,5},{7,4},{8,11},{9,10},{10,... | collective-permute-start | bytes 6152 | tf_op jit(solution)/shard_map/ppermute | solution.py:556
  38.2 1.9 %collective-permute-done.14.refs_2_ = f32[8,64]{1,0:T(8,128)S(1)} collective-permute-done((f32[8,64]{1,0:T(8,128)S(1)}, f32[8,64]{1,0:T(8,128)S(1)}, u32[]{:S(2)}, u32[]{:S(2)}) %collective-permute-start.14) | collective-permute-done | bytes 2080 | tf_op jit(solution)/shard_map/ppermute | solution.py:556
  40.1 0.4 collective-permute-done.15.refs_3_
  40.5 0.8 %weight_step.1 = f32[1,16]{1,0:T(1,128)} custom-call(s32[1]{0:T(128)} %bitcast.tile, s32[1]{0:T(128)} %bitcast.1.place, f32[8,128]{1,0:T(8,128)S(1)} %get-tuple-element.32.info, f32[8,64]{1,0:T(8,128)S(1)} %get-tuple-element.45.refs_0_, f32[8,64]{1,0:T(8,128)S(1)} %collective-permute-done.13.refs_1_, f32[8,64]{1,0:T(8,128)S(1)} %collective-permute-done.14.refs_2_, ...), custom_call_target="tpu_custom_call" | custom-call | tf_op jit(solution)/shard_map/weight_step/pallas_call | solution.py:713
  (29 shorter events, 1.6 us)
Async XLA Ops:
  0.6 8.6 %copy-start.5 = (bf16[1664,512]{1,0:T(8,128)(2,1)S(1)}, bf16[1664,512]{1,0:T(8,128)(2,1)}, u32[]{:S(2)}) copy-start(bf16[1664,512]{1,0:T(8,128)(2,1)} %constant.9.clone.table) | copy-start | bytes 5111812
  0.6 1.1 %copy-start = (f32[256,256]{1,0:T(8,128)S(1)}, f32[256,256]{1,0:T(8,128)}, u32[]{:S(2)}) copy-start(f32[256,256]{1,0:T(8,128)} %refs_0_.1) | copy-start | bytes 786436
  0.7 1.1 %copy-start.2 = (f32[16]{0:T(128)S(1)}, f32[16]{0:T(128)}, u32[]{:S(2)}) copy-start(f32[16]{0:T(128)} %param.8) | copy-start | bytes 196
  0.7 1.1 %copy-start.1 = (s32[16,2]{0,1:T(2,128)S(1)}, s32[16,2]{0,1:T(2,128)}, u32[]{:S(2)}) copy-start(s32[16,2]{0,1:T(2,128)} %param.9) | copy-start | bytes 388
  0.7 8.6 %copy-start.4 = (f32[2,32,32]{2,1,0:T(8,128)S(1)}, f32[2,32,32]{2,1,0:T(8,128)}, u32[]{:S(2)}) copy-start(f32[2,32,32]{2,1,0:T(8,128)} %pupil.1) | copy-start | bytes 24580
  0.7 8.6 %copy-start.3 = (f32[256,256]{1,0:T(8,128)S(1)}, f32[256,256]{1,0:T(8,128)}, u32[]{:S(2)}) copy-start(f32[256,256]{1,0:T(8,128)} %goal.1) | copy-start | bytes 786436
  0.7 8.6 %collective-permute-start = (f32[256,256]{1,0:T(8,128)}, f32[256,256]{1,0:T(8,128)S(1)}, u32[]{:S(2)}, u32[]{:S(2)}) collective-permute-start(f32[256,256]{1,0:T(8,128)} %refs_0_.1), channel_id=1, source_target_pairs={{0,1},{1,0},{2,3},{3,2},{4,5},{5,4},{6,7},{7,6},{8,9},{9,8},{10,11... | collective-permute-start | bytes 786440 | tf_op jit(solution)/shard_map/ppermute | solution.py:556
  1.8 6.8 %collective-permute-start.1 = (f32[64,256]{1,0:T(8,128)S(1)}, f32[64,256]{1,0:T(8,128)S(1)}, u32[]{:S(2)}, u32[]{:S(2)}) collective-permute-start(f32[64,256]{1,0:T(8,128)S(1)} %get-tuple-element.24), channel_id=1, source_target_pairs={{1,2},{3,0},{2,1},{0,3},{5,6},{7,4},{6,5},{4,7},{9,10},{11,8},{10,... | collective-permute-start | bytes 196616 | tf_op jit(solution)/shard_map/ppermute | solution.py:612
  4.2 5.7 %collective-permute-start.2 = (f32[8,128]{1,0:T(8,128)S(1)}, f32[8,128]{1,0:T(8,128)S(1)}, u32[]{:S(2)}, u32[]{:S(2)}) collective-permute-start(f32[8,128]{1,0:T(8,128)S(1)} %get-tuple-element.30.refs_0_), channel_id=1, source_target_pairs={{0,4},{4,0},{8,12},{12,8},{1,5},{5,1},{9,13},{13,9},{2,6},{6,2},{1... | collective-permute-start | bytes 12296 | tf_op jit(solution)/shard_map/ppermute | solution.py:556
  5.8 4.5 %collective-permute-start.3 = (f32[8,128]{1,0:T(8,128)S(1)}, f32[8,128]{1,0:T(8,128)S(1)}, u32[]{:S(2)}, u32[]{:S(2)}) collective-permute-start(f32[8,128]{1,0:T(8,128)S(1)} %get-tuple-element.30.refs_0_), channel_id=1, source_target_pairs={{0,8},{4,12},{8,0},{12,4},{1,9},{5,13},{9,1},{13,5},{2,10},{6,14},... | collective-permute-start | bytes 12296 | tf_op jit(solution)/shard_map/ppermute | solution.py:556
  8.4 5.4 %collective-permute-start.4 = (f32[8,128]{1,0:T(8,128)S(1)}, f32[8,128]{1,0:T(8,128)S(1)}, u32[]{:S(2)}, u32[]{:S(2)}) collective-permute-start(f32[8,128]{1,0:T(8,128)S(1)} %get-tuple-element.30.refs_0_), channel_id=1, source_target_pairs={{0,12},{4,8},{8,4},{12,0},{1,13},{5,9},{9,5},{13,1},{2,14},{6,10},... | collective-permute-start | bytes 12296 | tf_op jit(solution)/shard_map/ppermute | solution.py:556
  8.6 8.8 %collective-permute-start.5 = (f32[256,256]{1,0:T(8,128)S(1)}, f32[256,256]{1,0:T(8,128)S(1)}, u32[]{:S(2)}, u32[]{:S(2)}) collective-permute-start(f32[256,256]{1,0:T(8,128)S(1)} %copy-done), channel_id=1, source_target_pairs={{0,2},{1,3},{2,0},{3,1},{4,6},{5,7},{6,4},{7,5},{8,10},{9,11},{10,... | collective-permute-start | bytes 786440 | tf_op jit(solution)/shard_map/ppermute | solution.py:556
  17.5 4.9 %collective-permute-start.6 = (f32[256,256]{1,0:T(8,128)S(1)}, f32[256,256]{1,0:T(8,128)S(1)}, u32[]{:S(2)}, u32[]{:S(2)}) collective-permute-start(f32[256,256]{1,0:T(8,128)S(1)} %collective-permute-done.5.refs_0_.refs_2_), channel_id=1, source_target_pairs={{0,1},{1,0},{2,3},{3,2},{4,5},{5,4},{6,7},{7,6},{8,9},{9,8},{10,11... | collective-permute-start | bytes 786440 | tf_op jit(solution)/shard_map/ppermute | solution.py:556
  17.6 1.9 %collective-permute-start.7 = (f32[64,128]{1,0:T(8,128)S(1)}, f32[64,128]{1,0:T(8,128)S(1)}, u32[]{:S(2)}, u32[]{:S(2)}) collective-permute-start(f32[64,128]{1,0:T(8,128)S(1)} %get-tuple-element.37.value), channel_id=1, source_target_pairs={{0,1},{1,0},{2,3},{3,2},{4,5},{5,4},{6,7},{7,6},{8,9},{9,8},{10,11... | collective-permute-start | bytes 98312 | tf_op jit(solution)/shard_map/ppermute | solution.py:556
  18.1 4.2 %collective-permute-start.8 = (f32[64,128]{1,0:T(8,128)S(1)}, f32[64,128]{1,0:T(8,128)S(1)}, u32[]{:S(2)}, u32[]{:S(2)}) collective-permute-start(f32[64,128]{1,0:T(8,128)S(1)} %get-tuple-element.37.value), channel_id=1, source_target_pairs={{0,2},{1,3},{2,0},{3,1},{4,6},{5,7},{6,4},{7,5},{8,10},{9,11},{10,... | collective-permute-start | bytes 98312 | tf_op jit(solution)/shard_map/ppermute | solution.py:556
  18.7 3.7 %collective-permute-start.9 = (f32[64,128]{1,0:T(8,128)S(1)}, f32[64,128]{1,0:T(8,128)S(1)}, u32[]{:S(2)}, u32[]{:S(2)}) collective-permute-start(f32[64,128]{1,0:T(8,128)S(1)} %get-tuple-element.37.value), channel_id=1, source_target_pairs={{0,3},{1,2},{2,1},{3,0},{4,7},{5,6},{6,5},{7,4},{8,11},{9,10},{10,... | collective-permute-start | bytes 98312 | tf_op jit(solution)/shard_map/ppermute | solution.py:556
  27.4 2.2 %collective-permute-start.10 = (f32[64,128]{1,0:T(8,128)S(1)}, f32[64,128]{1,0:T(8,128)S(1)}, u32[]{:S(2)}, u32[]{:S(2)}) collective-permute-start(f32[64,128]{1,0:T(8,128)S(1)} %get-tuple-element.43.refs_0_), channel_id=1, source_target_pairs={{0,1},{1,0},{2,3},{3,2},{4,5},{5,4},{6,7},{7,6},{8,9},{9,8},{10,11... | collective-permute-start | bytes 98312 | tf_op jit(solution)/shard_map/ppermute | solution.py:556
  27.6 3.9 %collective-permute-start.11 = (f32[64,128]{1,0:T(8,128)S(1)}, f32[64,128]{1,0:T(8,128)S(1)}, u32[]{:S(2)}, u32[]{:S(2)}) collective-permute-start(f32[64,128]{1,0:T(8,128)S(1)} %get-tuple-element.43.refs_0_), channel_id=1, source_target_pairs={{0,2},{1,3},{2,0},{3,1},{4,6},{5,7},{6,4},{7,5},{8,10},{9,11},{10,... | collective-permute-start | bytes 98312 | tf_op jit(solution)/shard_map/ppermute | solution.py:556
  29.0 3.4 %collective-permute-start.12 = (f32[64,128]{1,0:T(8,128)S(1)}, f32[64,128]{1,0:T(8,128)S(1)}, u32[]{:S(2)}, u32[]{:S(2)}) collective-permute-start(f32[64,128]{1,0:T(8,128)S(1)} %get-tuple-element.43.refs_0_), channel_id=1, source_target_pairs={{0,3},{1,2},{2,1},{3,0},{4,7},{5,6},{6,5},{7,4},{8,11},{9,10},{10,... | collective-permute-start | bytes 98312 | tf_op jit(solution)/shard_map/ppermute | solution.py:556
  36.3 1.9 %collective-permute-start.13 = (f32[8,64]{1,0:T(8,128)S(1)}, f32[8,64]{1,0:T(8,128)S(1)}, u32[]{:S(2)}, u32[]{:S(2)}) collective-permute-start(f32[8,64]{1,0:T(8,128)S(1)} %get-tuple-element.45.refs_0_), channel_id=1, source_target_pairs={{0,1},{1,0},{2,3},{3,2},{4,5},{5,4},{6,7},{7,6},{8,9},{9,8},{10,11... | collective-permute-start | bytes 6152 | tf_op jit(solution)/shard_map/ppermute | solution.py:556
  36.5 3.6 %collective-permute-start.14 = (f32[8,64]{1,0:T(8,128)S(1)}, f32[8,64]{1,0:T(8,128)S(1)}, u32[]{:S(2)}, u32[]{:S(2)}) collective-permute-start(f32[8,64]{1,0:T(8,128)S(1)} %get-tuple-element.45.refs_0_), channel_id=1, source_target_pairs={{0,2},{1,3},{2,0},{3,1},{4,6},{5,7},{6,4},{7,5},{8,10},{9,11},{10,... | collective-permute-start | bytes 6152 | tf_op jit(solution)/shard_map/ppermute | solution.py:556
  37.5 3.0 %collective-permute-start.15 = (f32[8,64]{1,0:T(8,128)S(1)}, f32[8,64]{1,0:T(8,128)S(1)}, u32[]{:S(2)}, u32[]{:S(2)}) collective-permute-start(f32[8,64]{1,0:T(8,128)S(1)} %get-tuple-element.45.refs_0_), channel_id=1, source_target_pairs={{0,3},{1,2},{2,1},{3,0},{4,7},{5,6},{6,5},{7,4},{8,11},{9,10},{10,... | collective-permute-start | bytes 6152 | tf_op jit(solution)/shard_map/ppermute | solution.py:556

commit v10 on v9

--- a/solution.py
+++ b/solution.py
@@ -369,15 +369,18 @@
     out[...] = value[...]
 
 
-def pack_kernel(tile, place, head, weights, shifts, mask, packed, edge):
-    at = pl.multiple_of(lax.rem(tile[0], 2) * (mask.shape[0] - MARGIN), MARGIN)
-    edge[...] = mask[pl.ds(at, MARGIN), :]
+def pack_kernel(place, head, weights, shifts, packed):
     local = weights.shape[1]
     packed[...] = head[...]
     packed[0:1, :local] = weights[...]
     packed[1:3, :local] = shifts[...].astype(f32)
     packed[3:4, :local] = jnp.sqrt(weights[...])
     packed[...] = pltpu.roll(packed[...], place[0] * local, 1)
+
+
+def edge_kernel(tile, mask, edge):
+    at = pl.multiple_of(lax.rem(tile[0], 2) * (mask.shape[0] - MARGIN), MARGIN)
+    edge[...] = mask[pl.ds(at, MARGIN), :]
 
 
 def target_terms(target, t):
@@ -597,15 +600,25 @@
         cost_estimate=cost(1 << 34),
         name="head_step",
     )()
-    packed, edge = pl.pallas_call(
+    packed = pl.pallas_call(
         pack_kernel,
-        out_shape=[struct(8, 128), struct(MARGIN, tile_len)],
-        in_specs=[smem, smem] + [vmem] * 4,
-        out_specs=[vmem] * 2,
+        out_shape=struct(8, 128),
+        in_specs=[smem] + [vmem] * 3,
+        out_specs=vmem,
         compiler_params=params_of,
         cost_estimate=cost(1 << 20),
         name="pack_sources",
-    )(tile, place, head, source_weights[None], source_shifts.T, mask_param)
+    )(place, head, source_weights[None], source_shifts.T)
+    _, mask_now = lax.optimization_barrier((packed, mask_param))
+    edge = pl.pallas_call(
+        edge_kernel,
+        out_shape=struct(MARGIN, tile_len),
+        in_specs=[smem, vmem],
+        out_specs=vmem,
+        compiler_params=params_of,
+        cost_estimate=cost(1 << 20),
+        name="edge_rows",
+    )(tile, mask_now)
     packed = all_of(packed, "src")
 
     pairs = [(i, (i + 1) % tiles) for i in range(1, tiles, 2)]

time: 41.4 us -> 41.4 us (level)
  no operation moved by 1% of the time
where the time goes in v10:
time: 41.4 us; the launch traced here: 41.2 us
  Pallas kernels  14.4 us (35%)
  starting transfers between devices  13.9 us (34%)
  waiting for transfers between devices  11.7 us (28%)
  between operations  0.78 us (2%)
  local copies, waits for them, and re-layouts  0.44 us (1%)
    ppermute x15, waiting for transfers between devices, crossed(): lax.ppermute(value, axis, [(i, i ^ k) for i in range(lax.axis_size(axis))])  11.7 us
    ppermute x15, starting transfers between devices, crossed(): lax.ppermute(value, axis, [(i, i ^ k) for i in range(lax.axis_size(axis))])  11.4 us
    pallas_call x1, Pallas kernels, per_device(): pl.pallas_call(functools.partial(next_kernel, spots, tiles, scale), out_s...  5.05 us
    pallas_call x1, Pallas kernels, per_device(): pl.pallas_call(functools.partial(last_kernel, spots, tiles), out_shape=[s...  3.93 us
    pallas_call x1, Pallas kernels, per_device(): pl.pallas_call(functools.partial(first_kernel, spots, peers, scale), out_...  3.65 us
    ppermute x1, starting transfers between devices, per_device(): cross = lax.ppermute(edge, 'tile', pairs + [(j, i) for i, j in pairs])  2.43 us
  transfers between devices with their start and end apart: 16, of which 8 were waited for; matrix products, arithmetic and copies ran while one was open for 0% of the time, Pallas kernels for 11%

profile of v10, /device:TPU:0, one launch (start us, length us, event | category | flops | bytes accessed | tf_op | source)
XLA Modules:
  0.0 41.2 jit_solution(8736213728596597334)
XLA Ops:
  0.7 0.6 %collective-permute-start = (f32[256,256]{1,0:T(8,128)}, f32[256,256]{1,0:T(8,128)S(1)}, u32[]{:S(2)}, u32[]{:S(2)}) collective-permute-start(f32[256,256]{1,0:T(8,128)} %refs_0_.1), channel_id=1, source_target_pairs={{0,1},{1,0},{2,3},{3,2},{4,5},{5,4},{6,7},{7,6},{8,9},{9,8},{10,11... | collective-permute-start | bytes 786440 | tf_op jit(solution)/shard_map/ppermute | solution.py:559
  1.8 2.4 %collective-permute-start.1 = (f32[64,256]{1,0:T(8,128)S(1)}, f32[64,256]{1,0:T(8,128)S(1)}, u32[]{:S(2)}, u32[]{:S(2)}) collective-permute-start(f32[64,256]{1,0:T(8,128)S(1)} %edge_rows.1), channel_id=1, source_target_pairs={{1,2},{3,0},{2,1},{0,3},{5,6},{7,4},{6,5},{4,7},{9,10},{11,8},{10,... | collective-permute-start | bytes 196616 | tf_op jit(solution)/shard_map/ppermute | solution.py:625
  4.2 1.6 %collective-permute-start.2 = (f32[8,128]{1,0:T(8,128)S(1)}, f32[8,128]{1,0:T(8,128)S(1)}, u32[]{:S(2)}, u32[]{:S(2)}) collective-permute-start(f32[8,128]{1,0:T(8,128)S(1)} %pack_sources.1.refs_0_), channel_id=1, source_target_pairs={{0,4},{4,0},{8,12},{12,8},{1,5},{5,1},{9,13},{13,9},{2,6},{6,2},{1... | collective-permute-start | bytes 12296 | tf_op jit(solution)/shard_map/ppermute | solution.py:559
  5.8 2.6 %collective-permute-start.3 = (f32[8,128]{1,0:T(8,128)S(1)}, f32[8,128]{1,0:T(8,128)S(1)}, u32[]{:S(2)}, u32[]{:S(2)}) collective-permute-start(f32[8,128]{1,0:T(8,128)S(1)} %pack_sources.1.refs_0_), channel_id=1, source_target_pairs={{0,8},{4,12},{8,0},{12,4},{1,9},{5,13},{9,1},{13,5},{2,10},{6,14},... | collective-permute-start | bytes 12296 | tf_op jit(solution)/shard_map/ppermute | solution.py:559
  8.6 0.6 %collective-permute-start.5 = (f32[256,256]{1,0:T(8,128)S(1)}, f32[256,256]{1,0:T(8,128)S(1)}, u32[]{:S(2)}, u32[]{:S(2)}) collective-permute-start(f32[256,256]{1,0:T(8,128)S(1)} %copy-done), channel_id=1, source_target_pairs={{0,2},{1,3},{2,0},{3,1},{4,6},{5,7},{6,4},{7,5},{8,10},{9,11},{10,... | collective-permute-start | bytes 786440 | tf_op jit(solution)/shard_map/ppermute | solution.py:559
  9.2 0.7 %ready_step.1 = (f32[64,128]{1,0:T(8,128)S(1)}, f32[64,128]{1,0:T(8,128)S(1)}, f32[64,128]{1,0:T(8,128)S(1)}, f32[33,32,128]{2,1,0:T(8,128)S(1)}, f32[33,32,128]...) custom-call(s32[1]{0:T(128)} %bitcast.tile, bf16[1664,512]{1,0:T(8,128)(2,1)S(1)} %copy-done.5, ...), custom_call_target="tpu_custom_call" | custom-call | flops 1073741824 | bytes 1048576 | tf_op jit(solution)/shard_map/ready_step/pallas_call | solution.py:644
  9.9 0.4 collective-permute-done.3.refs_2_
  10.3 3.5 %collective-permute-done.4.refs_3_ = f32[8,128]{1,0:T(8,128)S(1)} collective-permute-done((f32[8,128]{1,0:T(8,128)S(1)}, f32[8,128]{1,0:T(8,128)S(1)}, u32[]{:S(2)}, u32[]{:S(2)}) %collective-permute-start.4) | collective-permute-done | bytes 4128 | tf_op jit(solution)/shard_map/ppermute | solution.py:559
  13.8 3.6 %first_step.1 = (f32[64,128]{1,0:T(8,128)S(1)}, f32[64,32,128]{2,1,0:T(8,128)S(1)}, f32[64,32,128]{2,1,0:T(8,128)S(1)}, f32[8,128]{1,0:T(8,128)S(1)}, s32[8,128]{1,0:T(8,128)S(1)}) custom-call(bf16[1664,512]{1,0:T(8,128)(2,1)S(1)} %copy-done.5, f32[64,128]{1,0:T(8,128)S(1)} %get-tuple-element.24.plain, f32[64,128]{1,0:T(8,128)S(1)} %get-tuple-element.25.crossed, ...), custom_call_target="tpu_custom_call" | custom-call | flops 4294967296 | bytes 1048576 | tf_op jit(solution)/shard_map/first_step/pallas_call | solution.py:656
  17.5 0.5 %collective-permute-start.7 = (f32[64,128]{1,0:T(8,128)S(1)}, f32[64,128]{1,0:T(8,128)S(1)}, u32[]{:S(2)}, u32[]{:S(2)}) collective-permute-start(f32[64,128]{1,0:T(8,128)S(1)} %get-tuple-element.35.value), channel_id=1, source_target_pairs={{0,1},{1,0},{2,3},{3,2},{4,5},{5,4},{6,7},{7,6},{8,9},{9,8},{10,11... | collective-permute-start | bytes 98312 | tf_op jit(solution)/shard_map/ppermute | solution.py:559
  18.0 0.6 %collective-permute-start.8 = (f32[64,128]{1,0:T(8,128)S(1)}, f32[64,128]{1,0:T(8,128)S(1)}, u32[]{:S(2)}, u32[]{:S(2)}) collective-permute-start(f32[64,128]{1,0:T(8,128)S(1)} %get-tuple-element.35.value), channel_id=1, source_target_pairs={{0,2},{1,3},{2,0},{3,1},{4,6},{5,7},{6,4},{7,5},{8,10},{9,11},{10,... | collective-permute-start | bytes 98312 | tf_op jit(solution)/shard_map/ppermute | solution.py:559
  18.6 0.8 %collective-permute-start.9 = (f32[64,128]{1,0:T(8,128)S(1)}, f32[64,128]{1,0:T(8,128)S(1)}, u32[]{:S(2)}, u32[]{:S(2)}) collective-permute-start(f32[64,128]{1,0:T(8,128)S(1)} %get-tuple-element.35.value), channel_id=1, source_target_pairs={{0,3},{1,2},{2,1},{3,0},{4,7},{5,6},{6,5},{7,4},{8,11},{9,10},{10,... | collective-permute-start | bytes 98312 | tf_op jit(solution)/shard_map/ppermute | solution.py:559
  19.4 2.8 %collective-permute-done.8.refs_4_ = f32[64,128]{1,0:T(8,128)S(1)} collective-permute-done((f32[64,128]{1,0:T(8,128)S(1)}, f32[64,128]{1,0:T(8,128)S(1)}, u32[]{:S(2)}, u32[]{:S(2)}) %collective-permute-start.8) | collective-permute-done | bytes 32800 | tf_op jit(solution)/shard_map/ppermute | solution.py:559
  22.3 5.1 %next_step.1 = (f32[384,256]{1,0:T(8,128)S(1)}, f32[4,256,256]{2,1,0:T(8,128)S(1)}, f32[8,128]{1,0:T(8,128)S(1)}, f32[64,128]{1,0:T(8,128)S(1)}) custom-call(s32[1]{0:T(128)} %bitcast.tile, bf16[1664,512]{1,0:T(8,128)(2,1)S(1)} %copy-done.5, s32[8,128]{1,0:T(8,128)S(1)} %get-tuple-element.29.shifts, f32[8,128]{1,0:T(8,128)S(1)} %get-tuple-element.30.info, ...), custom_call_target="tpu_custom_call" | custom-call | flops 4294967296 | bytes 1048576 | tf_op jit(solution)/shard_map/next_step/pallas_call | solution.py:689
  27.6 1.3 %collective-permute-start.11 = (f32[64,128]{1,0:T(8,128)S(1)}, f32[64,128]{1,0:T(8,128)S(1)}, u32[]{:S(2)}, u32[]{:S(2)}) collective-permute-start(f32[64,128]{1,0:T(8,128)S(1)} %get-tuple-element.41.refs_0_), channel_id=1, source_target_pairs={{0,2},{1,3},{2,0},{3,1},{4,6},{5,7},{6,4},{7,5},{8,10},{9,11},{10,... | collective-permute-start | bytes 98312 | tf_op jit(solution)/shard_map/ppermute | solution.py:559
  28.9 0.4 collective-permute-start.12
  29.6 1.9 %collective-permute-done.11.refs_2_ = f32[64,128]{1,0:T(8,128)S(1)} collective-permute-done((f32[64,128]{1,0:T(8,128)S(1)}, f32[64,128]{1,0:T(8,128)S(1)}, u32[]{:S(2)}, u32[]{:S(2)}) %collective-permute-start.11) | collective-permute-done | bytes 32800 | tf_op jit(solution)/shard_map/ppermute | solution.py:559
  31.5 0.8 %collective-permute-done.12.refs_3_ = f32[64,128]{1,0:T(8,128)S(1)} collective-permute-done((f32[64,128]{1,0:T(8,128)S(1)}, f32[64,128]{1,0:T(8,128)S(1)}, u32[]{:S(2)}, u32[]{:S(2)}) %collective-permute-start.12) | collective-permute-done | bytes 32800 | tf_op jit(solution)/shard_map/ppermute | solution.py:559
  32.3 3.9 %last_step.1 = (f32[256,256]{1,0:T(8,128)}, f32[8,64]{1,0:T(8,128)S(1)}) custom-call(s32[1]{0:T(128)} %bitcast.tile, bf16[1664,512]{1,0:T(8,128)(2,1)S(1)} %copy-done.5, s32[8,128]{1,0:T(8,128)S(1)} %get-tuple-element.29.shifts, f32[8,128]{1,0:T(8,128)S(1)} %get-tuple-element.30.info, f32[64,32,128]{2,1,0:T(8,128)S(1)} %get-tuple-element.31.pr, ...), custom_call_target="tpu_custom_call" | custom-call | flops 4294967296 | bytes 1048576 | tf_op jit(solution)/shard_map/last_step/pallas_call | solution.py:711
  36.4 1.0 %collective-permute-start.14 = (f32[8,64]{1,0:T(8,128)S(1)}, f32[8,64]{1,0:T(8,128)S(1)}, u32[]{:S(2)}, u32[]{:S(2)}) collective-permute-start(f32[8,64]{1,0:T(8,128)S(1)} %get-tuple-element.43.refs_0_), channel_id=1, source_target_pairs={{0,2},{1,3},{2,0},{3,1},{4,6},{5,7},{6,4},{7,5},{8,10},{9,11},{10,... | collective-permute-start | bytes 6152 | tf_op jit(solution)/shard_map/ppermute | solution.py:559
  37.4 0.7 %collective-permute-start.15 = (f32[8,64]{1,0:T(8,128)S(1)}, f32[8,64]{1,0:T(8,128)S(1)}, u32[]{:S(2)}, u32[]{:S(2)}) collective-permute-start(f32[8,64]{1,0:T(8,128)S(1)} %get-tuple-element.43.refs_0_), channel_id=1, source_target_pairs={{0,3},{1,2},{2,1},{3,0},{4,7},{5,6},{6,5},{7,4},{8,11},{9,10},{10,... | collective-permute-start | bytes 6152 | tf_op jit(solution)/shard_map/ppermute | solution.py:559
  38.2 1.9 %collective-permute-done.14.refs_2_ = f32[8,64]{1,0:T(8,128)S(1)} collective-permute-done((f32[8,64]{1,0:T(8,128)S(1)}, f32[8,64]{1,0:T(8,128)S(1)}, u32[]{:S(2)}, u32[]{:S(2)}) %collective-permute-start.14) | collective-permute-done | bytes 2080 | tf_op jit(solution)/shard_map/ppermute | solution.py:559
  40.0 0.4 collective-permute-done.15.refs_3_
  40.5 0.8 %weight_step.1 = f32[1,16]{1,0:T(1,128)} custom-call(s32[1]{0:T(128)} %bitcast.tile, s32[1]{0:T(128)} %bitcast.1.place, f32[8,128]{1,0:T(8,128)S(1)} %get-tuple-element.30.info, f32[8,64]{1,0:T(8,128)S(1)} %get-tuple-element.43.refs_0_, f32[8,64]{1,0:T(8,128)S(1)} %collective-permute-done.13.refs_1_, f32[8,64]{1,0:T(8,128)S(1)} %collective-permute-done.14.refs_2_, ...), custom_call_target="tpu_custom_call" | custom-call | tf_op jit(solution)/shard_map/weight_step/pallas_call | solution.py:726
  (30 shorter events, 1.6 us)
Async XLA Ops:
  0.6 8.6 %copy-start.5 = (bf16[1664,512]{1,0:T(8,128)(2,1)S(1)}, bf16[1664,512]{1,0:T(8,128)(2,1)}, u32[]{:S(2)}) copy-start(bf16[1664,512]{1,0:T(8,128)(2,1)} %constant.9.clone.table) | copy-start | bytes 5111812
  0.6 1.1 %copy-start = (f32[256,256]{1,0:T(8,128)S(1)}, f32[256,256]{1,0:T(8,128)}, u32[]{:S(2)}) copy-start(f32[256,256]{1,0:T(8,128)} %refs_0_.1) | copy-start | bytes 786436
  0.7 0.8 %copy-start.2 = (f32[16]{0:T(128)S(1)}, f32[16]{0:T(128)}, u32[]{:S(2)}) copy-start(f32[16]{0:T(128)} %param.8) | copy-start | bytes 196
  0.7 0.8 %copy-start.1 = (s32[16,2]{0,1:T(2,128)S(1)}, s32[16,2]{0,1:T(2,128)}, u32[]{:S(2)}) copy-start(s32[16,2]{0,1:T(2,128)} %param.9) | copy-start | bytes 388
  0.7 8.6 %copy-start.4 = (f32[2,32,32]{2,1,0:T(8,128)S(1)}, f32[2,32,32]{2,1,0:T(8,128)}, u32[]{:S(2)}) copy-start(f32[2,32,32]{2,1,0:T(8,128)} %pupil.1) | copy-start | bytes 24580
  0.7 8.5 %copy-start.3 = (f32[256,256]{1,0:T(8,128)S(1)}, f32[256,256]{1,0:T(8,128)}, u32[]{:S(2)}) copy-start(f32[256,256]{1,0:T(8,128)} %goal.1) | copy-start | bytes 786436
  0.7 8.5 %collective-permute-start = (f32[256,256]{1,0:T(8,128)}, f32[256,256]{1,0:T(8,128)S(1)}, u32[]{:S(2)}, u32[]{:S(2)}) collective-permute-start(f32[256,256]{1,0:T(8,128)} %refs_0_.1), channel_id=1, source_target_pairs={{0,1},{1,0},{2,3},{3,2},{4,5},{5,4},{6,7},{7,6},{8,9},{9,8},{10,11... | collective-permute-start | bytes 786440 | tf_op jit(solution)/shard_map/ppermute | solution.py:559
  1.8 6.8 %collective-permute-start.1 = (f32[64,256]{1,0:T(8,128)S(1)}, f32[64,256]{1,0:T(8,128)S(1)}, u32[]{:S(2)}, u32[]{:S(2)}) collective-permute-start(f32[64,256]{1,0:T(8,128)S(1)} %edge_rows.1), channel_id=1, source_target_pairs={{1,2},{3,0},{2,1},{0,3},{5,6},{7,4},{6,5},{4,7},{9,10},{11,8},{10,... | collective-permute-start | bytes 196616 | tf_op jit(solution)/shard_map/ppermute | solution.py:625
  4.2 5.7 %collective-permute-start.2 = (f32[8,128]{1,0:T(8,128)S(1)}, f32[8,128]{1,0:T(8,128)S(1)}, u32[]{:S(2)}, u32[]{:S(2)}) collective-permute-start(f32[8,128]{1,0:T(8,128)S(1)} %pack_sources.1.refs_0_), channel_id=1, source_target_pairs={{0,4},{4,0},{8,12},{12,8},{1,5},{5,1},{9,13},{13,9},{2,6},{6,2},{1... | collective-permute-start | bytes 12296 | tf_op jit(solution)/shard_map/ppermute | solution.py:559
  5.8 4.5 %collective-permute-start.3 = (f32[8,128]{1,0:T(8,128)S(1)}, f32[8,128]{1,0:T(8,128)S(1)}, u32[]{:S(2)}, u32[]{:S(2)}) collective-permute-start(f32[8,128]{1,0:T(8,128)S(1)} %pack_sources.1.refs_0_), channel_id=1, source_target_pairs={{0,8},{4,12},{8,0},{12,4},{1,9},{5,13},{9,1},{13,5},{2,10},{6,14},... | collective-permute-start | bytes 12296 | tf_op jit(solution)/shard_map/ppermute | solution.py:559
  8.4 5.4 %collective-permute-start.4 = (f32[8,128]{1,0:T(8,128)S(1)}, f32[8,128]{1,0:T(8,128)S(1)}, u32[]{:S(2)}, u32[]{:S(2)}) collective-permute-start(f32[8,128]{1,0:T(8,128)S(1)} %pack_sources.1.refs_0_), channel_id=1, source_target_pairs={{0,12},{4,8},{8,4},{12,0},{1,13},{5,9},{9,5},{13,1},{2,14},{6,10},... | collective-permute-start | bytes 12296 | tf_op jit(solution)/shard_map/ppermute | solution.py:559
  8.6 8.8 %collective-permute-start.5 = (f32[256,256]{1,0:T(8,128)S(1)}, f32[256,256]{1,0:T(8,128)S(1)}, u32[]{:S(2)}, u32[]{:S(2)}) collective-permute-start(f32[256,256]{1,0:T(8,128)S(1)} %copy-done), channel_id=1, source_target_pairs={{0,2},{1,3},{2,0},{3,1},{4,6},{5,7},{6,4},{7,5},{8,10},{9,11},{10,... | collective-permute-start | bytes 786440 | tf_op jit(solution)/shard_map/ppermute | solution.py:559
  17.4 4.9 %collective-permute-start.6 = (f32[256,256]{1,0:T(8,128)S(1)}, f32[256,256]{1,0:T(8,128)S(1)}, u32[]{:S(2)}, u32[]{:S(2)}) collective-permute-start(f32[256,256]{1,0:T(8,128)S(1)} %collective-permute-done.5.refs_0_.refs_2_), channel_id=1, source_target_pairs={{0,1},{1,0},{2,3},{3,2},{4,5},{5,4},{6,7},{7,6},{8,9},{9,8},{10,11... | collective-permute-start | bytes 786440 | tf_op jit(solution)/shard_map/ppermute | solution.py:559
  17.5 1.9 %collective-permute-start.7 = (f32[64,128]{1,0:T(8,128)S(1)}, f32[64,128]{1,0:T(8,128)S(1)}, u32[]{:S(2)}, u32[]{:S(2)}) collective-permute-start(f32[64,128]{1,0:T(8,128)S(1)} %get-tuple-element.35.value), channel_id=1, source_target_pairs={{0,1},{1,0},{2,3},{3,2},{4,5},{5,4},{6,7},{7,6},{8,9},{9,8},{10,11... | collective-permute-start | bytes 98312 | tf_op jit(solution)/shard_map/ppermute | solution.py:559
  18.0 4.2 %collective-permute-start.8 = (f32[64,128]{1,0:T(8,128)S(1)}, f32[64,128]{1,0:T(8,128)S(1)}, u32[]{:S(2)}, u32[]{:S(2)}) collective-permute-start(f32[64,128]{1,0:T(8,128)S(1)} %get-tuple-element.35.value), channel_id=1, source_target_pairs={{0,2},{1,3},{2,0},{3,1},{4,6},{5,7},{6,4},{7,5},{8,10},{9,11},{10,... | collective-permute-start | bytes 98312 | tf_op jit(solution)/shard_map/ppermute | solution.py:559
  18.6 3.7 %collective-permute-start.9 = (f32[64,128]{1,0:T(8,128)S(1)}, f32[64,128]{1,0:T(8,128)S(1)}, u32[]{:S(2)}, u32[]{:S(2)}) collective-permute-start(f32[64,128]{1,0:T(8,128)S(1)} %get-tuple-element.35.value), channel_id=1, source_target_pairs={{0,3},{1,2},{2,1},{3,0},{4,7},{5,6},{6,5},{7,4},{8,11},{9,10},{10,... | collective-permute-start | bytes 98312 | tf_op jit(solution)/shard_map/ppermute | solution.py:559
  27.4 2.2 %collective-permute-start.10 = (f32[64,128]{1,0:T(8,128)S(1)}, f32[64,128]{1,0:T(8,128)S(1)}, u32[]{:S(2)}, u32[]{:S(2)}) collective-permute-start(f32[64,128]{1,0:T(8,128)S(1)} %get-tuple-element.41.refs_0_), channel_id=1, source_target_pairs={{0,1},{1,0},{2,3},{3,2},{4,5},{5,4},{6,7},{7,6},{8,9},{9,8},{10,11... | collective-permute-start | bytes 98312 | tf_op jit(solution)/shard_map/ppermute | solution.py:559
  27.6 3.9 %collective-permute-start.11 = (f32[64,128]{1,0:T(8,128)S(1)}, f32[64,128]{1,0:T(8,128)S(1)}, u32[]{:S(2)}, u32[]{:S(2)}) collective-permute-start(f32[64,128]{1,0:T(8,128)S(1)} %get-tuple-element.41.refs_0_), channel_id=1, source_target_pairs={{0,2},{1,3},{2,0},{3,1},{4,6},{5,7},{6,4},{7,5},{8,10},{9,11},{10,... | collective-permute-start | bytes 98312 | tf_op jit(solution)/shard_map/ppermute | solution.py:559
  28.9 3.4 %collective-permute-start.12 = (f32[64,128]{1,0:T(8,128)S(1)}, f32[64,128]{1,0:T(8,128)S(1)}, u32[]{:S(2)}, u32[]{:S(2)}) collective-permute-start(f32[64,128]{1,0:T(8,128)S(1)} %get-tuple-element.41.refs_0_), channel_id=1, source_target_pairs={{0,3},{1,2},{2,1},{3,0},{4,7},{5,6},{6,5},{7,4},{8,11},{9,10},{10,... | collective-permute-start | bytes 98312 | tf_op jit(solution)/shard_map/ppermute | solution.py:559
  36.2 1.9 %collective-permute-start.13 = (f32[8,64]{1,0:T(8,128)S(1)}, f32[8,64]{1,0:T(8,128)S(1)}, u32[]{:S(2)}, u32[]{:S(2)}) collective-permute-start(f32[8,64]{1,0:T(8,128)S(1)} %get-tuple-element.43.refs_0_), channel_id=1, source_target_pairs={{0,1},{1,0},{2,3},{3,2},{4,5},{5,4},{6,7},{7,6},{8,9},{9,8},{10,11... | collective-permute-start | bytes 6152 | tf_op jit(solution)/shard_map/ppermute | solution.py:559
  36.4 3.6 %collective-permute-start.14 = (f32[8,64]{1,0:T(8,128)S(1)}, f32[8,64]{1,0:T(8,128)S(1)}, u32[]{:S(2)}, u32[]{:S(2)}) collective-permute-start(f32[8,64]{1,0:T(8,128)S(1)} %get-tuple-element.43.refs_0_), channel_id=1, source_target_pairs={{0,2},{1,3},{2,0},{3,1},{4,6},{5,7},{6,4},{7,5},{8,10},{9,11},{10,... | collective-permute-start | bytes 6152 | tf_op jit(solution)/shard_map/ppermute | solution.py:559
  37.4 3.0 %collective-permute-start.15 = (f32[8,64]{1,0:T(8,128)S(1)}, f32[8,64]{1,0:T(8,128)S(1)}, u32[]{:S(2)}, u32[]{:S(2)}) collective-permute-start(f32[8,64]{1,0:T(8,128)S(1)} %get-tuple-element.43.refs_0_), channel_id=1, source_target_pairs={{0,3},{1,2},{2,1},{3,0},{4,7},{5,6},{6,5},{7,4},{8,11},{9,10},{10,... | collective-permute-start | bytes 6152 | tf_op jit(solution)/shard_map/ppermute | solution.py:559
